TPU v7x, 128 devices: a whole 4x4x4 slice. The times are simulated.
128 devices in a mesh: req: 32 (over z, y, core), head: 4 (over x).
Axes of the slice: x: 4, y: 4, z: 4, core: 2. Of those that a mesh axis runs over, the one named last changes fastest.
Arguments:
- hidden_in: bfloat16 [512, 2048], P(None, 'req'), may hold values from -6 to 6
- lengths: int32 [512], P('req'), may hold values from 16 to 3072, as said below
- w_qkv: bfloat16 [3, 2048, 2048], P(None, 'req', 'head'), may hold values from -4 to 4, as said below
- qk_gain: float32 [2, 2048], P(None, 'head'), may hold values from 0.25 to 1.75
- cache_keys: bfloat16 [131072, 2048], P('req', 'head'), may hold values from -240 to 240
- cache_values: bfloat16 [131072, 2048], P('req', 'head'), may hold values from -6 to 6
- w_out: bfloat16 [2048, 2048], P('req', 'head'), may hold values from -3 to 3, as said below
- norm_gain: float32 [2, 2048], P(None, 'req'), may hold values from 0.25 to 1.75
- w_gate_up: bfloat16 [2, 2048, 8192], P(None, 'req', 'head'), may hold values from -0.125 to 0.125
- w_down: bfloat16 [2048, 8192], P('req', 'head'), may hold values from -3 to 3, as said below
Outputs:
- hidden_out: bfloat16 [512, 2048], P(None, 'req')
- new_keys: bfloat16 [512, 2048], P('req', 'head')
- new_values: bfloat16 [512, 2048], P('req', 'head')
Inputs may be any that keep to these rules, and one draw needn't show every extreme that they name: `lengths`: in each aligned group of requests 8 * 16 * k to 8 * 16 * k + 8 * 16 - 1 exactly one request, at a place drawn from the seed, has length 3072; every other length lies between 16 and 64. `w_qkv`: entries have magnitude at most 26 / sqrt(2048). `w_out`: entries have magnitude at most 23 / sqrt(2048). `w_down`: entries have magnitude at most 23 / sqrt(8192).
All inputs are finite; a program needn't handle non-finite values.
Results may differ from a plain program's by a relative error of at most 0.015.
Values may be sent and summed in bfloat16 or wider, within the bound.
No kernel may reach another device: no remote copies, remote signals or barrier semaphores. Data moves between devices by JAX's collectives and lax.ppermute only.
A program may use at most 128 MiB of HBM per device.

v0:
```python
import jax
import jax.numpy as jnp
from jax import lax
from jax.sharding import PartitionSpec as P

HEAD_DIM = 128


EPS = 1e-06
THETA = 500000.0


def rotate(values, positions):
    half = values.shape[-1] // 2
    freqs = jnp.power(THETA, -(jnp.arange(half, dtype=jnp.float32) * 2.0 / values.shape[-1]))
    angles = positions.astype(jnp.float32)[:, None] * freqs[None, :]
    cosine = jnp.cos(angles)[:, None, :]
    sine = jnp.sin(angles)[:, None, :]
    first = values[..., :half]
    second = values[..., half:]
    return jnp.concatenate(
        [first * cosine - second * sine, second * cosine + first * sine], axis=-1
    )


def contract_last(left, right):
    return lax.dot_general(
        left, right, (((1,), (1,)), ((), ())), preferred_element_type=jnp.float32
    )


def body(
    hidden_in,
    lengths,
    w_qkv,
    qk_gain,
    cache_keys,
    cache_values,
    w_out,
    norm_gain,
    w_gate_up,
    w_down,
):
    rows_here = lengths.shape[0]
    width_here = w_qkv.shape[2]
    heads_here = width_here // HEAD_DIM
    units_here = w_gate_up.shape[2]
    full_width = width_here * lax.axis_size("head")
    model_width = hidden_in.shape[1] * lax.axis_size("req")
    selected = hidden_in
    product = jnp.einsum("bd,gdf->bgf", selected, w_qkv, preferred_element_type=jnp.float32)
    projected = lax.psum_scatter(
        product.reshape(rows_here * lax.axis_size("req"), 3 * width_here),
        "req",
        scatter_dimension=0,
        tiled=True,
    )
    query = projected[:, :width_here]
    key_new = projected[:, width_here : 2 * width_here]
    value_new = projected[:, 2 * width_here :].astype(jnp.bfloat16)
    query_squares, key_squares = lax.psum(
        (jnp.sum(query * query, axis=1), jnp.sum(key_new * key_new, axis=1)), "head"
    )
    query = query * lax.rsqrt(query_squares[:, None] / full_width + EPS) * qk_gain[0]
    key_new = key_new * lax.rsqrt(key_squares[:, None] / full_width + EPS) * qk_gain[1]
    query_rot = rotate(query.reshape(rows_here, heads_here, HEAD_DIM), lengths).astype(jnp.bfloat16)
    key_rot = rotate(key_new.reshape(rows_here, heads_here, HEAD_DIM), lengths).astype(jnp.bfloat16)
    value_heads = value_new.reshape(rows_here, heads_here, HEAD_DIM)
    scale = HEAD_DIM ** (-0.5)
    starts = jnp.cumsum(lengths) - lengths
    ends = starts + lengths
    own_score = jnp.sum(query_rot.astype(jnp.float32) * key_rot.astype(jnp.float32), axis=2) * scale
    pool_rows = cache_keys.shape[0]
    block = 512

    def attend_block(index, carry):
        running_max, running_total, running_sum = carry
        offset = index * block
        block_keys = lax.dynamic_slice_in_dim(cache_keys, offset, block, 0).reshape(
            block, heads_here, HEAD_DIM
        )
        block_values = lax.dynamic_slice_in_dim(cache_values, offset, block, 0).reshape(
            block, heads_here, HEAD_DIM
        )
        scores = (
            jnp.einsum("rhd,phd->rhp", query_rot, block_keys, preferred_element_type=jnp.float32)
            * scale
        )
        positions = offset + jnp.arange(block, dtype=jnp.int32)
        inside = (positions[None, :] >= starts[:, None]) & (positions[None, :] < ends[:, None])
        scores = jnp.where(inside[:, None, :], scores, -jnp.inf)
        new_max = jnp.maximum(running_max, jnp.max(scores, axis=2))
        weights = jnp.exp(scores - new_max[:, :, None]).astype(jnp.bfloat16)
        factor = jnp.exp(running_max - new_max)
        running_total = running_total * factor + jnp.sum(weights.astype(jnp.float32), axis=2)
        running_sum = running_sum * factor[:, :, None] + jnp.einsum(
            "rhp,phd->rhd", weights, block_values, preferred_element_type=jnp.float32
        )
        return (new_max, running_total, running_sum)

    steps_count = pool_rows // block
    initial = (own_score, jnp.ones_like(own_score), value_heads.astype(jnp.float32))
    final_max, final_total, final_sum = lax.fori_loop(0, steps_count, attend_block, initial)
    attended = (
        (final_sum / final_total[:, :, None]).astype(jnp.bfloat16).reshape(rows_here, width_here)
    )
    attn_part = contract_last(lax.all_gather(attended, "req", axis=0, tiled=True), w_out)
    attn_full = lax.psum(attn_part, "head")
    attn_power = lax.psum(jnp.sum(attn_full * attn_full, axis=1), "req")
    attn_normed = attn_full * lax.rsqrt(attn_power[:, None] / model_width + EPS) * norm_gain[0]
    hidden_mid = (hidden_in.astype(jnp.float32) + attn_normed).astype(jnp.bfloat16)
    selected = hidden_mid
    product = jnp.einsum("bd,gdf->bgf", selected, w_gate_up, preferred_element_type=jnp.float32)
    combined = lax.psum_scatter(
        product.reshape(rows_here * lax.axis_size("req"), 2 * units_here),
        "req",
        scatter_dimension=0,
        tiled=True,
    )
    gated = combined[:, :units_here]
    lifted = combined[:, units_here:]
    activated = (jax.nn.silu(gated) * lifted).astype(jnp.bfloat16)
    down_part = contract_last(lax.all_gather(activated, "req", axis=0, tiled=True), w_down)
    ffn_full = lax.psum(down_part, "head")
    ffn_power = lax.psum(jnp.sum(ffn_full * ffn_full, axis=1), "req")
    ffn_normed = ffn_full * lax.rsqrt(ffn_power[:, None] / model_width + EPS) * norm_gain[1]
    hidden_out = (hidden_mid.astype(jnp.float32) + ffn_normed).astype(jnp.bfloat16)
    return (hidden_out, key_rot.reshape(rows_here, width_here), value_new)


def solution(mesh):
    return jax.shard_map(
        body,
        mesh=mesh,
        in_specs=(
            P(None, "req"),
            P("req"),
            P(None, "req", "head"),
            P(None, "head"),
            P("req", "head"),
            P("req", "head"),
            P("req", "head"),
            P(None, "req"),
            P(None, "req", "head"),
            P("req", "head"),
        ),
        out_specs=(P(None, "req"), P("req", "head"), P("req", "head")),
        check_vma=False,
    )
```

profile of v0, /device:TPU:1, one launch (start us, length us, event | category | flops | bytes accessed | tf_op | source)
XLA Modules:
  0.0 526.5 jit_solution(12049688516893260932)
XLA Ops:
  7.2 3.3 fusion.7
  10.6 3.6 copy.52
  14.6 81.9 %reduce-scatter.5.cloned.1.call-done = f32[16,1536]{1,0:T(8,128)} async-done(((f32[512,1536]{1,0:T(8,128)}), f32[16,1536]{1,0:T(8,128)}) %reduce-scatter.5.cloned.1.call-update) | async-done | bytes 98320 | tf_op jit(solution)/shard_map/reduce_scatter | solution.py:52
  96.5 0.9 multiply_reduce_fusion.4
  97.4 8.4 %all-reduce = (f32[16]{0:T(128)S(1)}, f32[16]{0:T(128)S(1)}) all-reduce(f32[16]{0:T(128)S(1)} %get-tuple-element.227, f32[16]{0:T(128)S(1)} %get-tuple-element.226), channel_id=1, replica_groups=mesh['req'=32,'head'=4] {'head'}, use_global_device_ids=true, to_apply=%region_4.0 | all-reduce | flops 32 | bytes 256 | tf_op jit(solution)/shard_map/psum | solution.py:61
  105.8 0.9 multiply_multiply_fusion
  106.7 1.4 convert_bitcast_fusion
  108.5 20.6 %while.18 = (s32[]{:T(128)}, f32[16,4]{0,1:T(4,128)S(1)}, f32[16,4]{0,1:T(4,128)S(1)}, f32[16,4,128]{2,0,1:T(8,128)S(1)}, s32[16]{0:T(128)S(1)}, /*index=5*/s32[...) while((s32[]{:T(128)}, f32[16,4]{0,1:T(4,128)S(1)}, ...), condition=%wide.region_10.11_spmd.clone, body=%wide.region_7.10_spmd.clone.sunk | while | flops 17113800 | bytes 5742917 | solution.py:103
  108.6 1.3 constant_dynamic-slice_fusion.3
  109.9 0.2 copy.94
  110.1 0.3 fusion.37
  110.6 0.2 copy.95
  110.8 0.3 fusion.39
  111.2 1.3 constant_dynamic-slice_fusion.3
  112.4 0.2 copy.94
  112.7 0.3 fusion.37
  113.1 0.2 copy.95
  113.4 0.3 fusion.39
  113.7 1.3 constant_dynamic-slice_fusion.3
  115.0 0.2 copy.94
  115.2 0.3 fusion.37
  115.7 0.2 copy.95
  115.9 0.3 fusion.39
  116.3 1.3 constant_dynamic-slice_fusion.3
  117.6 0.2 copy.94
  117.8 0.3 fusion.37
  118.3 0.2 copy.95
  118.5 0.3 fusion.39
  118.9 1.3 constant_dynamic-slice_fusion.3
  120.2 0.2 copy.94
  120.4 0.3 fusion.37
  120.9 0.2 copy.95
  121.1 0.3 fusion.39
  121.5 1.3 constant_dynamic-slice_fusion.3
  122.8 0.2 copy.94
  123.0 0.3 fusion.37
  123.5 0.2 copy.95
  123.7 0.3 fusion.39
  124.0 1.3 constant_dynamic-slice_fusion.3
  125.3 0.2 copy.94
  125.5 0.3 fusion.37
  126.0 0.2 copy.95
  126.2 0.3 fusion.39
  126.6 1.3 constant_dynamic-slice_fusion.3
  128.1 0.3 fusion.37
  128.6 0.2 copy.95
  128.8 0.3 fusion.39
  129.2 28.3 %all_gather.6 = bf16[512,512]{1,0:T(8,128)(2,1)S(1)} all-gather(bf16[16,512]{1,0:T(8,128)(2,1)S(1)} %copy_bitcast_fusion.2), channel_id=1, replica_groups=mesh['req'=32,'head'=4] {'req'}, dimensions={0}, use_global_device_ids=true | all-gather | bytes 540672 | tf_op jit(solution)/shard_map/all_gather | solution.py:107
  157.5 0.9 fusion.15
  158.5 34.9 %all-reduce.4.cloned.1.call-done = f32[512,64]{0,1:T(8,128)} async-done(((f32[512,64]{0,1:T(8,128)}), f32[512,64]{0,1:T(8,128)}) %all-reduce.4.cloned.1.call-update) | async-done | bytes 131088 | tf_op jit(solution)/shard_map/psum | solution.py:108
  193.5 0.9 multiply_reduce_fusion.1
  194.4 64.9 %psum.45 = f32[512]{0:T(512)S(1)} all-reduce(f32[512]{0:T(512)S(1)} %multiply_reduce_fusion.1), channel_id=1, replica_groups=mesh['req'=32,'head'=4] {'req'}, use_global_device_ids=true, to_apply=%region_13.14 | all-reduce | flops 512 | bytes 4096 | tf_op jit(solution)/shard_map/psum | solution.py:109
  259.4 1.0 add_convert_fusion.1
  260.4 4.5 fusion.5
  264.9 8.9 %copy.69 = f32[512,4096]{1,0:T(8,128)} copy(f32[512,4096]{0,1:T(8,128)} %bitcast.64) | data formatting | bytes 16777216
  273.9 89.2 %reduce-scatter.7.cloned.1.call-done = f32[16,4096]{1,0:T(8,128)} async-done(((f32[512,4096]{1,0:T(8,128)}), f32[16,4096]{1,0:T(8,128)}) %reduce-scatter.7.cloned.1.call-update) | async-done | bytes 262160 | tf_op jit(solution)/shard_map/reduce_scatter | solution.py:114
  363.1 1.6 fusion.4
  364.8 46.6 %all-gather.2.cloned.1.call-done = bf16[512,2048]{1,0:T(8,128)(2,1)} async-done(((bf16[16,2048]{1,0:T(8,128)(2,1)}), bf16[512,2048]{1,0:T(8,128)(2,1)}) %all-gather.2.cloned.1.call-update) | async-done | bytes 2097168 | tf_op jit(solution)/shard_map/all_gather | solution.py:123
  411.4 3.0 fusion.16
  414.4 0.6 copy_bitcast_fusion.1
  415.0 37.4 %all-reduce.6.cloned.1.call-done = f32[512,64]{0,1:T(8,128)} async-done(((f32[512,64]{0,1:T(8,128)}), f32[512,64]{0,1:T(8,128)}) %all-reduce.6.cloned.1.call-update) | async-done | bytes 131088 | tf_op jit(solution)/shard_map/psum | solution.py:124
  452.4 0.9 multiply_reduce_fusion
  453.4 64.9 %psum.47 = f32[512]{0:T(512)S(1)} all-reduce(f32[512]{0:T(512)S(1)} %multiply_reduce_fusion), channel_id=1, replica_groups=mesh['req'=32,'head'=4] {'req'}, use_global_device_ids=true, to_apply=%region_17.18 | all-reduce | flops 512 | bytes 4096 | tf_op jit(solution)/shard_map/psum | solution.py:125
  518.3 1.6 add_convert_fusion
  (95 shorter events, 3.8 us)
Async XLA Ops:
  7.2 253.2 %copy-start = (bf16[2,64,2048]{2,1,0:T(8,128)(2,1)S(1)}, bf16[2,64,2048]{2,1,0:T(8,128)(2,1)}, u32[]{:S(2)}) copy-start(bf16[2,64,2048]{2,1,0:T(8,128)(2,1)} %param.20) | copy-start | bytes 1572868
  7.2 89.3 %reduce-scatter.5.cloned.1.call-start = ((), (), s32[]{:S(2)}) async-start(), calls=%async_computation.2 | async-start | bytes 3244032 | tf_op jit(solution)/shard_map/reduce_scatter | solution.py:52
  10.6 3.7 copy-start.5
  10.6 3.9 copy-start.4
  14.2 179.3 %all-reduce.4.cloned.1.call-start = ((), (), s32[]{:S(2)}) async-start(), calls=%async_computation.3 | async-start | bytes 262144 | tf_op jit(solution)/shard_map/psum | solution.py:108
  108.4 49.1 %copy-start.3 = (bf16[64,512]{1,0:T(8,128)(2,1)S(1)}, bf16[64,512]{1,0:T(8,128)(2,1)}, u32[]{:S(2)}) copy-start(bf16[64,512]{1,0:T(8,128)(2,1)} %param.18) | copy-start | bytes 196612
  108.4 50.1 %copy-start.6 = (f32[2,64]{1,0:T(2,128)S(1)}, f32[2,64]{1,0:T(2,128)}, u32[]{:S(2)}) copy-start(f32[2,64]{1,0:T(2,128)} %param.19) | copy-start | bytes 1540
  108.5 150.9 %copy-start.2 = (bf16[512,64]{0,1:T(8,128)(2,1)S(1)}, bf16[512,64]{0,1:T(8,128)(2,1)}, u32[]{:S(2)}) copy-start(bf16[512,64]{0,1:T(8,128)(2,1)} %param.12) | copy-start | bytes 196612
  158.5 204.6 %reduce-scatter.7.cloned.1.call-start = ((), (), s32[]{:S(2)}) async-start(), calls=%async_computation.6 | async-start | bytes 8650752 | tf_op jit(solution)/shard_map/reduce_scatter | solution.py:114
  273.8 137.6 %copy-start.1 = (bf16[64,2048]{1,0:T(8,128)(2,1)S(1)}, bf16[64,2048]{1,0:T(8,128)(2,1)}, u32[]{:S(2)}) copy-start(bf16[64,2048]{1,0:T(8,128)(2,1)} %param.21) | copy-start | bytes 786436
  273.8 137.6 %all-gather.2.cloned.1.call-start = ((), (), s32[]{:S(2)}) async-start(), calls=%async_computation.4 | async-start | bytes 2162688 | tf_op jit(solution)/shard_map/all_gather | solution.py:123
  364.8 87.7 %all-reduce.6.cloned.1.call-start = ((), (), s32[]{:S(2)}) async-start(), calls=%async_computation.5 | async-start | bytes 262144 | tf_op jit(solution)/shard_map/psum | solution.py:124
Sparse Core Ops, SparseCore 0:
  14.3 82.1 reduce-scatter.4
  158.6 34.8 all-reduce.3
  274.0 89.0 reduce-scatter.6
  366.0 45.3 all-gather.1
  414.6 37.8 all-reduce.5
where the time goes:
time: 529 us; the launch traced here: 526 us
  waiting for transfers between devices  290 us (55%)
  blocking collectives  167 us (32%)
  local copies, waits for them, and re-layouts  27.1 us (5%)
  matrix products  16.1 us (3%)
  between operations  13.9 us (3%)
  other arithmetic  12.2 us (2%)
    reduce_scatter x1, waiting for transfers between devices, body(): lax.psum_scatter(product.reshape(rows_here * lax.axis_size('req'), 2 * un...  89.2 us
    reduce_scatter x1, waiting for transfers between devices, body(): lax.psum_scatter(product.reshape(rows_here * lax.axis_size('req'), 3 * wi...  81.9 us
    psum x1, blocking collectives, body(): ffn_power = lax.psum(jnp.sum(ffn_full * ffn_full, axis=1), 'req')  64.9 us
    psum x1, blocking collectives, body(): attn_power = lax.psum(jnp.sum(attn_full * attn_full, axis=1), 'req')  64.9 us
    all_gather x1, waiting for transfers between devices, body(): lax.all_gather(activated, 'req', axis=0, tiled=True)  46.6 us
    psum x1, waiting for transfers between devices, body(): ffn_full = lax.psum(down_part, 'head')  37.4 us
    psum x1, waiting for transfers between devices, body(): attn_full = lax.psum(attn_part, 'head')  34.9 us
    all_gather x1, blocking collectives, body(): lax.all_gather(attended, 'req', axis=0, tiled=True)  28.3 us
  transfers between devices with their start and end apart: 5, of which 5 were waited for; matrix products, arithmetic and copies ran while one was open for 0% of the time, Pallas kernels for 0%

commit v1 on v0

v1 whole, which is shorter than its diff:
```python
import functools

import jax
import jax.numpy as jnp
from jax import lax
from jax.experimental import pallas as pl
from jax.experimental.pallas import tpu as pltpu
from jax.sharding import Mesh, PartitionSpec as P

HEAD_DIM = 128
EPS = 1e-06
THETA = 500000.0
NT = (((1,), (1,)), ((), ()))
BLOCK = 512


def rotate(values, cosine, sine):
    half = HEAD_DIM // 2
    first = values[..., :half]
    second = values[..., half:]
    return jnp.concatenate(
        [first * cosine - second * sine, second * cosine + first * sine], axis=-1
    )


def attend_kernel(len_ref, q_ref, kn_ref, vn_ref, bounds_ref, keys_hbm, values_hbm, out_ref,
                  kbuf, vbuf, score, acc, top, total, ksem, vsem):
    rows, width = q_ref.shape
    heads = width // HEAD_DIM
    wide = rows * heads
    pool = keys_hbm.shape[0]
    blocks = pool // BLOCK
    used = len_ref[0]
    for r in range(1, rows):
        used = used + len_ref[r]

    def key_copy(i):
        return pltpu.make_async_copy(keys_hbm.at[pl.ds(i * BLOCK, BLOCK)], kbuf.at[i], ksem.at[i])

    def value_copy(i):
        return pltpu.make_async_copy(values_hbm.at[pl.ds(i * BLOCK, BLOCK)], vbuf.at[i], vsem.at[i])

    for i in range(blocks):
        @pl.when(i * BLOCK < used)
        def _():
            key_copy(i).start()
    for i in range(blocks):
        @pl.when(i * BLOCK < used)
        def _():
            value_copy(i).start()

    scale = HEAD_DIM ** (-0.5)
    row_head = lax.broadcasted_iota(jnp.int32, (wide, width), 0) // rows
    col_head = lax.broadcasted_iota(jnp.int32, (wide, width), 1) // HEAD_DIM
    own_head = row_head == col_head
    q = q_ref[...].astype(jnp.float32)
    kn = kn_ref[...].astype(jnp.float32)
    q_all = jnp.concatenate([q] * heads, axis=0)
    kn_all = jnp.concatenate([kn] * heads, axis=0)
    vn_all = jnp.concatenate([vn_ref[...].astype(jnp.float32)] * heads, axis=0)
    q_all = jnp.where(own_head, q_all, 0.0)
    own_score = jnp.sum(q_all * kn_all, axis=1, keepdims=True) * scale
    q_block = q_all.astype(jnp.bfloat16)
    starts = bounds_ref[:, 0:1]
    ends = bounds_ref[:, 1:2]
    top[...] = jnp.broadcast_to(own_score, top.shape)

    for i in range(blocks):
        @pl.when(i * BLOCK < used)
        def _():
            key_copy(i).wait()
            s = lax.dot_general(q_block, kbuf[i], NT, preferred_element_type=jnp.float32) * scale
            place = lax.broadcasted_iota(jnp.int32, s.shape, 1) + i * BLOCK
            s = jnp.where((place >= starts) & (place < ends), s, -jnp.inf)
            score[i] = s
            top[...] = jnp.maximum(top[...], jnp.max(s, axis=1, keepdims=True))

    highest = top[:, 0:1]
    own_weight = jnp.exp(own_score - highest).astype(jnp.bfloat16).astype(jnp.float32)
    total[...] = jnp.broadcast_to(own_weight, total.shape)
    acc[...] = own_weight * vn_all

    for i in range(blocks):
        @pl.when(i * BLOCK < used)
        def _():
            value_copy(i).wait()
            w = jnp.exp(score[i] - highest).astype(jnp.bfloat16)
            total[...] += jnp.sum(w.astype(jnp.float32), axis=1, keepdims=True)
            acc[...] += jnp.dot(w, vbuf[i], preferred_element_type=jnp.float32)

    result = acc[...] / total[:, 0:1]
    out_ref[...] = jnp.concatenate(
        [
            result[h * rows : (h + 1) * rows, h * HEAD_DIM : (h + 1) * HEAD_DIM]
            for h in range(heads)
        ],
        axis=1,
    ).astype(out_ref.dtype)


def attend(lengths, query, key_new, value_new, cache_keys, cache_values):
    rows, width = query.shape
    heads = width // HEAD_DIM
    wide = rows * heads
    pool = cache_keys.shape[0]
    blocks = pool // BLOCK
    ends = jnp.cumsum(lengths)
    starts = ends - lengths
    bounds = jnp.tile(jnp.stack([starts, ends], axis=1), (heads, 1))
    vmem = pl.BlockSpec(memory_space=pltpu.VMEM)
    return pl.pallas_call(
        attend_kernel,
        out_shape=jax.ShapeDtypeStruct((rows, width), jnp.bfloat16),
        in_specs=[pl.BlockSpec(memory_space=pltpu.SMEM), vmem, vmem, vmem, vmem,
                  pl.BlockSpec(memory_space=pl.ANY), pl.BlockSpec(memory_space=pl.ANY)],
        out_specs=vmem,
        scratch_shapes=[
            pltpu.VMEM((blocks, BLOCK, width), jnp.bfloat16),
            pltpu.VMEM((blocks, BLOCK, width), jnp.bfloat16),
            pltpu.VMEM((blocks, wide, BLOCK), jnp.float32),
            pltpu.VMEM((wide, width), jnp.float32),
            pltpu.VMEM((wide, 128), jnp.float32),
            pltpu.VMEM((wide, 128), jnp.float32),
            pltpu.SemaphoreType.DMA((blocks,)),
            pltpu.SemaphoreType.DMA((blocks,)),
        ],
        compiler_params=pltpu.CompilerParams(vmem_limit_bytes=24 * 1024 * 1024),
        cost_estimate=pl.CostEstimate(flops=1 << 29, bytes_accessed=8 << 20, transcendentals=1 << 18),
        name="attend",
    )(lengths, query, key_new, value_new, bounds, cache_keys, cache_values)


def ffn_kernel(a_ref, h_ref, gain_ref, w_hbm, mid_ref, out_ref, wbuf, sem):
    groups = w_hbm.shape[0]
    for g in range(groups):
        pltpu.make_async_copy(w_hbm.at[g], wbuf.at[g], sem.at[g]).start()
    a = a_ref[...].astype(jnp.float32)
    power = jnp.mean(a * a, axis=1, keepdims=True)
    mid = h_ref[...].astype(jnp.float32) + a * lax.rsqrt(power + EPS) * gain_ref[...]
    mid = mid.astype(jnp.bfloat16)
    mid_ref[...] = mid
    rows, width = mid.shape
    part = width // groups
    units = wbuf.shape[-1]
    gate = jnp.zeros((rows, units), jnp.float32)
    lift = jnp.zeros((rows, units), jnp.float32)
    for g in range(groups):
        pltpu.make_async_copy(w_hbm.at[g], wbuf.at[g], sem.at[g]).wait()
        m = mid[:, g * part : (g + 1) * part]
        gate += jnp.dot(m, wbuf[g, :, 0].reshape(part, units), preferred_element_type=jnp.float32)
        lift += jnp.dot(m, wbuf[g, :, 1].reshape(part, units), preferred_element_type=jnp.float32)
    act = (gate / (1.0 + jnp.exp(-gate)) * lift).astype(jnp.bfloat16)
    for g in range(groups):
        out_ref[:, g * part : (g + 1) * part] = lax.dot_general(
            act, wbuf[g, :, 2].reshape(part, units), NT, preferred_element_type=jnp.float32
        ).astype(out_ref.dtype)


def feed_forward(a, h, gain, weights):
    rows, width = a.shape
    vmem = pl.BlockSpec(memory_space=pltpu.VMEM)
    return pl.pallas_call(
        ffn_kernel,
        out_shape=(
            jax.ShapeDtypeStruct((rows, width), jnp.bfloat16),
            jax.ShapeDtypeStruct((rows, width), jnp.float32),
        ),
        in_specs=[vmem, vmem, vmem, pl.BlockSpec(memory_space=pl.ANY)],
        out_specs=(vmem, vmem),
        scratch_shapes=[
            pltpu.VMEM(weights.shape, jnp.bfloat16),
            pltpu.SemaphoreType.DMA((weights.shape[0],)),
        ],
        compiler_params=pltpu.CompilerParams(vmem_limit_bytes=24 * 1024 * 1024),
        cost_estimate=pl.CostEstimate(flops=1 << 29, bytes_accessed=7 << 20, transcendentals=1 << 15),
        name="feed_forward",
    )(a, h, gain, weights)


def body(hidden_in, lengths, w_qkv, qk_gain, cache_keys, cache_values, w_out, norm_gain,
         w_gate_up, w_down):
    bf16 = jnp.bfloat16
    nz, ny, nc, nx = (lax.axis_size(a) for a in ("z", "y", "c", "x"))
    core = lax.axis_index("c")
    y_here = lax.axis_index("y")
    x_here = lax.axis_index("x")
    rows = lengths.shape[0]
    width = w_qkv.shape[2]
    heads = width // HEAD_DIM
    feats = hidden_in.shape[1]
    model = width * nx
    swap = [(0, 1), (1, 0)]

    units = w_gate_up.shape[2] // ny
    stacked = jnp.concatenate([w_gate_up, w_down[None]], axis=0)

    def unit_block(i):
        return lax.dynamic_slice_in_dim(stacked, i * units, units, 2)

    pieces = [unit_block(y_here)]
    for shift in range(1, ny):
        pieces.append(
            lax.ppermute(unit_block((y_here + shift) % ny), "y",
                         [(i, (i + shift) % ny) for i in range(ny)])
        )
    piled = jnp.stack(pieces, axis=0)
    order = (y_here - jnp.arange(ny)) % ny
    mine = jnp.concatenate(
        [lax.dynamic_index_in_dim(piled, order[i], 0, keepdims=True) for i in range(ny)], axis=0
    )
    ffn_weights = lax.all_gather(mine, ("z", "c"), axis=0, tiled=False)
    out_weights = lax.all_gather(w_out, ("z", "c", "y"), axis=0, tiled=True)

    by_core = hidden_in.reshape(nz * ny, nc, rows, feats)
    own_rows = lax.dynamic_index_in_dim(by_core, core, 1, keepdims=False)
    other_rows = lax.dynamic_index_in_dim(by_core, 1 - core, 1, keepdims=False)
    mate_rows = lax.ppermute(other_rows, "c", swap)
    mate_w = lax.ppermute(w_qkv, "c", swap)
    first = core == 0
    left = jnp.where(first, own_rows, mate_rows)
    right = jnp.where(first, mate_rows, own_rows)
    both_rows = jnp.concatenate([left, right], axis=2)
    both_w = jnp.concatenate(
        [jnp.where(first, w_qkv, mate_w), jnp.where(first, mate_w, w_qkv)], axis=1
    )
    product = jnp.einsum(
        "brd,gdf->brgf", both_rows, both_w, preferred_element_type=jnp.float32
    ).astype(bf16).reshape(nz * ny, rows, 3 * width)
    message = jnp.concatenate([product, both_rows], axis=2)
    got = lax.all_to_all(message, ("z", "y"), 0, 0, tiled=True)
    summed = jnp.sum(got[:, :, : 3 * width].astype(jnp.float32), axis=0)
    query = summed[:, :width]
    key_new = summed[:, width : 2 * width]
    value_new = summed[:, 2 * width :].astype(bf16)
    rest = got[:, :, 3 * width :].reshape(nz, ny, rows, nc, feats)
    rest = lax.dynamic_index_in_dim(rest, x_here, 0, keepdims=False)
    rest = rest.transpose(1, 2, 0, 3).reshape(rows, width)

    squares = lax.psum(jnp.stack([jnp.sum(query * query, axis=1), jnp.sum(key_new * key_new, axis=1)]), "x")
    half = HEAD_DIM // 2
    freqs = jnp.power(THETA, -(jnp.arange(half, dtype=jnp.float32) * 2.0 / HEAD_DIM))
    angles = lengths.astype(jnp.float32)[:, None] * freqs[None, :]
    cosine = jnp.cos(angles)[:, None, :]
    sine = jnp.sin(angles)[:, None, :]
    query = query * lax.rsqrt(squares[0][:, None] / model + EPS) * qk_gain[0]
    key_new = key_new * lax.rsqrt(squares[1][:, None] / model + EPS) * qk_gain[1]
    query = rotate(query.reshape(rows, heads, HEAD_DIM), cosine, sine).astype(bf16).reshape(rows, width)
    key_new = rotate(key_new.reshape(rows, heads, HEAD_DIM), cosine, sine).astype(bf16).reshape(rows, width)
    attended = attend(lengths, query, key_new, value_new, cache_keys, cache_values)

    partial = lax.dot_general(attended, out_weights, NT, preferred_element_type=jnp.float32)
    partial = partial.reshape(rows, nx, width).transpose(1, 0, 2)
    branch = jnp.sum(lax.all_to_all(partial, "x", 0, 0, tiled=True), axis=0).astype(bf16)
    message = jnp.concatenate([branch, rest], axis=1)
    message = jnp.broadcast_to(message[None], (ny * nx, rows, 2 * width))
    got = lax.all_to_all(message, ("y", "x"), 0, 0, tiled=True)
    got = got.reshape(ny, nx, rows, 2, width).transpose(3, 0, 2, 1, 4).reshape(2, ny * rows, model)

    gain = lax.all_gather(norm_gain, ("z", "c", "y"), axis=1, tiled=True)
    mid, partial = feed_forward(got[0], got[1], gain[0:1], ffn_weights)
    mine_rows = rows // nx
    partial = partial.reshape(ny * nx, mine_rows, model)
    full = jnp.sum(lax.all_to_all(partial, ("y", "x"), 0, 0, tiled=True), axis=0)
    mid_here = lax.dynamic_slice_in_dim(mid, (y_here * nx + x_here) * mine_rows, mine_rows, 0)
    power = jnp.mean(full * full, axis=1, keepdims=True)
    hidden = (mid_here.astype(jnp.float32) + full * lax.rsqrt(power + EPS) * gain[1:2]).astype(bf16)
    hidden = hidden.reshape(mine_rows, nz, nc, ny, feats).transpose(1, 3, 2, 0, 4)
    hidden = jnp.broadcast_to(
        hidden[:, :, :, None], (nz, ny, nc, nx, mine_rows, feats)
    ).reshape(nz * ny * nc * nx, mine_rows, feats)
    hidden = lax.all_to_all(hidden, ("z", "y", "c", "x"), 0, 0, tiled=True)
    return hidden.reshape(-1, feats), key_new, value_new


def solution(mesh):
    fine = Mesh(mesh.devices.reshape(4, 4, 2, 4), ("z", "y", "c", "x"))
    req = ("z", "y", "c")
    return jax.shard_map(
        body,
        mesh=fine,
        in_specs=(
            P(None, req),
            P(req),
            P(None, req, "x"),
            P(None, "x"),
            P(req, "x"),
            P(req, "x"),
            P(req, "x"),
            P(None, req),
            P(None, req, "x"),
            P(req, "x"),
        ),
        out_specs=(P(None, req), P(req, "x"), P(req, "x")),
        check_vma=False,
    )
```

time: 529 us -> 178 us (0.34)
  waiting for transfers between devices: 290 us -> 32.2 us
  blocking collectives: 167 us -> 68.7 us
  starting transfers between devices: 0.21 us -> 26.8 us
  matrix products: 16.1 us -> 2.64 us
  local copies, waits for them, and re-layouts: 27.1 us -> 15.8 us
  other arithmetic: 12.2 us -> 3.55 us
  between operations: 13.9 us -> 22.5 us
    reduce_scatter x2 -> x0, waiting for transfers between devices: 171 us -> none  [the longest x1 89.2 us: body(): lax.psum_scatter(product.reshape(rows_here * lax.axis_size('req'), 2 * un...]
    psum x3 -> x1, blocking collectives: 138 us -> 8.54 us  [body(): lax.psum(jnp.stack([jnp.sum(query * query, axis=1), jnp.sum(key_new * key...]
    psum x2 -> x0, waiting for transfers between devices: 72.3 us -> none  [the longest x1 37.4 us: body(): ffn_full = lax.psum(down_part, 'head')]
    all_gather x1 -> x2, waiting for transfers between devices: 46.6 us -> 0.04 us  [the longest x1 0.02 us: body(): out_weights = lax.all_gather(w_out, ('z', 'c', 'y'), axis=0, tiled=True)]
    all_to_all x0 -> x4, waiting for transfers between devices: none -> 30.4 us  [the longest x1 15.3 us: body(): got = lax.all_to_all(message, ('z', 'y'), 0, 0, tiled=True)]
    all_to_all x0 -> x4, starting transfers between devices: none -> 19.2 us  [the longest x1 6.22 us: body(): lax.all_to_all(partial, ('y', 'x'), 0, 0, tiled=True)]
    all_gather x1, blocking collectives: 28.3 us -> 45.6 us  [body(): gain = lax.all_gather(norm_gain, ('z', 'c', 'y'), axis=1, tiled=True)]
    all_to_all x0 -> x1, blocking collectives: none -> 14.6 us  [body(): hidden = lax.all_to_all(hidden, ('z', 'y', 'c', 'x'), 0, 0, tiled=True)]
  transfers between devices with their start and end apart: 5 -> 11, of which waited for: 5 -> 5; matrix products, arithmetic and copies ran while one was open for 0% -> 7% of each run, Pallas kernels for 0% -> 1%
where the time goes in v1:
time: 178 us; the launch traced here: 177 us
  blocking collectives  68.7 us (39%)
  waiting for transfers between devices  32.2 us (18%)
  starting transfers between devices  26.8 us (15%)
  between operations  22.5 us (13%)
  local copies, waits for them, and re-layouts  15.8 us (9%)
  Pallas kernels  4.82 us (3%)
  other arithmetic  3.55 us (2%)
  matrix products  2.64 us (1%)
    all_gather x1, blocking collectives, body(): gain = lax.all_gather(norm_gain, ('z', 'c', 'y'), axis=1, tiled=True)  45.6 us
    all_to_all x1, waiting for transfers between devices, body(): got = lax.all_to_all(message, ('z', 'y'), 0, 0, tiled=True)  15.3 us
    all_to_all x1, blocking collectives, body(): hidden = lax.all_to_all(hidden, ('z', 'y', 'c', 'x'), 0, 0, tiled=True)  14.6 us
    all_to_all x1, waiting for transfers between devices, body(): lax.all_to_all(partial, ('y', 'x'), 0, 0, tiled=True)  10.5 us
    psum x1, blocking collectives, body(): lax.psum(jnp.stack([jnp.sum(query * query, axis=1), jnp.sum(key_new * key...  8.54 us
    unnamed x30, local copies, waits for them, and re-layouts  8.53 us
    all_to_all x1, starting transfers between devices, body(): lax.all_to_all(partial, ('y', 'x'), 0, 0, tiled=True)  6.22 us
    all_to_all x1, starting transfers between devices, body(): got = lax.all_to_all(message, ('z', 'y'), 0, 0, tiled=True)  6.03 us
  transfers between devices with their start and end apart: 11, of which 5 were waited for; matrix products, arithmetic and copies ran while one was open for 7% of the time, Pallas kernels for 1%

profile of v1, /device:TPU:1, one launch (start us, length us, event | category | flops | bytes accessed | tf_op | source)
XLA Modules:
  0.0 177.0 jit_solution(14792473676982575094)
XLA Ops:
  7.2 0.0 all-gather.5.cloned.1.call-start
  7.2 0.7 all-gather.5.cloned.1.call-update
  7.9 0.0 all-gather.7.cloned.1.call-start
  8.0 1.3 fusion.5
  9.3 2.2 %collective-permute-start.2 = (bf16[3,64,512]{2,1,0:T(8,128)(2,1)S(1)}, bf16[3,64,512]{2,1,0:T(8,128)(2,1)S(1)}, u32[]{:S(2)}, u32[]{:S(2)}) collective-permute-start(bf16[3,64,512]{2,1,0:T(8,128)(2,1)S(1)} %get-tuple-element.20), channel_id=1, source_target_pairs={{0,8},{8,16},{16,24},{24,0},{1,9},{9,17},{17,25},{25,1},{2,10},{10... | collective-permute-start | bytes 589832 | tf_op jit(solution)/shard_map/ppermute | solution.py:203
  11.4 2.6 %collective-permute-start.3 = (bf16[3,64,512]{2,1,0:T(8,128)(2,1)S(1)}, bf16[3,64,512]{2,1,0:T(8,128)(2,1)S(1)}, u32[]{:S(2)}, u32[]{:S(2)}) collective-permute-start(bf16[3,64,512]{2,1,0:T(8,128)(2,1)S(1)} %get-tuple-element.21), channel_id=1, source_target_pairs={{0,16},{8,24},{16,0},{24,8},{1,17},{9,25},{17,1},{25,9},{2,18},{10... | collective-permute-start | bytes 589832 | tf_op jit(solution)/shard_map/ppermute | solution.py:203
  14.1 1.1 collective-permute-start.4
  15.1 0.7 fusion.15
  23.7 0.1 pad_maximum_fusion
  23.9 0.1 constant_dynamic-slice_fusion.3
  24.0 1.0 pad_maximum_fusion.1
  25.0 0.1 copy.33
  25.1 1.6 collective-permute-start
  26.7 0.1 collective-permute-start.1
  26.8 0.1 copy.35
  26.9 0.1 copy.36
  27.0 0.1 reduce
  27.1 0.5 collective-permute-done
  27.6 0.5 collective-permute-done.1
  28.2 0.4 fusion
  28.6 0.1 copy.49
  28.7 1.2 concatenate.29
  29.9 6.0 %all-to-all-start = ((bf16[16,16,1664]{2,1,0:T(8,128)(2,1)}), bf16[16,16,1664]{2,1,0:T(8,128)(2,1)S(1)}, u32[]{:S(2)}, u32[]{:S(2)}) async-start(bf16[16,16,1664]{2,1,0:T(8,128)(2,1)} %concatenate.29), calls=%async_computation | async-start | bytes 1703936 | tf_op jit(solution)/shard_map/all_to_all | solution.py:230
  35.9 0.1 copy.47
  36.0 0.1 multiply_cosine_fusion
  36.2 15.3 %all-to-all-done = bf16[16,16,1664]{2,1,0:T(8,128)(2,1)S(1)} async-done(((bf16[16,16,1664]{2,1,0:T(8,128)(2,1)}), bf16[16,16,1664]{2,1,0:T(8,128)(2,1)S(1)}, u32[]{:S(2)}, u32[]{:S(2)}) %all-to-all-start) | async-done | bytes 852000 | tf_op jit(solution)/shard_map/all_to_all | solution.py:230
  51.4 0.1 convert_reduce_fusion
  51.6 0.1 multiply_reduce_fusion.2
  51.7 8.5 %psum.7 = f32[2,16]{1,0:T(2,128)S(1)} all-reduce(f32[2,16]{1,0:T(2,128)S(1)} %pad_maximum_fusion.5), channel_id=1, replica_groups=mesh['z'=4,'y'=4,'c'=2,'x'=4] {'x'}, use_global_device_ids=true, to_apply=%region_3.4 | all-reduce | flops 32 | bytes 256 | tf_op jit(solution)/shard_map/psum | solution.py:239
  60.2 0.1 multiply_multiply_fusion
  60.4 0.1 subtract_convert_fusion
  60.5 0.1 pad_maximum_fusion.3
  60.6 0.1 reshape.164
  60.8 2.2 %copy-done.1 = bf16[4096,512]{1,0:T(8,128)(2,1)S(1)} copy-done((bf16[4096,512]{1,0:T(8,128)(2,1)S(1)}, bf16[4096,512]{1,0:T(8,128)(2,1)}, u32[]{:S(2)}) %copy-start.1) | copy-done | bytes 4194328
  63.0 2.2 %copy-done.2 = bf16[4096,512]{1,0:T(8,128)(2,1)S(1)} copy-done((bf16[4096,512]{1,0:T(8,128)(2,1)S(1)}, bf16[4096,512]{1,0:T(8,128)(2,1)}, u32[]{:S(2)}) %copy-start.2) | copy-done | bytes 4194328
  65.1 2.5 %attend.1 = bf16[16,512]{1,0:T(8,128)(2,1)S(1)} custom-call(s32[16]{0:T(128)S(1)} %copy-done.5, bf16[16,512]{1,0:T(8,128)(2,1)S(1)} %bitcast.85, bf16[16,512]{1,0:T(8,128)(2,1)S(1)} %bitcast.83, bf16[16,512]{1,0:T(8,128)(2,1)S(1)} %slice.116.vn_ref, s32[64,2]{1,0:T(8,128)S(1)} %bitcast.82, bf16[4096,512]{1,0:T(8,128)(2,1)S(1)} %copy-done.1, ...), custom_call_target="tpu_custom_call" | custom-call | flops 536870912 | bytes 8388608 | tf_op jit(solution)/shard_map/attend/pallas_call | solution.py:111
  67.6 0.0 all-gather.5.cloned.1.call-done
  67.7 2.2 %fusion.16 = f32[16,2048]{1,0:T(8,128)S(1)} fusion(bf16[16,512]{1,0:T(8,128)(2,1)S(1)} %attend.1, bf16[2048,512]{1,0:T(8,128)(2,1)} %all-gather.5.cloned.1.call-done), kind=kOutput, calls=%fused_computation.70 | convolution fusion | flops 33554432 | bytes 2244608 | tf_op jit(solution)/shard_map/dot_general | solution.py:251
  69.9 0.7 copy.58
  70.6 3.3 %all-to-all-start.1 = ((f32[4,16,512]{2,1,0:T(8,128)}), f32[4,16,512]{2,1,0:T(8,128)S(1)}, u32[]{:S(2)}, u32[]{:S(2)}) async-start(f32[4,16,512]{2,1,0:T(8,128)} %bitcast.75), calls=%async_computation.1 | async-start | bytes 262144 | tf_op jit(solution)/shard_map/all_to_all | solution.py:253
  74.0 0.1 reshape.165
  74.1 4.7 %all-to-all-done.1 = f32[4,16,512]{2,1,0:T(8,128)S(1)} async-done(((f32[4,16,512]{2,1,0:T(8,128)}), f32[4,16,512]{2,1,0:T(8,128)S(1)}, u32[]{:S(2)}, u32[]{:S(2)}) %all-to-all-start.1) | async-done | bytes 131104 | tf_op jit(solution)/shard_map/all_to_all | solution.py:253
  78.8 0.9 broadcast_in_dim.6
  79.6 3.6 %all-to-all-start.2 = ((bf16[16,16,1024]{2,1,0:T(8,128)(2,1)}), bf16[16,16,1024]{2,1,0:T(8,128)(2,1)S(1)}, u32[]{:S(2)}, u32[]{:S(2)}) async-start(bf16[16,16,1024]{2,1,0:T(8,128)(2,1)} %broadcast_in_dim.6), calls=%async_computation.2 | async-start | bytes 1048576 | tf_op jit(solution)/shard_map/all_to_all | solution.py:256
  83.2 45.6 %all-gather.1 = f32[32,64,2]{1,2,0:T(2,128)S(1)} all-gather(f32[1,64,2]{1,2,0:T(2,128)S(1)} %bitcast.110), channel_id=1, replica_groups=mesh['z'=4,'y'=4,'c'=2,'x'=4] {'z','c','y'}, dimensions={0}, use_global_device_ids=true | all-gather | bytes 16896 | tf_op jit(solution)/shard_map/all_gather | solution.py:259
  128.8 0.1 reshape.173
  128.9 0.4 reshape.166
  129.3 1.1 fusion.12
  130.4 0.3 copy.41
  130.8 0.3 copy.40
  131.2 0.0 all-gather.7.cloned.1.call-done
  131.3 2.8 %copy-done = bf16[32,3,64,512]{3,2,1,0:T(8,128)(2,1)S(1)} copy-done((bf16[32,3,64,512]{3,2,1,0:T(8,128)(2,1)S(1)}, bf16[32,3,64,512]{3,2,1,0:T(8,128)(2,1)}, u32[]{:S(2)}) %copy-start) | copy-done | bytes 6291480
  134.1 2.4 %feed_forward.1 = (bf16[64,2048]{1,0:T(8,128)(2,1)S(1)}, f32[64,2048]{1,0:T(8,128)S(1)}) custom-call(bf16[64,2048]{1,0:T(8,128)(2,1)S(1)} %bitcast.81, bf16[64,2048]{1,0:T(8,128)(2,1)S(1)} %bitcast.80, f32[1,2048]{1,0:T(1,128)S(1)} %get-tuple-element.36.gain_ref, bf16[8,4,3,64,512]{4,3,2,1,0:T(8,128)(2,1)S(1)} %bitcast.79), custom_call_target="tpu_custom_call" | custom-call | flops 536870912 | bytes 7340032 | tf_op jit(solution)/shard_map/feed_forward/pallas_call | solution.py:162
  136.4 1.0 reshape.167
  137.4 6.2 %all-to-all-start.3 = ((f32[16,4,2048]{2,1,0:T(4,128)}), f32[16,4,2048]{2,1,0:T(4,128)S(1)}, u32[]{:S(2)}, u32[]{:S(2)}) async-start(f32[16,4,2048]{2,1,0:T(4,128)} %reshape.167), calls=%async_computation.3 | async-start | bytes 1048576 | tf_op jit(solution)/shard_map/all_to_all | solution.py:263
  143.6 10.5 %all-to-all-done.3 = f32[16,4,2048]{2,1,0:T(4,128)S(1)} async-done(((f32[16,4,2048]{2,1,0:T(4,128)}), f32[16,4,2048]{2,1,0:T(4,128)S(1)}, u32[]{:S(2)}, u32[]{:S(2)}) %all-to-all-start.3) | async-done | bytes 524320 | tf_op jit(solution)/shard_map/all_to_all | solution.py:263
  154.1 0.1 reduce_sum.58
  154.2 0.1 multiply_reduce_fusion
  154.3 0.1 add_convert_fusion
  154.4 0.1 reshape.168
  154.6 0.1 reshape.177
  154.7 14.6 %all_to_all.25 = bf16[128,2,128]{2,1,0:T(2,128)(2,1)S(1)} all-to-all(bf16[128,2,128]{2,1,0:T(2,128)(2,1)S(1)} %reshape.177), channel_id=1, replica_groups=mesh['z'=4,'y'=4,'c'=2,'x'=4] {'z','y','c','x'}, dimensions={0} | all-to-all | bytes 131072 | tf_op jit(solution)/shard_map/all_to_all | solution.py:271
  169.3 0.1 reshape.178
  169.4 0.7 copy.44
  (51 shorter events, 0.6 us)
Async XLA Ops:
  7.2 60.5 %all-gather.5.cloned.1.call-start = ((), (), s32[]{:S(2)}) async-start(), calls=%async_computation.5 | async-start | bytes 2162688 | tf_op jit(solution)/shard_map/all_gather | solution.py:212
  7.9 123.4 %all-gather.7.cloned.1.call-start = ((), (), s32[]{:S(2)}) async-start(), calls=%async_computation.6 | async-start | bytes 7077888 | tf_op jit(solution)/shard_map/all_gather | solution.py:211
  9.3 14.5 %collective-permute-start.2 = (bf16[3,64,512]{2,1,0:T(8,128)(2,1)S(1)}, bf16[3,64,512]{2,1,0:T(8,128)(2,1)S(1)}, u32[]{:S(2)}, u32[]{:S(2)}) collective-permute-start(bf16[3,64,512]{2,1,0:T(8,128)(2,1)S(1)} %get-tuple-element.20), channel_id=1, source_target_pairs={{0,8},{8,16},{16,24},{24,0},{1,9},{9,17},{17,25},{25,1},{2,10},{10... | collective-permute-start | bytes 589832 | tf_op jit(solution)/shard_map/ppermute | solution.py:203
  11.4 12.3 %collective-permute-start.3 = (bf16[3,64,512]{2,1,0:T(8,128)(2,1)S(1)}, bf16[3,64,512]{2,1,0:T(8,128)(2,1)S(1)}, u32[]{:S(2)}, u32[]{:S(2)}) collective-permute-start(bf16[3,64,512]{2,1,0:T(8,128)(2,1)S(1)} %get-tuple-element.21), channel_id=1, source_target_pairs={{0,16},{8,24},{16,0},{24,8},{1,17},{9,25},{17,1},{25,9},{2,18},{10... | collective-permute-start | bytes 589832 | tf_op jit(solution)/shard_map/ppermute | solution.py:203
  14.1 9.7 %collective-permute-start.4 = (bf16[3,64,512]{2,1,0:T(8,128)(2,1)S(1)}, bf16[3,64,512]{2,1,0:T(8,128)(2,1)S(1)}, u32[]{:S(2)}, u32[]{:S(2)}) collective-permute-start(bf16[3,64,512]{2,1,0:T(8,128)(2,1)S(1)} %get-tuple-element.22), channel_id=1, source_target_pairs={{0,24},{8,0},{16,8},{24,16},{1,25},{9,1},{17,9},{25,17},{2,26},{10... | collective-permute-start | bytes 589832 | tf_op jit(solution)/shard_map/ppermute | solution.py:203
  23.8 1.1 copy-start.7
  23.9 2.9 %copy-start.6 = (bf16[3,64,512]{2,1,0:T(8,128)(2,1)S(1)}, bf16[3,64,512]{2,1,0:T(8,128)(2,1)}, u32[]{:S(2)}) copy-start(bf16[3,64,512]{2,1,0:T(8,128)(2,1)} %param.12) | copy-start | bytes 589828
  23.9 3.0 %copy-start.5 = (s32[16]{0:T(128)S(1)}, s32[16]{0:T(128)}, u32[]{:S(2)}) copy-start(s32[16]{0:T(128)} %len_ref.1) | copy-start | bytes 196
  25.1 2.5 %collective-permute-start = (bf16[16,16,64]{2,1,0:T(8,128)(2,1)S(1)}, bf16[16,16,64]{2,1,0:T(8,128)(2,1)S(1)}, u32[]{:S(2)}, u32[]{:S(2)}) collective-permute-start(bf16[16,16,64]{2,1,0:T(8,128)(2,1)S(1)} %dynamic-slice_bitcast_fusion), channel_id=1, source_target_pairs={{0,4},{4,0},{1,5},{5,1},{2,6},{6,2},{3,7},{7,3},{8,12},{12,8},{9,1... | collective-permute-start | bytes 98312 | tf_op jit(solution)/shard_map/ppermute | solution.py:217
  26.7 1.4 collective-permute-start.1
  28.7 7.3 %copy-start.8 = (f32[2,512]{1,0:T(2,128)S(1)}, f32[2,512]{1,0:T(2,128)}, u32[]{:S(2)}) copy-start(f32[2,512]{1,0:T(2,128)} %param.13) | copy-start | bytes 12292
  29.9 21.6 %all-to-all-start = ((bf16[16,16,1664]{2,1,0:T(8,128)(2,1)}), bf16[16,16,1664]{2,1,0:T(8,128)(2,1)S(1)}, u32[]{:S(2)}, u32[]{:S(2)}) async-start(bf16[16,16,1664]{2,1,0:T(8,128)(2,1)} %concatenate.29), calls=%async_computation | async-start | bytes 1703936 | tf_op jit(solution)/shard_map/all_to_all | solution.py:230
  51.5 16.1 %copy-start.3 = (bf16[16,512]{1,0:T(8,128)(2,1)}, bf16[16,512]{1,0:T(8,128)(2,1)S(1)}, u32[]{:S(2)}) copy-start(bf16[16,512]{1,0:T(8,128)(2,1)S(1)} %slice.116.vn_ref) | copy-start | bytes 49156
  60.6 7.0 %copy-start.4 = (bf16[2,8,4,128]{3,1,2,0:T(8,128)(2,1)}, bf16[2,8,4,128]{3,1,2,0:T(8,128)(2,1)S(1)}, u32[]{:S(2)}) copy-start(bf16[2,8,4,128]{3,1,2,0:T(8,128)(2,1)S(1)} %copy.60) | copy-start | bytes 49156
  60.8 2.2 %copy-start.1 = (bf16[4096,512]{1,0:T(8,128)(2,1)S(1)}, bf16[4096,512]{1,0:T(8,128)(2,1)}, u32[]{:S(2)}) copy-start(bf16[4096,512]{1,0:T(8,128)(2,1)} %keys_hbm.1) | copy-start | bytes 12582916
  62.9 2.2 %copy-start.2 = (bf16[4096,512]{1,0:T(8,128)(2,1)S(1)}, bf16[4096,512]{1,0:T(8,128)(2,1)}, u32[]{:S(2)}) copy-start(bf16[4096,512]{1,0:T(8,128)(2,1)} %values_hbm.1) | copy-start | bytes 12582916
  67.6 15.6 %copy-start.9 = (f32[2,64]{1,0:T(2,128)S(1)}, f32[2,64]{1,0:T(2,128)}, u32[]{:S(2)}) copy-start(f32[2,64]{1,0:T(2,128)} %param.17) | copy-start | bytes 1540
  70.6 8.2 %all-to-all-start.1 = ((f32[4,16,512]{2,1,0:T(8,128)}), f32[4,16,512]{2,1,0:T(8,128)S(1)}, u32[]{:S(2)}, u32[]{:S(2)}) async-start(f32[4,16,512]{2,1,0:T(8,128)} %bitcast.75), calls=%async_computation.1 | async-start | bytes 262144 | tf_op jit(solution)/shard_map/all_to_all | solution.py:253
  79.6 49.3 %all-to-all-start.2 = ((bf16[16,16,1024]{2,1,0:T(8,128)(2,1)}), bf16[16,16,1024]{2,1,0:T(8,128)(2,1)S(1)}, u32[]{:S(2)}, u32[]{:S(2)}) async-start(bf16[16,16,1024]{2,1,0:T(8,128)(2,1)} %broadcast_in_dim.6), calls=%async_computation.2 | async-start | bytes 1048576 | tf_op jit(solution)/shard_map/all_to_all | solution.py:256
  131.3 2.8 %copy-start = (bf16[32,3,64,512]{3,2,1,0:T(8,128)(2,1)S(1)}, bf16[32,3,64,512]{3,2,1,0:T(8,128)(2,1)}, u32[]{:S(2)}) copy-start(bf16[32,3,64,512]{3,2,1,0:T(8,128)(2,1)} %all-gather.7.cloned.1.call-done) | copy-start | bytes 18874372
  137.4 16.7 %all-to-all-start.3 = ((f32[16,4,2048]{2,1,0:T(4,128)}), f32[16,4,2048]{2,1,0:T(4,128)S(1)}, u32[]{:S(2)}, u32[]{:S(2)}) async-start(f32[16,4,2048]{2,1,0:T(4,128)} %reshape.167), calls=%async_computation.3 | async-start | bytes 1048576 | tf_op jit(solution)/shard_map/all_to_all | solution.py:263
Sparse Core Ops, SparseCore 0:
  10.3 50.3 all-gather.4
  62.3 39.9 all-gather.6

commit v2 on v0

v2 whole, which is shorter than its diff:
```python
import functools

import jax
import jax.numpy as jnp
from jax import lax
from jax.experimental import pallas as pl
from jax.experimental.pallas import tpu as pltpu
from jax.sharding import Mesh, PartitionSpec as P

HEAD_DIM = 128
EPS = 1e-06
THETA = 500000.0
NT = (((1,), (1,)), ((), ()))
BLOCK = 512
F32 = jnp.float32
BF16 = jnp.bfloat16
NZ, NY, NC, NX = 4, 4, 2, 4
VMEM = pl.BlockSpec(memory_space=pltpu.VMEM)
HBM = pl.BlockSpec(memory_space=pltpu.HBM)
ANY = pl.BlockSpec(memory_space=pl.ANY)
SMEM = pl.BlockSpec(memory_space=pltpu.SMEM)
LIMIT = 32 * 1024 * 1024


def call(kernel, out_shape, in_specs, out_specs, scratch=(), cost=(1 << 20, 1 << 20), name=None):
    return pl.pallas_call(
        kernel,
        out_shape=out_shape,
        in_specs=in_specs,
        out_specs=out_specs,
        scratch_shapes=list(scratch),
        compiler_params=pltpu.CompilerParams(vmem_limit_bytes=LIMIT),
        cost_estimate=pl.CostEstimate(flops=cost[0], bytes_accessed=cost[1], transcendentals=0),
        name=name,
    )


def shape(dims, dtype):
    return jax.ShapeDtypeStruct(dims, dtype)


def pack_kernel(gate_up, down, out_w, gains, token, *refs):
    outs, sem = refs[:NY], refs[NY]
    y = lax.axis_index("y")
    copies = []
    feats = down.shape[0]
    units = down.shape[1] // NY
    for s in range(NY):
        place = lax.rem(y + s, NY)
        cols = pl.ds(pl.multiple_of(place * units, units), units)
        sources = [gate_up.at[0, :, cols], gate_up.at[1, :, cols], down.at[:, cols], out_w, gains]
        at = 0
        for j, source in enumerate(sources):
            size = source.shape[0]
            copies.append(pltpu.make_async_copy(source, outs[s].at[pl.ds(at, size)], sem.at[s, j]))
            at += size
    for copy in copies:
        copy.start()
    for copy in copies:
        copy.wait()


def sort_kernel(*refs):
    pieces, (ffn, out_w), sem = refs[:NY], refs[NY : NY + 2], refs[NY + 2]
    y = lax.axis_index("y")
    copies = []
    size = ffn.shape[1]
    rest = out_w.shape[1]
    for s in range(NY):
        place = lax.rem(y - s + NY, NY)
        copies.append(pltpu.make_async_copy(pieces[s].at[pl.ds(size, rest)], out_w.at[place], sem.at[s, 0]))
        copies.append(pltpu.make_async_copy(pieces[s].at[pl.ds(0, size)], ffn.at[place], sem.at[s, 1]))
    for copy in copies:
        copy.start()
    for copy in copies:
        copy.wait()


def project_kernel(h_own, h_mate, w_own, w_mate, out, token, hbuf, wbuf, rows_buf):
    core = lax.axis_index("c")
    hbuf[core] = h_own[...].astype(F32)
    hbuf[1 - core] = h_mate[...].astype(F32)
    wbuf[core] = w_own[...]
    wbuf[1 - core] = w_mate[...]
    rows_buf[...] = jnp.concatenate([hbuf[0].T, hbuf[1].T], axis=1)
    blocks, rows, _ = out.shape
    width = w_own.shape[2]
    chosen = jnp.concatenate(
        [
            rows_buf[pl.ds(pl.multiple_of((2 * b + core) * rows, rows), rows), :]
            for b in range(blocks)
        ],
        axis=0,
    ).astype(BF16)
    for g in range(3):
        weights = jnp.concatenate([wbuf[0, g], wbuf[1, g]], axis=0)
        part = jnp.dot(chosen, weights, preferred_element_type=F32).astype(BF16)
        out[:, :, g * width : (g + 1) * width] = part.reshape(blocks, rows, width)
    out[:, :, 3 * width :] = chosen.reshape(blocks, rows, chosen.shape[1])
    token[...] = jnp.zeros(token.shape, F32)


def collect_kernel(got, qk, value, squares, rest):
    x = lax.axis_index("x")
    rows, width = value.shape
    total = got[0, :, : 3 * width].astype(F32)
    for i in range(1, got.shape[0]):
        total += got[i, :, : 3 * width].astype(F32)
    q = total[:, :width]
    k = total[:, width : 2 * width]
    qk[0] = q
    qk[1] = k
    value[...] = total[:, 2 * width :].astype(BF16)
    lane = lax.broadcasted_iota(jnp.int32, squares.shape, 1)
    squares[...] = jnp.where(
        lane < 64, jnp.sum(q * q, axis=1, keepdims=True), jnp.sum(k * k, axis=1, keepdims=True)
    )
    step = width // NY
    for j in range(NY):
        rest[:, j * step : (j + 1) * step] = got[x * NY + j, :, 3 * width :]


def turn(values, cosine, sine):
    heads = values.shape[1] // HEAD_DIM
    parts = []
    for h in range(heads):
        v = values[:, h * HEAD_DIM : (h + 1) * HEAD_DIM]
        parts.append(v * cosine + pltpu.roll(v, HEAD_DIM // 2, 1) * sine)
    return jnp.concatenate(parts, axis=1)


def spread(values, heads):
    rows, width = values.shape
    wide = rows * heads
    row_head = lax.broadcasted_iota(jnp.int32, (wide, width), 0) // rows
    col_head = lax.broadcasted_iota(jnp.int32, (wide, width), 1) // HEAD_DIM
    return jnp.where(row_head == col_head, jnp.concatenate([values] * heads, axis=0), 0.0)


def used_rows(lengths, rows):
    used = lengths[0]
    for r in range(1, rows):
        used = used + lengths[r]
    return used


def score_kernel(lengths, qk, gains, tables, bounds, keys, score, top, turned, kbuf, sem):
    rows, width = turned.shape
    heads = width // HEAD_DIM
    blocks = score.shape[0]
    used = used_rows(lengths, rows)

    def fetch(i):
        return pltpu.make_async_copy(keys.at[pl.ds(i * BLOCK, BLOCK)], kbuf.at[i], sem.at[i])

    for i in range(blocks):
        @pl.when(i * BLOCK < used)
        def _():
            fetch(i).start()

    q = turn(qk[0] * gains[0:1, :], tables[0], tables[1]).astype(BF16)
    turned[...] = q
    q_block = spread(q.astype(F32), heads).astype(BF16)
    starts = bounds[:, 0:1]
    ends = bounds[:, 1:2]
    top[...] = jnp.full(top.shape, -jnp.inf, F32)
    for i in range(blocks):
        @pl.when(i * BLOCK < used)
        def _():
            fetch(i).wait()
            s = lax.dot_general(q_block, kbuf[i], NT, preferred_element_type=F32)
            place = lax.broadcasted_iota(jnp.int32, s.shape, 1) + i * BLOCK
            s = jnp.where((place >= starts) & (place < ends), s, -jnp.inf)
            score[i] = s
            top[...] = jnp.maximum(top[...], jnp.max(s, axis=1, keepdims=True))


def attend_kernel(lengths, sq0, sq1, sq2, sq3, qk, turned, value, gains, tables, score, top, values, *refs):
    pieces = refs[: 2 * NZ]
    key_out, partial, gain_out = refs[2 * NZ : 2 * NZ + 3]
    vbuf, wbuf, acc, total, vsem, wsem = refs[2 * NZ + 3 :]
    rows, width = turned.shape
    heads = width // HEAD_DIM
    blocks = score.shape[0]
    model = width * NX
    used = used_rows(lengths, rows)
    z = lax.axis_index("z")
    core = lax.axis_index("c")

    def fetch(i):
        return pltpu.make_async_copy(values.at[pl.ds(i * BLOCK, BLOCK)], vbuf.at[i], vsem.at[i])

    for i in range(blocks):
        @pl.when(i * BLOCK < used)
        def _():
            fetch(i).start()
    copies = []
    for s in range(NZ):
        place = lax.rem(z - s + NZ, NZ)
        copies.append(pltpu.make_async_copy(pieces[2 * s], wbuf.at[place, core], wsem.at[s, 0]))
        copies.append(pltpu.make_async_copy(pieces[2 * s + 1], wbuf.at[place, 1 - core], wsem.at[s, 1]))
    for copy in copies:
        copy.start()

    squares = sq0[...] + sq1[...] + sq2[...] + sq3[...]
    q_factor = lax.rsqrt(squares[:, 0:1] / model + EPS)
    k_factor = lax.rsqrt(squares[:, 64:65] / model + EPS)
    new_key = turn(qk[1] * k_factor * gains[1:2, :], tables[0], tables[1]).astype(BF16)
    key_out[...] = new_key
    factor = jnp.concatenate([q_factor] * heads, axis=0) * HEAD_DIM ** (-0.5)
    q_all = spread(turned[...].astype(F32), heads)
    k_all = jnp.concatenate([new_key.astype(F32)] * heads, axis=0)
    v_all = jnp.concatenate([value[...].astype(F32)] * heads, axis=0)
    own = jnp.sum(q_all * k_all, axis=1, keepdims=True) * factor
    highest = jnp.maximum(own, top[:, 0:1] * factor)
    own_weight = jnp.exp(own - highest).astype(BF16).astype(F32)
    total[...] = jnp.broadcast_to(own_weight, total.shape)
    acc[...] = own_weight * v_all
    for i in range(blocks):
        @pl.when(i * BLOCK < used)
        def _():
            fetch(i).wait()
            w = jnp.exp(score[i] * factor - highest).astype(BF16)
            total[...] += jnp.sum(w.astype(F32), axis=1, keepdims=True)
            acc[...] += jnp.dot(w, vbuf[i], preferred_element_type=F32)
    result = acc[...] / total[:, 0:1]
    attended = jnp.concatenate(
        [
            result[h * rows : (h + 1) * rows, h * HEAD_DIM : (h + 1) * HEAD_DIM]
            for h in range(heads)
        ],
        axis=1,
    ).astype(BF16)
    for copy in copies:
        copy.wait()
    feats = width // (NY * NC)
    for b in range(NZ):
        weights = jnp.concatenate(
            [wbuf[b, c, y, :feats] for y in range(NY) for c in range(NC)], axis=0
        )
        partial[b] = lax.dot_general(attended, weights, NT, preferred_element_type=F32)
        both = wbuf[b, 0, 0, feats:].astype(F32)
        for y in range(NY):
            for c in range(NC):
                if y or c:
                    both += wbuf[b, c, y, feats:].astype(F32)
        gain_out[b, 0:1] = both[0:1] + both[1:2]
        gain_out[b, 1:2] = both[2:3] + both[3:4]


def fan_kernel(got, rest, out):
    total = got[0] + got[1] + got[2] + got[3]
    message = jnp.concatenate([total.astype(BF16), rest[...]], axis=1)
    for i in range(out.shape[0]):
        out[i] = message


def ffn_kernel(got, gains, w_hbm, own_mid, out, wbuf, mid_buf, sem):
    width = got.shape[2] // 2
    model = width * NX
    place = lax.axis_index("y") * NX + lax.axis_index("x")
    copies = [
        pltpu.make_async_copy(w_hbm.at[g], wbuf.at[g], sem.at[g]) for g in range(w_hbm.shape[0])
    ]
    for copy in copies:
        copy.start()

    def block(x, part):
        return jnp.concatenate(
            [got[y * NX + x, :, part * width : (part + 1) * width] for y in range(NY)], axis=0
        ).astype(F32)

    branch = [block(x, 0) for x in range(NX)]
    power = jnp.sum(branch[0] * branch[0], axis=1, keepdims=True)
    for x in range(1, NX):
        power += jnp.sum(branch[x] * branch[x], axis=1, keepdims=True)
    factor = lax.rsqrt(power / model + EPS)
    mid = []
    for x in range(NX):
        m = (block(x, 1) + branch[x] * factor * gains[x, 0:1]).astype(BF16)
        mid_buf[:, x * width : (x + 1) * width] = m.astype(F32)
        mid.append(m)
    feats = wbuf.shape[2] // 3

    def weights(z, part):
        return jnp.concatenate(
            [
                wbuf[z * NC + c, y, part * feats : (part + 1) * feats]
                for y in range(NY)
                for c in range(NC)
            ],
            axis=0,
        )

    gate = lift = None
    for z in range(NZ):
        copies[2 * z].wait()
        copies[2 * z + 1].wait()
        g = jnp.dot(mid[z], weights(z, 0), preferred_element_type=F32)
        u = jnp.dot(mid[z], weights(z, 1), preferred_element_type=F32)
        gate = g if gate is None else gate + g
        lift = u if lift is None else lift + u
    act = (gate / (1.0 + jnp.exp(-gate)) * lift).astype(BF16)
    own = out.shape[1]
    for z in range(NZ):
        f = lax.dot_general(act, weights(z, 2), NT, preferred_element_type=F32)
        for d in range(out.shape[0]):
            out[d, :, z * width : (z + 1) * width] = f[d * own : (d + 1) * own]
    pair = mid_buf[pl.ds(pl.multiple_of(place // 2 * 8, 8), 8), :]
    own_mid[...] = jnp.where(lax.rem(place, 2) == 0, pair[:own], pair[own:])


def finish_kernel(got, own_mid, gains, out):
    total = got[0]
    for i in range(1, got.shape[0]):
        total += got[i]
    model = total.shape[1]
    power = jnp.sum(total * total, axis=1, keepdims=True) / model
    gain = jnp.concatenate([gains[z, 1:2] for z in range(NZ)], axis=1)
    hidden = (own_mid[...] + total * lax.rsqrt(power + EPS) * gain).astype(BF16)
    feats = out.shape[2]
    for r in range(model // feats):
        part = hidden[:, r * feats : (r + 1) * feats]
        for x in range(NX):
            out[r * NX + x] = part


def ring(shift, size):
    return [(i, (i + shift) % size) for i in range(size)]


def body(hidden_in, lengths, w_qkv, qk_gain, cache_keys, cache_values, w_out, norm_gain,
         w_gate_up, w_down):
    rows = lengths.shape[0]
    width = w_qkv.shape[2]
    heads = width // HEAD_DIM
    feats = hidden_in.shape[1]
    model = width * NX
    wide = rows * heads
    blocks = cache_keys.shape[0] // BLOCK
    y_here = lax.axis_index("y")
    c_here = lax.axis_index("c")

    flipped = hidden_in.T
    mate_rows = lax.ppermute(flipped, "c", ring(1, NC))
    mate_w = lax.ppermute(w_qkv, "c", ring(1, NC))
    message, token = call(
        project_kernel,
        (shape((NZ * NY, rows, 3 * width + 2 * feats), BF16), shape((8, 128), F32)),
        [VMEM] * 4,
        (VMEM, VMEM),
        [
            pltpu.VMEM((2, feats, flipped.shape[1]), F32),
            pltpu.VMEM((2,) + w_qkv.shape, BF16),
            pltpu.VMEM((flipped.shape[1], 2 * feats), F32),
        ],
        (1 << 27, 2 << 20),
        "project",
    )(flipped, mate_rows, w_qkv, mate_w)
    got = lax.all_to_all(message, ("z", "y"), 0, 0, tiled=True)

    high = norm_gain.astype(BF16)
    low = (norm_gain - high.astype(F32)).astype(BF16)
    gain_rows = jnp.stack([high[0], low[0], high[1], low[1]])
    gain_tile = jnp.zeros((8, width), BF16)
    gain_tile = lax.dynamic_update_slice(
        gain_tile, gain_rows, (jnp.int32(0), (y_here * NC + c_here) * feats)
    )
    units = w_down.shape[1] // NY
    height = 4 * feats + 8
    pieces = call(
        pack_kernel,
        (shape((height, units), BF16),) * NY,
        [ANY] * 5,
        (ANY,) * NY,
        [pltpu.SemaphoreType.DMA((NY, 5))],
        (0, 2 << 20),
        "pack",
    )(w_gate_up, w_down, w_out, gain_tile, token)
    pieces = [pieces[0]] + [lax.ppermute(pieces[s], "y", ring(s, NY)) for s in range(1, NY)]
    ffn_part, out_part = call(
        sort_kernel,
        (shape((NY, 3 * feats, units), BF16), shape((NY, feats + 8, units), BF16)),
        [ANY] * NY,
        (ANY, ANY),
        [pltpu.SemaphoreType.DMA((NY, 2))],
        (0, 2 << 20),
        "sort",
    )(*pieces)
    ffn_weights = lax.all_gather(ffn_part, ("z", "c"), axis=0, tiled=False)
    out_pieces = []
    for s in range(NZ):
        piece = out_part if s == 0 else lax.ppermute(out_part, "z", ring(s, NZ))
        out_pieces += [piece, lax.ppermute(piece, "c", ring(1, NC))]

    qk, value_new, squares, rest = call(
        collect_kernel,
        (
            shape((2, rows, width), F32),
            shape((rows, width), BF16),
            shape((rows, 128), F32),
            shape((rows, width), BF16),
        ),
        [VMEM],
        (VMEM,) * 4,
        (),
        (1 << 20, 1 << 20),
        "collect",
    )(got)
    others = [lax.ppermute(squares, "x", ring(s, NX)) for s in range(1, NX)]
    half = HEAD_DIM // 2
    freqs = jnp.power(THETA, -(jnp.arange(half, dtype=F32) * 2.0 / HEAD_DIM))
    angles = lengths.astype(F32)[:, None] * freqs[None, :]
    cosine = jnp.cos(angles)
    sine = jnp.sin(angles)
    tables = jnp.stack(
        [jnp.concatenate([cosine, cosine], axis=1), jnp.concatenate([-sine, sine], axis=1)]
    )
    ends = jnp.cumsum(lengths)
    bounds = jnp.tile(jnp.stack([ends - lengths, ends], axis=1), (heads, 1))
    score, top, turned = call(
        score_kernel,
        (
            shape((blocks, wide, BLOCK), F32),
            shape((wide, 128), F32),
            shape((rows, width), BF16),
        ),
        [SMEM, VMEM, VMEM, VMEM, VMEM, HBM],
        (VMEM,) * 3,
        [pltpu.VMEM((blocks, BLOCK, width), BF16), pltpu.SemaphoreType.DMA((blocks,))],
        (1 << 28, 4 << 20),
        "score",
    )(lengths, qk, qk_gain, tables, bounds, cache_keys)
    key_new, partial, gains = call(
        attend_kernel,
        (
            shape((rows, width), BF16),
            shape((NX, rows, width), F32),
            shape((NZ, 8, width), F32),
        ),
        [SMEM] + [VMEM] * 11 + [HBM] + [ANY] * (2 * NZ),
        (VMEM,) * 3,
        [
            pltpu.VMEM((blocks, BLOCK, width), BF16),
            pltpu.VMEM((NZ, NC, NY, feats + 8, units), BF16),
            pltpu.VMEM((wide, width), F32),
            pltpu.VMEM((wide, 128), F32),
            pltpu.SemaphoreType.DMA((blocks,)),
            pltpu.SemaphoreType.DMA((NZ, 2)),
        ],
        (1 << 28, 6 << 20),
        "attend",
    )(lengths, squares, *others, qk, turned, value_new, qk_gain, tables, score, top, cache_values,
      *out_pieces)

    got = lax.all_to_all(partial, "x", 0, 0, tiled=True)
    message = call(
        fan_kernel,
        shape((NY * NX, rows, 2 * width), BF16),
        [VMEM] * 2,
        VMEM,
        (),
        (1 << 16, 1 << 19),
        "fan",
    )(got, rest)
    got = lax.all_to_all(message, ("y", "x"), 0, 0, tiled=True)
    mine = rows // NX
    own_mid, partial = call(
        ffn_kernel,
        (shape((mine, model), F32), shape((NY * NX, mine, model), F32)),
        [VMEM, VMEM, HBM],
        (VMEM, VMEM),
        [
            pltpu.VMEM(ffn_weights.shape, BF16),
            pltpu.VMEM((NY * rows, model), F32),
            pltpu.SemaphoreType.DMA((ffn_weights.shape[0],)),
        ],
        (1 << 28, 7 << 20),
        "feed_forward",
    )(got, gains, ffn_weights)
    got = lax.all_to_all(partial, ("y", "x"), 0, 0, tiled=True)
    message = call(
        finish_kernel,
        shape((NZ * NY * NC * NX, mine, feats), BF16),
        [VMEM] * 3,
        VMEM,
        (),
        (1 << 18, 1 << 19),
        "finish",
    )(got, own_mid, gains)
    hidden = lax.all_to_all(message, ("z", "y", "c", "x"), 0, 0, tiled=True)
    return hidden.reshape(-1, feats), key_new, value_new


def solution(mesh):
    fine = Mesh(mesh.devices.reshape(NZ, NY, NC, NX), ("z", "y", "c", "x"))
    req = ("z", "y", "c")
    return jax.shard_map(
        body,
        mesh=fine,
        in_specs=(
            P(None, req),
            P(req),
            P(None, req, "x"),
            P(None, "x"),
            P(req, "x"),
            P(req, "x"),
            P(req, "x"),
            P(None, req),
            P(None, req, "x"),
            P(req, "x"),
        ),
        out_specs=(P(None, req), P(req, "x"), P(req, "x")),
        check_vma=False,
    )
```

time: 529 us -> 164 us (0.31)
  waiting for transfers between devices: 290 us -> 33.9 us
  blocking collectives: 167 us -> 49.4 us
  starting transfers between devices: 0.21 us -> 37 us
  matrix products: 16.1 us -> 0 us
  local copies, waits for them, and re-layouts: 27.1 us -> 11.3 us
  Pallas kernels: 0 us -> 15.7 us
  other arithmetic: 12.2 us -> 1.15 us
    reduce_scatter x2 -> x0, waiting for transfers between devices: 171 us -> none  [the longest x1 89.2 us: body(): lax.psum_scatter(product.reshape(rows_here * lax.axis_size('req'), 2 * un...]
    psum x3 -> x0, blocking collectives: 138 us -> none  [the longest x1 64.9 us: body(): ffn_power = lax.psum(jnp.sum(ffn_full * ffn_full, axis=1), 'req')]
    psum x2 -> x0, waiting for transfers between devices: 72.3 us -> none  [the longest x1 37.4 us: body(): ffn_full = lax.psum(down_part, 'head')]
    all_to_all x0 -> x4, blocking collectives: none -> 49.4 us  [the longest x1 15.8 us: body(): hidden = lax.all_to_all(message, ('z', 'y', 'c', 'x'), 0, 0, tiled=True)]
    all_gather x1, waiting for transfers between devices: 46.6 us -> 0.01 us  [body(): ffn_weights = lax.all_gather(ffn_part, ('z', 'c'), axis=0, tiled=False)]
    ppermute x0 -> x15, waiting for transfers between devices: none -> 33.9 us  [the longest x3 22.1 us: body(): piece = out_part if s == 0 else lax.ppermute(out_part, 'z', ring(s, NZ))]
    ppermute x0 -> x15, starting transfers between devices: none -> 29.8 us  [the longest x4 13.1 us: body(): out_pieces += [piece, lax.ppermute(piece, 'c', ring(1, NC))]]
    all_gather x1 -> x0, blocking collectives: 28.3 us -> none  [body(): lax.all_gather(attended, 'req', axis=0, tiled=True)]
  transfers between devices with their start and end apart: 5 -> 17, of which waited for: 5 -> 6; matrix products, arithmetic and copies ran while one was open for 0% -> 1% of each run, Pallas kernels for 0% -> 6%
where the time goes in v2:
time: 164 us; the launch traced here: 163 us
  blocking collectives  49.4 us (30%)
  starting transfers between devices  37 us (23%)
  waiting for transfers between devices  33.9 us (21%)
  Pallas kernels  15.7 us (10%)
  between operations  14.3 us (9%)
  local copies, waits for them, and re-layouts  11.3 us (7%)
    ppermute x3, waiting for transfers between devices, body(): piece = out_part if s == 0 else lax.ppermute(out_part, 'z', ring(s, NZ))  22.1 us
    all_to_all x1, blocking collectives, body(): hidden = lax.all_to_all(message, ('z', 'y', 'c', 'x'), 0, 0, tiled=True)  15.8 us
    all_to_all x1, blocking collectives, body(): got = lax.all_to_all(partial, ('y', 'x'), 0, 0, tiled=True)  13.3 us
    all_to_all x1, blocking collectives, body(): got = lax.all_to_all(message, ('y', 'x'), 0, 0, tiled=True)  13.1 us
    ppermute x4, starting transfers between devices, body(): out_pieces += [piece, lax.ppermute(piece, 'c', ring(1, NC))]  13.1 us
    ppermute x3, waiting for transfers between devices, body(): lax.ppermute(pieces[s], 'y', ring(s, NY))  11.2 us
    unnamed x26, local copies, waits for them, and re-layouts  10.7 us
    all_to_all x1, blocking collectives, body(): got = lax.all_to_all(partial, 'x', 0, 0, tiled=True)  7.21 us
  transfers between devices with their start and end apart: 17, of which 6 were waited for; matrix products, arithmetic and copies ran while one was open for 1% of the time, Pallas kernels for 6%

profile of v2, /device:TPU:1, one launch (start us, length us, event | category | flops | bytes accessed | tf_op | source)
XLA Modules:
  0.0 162.6 jit_solution(11873163982901417935)
XLA Ops:
  7.2 0.0 all-gather.3.cloned.1.call-start
  7.2 1.5 collective-permute-start
  8.7 0.1 collective-permute-start.1
  8.8 0.8 subtract_convert_fusion
  9.6 0.5 dynamic_update_slice.3.gains
  10.1 0.0 collective-permute-done.h_mate
  10.1 0.2 collective-permute-done.1.w_mate
  10.4 0.9 copy-done.5
  11.3 0.8 copy-done.6
  12.2 1.7 %project.1 = (bf16[16,16,1664]{2,1,0:T(8,128)(2,1)}, f32[8,128]{1,0:T(8,128)S(1)}) custom-call(bf16[64,512]{1,0:T(8,128)(2,1)S(1)} %bitcast.14, bf16[64,512]{1,0:T(8,128)(2,1)S(1)} %collective-permute-done.h_mate, bf16[3,64,512]{2,1,0:T(8,128)(2,1)S(1)} %copy-done.5, bf16[3,64,512]{2,1,0:T(8,128)(2,1)S(1)} %collective-permute-done.1.w_mate), custom_call_target="tpu_custom_call" | custom-call | flops 134217728 | bytes 2097152 | tf_op jit(solution)/shard_map/project/pallas_call | solution.py:347
  13.8 1.0 copy-done.3
  14.9 0.9 copy-done.4
  15.8 0.8 copy-done.7
  16.6 0.7 pack.1
  17.4 1.4 collective-permute-start.5
  18.8 2.6 %collective-permute-start.6 = (bf16[264,512]{1,0:T(8,128)(2,1)S(1)}, bf16[264,512]{1,0:T(8,128)(2,1)S(1)}, u32[]{:S(2)}, u32[]{:S(2)}) collective-permute-start(bf16[264,512]{1,0:T(8,128)(2,1)S(1)} %get-tuple-element.33), channel_id=1, source_target_pairs={{0,16},{8,24},{16,0},{24,8},{1,17},{9,25},{17,1},{25,9},{2,18},{10... | collective-permute-start | bytes 811016 | tf_op jit(solution)/shard_map/ppermute | solution.py:380
  21.5 1.1 collective-permute-start.7
  22.5 4.4 %collective-permute-done.5.refs_1_ = bf16[264,512]{1,0:T(8,128)(2,1)S(1)} collective-permute-done((bf16[264,512]{1,0:T(8,128)(2,1)S(1)}, bf16[264,512]{1,0:T(8,128)(2,1)S(1)}, u32[]{:S(2)}, u32[]{:S(2)}) %collective-permute-start.5) | collective-permute-done | bytes 270368 | tf_op jit(solution)/shard_map/ppermute | solution.py:380
  26.9 6.8 %collective-permute-done.6.refs_2_ = bf16[264,512]{1,0:T(8,128)(2,1)S(1)} collective-permute-done((bf16[264,512]{1,0:T(8,128)(2,1)S(1)}, bf16[264,512]{1,0:T(8,128)(2,1)S(1)}, u32[]{:S(2)}, u32[]{:S(2)}) %collective-permute-start.6) | collective-permute-done | bytes 270368 | tf_op jit(solution)/shard_map/ppermute | solution.py:380
  33.7 0.0 collective-permute-done.7.refs_3_
  33.7 1.1 sort.1
  34.9 0.0 all-gather.3.cloned.1.call-update
  34.9 7.2 %all-to-all-start = ((bf16[16,16,1664]{2,1,0:T(8,128)(2,1)}), bf16[16,16,1664]{2,1,0:T(8,128)(2,1)S(1)}, u32[]{:S(2)}, u32[]{:S(2)}) async-start(bf16[16,16,1664]{2,1,0:T(8,128)(2,1)} %get-tuple-element.23), calls=%async_computation | async-start | bytes 1703936 | tf_op jit(solution)/shard_map/all_to_all | solution.py:360
  42.1 0.1 copy.23
  42.2 0.1 reduce
  42.3 1.4 collective-permute-start.9
  43.8 2.4 %collective-permute-start.11 = (bf16[4,72,512]{2,1,0:T(8,128)(2,1)S(1)}, bf16[4,72,512]{2,1,0:T(8,128)(2,1)S(1)}, u32[]{:S(2)}, u32[]{:S(2)}) collective-permute-start(bf16[4,72,512]{2,1,0:T(8,128)(2,1)S(1)} %get-tuple-element.35.refs_0_), channel_id=1, source_target_pairs={{0,64},{32,96},{64,0},{96,32},{1,65},{33,97},{65,1},{97,33},{2,66}... | collective-permute-start | bytes 884744 | tf_op jit(solution)/shard_map/ppermute | solution.py:393
  46.2 1.2 collective-permute-start.13
  47.3 0.1 multiply_cosine_fusion
  47.5 2.4 %collective-permute-start.8 = (bf16[4,72,512]{2,1,0:T(8,128)(2,1)S(1)}, bf16[4,72,512]{2,1,0:T(8,128)(2,1)S(1)}, u32[]{:S(2)}, u32[]{:S(2)}) collective-permute-start(bf16[4,72,512]{2,1,0:T(8,128)(2,1)S(1)} %get-tuple-element.35.refs_0_), channel_id=1, source_target_pairs={{0,4},{4,0},{1,5},{5,1},{2,6},{6,2},{3,7},{7,3},{8,12},{12,8},{9,1... | collective-permute-start | bytes 884744 | tf_op jit(solution)/shard_map/ppermute | solution.py:394
  49.9 14.6 %collective-permute-done.9.refs_2_ = bf16[4,72,512]{2,1,0:T(8,128)(2,1)S(1)} collective-permute-done((bf16[4,72,512]{2,1,0:T(8,128)(2,1)S(1)}, bf16[4,72,512]{2,1,0:T(8,128)(2,1)S(1)}, u32[]{:S(2)}, u32[]{:S(2)}) %collective-permute-start.9) | collective-permute-done | bytes 294944 | tf_op jit(solution)/shard_map/ppermute | solution.py:393
  64.5 5.0 %collective-permute-start.10 = (bf16[4,72,512]{2,1,0:T(8,128)(2,1)S(1)}, bf16[4,72,512]{2,1,0:T(8,128)(2,1)S(1)}, u32[]{:S(2)}, u32[]{:S(2)}) collective-permute-start(bf16[4,72,512]{2,1,0:T(8,128)(2,1)S(1)} %collective-permute-done.9.refs_2_), channel_id=1, source_target_pairs={{0,4},{4,0},{1,5},{5,1},{2,6},{6,2},{3,7},{7,3},{8,12},{12,8},{9,1... | collective-permute-start | bytes 884744 | tf_op jit(solution)/shard_map/ppermute | solution.py:394
  69.5 7.4 %collective-permute-done.11.refs_4_ = bf16[4,72,512]{2,1,0:T(8,128)(2,1)S(1)} collective-permute-done((bf16[4,72,512]{2,1,0:T(8,128)(2,1)S(1)}, bf16[4,72,512]{2,1,0:T(8,128)(2,1)S(1)}, u32[]{:S(2)}, u32[]{:S(2)}) %collective-permute-start.11) | collective-permute-done | bytes 294944 | tf_op jit(solution)/shard_map/ppermute | solution.py:393
  77.0 5.7 %collective-permute-start.12 = (bf16[4,72,512]{2,1,0:T(8,128)(2,1)S(1)}, bf16[4,72,512]{2,1,0:T(8,128)(2,1)S(1)}, u32[]{:S(2)}, u32[]{:S(2)}) collective-permute-start(bf16[4,72,512]{2,1,0:T(8,128)(2,1)S(1)} %collective-permute-done.11.refs_4_), channel_id=1, source_target_pairs={{0,4},{4,0},{1,5},{5,1},{2,6},{6,2},{3,7},{7,3},{8,12},{12,8},{9,1... | collective-permute-start | bytes 884744 | tf_op jit(solution)/shard_map/ppermute | solution.py:394
  82.6 0.0 collective-permute-done.13.refs_6_
  82.6 0.0 collective-permute-start.14
  82.6 0.1 maximum_bitcast_fusion
  82.7 0.1 copy.24
  82.8 0.0 all-to-all-done.got
  82.8 0.7 collect.1
  83.5 1.2 collective-permute-start.2
  84.7 0.1 copy.28
  84.8 0.0 collective-permute-done.8.refs_1_
  84.8 2.5 %collective-permute-start.3 = (f32[16,128]{1,0:T(8,128)S(1)}, f32[16,128]{1,0:T(8,128)S(1)}, u32[]{:S(2)}, u32[]{:S(2)}) collective-permute-start(f32[16,128]{1,0:T(8,128)S(1)} %get-tuple-element.24.sq0), channel_id=1, source_target_pairs={{0,2},{1,3},{2,0},{3,1},{4,6},{5,7},{6,4},{7,5},{8,10},{9,11},{10,... | collective-permute-start | bytes 24584 | tf_op jit(solution)/shard_map/ppermute | solution.py:410
  87.3 0.3 collective-permute-done.2.sq1
  87.6 1.3 collective-permute-start.4
  88.9 2.2 %copy-done.2 = bf16[4096,512]{1,0:T(8,128)(2,1)S(1)} copy-done((bf16[4096,512]{1,0:T(8,128)(2,1)S(1)}, bf16[4096,512]{1,0:T(8,128)(2,1)}, u32[]{:S(2)}) %copy-start.2) | copy-done | bytes 4194328
  91.1 4.0 %score.1 = (f32[8,64,512]{2,1,0:T(8,128)S(1)}, f32[64,128]{1,0:T(8,128)S(1)}, bf16[16,512]{1,0:T(8,128)(2,1)S(1)}) custom-call(s32[16]{0:T(128)S(1)} %copy-done.10, f32[2,16,512]{2,1,0:T(8,128)S(1)} %get-tuple-element.25.qk, f32[2,512]{1,0:T(2,128)S(1)} %copy-done.8, f32[2,16,128]{2,1,0:T(8,128)S(1)} %pad_maximum_fusion.tables, s32[64,2]{1,0:T(8,128)S(1)} %bitcast.12, ...), custom_call_target="tpu_custom_call" | custom-call | flops 268435456 | bytes 4194304 | tf_op jit(solution)/shard_map/score/pallas_call | solution.py:421
  95.1 0.0 collective-permute-done.3.sq2
  95.1 0.0 collective-permute-done.4.sq3
  95.1 0.0 collective-permute-done.10.refs_3_
  95.1 0.0 collective-permute-done.12.refs_5_
  95.1 0.0 collective-permute-done.14.refs_7_
  95.2 4.9 %attend.1 = (bf16[16,512]{1,0:T(8,128)(2,1)}, f32[4,16,512]{2,1,0:T(8,128)S(1)}, f32[4,8,512]{2,1,0:T(8,128)S(1)}) custom-call(s32[16]{0:T(128)S(1)} %copy-done.10, f32[16,128]{1,0:T(8,128)S(1)} %get-tuple-element.24.sq0, f32[16,128]{1,0:T(8,128)S(1)} %collective-permute-done.2.sq1, f32[16,128]{1,0:T(8,128)S(1)} %collective-permute-done.3.sq2, ...), custom_call_target="tpu_custom_call" | custom-call | flops 268435456 | bytes 6291456 | tf_op jit(solution)/shard_map/attend/pallas_call | solution.py:434
  100.1 7.2 %all_to_all.25.got = f32[4,16,512]{2,1,0:T(8,128)S(1)} all-to-all(f32[4,16,512]{2,1,0:T(8,128)S(1)} %get-tuple-element.36), channel_id=1, replica_groups=mesh['z'=4,'y'=4,'c'=2,'x'=4] {'x'}, dimensions={0} | all-to-all | bytes 262144 | tf_op jit(solution)/shard_map/all_to_all | solution.py:456
  107.3 13.1 %all_to_all.26.got = bf16[16,16,1024]{2,1,0:T(8,128)(2,1)S(1)} all-to-all(bf16[16,16,1024]{2,1,0:T(8,128)(2,1)S(1)} %fan.1), channel_id=1, replica_groups=mesh['z'=4,'y'=4,'c'=2,'x'=4] {'y','x'}, dimensions={0} | all-to-all | bytes 1048576 | tf_op jit(solution)/shard_map/all_to_all | solution.py:466
  120.4 2.8 %copy-done = bf16[32,192,512]{2,1,0:T(8,128)(2,1)S(1)} copy-done((bf16[32,192,512]{2,1,0:T(8,128)(2,1)S(1)}, bf16[32,192,512]{2,1,0:T(8,128)(2,1)}, u32[]{:S(2)}) %copy-start) | copy-done | bytes 6291480
  123.2 2.4 %feed_forward.1 = (f32[4,2048]{1,0:T(4,128)S(1)}, f32[16,4,2048]{2,1,0:T(4,128)S(1)}) custom-call(bf16[16,16,1024]{2,1,0:T(8,128)(2,1)S(1)} %all_to_all.26.got, f32[4,8,512]{2,1,0:T(8,128)S(1)} %get-tuple-element.38.gains, bf16[8,4,192,512]{3,2,1,0:T(8,128)(2,1)S(1)} %bitcast.11), custom_call_target="tpu_custom_call" | custom-call | flops 268435456 | bytes 7340032 | tf_op jit(solution)/shard_map/feed_forward/pallas_call | solution.py:468
  125.6 13.3 %all_to_all.27.got = f32[16,4,2048]{2,1,0:T(4,128)S(1)} all-to-all(f32[16,4,2048]{2,1,0:T(4,128)S(1)} %get-tuple-element.40), channel_id=1, replica_groups=mesh['z'=4,'y'=4,'c'=2,'x'=4] {'y','x'}, dimensions={0} | all-to-all | bytes 1048576 | tf_op jit(solution)/shard_map/all_to_all | solution.py:481
  138.9 0.2 finish.1
  139.1 0.1 reshape.32
  139.2 15.8 %all_to_all.28 = bf16[128,2,128]{2,1,0:T(2,128)(2,1)S(1)} all-to-all(bf16[128,2,128]{2,1,0:T(2,128)(2,1)S(1)} %reshape.32), channel_id=1, replica_groups=mesh['z'=4,'y'=4,'c'=2,'x'=4] {'z','y','c','x'}, dimensions={0} | all-to-all | bytes 131072 | tf_op jit(solution)/shard_map/all_to_all | solution.py:491
  155.0 0.1 reshape.33
  155.1 0.7 copy.26
  (26 shorter events, 0.2 us)
Async XLA Ops:
  7.2 34.9 %copy-start.10 = (s32[16]{0:T(128)S(1)}, s32[16]{0:T(128)}, u32[]{:S(2)}) copy-start(s32[16]{0:T(128)} %lengths.3) | copy-start | bytes 196
  7.2 81.7 %copy-start.8 = (f32[2,512]{1,0:T(2,128)S(1)}, f32[2,512]{1,0:T(2,128)}, u32[]{:S(2)}) copy-start(f32[2,512]{1,0:T(2,128)} %gains.3) | copy-start | bytes 12292
  7.2 113.2 %all-gather.3.cloned.1.call-start = ((), (), s32[]{:S(2)}) async-start(), calls=%async_computation.5 | async-start | bytes 7077888 | tf_op jit(solution)/shard_map/all_gather | solution.py:390
  7.2 2.9 %collective-permute-start = (bf16[64,512]{1,0:T(8,128)(2,1)}, bf16[64,512]{1,0:T(8,128)(2,1)S(1)}, u32[]{:S(2)}, u32[]{:S(2)}) collective-permute-start(bf16[64,512]{1,0:T(8,128)(2,1)} %bitcast.13), channel_id=1, source_target_pairs={{0,4},{4,0},{1,5},{5,1},{2,6},{6,2},{3,7},{7,3},{8,12},{12,8},{9,1... | collective-permute-start | bytes 196616 | tf_op jit(solution)/shard_map/ppermute | solution.py:345
  8.7 1.7 %collective-permute-start.1 = (bf16[3,64,512]{2,1,0:T(8,128)(2,1)}, bf16[3,64,512]{2,1,0:T(8,128)(2,1)S(1)}, u32[]{:S(2)}, u32[]{:S(2)}) collective-permute-start(bf16[3,64,512]{2,1,0:T(8,128)(2,1)} %w_own.1), channel_id=1, source_target_pairs={{0,4},{4,0},{1,5},{5,1},{2,6},{6,2},{3,7},{7,3},{8,12},{12,8},{9,1... | collective-permute-start | bytes 589832 | tf_op jit(solution)/shard_map/ppermute | solution.py:346
  10.4 0.9 copy-start.5
  11.3 0.8 copy-start.6
  13.8 1.0 copy-start.3
  14.9 0.9 copy-start.4
  15.8 0.8 copy-start.7
  17.4 9.5 %collective-permute-start.5 = (bf16[264,512]{1,0:T(8,128)(2,1)S(1)}, bf16[264,512]{1,0:T(8,128)(2,1)S(1)}, u32[]{:S(2)}, u32[]{:S(2)}) collective-permute-start(bf16[264,512]{1,0:T(8,128)(2,1)S(1)} %get-tuple-element.32), channel_id=1, source_target_pairs={{0,8},{8,16},{16,24},{24,0},{1,9},{9,17},{17,25},{25,1},{2,10},{10... | collective-permute-start | bytes 811016 | tf_op jit(solution)/shard_map/ppermute | solution.py:380
  18.8 14.9 %collective-permute-start.6 = (bf16[264,512]{1,0:T(8,128)(2,1)S(1)}, bf16[264,512]{1,0:T(8,128)(2,1)S(1)}, u32[]{:S(2)}, u32[]{:S(2)}) collective-permute-start(bf16[264,512]{1,0:T(8,128)(2,1)S(1)} %get-tuple-element.33), channel_id=1, source_target_pairs={{0,16},{8,24},{16,0},{24,8},{1,17},{9,25},{17,1},{25,9},{2,18},{10... | collective-permute-start | bytes 811016 | tf_op jit(solution)/shard_map/ppermute | solution.py:380
  21.5 12.3 %collective-permute-start.7 = (bf16[264,512]{1,0:T(8,128)(2,1)S(1)}, bf16[264,512]{1,0:T(8,128)(2,1)S(1)}, u32[]{:S(2)}, u32[]{:S(2)}) collective-permute-start(bf16[264,512]{1,0:T(8,128)(2,1)S(1)} %get-tuple-element.34), channel_id=1, source_target_pairs={{0,24},{8,0},{16,8},{24,16},{1,25},{9,1},{17,9},{25,17},{2,26},{10... | collective-permute-start | bytes 811016 | tf_op jit(solution)/shard_map/ppermute | solution.py:380
  34.9 47.9 %all-to-all-start = ((bf16[16,16,1664]{2,1,0:T(8,128)(2,1)}), bf16[16,16,1664]{2,1,0:T(8,128)(2,1)S(1)}, u32[]{:S(2)}, u32[]{:S(2)}) async-start(bf16[16,16,1664]{2,1,0:T(8,128)(2,1)} %get-tuple-element.23), calls=%async_computation | async-start | bytes 1703936 | tf_op jit(solution)/shard_map/all_to_all | solution.py:360
  42.3 22.2 %collective-permute-start.9 = (bf16[4,72,512]{2,1,0:T(8,128)(2,1)S(1)}, bf16[4,72,512]{2,1,0:T(8,128)(2,1)S(1)}, u32[]{:S(2)}, u32[]{:S(2)}) collective-permute-start(bf16[4,72,512]{2,1,0:T(8,128)(2,1)S(1)} %get-tuple-element.35.refs_0_), channel_id=1, source_target_pairs={{0,32},{32,64},{64,96},{96,0},{1,33},{33,65},{65,97},{97,1},{2,34}... | collective-permute-start | bytes 884744 | tf_op jit(solution)/shard_map/ppermute | solution.py:393
  43.8 33.2 %collective-permute-start.11 = (bf16[4,72,512]{2,1,0:T(8,128)(2,1)S(1)}, bf16[4,72,512]{2,1,0:T(8,128)(2,1)S(1)}, u32[]{:S(2)}, u32[]{:S(2)}) collective-permute-start(bf16[4,72,512]{2,1,0:T(8,128)(2,1)S(1)} %get-tuple-element.35.refs_0_), channel_id=1, source_target_pairs={{0,64},{32,96},{64,0},{96,32},{1,65},{33,97},{65,1},{97,33},{2,66}... | collective-permute-start | bytes 884744 | tf_op jit(solution)/shard_map/ppermute | solution.py:393
  46.2 36.5 %collective-permute-start.13 = (bf16[4,72,512]{2,1,0:T(8,128)(2,1)S(1)}, bf16[4,72,512]{2,1,0:T(8,128)(2,1)S(1)}, u32[]{:S(2)}, u32[]{:S(2)}) collective-permute-start(bf16[4,72,512]{2,1,0:T(8,128)(2,1)S(1)} %get-tuple-element.35.refs_0_), channel_id=1, source_target_pairs={{0,96},{32,0},{64,32},{96,64},{1,97},{33,1},{65,33},{97,65},{2,98}... | collective-permute-start | bytes 884744 | tf_op jit(solution)/shard_map/ppermute | solution.py:393
  47.5 37.3 %collective-permute-start.8 = (bf16[4,72,512]{2,1,0:T(8,128)(2,1)S(1)}, bf16[4,72,512]{2,1,0:T(8,128)(2,1)S(1)}, u32[]{:S(2)}, u32[]{:S(2)}) collective-permute-start(bf16[4,72,512]{2,1,0:T(8,128)(2,1)S(1)} %get-tuple-element.35.refs_0_), channel_id=1, source_target_pairs={{0,4},{4,0},{1,5},{5,1},{2,6},{6,2},{3,7},{7,3},{8,12},{12,8},{9,1... | collective-permute-start | bytes 884744 | tf_op jit(solution)/shard_map/ppermute | solution.py:394
  64.5 30.6 %collective-permute-start.10 = (bf16[4,72,512]{2,1,0:T(8,128)(2,1)S(1)}, bf16[4,72,512]{2,1,0:T(8,128)(2,1)S(1)}, u32[]{:S(2)}, u32[]{:S(2)}) collective-permute-start(bf16[4,72,512]{2,1,0:T(8,128)(2,1)S(1)} %collective-permute-done.9.refs_2_), channel_id=1, source_target_pairs={{0,4},{4,0},{1,5},{5,1},{2,6},{6,2},{3,7},{7,3},{8,12},{12,8},{9,1... | collective-permute-start | bytes 884744 | tf_op jit(solution)/shard_map/ppermute | solution.py:394
  77.0 18.2 %collective-permute-start.12 = (bf16[4,72,512]{2,1,0:T(8,128)(2,1)S(1)}, bf16[4,72,512]{2,1,0:T(8,128)(2,1)S(1)}, u32[]{:S(2)}, u32[]{:S(2)}) collective-permute-start(bf16[4,72,512]{2,1,0:T(8,128)(2,1)S(1)} %collective-permute-done.11.refs_4_), channel_id=1, source_target_pairs={{0,4},{4,0},{1,5},{5,1},{2,6},{6,2},{3,7},{7,3},{8,12},{12,8},{9,1... | collective-permute-start | bytes 884744 | tf_op jit(solution)/shard_map/ppermute | solution.py:394
  82.6 12.5 %collective-permute-start.14 = (bf16[4,72,512]{2,1,0:T(8,128)(2,1)S(1)}, bf16[4,72,512]{2,1,0:T(8,128)(2,1)S(1)}, u32[]{:S(2)}, u32[]{:S(2)}) collective-permute-start(bf16[4,72,512]{2,1,0:T(8,128)(2,1)S(1)} %collective-permute-done.13.refs_6_), channel_id=1, source_target_pairs={{0,4},{4,0},{1,5},{5,1},{2,6},{6,2},{3,7},{7,3},{8,12},{12,8},{9,1... | collective-permute-start | bytes 884744 | tf_op jit(solution)/shard_map/ppermute | solution.py:394
  83.5 4.1 %collective-permute-start.2 = (f32[16,128]{1,0:T(8,128)S(1)}, f32[16,128]{1,0:T(8,128)S(1)}, u32[]{:S(2)}, u32[]{:S(2)}) collective-permute-start(f32[16,128]{1,0:T(8,128)S(1)} %get-tuple-element.24.sq0), channel_id=1, source_target_pairs={{0,1},{1,2},{2,3},{3,0},{4,5},{5,6},{6,7},{7,4},{8,9},{9,10},{10,1... | collective-permute-start | bytes 24584 | tf_op jit(solution)/shard_map/ppermute | solution.py:410
  84.8 10.4 %copy-start.1 = (bf16[4096,512]{1,0:T(8,128)(2,1)S(1)}, bf16[4096,512]{1,0:T(8,128)(2,1)}, u32[]{:S(2)}) copy-start(bf16[4096,512]{1,0:T(8,128)(2,1)} %values.1) | copy-start | bytes 12582916
  84.8 10.3 %collective-permute-start.3 = (f32[16,128]{1,0:T(8,128)S(1)}, f32[16,128]{1,0:T(8,128)S(1)}, u32[]{:S(2)}, u32[]{:S(2)}) collective-permute-start(f32[16,128]{1,0:T(8,128)S(1)} %get-tuple-element.24.sq0), channel_id=1, source_target_pairs={{0,2},{1,3},{2,0},{3,1},{4,6},{5,7},{6,4},{7,5},{8,10},{9,11},{10,... | collective-permute-start | bytes 24584 | tf_op jit(solution)/shard_map/ppermute | solution.py:410
  87.6 7.5 %collective-permute-start.4 = (f32[16,128]{1,0:T(8,128)S(1)}, f32[16,128]{1,0:T(8,128)S(1)}, u32[]{:S(2)}, u32[]{:S(2)}) collective-permute-start(f32[16,128]{1,0:T(8,128)S(1)} %get-tuple-element.24.sq0), channel_id=1, source_target_pairs={{0,3},{1,0},{2,1},{3,2},{4,7},{5,4},{6,5},{7,6},{8,11},{9,8},{10,9... | collective-permute-start | bytes 24584 | tf_op jit(solution)/shard_map/ppermute | solution.py:410
  88.9 2.3 %copy-start.2 = (bf16[4096,512]{1,0:T(8,128)(2,1)S(1)}, bf16[4096,512]{1,0:T(8,128)(2,1)}, u32[]{:S(2)}) copy-start(bf16[4096,512]{1,0:T(8,128)(2,1)} %keys.1) | copy-start | bytes 12582916
  91.1 4.0 %copy-start.9 = (bf16[16,512]{1,0:T(8,128)(2,1)S(1)}, bf16[16,512]{1,0:T(8,128)(2,1)}, u32[]{:S(2)}) copy-start(bf16[16,512]{1,0:T(8,128)(2,1)} %get-tuple-element.51.value) | copy-start | bytes 49156
  120.4 2.8 %copy-start = (bf16[32,192,512]{2,1,0:T(8,128)(2,1)S(1)}, bf16[32,192,512]{2,1,0:T(8,128)(2,1)}, u32[]{:S(2)}) copy-start(bf16[32,192,512]{2,1,0:T(8,128)(2,1)} %all-gather.3.cloned.1.call-done) | copy-start | bytes 18874372
Sparse Core Ops, SparseCore 0:
  35.0 60.0 all-gather.2

commit v3 on v2

v3 whole, which is shorter than its diff:
```python
import functools

import jax
import jax.numpy as jnp
from jax import lax
from jax.experimental import pallas as pl
from jax.experimental.pallas import tpu as pltpu
from jax.sharding import Mesh, PartitionSpec as P

HEAD_DIM = 128
EPS = 1e-06
THETA = 500000.0
NT = (((1,), (1,)), ((), ()))
BLOCK = 512
F32 = jnp.float32
BF16 = jnp.bfloat16
NZ, NY, NC, NX = 4, 4, 2, 4
VMEM = pl.BlockSpec(memory_space=pltpu.VMEM)
HBM = pl.BlockSpec(memory_space=pltpu.HBM)
ANY = pl.BlockSpec(memory_space=pl.ANY)
SMEM = pl.BlockSpec(memory_space=pltpu.SMEM)


def call(kernel, out_shape, in_specs, out_specs, scratch=(), cost=(1 << 20, 1 << 20), name=None, limit=4):
    return pl.pallas_call(
        kernel,
        out_shape=out_shape,
        in_specs=in_specs,
        out_specs=out_specs,
        scratch_shapes=list(scratch),
        compiler_params=pltpu.CompilerParams(vmem_limit_bytes=limit * 1024 * 1024),
        cost_estimate=pl.CostEstimate(flops=cost[0], bytes_accessed=cost[1], transcendentals=0),
        name=name,
    )


def hbm(array):
    return pltpu.with_memory_space_constraint(array, pltpu.HBM)


def shape(dims, dtype):
    return jax.ShapeDtypeStruct(dims, dtype)


def run(copies, sem):
    copies = [pltpu.make_async_copy(a, b, sem.at[i]) for i, (a, b) in enumerate(copies)]
    for copy in copies:
        copy.start()
    for copy in copies:
        copy.wait()


def pack_kernel(gate_up, down, token, *refs):
    outs, sem = refs[:NY], refs[NY]
    y = lax.axis_index("y")
    feats = down.shape[0]
    units = down.shape[1] // NY
    copies = []
    for s in range(NY):
        cols = pl.ds(pl.multiple_of(lax.rem(y + s, NY) * units, units), units)
        for part in range(3):
            source = down.at[:, cols] if part == 2 else gate_up.at[part, :, cols]
            copies.append((source, outs[s].at[pl.ds(part * feats, feats)]))
    run(copies, sem)


def sort_kernel(*refs):
    pieces, (out, sem) = refs[:NY], refs[NY + 1 :]
    y = lax.axis_index("y")
    run([(pieces[s], out.at[lax.rem(y + NY - s, NY)]) for s in range(NY)], sem)


def sort(pieces, token, name):
    return call(
        sort_kernel,
        shape((NY,) + pieces[0].shape, BF16),
        [ANY] * (NY + 1),
        ANY,
        [pltpu.SemaphoreType.DMA((NY,))],
        (0, 1 << 20),
        name,
        1,
    )(*pieces, token)


def join_kernel(first, second, token, out, sem):
    half = first.shape[0]
    run([(first, out.at[pl.ds(0, half)]), (second, out.at[pl.ds(half, half)])], sem)


def join(first, second, token):
    return call(
        join_kernel,
        shape((2 * first.shape[0],) + first.shape[1:], first.dtype),
        [ANY] * 3,
        ANY,
        [pltpu.SemaphoreType.DMA((2,))],
        (0, 1 << 20),
        "join",
        1,
    )(first, second, token)


def halves_kernel(up, dn, token, up_half, dn_half, sem):
    half = up_half.shape[0]
    copies = [
        pltpu.make_async_copy(up.at[pl.ds(0, half)], up_half, sem.at[0]),
        pltpu.make_async_copy(dn.at[pl.ds(half, half)], dn_half, sem.at[1]),
    ]
    for copy in copies:
        copy.start()
    for copy in copies:
        copy.wait()


def halves(up, dn, token):
    out = shape((up.shape[0] // 2,) + up.shape[1:], up.dtype)
    return call(
        halves_kernel,
        (out, out),
        [ANY] * 3,
        (ANY, ANY),
        [pltpu.SemaphoreType.DMA((2,))],
        (0, 1 << 20),
        "halves",
        1,
    )(up, dn, token)


def piece_copies(pieces, buf, sem):
    z = lax.axis_index("z")
    core = lax.axis_index("c")
    copies = []
    for m in range(NC):
        c = core if m == 0 else 1 - core
        for i, shift in enumerate((0, NZ - 1, 1, 2)):
            target = buf.at[lax.rem(z + shift, NZ), c]
            copies.append(pltpu.make_async_copy(pieces[m * 4 + i], target, sem.at[m, i]))
    return copies


def project_kernel(h_own, h_mate, w_own, w_mate, out, token, hbuf, wbuf, rows_buf, sem):
    core = lax.axis_index("c")
    copies = [
        pltpu.make_async_copy(w_own, wbuf.at[core], sem.at[0]),
        pltpu.make_async_copy(w_mate, wbuf.at[1 - core], sem.at[1]),
        pltpu.make_async_copy(h_own, hbuf.at[core], sem.at[2]),
        pltpu.make_async_copy(h_mate, hbuf.at[1 - core], sem.at[3]),
    ]
    for copy in copies:
        copy.start()
    copies[2].wait()
    copies[3].wait()
    rows_buf[...] = jnp.concatenate([hbuf[0].astype(F32).T, hbuf[1].astype(F32).T], axis=1)
    blocks, rows, _ = out.shape
    width = w_own.shape[2]
    chosen = jnp.concatenate(
        [
            rows_buf[pl.ds(pl.multiple_of((2 * b + core) * rows, rows), rows), :]
            for b in range(blocks)
        ],
        axis=0,
    ).astype(BF16)
    copies[0].wait()
    copies[1].wait()
    for g in range(3):
        weights = jnp.concatenate([wbuf[0, g], wbuf[1, g]], axis=0)
        part = jnp.dot(chosen, weights, preferred_element_type=F32).astype(BF16)
        out[:, :, g * width : (g + 1) * width] = part.reshape(blocks, rows, width)
    out[:, :, 3 * width :] = chosen.reshape(blocks, rows, chosen.shape[1])
    token[...] = jnp.zeros(token.shape, F32)


def quarter(ref, x):
    pair = ref[pl.ds(pl.multiple_of(x // 2 * 8, 8), 8), :]
    return jnp.where(lax.rem(x, 2) == 0, pair[:4], pair[4:])


def collect_kernel(got, qk, value, squares, rest, rest_buf):
    rows, width = value.shape
    total = got[0, :, : 3 * width].astype(F32)
    for i in range(1, got.shape[0]):
        total += got[i, :, : 3 * width].astype(F32)
    q = total[:, :width]
    k = total[:, width : 2 * width]
    qk[0] = q
    qk[1] = k
    value[...] = total[:, 2 * width :].astype(BF16)
    lane = lax.broadcasted_iota(jnp.int32, squares.shape[1:], 1)
    both = jnp.where(
        lane < 64, jnp.sum(q * q, axis=1, keepdims=True), jnp.sum(k * k, axis=1, keepdims=True)
    )
    for i in range(NX):
        squares[i] = both
    step = got.shape[2] - 3 * width
    for i in range(got.shape[0]):
        rest_buf[:, i * step : (i + 1) * step] = got[i, :, 3 * width :].astype(F32)
    rest[...] = quarter(rest_buf, lax.axis_index("x"))


def turn(values, cosine, sine):
    heads = values.shape[1] // HEAD_DIM
    parts = []
    for h in range(heads):
        v = values[:, h * HEAD_DIM : (h + 1) * HEAD_DIM]
        parts.append(v * cosine + pltpu.roll(v, HEAD_DIM // 2, 1) * sine)
    return jnp.concatenate(parts, axis=1)


def spread(values, heads):
    rows, width = values.shape
    wide = rows * heads
    row_head = lax.broadcasted_iota(jnp.int32, (wide, width), 0) // rows
    col_head = lax.broadcasted_iota(jnp.int32, (wide, width), 1) // HEAD_DIM
    return jnp.where(row_head == col_head, jnp.concatenate([values] * heads, axis=0), 0.0)


def used_rows(lengths, rows):
    used = lengths[0]
    for r in range(1, rows):
        used = used + lengths[r]
    return used


def score_kernel(lengths, qk, gains, tables, bounds, keys, score, top, turned, kbuf, sem):
    rows, width = turned.shape
    heads = width // HEAD_DIM
    blocks = score.shape[0]
    used = used_rows(lengths, rows)

    def fetch(i):
        return pltpu.make_async_copy(keys.at[pl.ds(i * BLOCK, BLOCK)], kbuf.at[i], sem.at[i])

    for i in range(blocks):
        @pl.when(i * BLOCK < used)
        def _():
            fetch(i).start()

    q = turn(qk[0] * gains[0:1, :], tables[0], tables[1]).astype(BF16)
    turned[...] = q
    q_block = spread(q.astype(F32), heads).astype(BF16)
    starts = bounds[:, 0:1]
    ends = bounds[:, 1:2]
    top[...] = jnp.full(top.shape, -jnp.inf, F32)
    for i in range(blocks):
        @pl.when(i * BLOCK < used)
        def _():
            fetch(i).wait()
            s = lax.dot_general(q_block, kbuf[i], NT, preferred_element_type=F32)
            place = lax.broadcasted_iota(jnp.int32, s.shape, 1) + i * BLOCK
            s = jnp.where((place >= starts) & (place < ends), s, -jnp.inf)
            score[i] = s
            top[...] = jnp.maximum(top[...], jnp.max(s, axis=1, keepdims=True))


def attend_kernel(lengths, squares_in, qk, turned, value, gains, tables, score, top, values, *refs):
    pieces = refs[: 4 * NC]
    key_out, partial, gain_out = refs[4 * NC : 4 * NC + 3]
    vbuf, wbuf, acc, total, vsem, wsem = refs[4 * NC + 3 :]
    rows, width = turned.shape
    heads = width // HEAD_DIM
    blocks = score.shape[0]
    model = width * NX
    used = used_rows(lengths, rows)

    def fetch(i):
        return pltpu.make_async_copy(values.at[pl.ds(i * BLOCK, BLOCK)], vbuf.at[i], vsem.at[i])

    for i in range(blocks):
        @pl.when(i * BLOCK < used)
        def _():
            fetch(i).start()
    copies = piece_copies(pieces, wbuf, wsem)
    for copy in copies:
        copy.start()

    squares = squares_in[0] + squares_in[1] + squares_in[2] + squares_in[3]
    q_factor = lax.rsqrt(squares[:, 0:1] / model + EPS)
    k_factor = lax.rsqrt(squares[:, 64:65] / model + EPS)
    new_key = turn(qk[1] * k_factor * gains[1:2, :], tables[0], tables[1]).astype(BF16)
    key_out[...] = new_key
    factor = jnp.concatenate([q_factor] * heads, axis=0) * HEAD_DIM ** (-0.5)
    q_all = spread(turned[...].astype(F32), heads)
    k_all = jnp.concatenate([new_key.astype(F32)] * heads, axis=0)
    v_all = jnp.concatenate([value[...].astype(F32)] * heads, axis=0)
    own = jnp.sum(q_all * k_all, axis=1, keepdims=True) * factor
    highest = jnp.maximum(own, top[:, 0:1] * factor)
    own_weight = jnp.exp(own - highest).astype(BF16).astype(F32)
    total[...] = jnp.broadcast_to(own_weight, total.shape)
    acc[...] = own_weight * v_all
    for i in range(blocks):
        @pl.when(i * BLOCK < used)
        def _():
            fetch(i).wait()
            w = jnp.exp(score[i] * factor - highest).astype(BF16)
            total[...] += jnp.sum(w.astype(F32), axis=1, keepdims=True)
            acc[...] += jnp.dot(w, vbuf[i], preferred_element_type=F32)
    result = acc[...] / total[:, 0:1]
    attended = jnp.concatenate(
        [
            result[h * rows : (h + 1) * rows, h * HEAD_DIM : (h + 1) * HEAD_DIM]
            for h in range(heads)
        ],
        axis=1,
    ).astype(BF16)
    for copy in copies:
        copy.wait()
    feats = width // (NY * NC)
    for b in range(NZ):
        weights = jnp.concatenate(
            [wbuf[b, c, y, :feats] for y in range(NY) for c in range(NC)], axis=0
        )
        a = lax.dot_general(attended, weights, NT, preferred_element_type=F32)
        mine = rows // NX
        for x in range(NX):
            partial[x, :, b * width : (b + 1) * width] = a[x * mine : (x + 1) * mine]
        both = wbuf[b, 0, 0, feats:].astype(F32)
        for y in range(NY):
            for c in range(NC):
                if y or c:
                    both += wbuf[b, c, y, feats:].astype(F32)
        gain_out[b, 0:1] = both[0:1] + both[1:2]
        gain_out[b, 1:2] = both[2:3] + both[3:4]


def fan_kernel(got, rest, gains, own_mid, out):
    total = got[0] + got[1] + got[2] + got[3]
    model = total.shape[1]
    power = jnp.sum(total * total, axis=1, keepdims=True) / model
    gain = jnp.concatenate([gains[z, 0:1] for z in range(NZ)], axis=1)
    mid = (rest[...] + total * lax.rsqrt(power + EPS) * gain).astype(BF16)
    mid32 = mid.astype(F32)
    own_mid[...] = mid32
    message = jnp.concatenate([mid32[:, : model // 2], mid32[:, model // 2 :]], axis=0).astype(BF16)
    for i in range(out.shape[0]):
        out[i] = message


def ffn_kernel(got, *refs):
    pieces = refs[: 4 * NC]
    out, wbuf, sem = refs[4 * NC :]
    copies = piece_copies(pieces, wbuf, sem)
    for copy in copies:
        copy.start()
    places, lines, span = got.shape
    mine = lines // 2
    width = span // 2
    whole = [got[d].astype(F32) for d in range(places)]

    def features(z):
        half, at = z // 2, (z % 2) * width
        return jnp.concatenate(
            [w[half * mine : (half + 1) * mine, at : at + width] for w in whole], axis=0
        ).astype(BF16)

    feats = wbuf.shape[3] // 3

    def weights(z, part):
        return jnp.concatenate(
            [
                wbuf[z, c, y, part * feats : (part + 1) * feats]
                for y in range(NY)
                for c in range(NC)
            ],
            axis=0,
        )

    for copy in copies:
        copy.wait()
    gate = lift = None
    for z in range(NZ):
        mid = features(z)
        g = jnp.dot(mid, weights(z, 0), preferred_element_type=F32)
        u = jnp.dot(mid, weights(z, 1), preferred_element_type=F32)
        gate = g if gate is None else gate + g
        lift = u if lift is None else lift + u
    act = (gate / (1.0 + jnp.exp(-gate)) * lift).astype(BF16)
    for z in range(NZ):
        f = lax.dot_general(act, weights(z, 2), NT, preferred_element_type=F32)
        half, at = z // 2, (z % 2) * width
        for d in range(places):
            out[d, half * mine : (half + 1) * mine, at : at + width] = f[d * mine : (d + 1) * mine]


def finish_kernel(got, own_mid, gains, out):
    total = got[0]
    for i in range(1, got.shape[0]):
        total += got[i]
    mine = own_mid.shape[0]
    total = jnp.concatenate([total[:mine], total[mine:]], axis=1)
    model = total.shape[1]
    power = jnp.sum(total * total, axis=1, keepdims=True) / model
    gain = jnp.concatenate([gains[z, 1:2] for z in range(NZ)], axis=1)
    hidden = (own_mid[...] + total * lax.rsqrt(power + EPS) * gain).astype(BF16)
    feats = out.shape[2]
    for r in range(model // feats):
        part = hidden[:, r * feats : (r + 1) * feats]
        for x in range(NX):
            out[r * NX + x] = part


def ring(shift, size):
    return [(i, (i + shift) % size) for i in range(size)]


def body(hidden_in, lengths, w_qkv, qk_gain, cache_keys, cache_values, w_out, norm_gain,
         w_gate_up, w_down):
    rows = lengths.shape[0]
    width = w_qkv.shape[2]
    heads = width // HEAD_DIM
    feats = hidden_in.shape[1]
    model = width * NX
    wide = rows * heads
    blocks = cache_keys.shape[0] // BLOCK
    y_here = lax.axis_index("y")
    c_here = lax.axis_index("c")

    flipped = hidden_in.T
    mate_rows = lax.ppermute(flipped, "c", ring(1, NC))
    mate_w = lax.ppermute(w_qkv, "c", ring(1, NC))
    message, started = call(
        project_kernel,
        (shape((NZ * NY, rows, 3 * width + 2 * feats), BF16), shape((8, 128), F32)),
        [ANY] * 4,
        (VMEM, VMEM),
        [
            pltpu.VMEM((2, feats, flipped.shape[1]), BF16),
            pltpu.VMEM((2,) + w_qkv.shape, BF16),
            pltpu.VMEM((flipped.shape[1], 2 * feats), F32),
            pltpu.SemaphoreType.DMA((4,)),
        ],
        (1 << 27, 2 << 20),
        "project",
        8,
    )(hbm(flipped), mate_rows, hbm(w_qkv), mate_w)
    got = lax.all_to_all(message, ("z", "y"), 0, 0, tiled=True)

    high = norm_gain.astype(BF16)
    low = (norm_gain - high.astype(F32)).astype(BF16)
    gain_rows = jnp.stack([high[0], low[0], high[1], low[1]])
    gain_tile = jnp.zeros((8, width), BF16)
    gain_tile = lax.dynamic_update_slice(
        gain_tile, gain_rows, (jnp.int32(0), (y_here * NC + c_here) * feats)
    )
    out_part = jnp.concatenate([w_out, gain_tile], axis=0)
    out_part = [out_part] + [lax.ppermute(out_part, "y", ring(s, NY)) for s in range(1, NY)]
    out_part = sort(out_part, started, "sort_out")
    units = w_down.shape[1] // NY
    ffn_part = call(
        pack_kernel,
        (shape((3 * feats, units), BF16),) * NY,
        [ANY] * 3,
        (ANY,) * NY,
        [pltpu.SemaphoreType.DMA((3 * NY,))],
        (0, 2 << 20),
        "pack",
        1,
    )(hbm(w_gate_up), hbm(w_down), started)
    ffn_part = [ffn_part[0]] + [lax.ppermute(ffn_part[s], "y", ring(s, NY)) for s in range(1, NY)]

    def near(part):
        return lax.ppermute(part, "z", ring(1, NZ)), lax.ppermute(part, "z", ring(-1, NZ))

    def far(up, dn, token):
        up_half, dn_half = halves(up, dn, token)
        return (
            lax.ppermute(up_half, "z", ring(1, NZ)),
            lax.ppermute(dn_half, "z", ring(-1, NZ)),
        )

    def both(pieces):
        return pieces + [lax.ppermute(p, "c", ring(1, NC)) for p in pieces]

    out_near = near(out_part)
    out_far = far(*out_near, started)

    qk, value_new, squares, rest = call(
        collect_kernel,
        (
            shape((2, rows, width), F32),
            shape((rows, width), BF16),
            shape((NX, rows, 128), F32),
            shape((rows // NX, model), F32),
        ),
        [VMEM],
        (VMEM,) * 4,
        [pltpu.VMEM((rows, model), F32)],
        (1 << 20, 1 << 20),
        "collect",
    )(got)
    ffn_part = sort(ffn_part, squares, "sort_ffn")
    ffn_near = near(ffn_part)
    squares = lax.all_to_all(squares, "x", 0, 0, tiled=True)
    half = HEAD_DIM // 2
    freqs = jnp.power(THETA, -(jnp.arange(half, dtype=F32) * 2.0 / HEAD_DIM))
    angles = lengths.astype(F32)[:, None] * freqs[None, :]
    cosine = jnp.cos(angles)
    sine = jnp.sin(angles)
    tables = jnp.stack(
        [jnp.concatenate([cosine, cosine], axis=1), jnp.concatenate([-sine, sine], axis=1)]
    )
    ends = jnp.cumsum(lengths)
    bounds = jnp.tile(jnp.stack([ends - lengths, ends], axis=1), (heads, 1))
    score, top, turned = call(
        score_kernel,
        (
            shape((blocks, wide, BLOCK), F32),
            shape((wide, 128), F32),
            shape((rows, width), BF16),
        ),
        [SMEM, VMEM, VMEM, VMEM, VMEM, HBM],
        (VMEM,) * 3,
        [pltpu.VMEM((blocks, BLOCK, width), BF16), pltpu.SemaphoreType.DMA((blocks,))],
        (1 << 28, 4 << 20),
        "score",
        8,
    )(lengths, qk, qk_gain, tables, bounds, hbm(cache_keys))
    out_pieces = both([out_part, *out_near, join(*out_far, top)])
    key_new, partial, gains = call(
        attend_kernel,
        (
            shape((rows, width), BF16),
            shape((NX, rows // NX, model), F32),
            shape((NZ, 8, width), F32),
        ),
        [SMEM] + [VMEM] * 8 + [HBM] + [ANY] * (4 * NC),
        (VMEM,) * 3,
        [
            pltpu.VMEM((blocks, BLOCK, width), BF16),
            pltpu.VMEM((NZ, NC, NY, feats + 8, units), BF16),
            pltpu.VMEM((wide, width), F32),
            pltpu.VMEM((wide, 128), F32),
            pltpu.SemaphoreType.DMA((blocks,)),
            pltpu.SemaphoreType.DMA((NC, 4)),
        ],
        (1 << 28, 6 << 20),
        "attend",
        12,
    )(lengths, squares, qk, turned, value_new, qk_gain, tables, score, top, hbm(cache_values),
      *out_pieces)

    ffn_far = far(*ffn_near, gains)

    got = lax.all_to_all(partial, "x", 0, 0, tiled=True)
    mine = rows // NX
    own_mid, message = call(
        fan_kernel,
        (shape((mine, model), F32), shape((NY * NX, 2 * mine, model // 2), BF16)),
        [VMEM] * 3,
        (VMEM, VMEM),
        (),
        (1 << 16, 1 << 19),
        "fan",
    )(got, rest, gains)
    got = lax.all_to_all(message, ("y", "x"), 0, 0, tiled=True)
    ffn_pieces = both([ffn_part, *ffn_near, join(*ffn_far, own_mid)])
    partial = call(
        ffn_kernel,
        shape((NY * NX, 2 * mine, model // 2), F32),
        [VMEM] + [ANY] * (4 * NC),
        VMEM,
        [
            pltpu.VMEM((NZ, NC) + ffn_part.shape, BF16),
            pltpu.SemaphoreType.DMA((NC, 4)),
        ],
        (1 << 28, 7 << 20),
        "feed_forward",
        16,
    )(got, *ffn_pieces)
    got = lax.all_to_all(partial, ("y", "x"), 0, 0, tiled=True)
    message = call(
        finish_kernel,
        shape((NZ * NY * NC * NX, mine, feats), BF16),
        [VMEM] * 3,
        VMEM,
        (),
        (1 << 18, 1 << 19),
        "finish",
    )(got, own_mid, gains)
    hidden = lax.all_to_all(message, ("z", "y", "c", "x"), 0, 0, tiled=True)
    return hidden.reshape(-1, feats), key_new, value_new


def solution(mesh):
    fine = Mesh(mesh.devices.reshape(NZ, NY, NC, NX), ("z", "y", "c", "x"))
    req = ("z", "y", "c")
    return jax.shard_map(
        body,
        mesh=fine,
        in_specs=(
            P(None, req),
            P(req),
            P(None, req, "x"),
            P(None, "x"),
            P(req, "x"),
            P(req, "x"),
            P(req, "x"),
            P(None, req),
            P(None, req, "x"),
            P(req, "x"),
        ),
        out_specs=(P(None, req), P(req, "x"), P(req, "x")),
        check_vma=False,
    )
```

time: 164 us -> 159 us (0.970)
  between operations: 14.3 us -> 0.97 us
  starting transfers between devices: 37 us -> 47.9 us
  waiting for transfers between devices: 33.9 us -> 25.1 us
  Pallas kernels: 15.7 us -> 24.1 us
  blocking collectives: 49.4 us -> 41.5 us
  local copies, waits for them, and re-layouts: 11.3 us -> 15.1 us
    ppermute x13 -> x22, waiting for transfers between devices: 33.6 us -> 16.6 us  [the longest x3 8.65 us: body(): lax.ppermute(out_part, 'y', ring(s, NY))]
    pallas_call x5 -> x10, Pallas kernels: 9.13 us -> 18.1 us  [the longest x1 7.19 us: body(): call(pack_kernel, (shape((3 * feats, units), BF16),) * NY, [ANY] * 3, (AN...]
    all_to_all x0 -> x2, starting transfers between devices: none -> 7.34 us  [the longest x1 4.02 us: body(): squares = lax.all_to_all(squares, 'x', 0, 0, tiled=True)]
    all_to_all x1 -> x0, blocking collectives: 7.21 us -> none  [body(): got = lax.all_to_all(partial, 'x', 0, 0, tiled=True)]
    all_to_all x0 -> x2, waiting for transfers between devices: none -> 7.11 us  [the longest x1 4.4 us: body(): squares = lax.all_to_all(squares, 'x', 0, 0, tiled=True)]
    unnamed x26 -> x48, local copies, waits for them, and re-layouts: 10.7 us -> 13.8 us
    ppermute x13 -> x22, starting transfers between devices: 28.2 us -> 31.1 us  [the longest x8 13 us: both(): return pieces + [lax.ppermute(p, 'c', ring(1, NC)) for p in pieces]]
  transfers between devices with their start and end apart: 17 -> 27, of which waited for: 6 -> 5; matrix products, arithmetic and copies ran while one was open for 1% -> 3% of each run, Pallas kernels for 6% -> 12%
where the time goes in v3:
time: 159 us; the launch traced here: 157 us
  starting transfers between devices  47.9 us (30%)
  blocking collectives  41.5 us (26%)
  waiting for transfers between devices  25.1 us (16%)
  Pallas kernels  24.1 us (15%)
  local copies, waits for them, and re-layouts  15.1 us (9%)
  other arithmetic  2.73 us (2%)
    all_to_all x1, blocking collectives, body(): hidden = lax.all_to_all(message, ('z', 'y', 'c', 'x'), 0, 0, tiled=True)  15.1 us
    unnamed x48, local copies, waits for them, and re-layouts  13.8 us
    all_to_all x1, blocking collectives, body(): got = lax.all_to_all(message, ('y', 'x'), 0, 0, tiled=True)  13.6 us
    ppermute x8, starting transfers between devices, both(): return pieces + [lax.ppermute(p, 'c', ring(1, NC)) for p in pieces]  13 us
    all_to_all x1, blocking collectives, body(): got = lax.all_to_all(partial, ('y', 'x'), 0, 0, tiled=True)  12.8 us
    ppermute x3, waiting for transfers between devices, body(): lax.ppermute(out_part, 'y', ring(s, NY))  8.65 us
    ppermute x2, waiting for transfers between devices, far(): lax.ppermute(up_half, 'z', ring(1, NZ))  7.88 us
    all_to_all x1, starting transfers between devices, body(): got = lax.all_to_all(message, ('z', 'y'), 0, 0, tiled=True)  7.86 us
  transfers between devices with their start and end apart: 27, of which 5 were waited for; matrix products, arithmetic and copies ran while one was open for 3% of the time, Pallas kernels for 12%

profile of v3, /device:TPU:1, one launch (start us, length us, event | category | flops | bytes accessed | tf_op | source)
XLA Modules:
  0.0 157.4 jit_solution(5006361185244319224)
XLA Ops:
  0.7 1.5 collective-permute-start.1
  2.2 1.4 collective-permute-done.h_mate
  3.6 2.7 %project.1 = (bf16[16,16,1664]{2,1,0:T(8,128)(2,1)}, f32[8,128]{1,0:T(8,128)S(1)}) custom-call(bf16[64,512]{1,0:T(8,128)(2,1)} %bitcast.14, bf16[64,512]{1,0:T(8,128)(2,1)S(1)} %collective-permute-done.h_mate, bf16[3,64,512]{2,1,0:T(8,128)(2,1)} %w_own.1, bf16[3,64,512]{2,1,0:T(8,128)(2,1)S(1)} %collective-permute-done.1.w_mate), custom_call_target="tpu_custom_call" | custom-call | flops 134217728 | bytes 2097152 | tf_op jit(solution)/shard_map/project/pallas_call | solution.py:421
  6.3 7.9 %all-to-all-start = ((bf16[16,16,1664]{2,1,0:T(8,128)(2,1)}), bf16[16,16,1664]{2,1,0:T(8,128)(2,1)S(1)}, u32[]{:S(2)}, u32[]{:S(2)}) async-start(bf16[16,16,1664]{2,1,0:T(8,128)(2,1)} %get-tuple-element.25), calls=%async_computation | async-start | bytes 1703936 | tf_op jit(solution)/shard_map/all_to_all | solution.py:436
  14.2 0.8 subtract_convert_fusion
  15.0 0.5 dynamic_update_slice.3
  15.5 0.9 pad_maximum_fusion.refs_0_
  16.3 1.4 collective-permute-start.2
  17.7 2.4 %collective-permute-start.3 = (bf16[72,512]{1,0:T(8,128)(2,1)S(1)}, bf16[72,512]{1,0:T(8,128)(2,1)S(1)}, u32[]{:S(2)}, u32[]{:S(2)}) collective-permute-start(bf16[72,512]{1,0:T(8,128)(2,1)S(1)} %pad_maximum_fusion.refs_0_), channel_id=1, source_target_pairs={{0,16},{8,24},{16,0},{24,8},{1,17},{9,25},{17,1},{25,9},{2,18},{10... | collective-permute-start | bytes 221192 | tf_op jit(solution)/shard_map/ppermute | solution.py:446
  20.1 0.7 copy.23
  21.0 7.2 %pack.1 = (bf16[192,512]{1,0:T(8,128)(2,1)S(1)}, bf16[192,512]{1,0:T(8,128)(2,1)}, bf16[192,512]{1,0:T(8,128)(2,1)S(1)}, bf16[192,512]{1,0:T(8,128)(2,1)S(1)}) custom-call(bf16[2,64,2048]{2,1,0:T(8,128)(2,1)} %gate_up.1, bf16[64,2048]{1,0:T(8,128)(2,1)} %down.1, f32[8,128]{1,0:T(8,128)S(1)} %get-tuple-element.32.refs_4_.token), custom_call_target="tpu_custom_call" | custom-call | bytes 2097152 | tf_op jit(solution)/shard_map/pack/pallas_call | solution.py:449
  28.2 2.4 %collective-permute-start.14 = (bf16[192,512]{1,0:T(8,128)(2,1)S(1)}, bf16[192,512]{1,0:T(8,128)(2,1)S(1)}, u32[]{:S(2)}, u32[]{:S(2)}) collective-permute-start(bf16[192,512]{1,0:T(8,128)(2,1)S(1)} %get-tuple-element.41), channel_id=1, source_target_pairs={{0,16},{8,24},{16,0},{24,8},{1,17},{9,25},{17,1},{25,9},{2,18},{10... | collective-permute-start | bytes 589832 | tf_op jit(solution)/shard_map/ppermute | solution.py:459
  30.6 0.3 collective-permute-start.15
  30.9 0.7 subtract_bitcast_fusion
  31.6 0.7 collective-permute-start.4
  32.3 8.6 %collective-permute-done.4.refs_3_ = bf16[72,512]{1,0:T(8,128)(2,1)S(1)} collective-permute-done((bf16[72,512]{1,0:T(8,128)(2,1)S(1)}, bf16[72,512]{1,0:T(8,128)(2,1)S(1)}, u32[]{:S(2)}, u32[]{:S(2)}) %collective-permute-start.4) | collective-permute-done | bytes 73760 | tf_op jit(solution)/shard_map/ppermute | solution.py:446
  41.0 0.4 sort_out.1.refs_0_
  41.4 1.3 collective-permute-start.5
  42.6 1.5 collective-permute-start.6
  44.1 0.7 collect.1
  44.8 0.6 copy-done.13
  45.4 0.6 copy-done.11
  46.0 1.0 sort_ffn.1.refs_0_
  47.1 2.7 %collective-permute-start.17 = (bf16[4,192,512]{2,1,0:T(8,128)(2,1)S(1)}, bf16[4,192,512]{2,1,0:T(8,128)(2,1)S(1)}, u32[]{:S(2)}, u32[]{:S(2)}) collective-permute-start(bf16[4,192,512]{2,1,0:T(8,128)(2,1)S(1)} %sort_ffn.1.refs_0_), channel_id=1, source_target_pairs={{0,96},{32,0},{64,32},{96,64},{1,97},{33,1},{65,33},{97,65},{2,98}... | collective-permute-start | bytes 2359304 | tf_op jit(solution)/shard_map/ppermute | solution.py:462
  49.9 3.4 %collective-permute-start.9 = (bf16[4,72,512]{2,1,0:T(8,128)(2,1)S(1)}, bf16[4,72,512]{2,1,0:T(8,128)(2,1)}, u32[]{:S(2)}, u32[]{:S(2)}) collective-permute-start(bf16[4,72,512]{2,1,0:T(8,128)(2,1)S(1)} %sort_out.1.refs_0_), channel_id=1, source_target_pairs={{0,4},{4,0},{1,5},{5,1},{2,6},{6,2},{3,7},{7,3},{8,12},{12,8},{9,1... | collective-permute-start | bytes 884744 | tf_op jit(solution)/shard_map/ppermute | solution.py:472
  53.5 0.7 halves.2
  54.3 2.7 %collective-permute-start.8 = (bf16[2,72,512]{2,1,0:T(8,128)(2,1)}, bf16[2,72,512]{2,1,0:T(8,128)(2,1)}, u32[]{:S(2)}, u32[]{:S(2)}) collective-permute-start(bf16[2,72,512]{2,1,0:T(8,128)(2,1)} %get-tuple-element.34), channel_id=1, source_target_pairs={{0,96},{32,0},{64,32},{96,64},{1,97},{33,1},{65,33},{97,65},{2,98}... | collective-permute-start | bytes 442376 | tf_op jit(solution)/shard_map/ppermute | solution.py:468
  57.1 2.4 %score.1 = (f32[8,64,512]{2,1,0:T(8,128)S(1)}, f32[64,128]{1,0:T(8,128)S(1)}, bf16[16,512]{1,0:T(8,128)(2,1)S(1)}) custom-call(s32[16]{0:T(128)S(1)} %copy-done.20, f32[2,16,512]{2,1,0:T(8,128)S(1)} %get-tuple-element.27.qk, f32[2,512]{1,0:T(2,128)S(1)} %copy-done.15, f32[2,16,128]{2,1,0:T(8,128)S(1)} %pad_maximum_fusion.1.tables, s32[64,2]{1,0:T(8,128)S(1)} %bitcast.10, ...), custom_call_target="tpu_custom_call" | custom-call | flops 268435456 | bytes 4194304 | tf_op jit(solution)/shard_map/score/pallas_call | solution.py:504
  59.5 1.0 copy-done
  60.5 0.6 copy-done.18
  61.1 7.9 %collective-permute-done.7.first = bf16[2,72,512]{2,1,0:T(8,128)(2,1)S(1)} collective-permute-done((bf16[2,72,512]{2,1,0:T(8,128)(2,1)}, bf16[2,72,512]{2,1,0:T(8,128)(2,1)S(1)}, u32[]{:S(2)}, u32[]{:S(2)}) %collective-permute-start.7) | collective-permute-done | bytes 147488 | tf_op jit(solution)/shard_map/ppermute | solution.py:467
  69.0 0.7 copy-done.7
  69.7 3.1 %collective-permute-start.10 = (bf16[4,72,512]{2,1,0:T(8,128)(2,1)S(1)}, bf16[4,72,512]{2,1,0:T(8,128)(2,1)}, u32[]{:S(2)}, u32[]{:S(2)}) collective-permute-start(bf16[4,72,512]{2,1,0:T(8,128)(2,1)S(1)} %collective-permute-done.5.up.refs_1_), channel_id=1, source_target_pairs={{0,4},{4,0},{1,5},{5,1},{2,6},{6,2},{3,7},{7,3},{8,12},{12,8},{9,1... | collective-permute-start | bytes 884744 | tf_op jit(solution)/shard_map/ppermute | solution.py:472
  72.8 0.9 copy-done.8
  73.7 1.1 join.2.refs_3_
  74.8 0.6 copy-done.9
  75.4 0.5 collective-permute-start.12
  75.9 4.0 %all-to-all-start.1 = ((f32[4,16,128]{2,1,0:T(8,128)}), f32[4,16,128]{2,1,0:T(8,128)}, u32[]{:S(2)}, u32[]{:S(2)}) async-start(f32[4,16,128]{2,1,0:T(8,128)} %copy-done.11), calls=%async_computation.1 | async-start | bytes 65536 | tf_op jit(solution)/shard_map/all_to_all | solution.py:493
  79.9 4.4 %all-to-all-done.1.squares_in = f32[4,16,128]{2,1,0:T(8,128)} async-done(((f32[4,16,128]{2,1,0:T(8,128)}), f32[4,16,128]{2,1,0:T(8,128)}, u32[]{:S(2)}, u32[]{:S(2)}) %all-to-all-start.1) | async-done | bytes 32800 | tf_op jit(solution)/shard_map/all_to_all | solution.py:493
  84.3 1.2 copy-done.1
  85.5 0.8 copy-done.6
  86.4 0.8 copy-done.10
  87.1 0.7 copy-done.16
  87.8 0.7 copy-done.17
  88.5 0.7 copy-done.19
  89.2 0.7 copy-done.21
  89.9 3.4 %attend.1 = (bf16[16,512]{1,0:T(8,128)(2,1)}, f32[4,4,2048]{2,1,0:T(4,128)S(1)}, f32[4,8,512]{2,1,0:T(8,128)S(1)}) custom-call(s32[16]{0:T(128)S(1)} %copy-done.21, f32[4,16,128]{2,1,0:T(8,128)} %all-to-all-done.1.squares_in, f32[2,16,512]{2,1,0:T(8,128)S(1)} %copy-done.6, bf16[16,512]{1,0:T(8,128)(2,1)S(1)} %copy-done.19, bf16[16,512]{1,0:T(8,128)(2,1)S(1)} %copy-done.17, ...), custom_call_target="tpu_custom_call" | custom-call | flops 268435456 | bytes 6291456 | tf_op jit(solution)/shard_map/attend/pallas_call | solution.py:519
  93.3 0.9 halves.3
  94.3 0.6 copy-done.2
  95.0 2.6 %collective-permute-start.19 = (bf16[2,192,512]{2,1,0:T(8,128)(2,1)}, bf16[2,192,512]{2,1,0:T(8,128)(2,1)}, u32[]{:S(2)}, u32[]{:S(2)}) collective-permute-start(bf16[2,192,512]{2,1,0:T(8,128)(2,1)} %get-tuple-element.44), channel_id=1, source_target_pairs={{0,96},{32,0},{64,32},{96,64},{1,97},{33,1},{65,33},{97,65},{2,98}... | collective-permute-start | bytes 1179656 | tf_op jit(solution)/shard_map/ppermute | solution.py:468
  97.6 3.3 %all-to-all-start.2 = ((f32[4,4,2048]{2,1,0:T(4,128)}), f32[4,4,2048]{2,1,0:T(4,128)S(1)}, u32[]{:S(2)}, u32[]{:S(2)}) async-start(f32[4,4,2048]{2,1,0:T(4,128)} %copy-done.12), calls=%async_computation.2 | async-start | bytes 262144 | tf_op jit(solution)/shard_map/all_to_all | solution.py:544
  100.9 2.1 %collective-permute-start.20 = (bf16[4,192,512]{2,1,0:T(8,128)(2,1)S(1)}, bf16[4,192,512]{2,1,0:T(8,128)(2,1)S(1)}, u32[]{:S(2)}, u32[]{:S(2)}) collective-permute-start(bf16[4,192,512]{2,1,0:T(8,128)(2,1)S(1)} %sort_ffn.1.refs_0_), channel_id=1, source_target_pairs={{0,4},{4,0},{1,5},{5,1},{2,6},{6,2},{3,7},{7,3},{8,12},{12,8},{9,1... | collective-permute-start | bytes 2359304 | tf_op jit(solution)/shard_map/ppermute | solution.py:472
  103.0 2.7 %all-to-all-done.2.got = f32[4,4,2048]{2,1,0:T(4,128)S(1)} async-done(((f32[4,4,2048]{2,1,0:T(4,128)}), f32[4,4,2048]{2,1,0:T(4,128)S(1)}, u32[]{:S(2)}, u32[]{:S(2)}) %all-to-all-start.2) | async-done | bytes 131104 | tf_op jit(solution)/shard_map/all_to_all | solution.py:544
  105.7 0.8 copy-done.3
  106.5 0.8 copy-done.14
  107.4 3.4 %collective-permute-start.21 = (bf16[4,192,512]{2,1,0:T(8,128)(2,1)S(1)}, bf16[4,192,512]{2,1,0:T(8,128)(2,1)S(1)}, u32[]{:S(2)}, u32[]{:S(2)}) collective-permute-start(bf16[4,192,512]{2,1,0:T(8,128)(2,1)S(1)} %collective-permute-done.16.up.refs_1_), channel_id=1, source_target_pairs={{0,4},{4,0},{1,5},{5,1},{2,6},{6,2},{3,7},{7,3},{8,12},{12,8},{9,1... | collective-permute-start | bytes 2359304 | tf_op jit(solution)/shard_map/ppermute | solution.py:472
  110.9 1.1 join.3.refs_3_
  112.1 0.5 collective-permute-start.23
  112.6 13.6 %all_to_all.30.got = bf16[16,8,1024]{2,1,0:T(8,128)(2,1)S(1)} all-to-all(bf16[16,8,1024]{2,1,0:T(8,128)(2,1)S(1)} %get-tuple-element.38), channel_id=1, replica_groups=mesh['z'=4,'y'=4,'c'=2,'x'=4] {'y','x'}, dimensions={0} | all-to-all | bytes 524288 | tf_op jit(solution)/shard_map/all_to_all | solution.py:555
  126.2 2.1 %feed_forward.1 = f32[16,8,1024]{2,1,0:T(8,128)S(1)} custom-call(bf16[16,8,1024]{2,1,0:T(8,128)(2,1)S(1)} %all_to_all.30.got, bf16[4,192,512]{2,1,0:T(8,128)(2,1)S(1)} %sort_ffn.1.refs_0_, bf16[4,192,512]{2,1,0:T(8,128)(2,1)S(1)} %collective-permute-done.16.up.refs_1_, bf16[4,192,512]{2,1,0:T(8,128)(2,1)S(1)} %collective-permute-done.17.dn.refs_2_, ...), custom_call_target="tpu_custom_call" | custom-call | flops 268435456 | bytes 7340032 | tf_op jit(solution)/shard_map/feed_forward/pallas_call | solution.py:557
  128.3 12.8 %all_to_all.31.got = f32[16,8,1024]{2,1,0:T(8,128)S(1)} all-to-all(f32[16,8,1024]{2,1,0:T(8,128)S(1)} %feed_forward.1), channel_id=1, replica_groups=mesh['z'=4,'y'=4,'c'=2,'x'=4] {'y','x'}, dimensions={0} | all-to-all | bytes 1048576 | tf_op jit(solution)/shard_map/all_to_all | solution.py:570
  141.1 0.2 finish.1
  141.5 15.1 %all_to_all.32 = bf16[128,2,128]{2,1,0:T(2,128)(2,1)S(1)} all-to-all(bf16[128,2,128]{2,1,0:T(2,128)(2,1)S(1)} %reshape.31), channel_id=1, replica_groups=mesh['z'=4,'y'=4,'c'=2,'x'=4] {'z','y','c','x'}, dimensions={0} | all-to-all | bytes 131072 | tf_op jit(solution)/shard_map/all_to_all | solution.py:580
  156.6 0.7 copy.26
  (72 shorter events, 1.5 us)
Async XLA Ops:
  0.6 56.5 %copy-start.20 = (s32[16]{0:T(128)S(1)}, s32[16]{0:T(128)}, u32[]{:S(2)}) copy-start(s32[16]{0:T(128)} %lengths.3) | copy-start | bytes 196
  0.6 56.5 %copy-start.15 = (f32[2,512]{1,0:T(2,128)S(1)}, f32[2,512]{1,0:T(2,128)}, u32[]{:S(2)}) copy-start(f32[2,512]{1,0:T(2,128)} %gains.3) | copy-start | bytes 12292
  0.7 3.0 %collective-permute-start.1 = (bf16[3,64,512]{2,1,0:T(8,128)(2,1)}, bf16[3,64,512]{2,1,0:T(8,128)(2,1)S(1)}, u32[]{:S(2)}, u32[]{:S(2)}) collective-permute-start(bf16[3,64,512]{2,1,0:T(8,128)(2,1)} %w_own.1), channel_id=1, source_target_pairs={{0,4},{4,0},{1,5},{5,1},{2,6},{6,2},{3,7},{7,3},{8,12},{12,8},{9,1... | collective-permute-start | bytes 589832 | tf_op jit(solution)/shard_map/ppermute | solution.py:420
  2.2 1.5 collective-permute-start
  6.3 37.8 %all-to-all-start = ((bf16[16,16,1664]{2,1,0:T(8,128)(2,1)}), bf16[16,16,1664]{2,1,0:T(8,128)(2,1)S(1)}, u32[]{:S(2)}, u32[]{:S(2)}) async-start(bf16[16,16,1664]{2,1,0:T(8,128)(2,1)} %get-tuple-element.25), calls=%async_computation | async-start | bytes 1703936 | tf_op jit(solution)/shard_map/all_to_all | solution.py:436
  16.3 15.3 %collective-permute-start.2 = (bf16[72,512]{1,0:T(8,128)(2,1)S(1)}, bf16[72,512]{1,0:T(8,128)(2,1)S(1)}, u32[]{:S(2)}, u32[]{:S(2)}) collective-permute-start(bf16[72,512]{1,0:T(8,128)(2,1)S(1)} %pad_maximum_fusion.refs_0_), channel_id=1, source_target_pairs={{0,8},{8,16},{16,24},{24,0},{1,9},{9,17},{17,25},{25,1},{2,10},{10... | collective-permute-start | bytes 221192 | tf_op jit(solution)/shard_map/ppermute | solution.py:446
  17.7 14.6 %collective-permute-start.3 = (bf16[72,512]{1,0:T(8,128)(2,1)S(1)}, bf16[72,512]{1,0:T(8,128)(2,1)S(1)}, u32[]{:S(2)}, u32[]{:S(2)}) collective-permute-start(bf16[72,512]{1,0:T(8,128)(2,1)S(1)} %pad_maximum_fusion.refs_0_), channel_id=1, source_target_pairs={{0,16},{8,24},{16,0},{24,8},{1,17},{9,25},{17,1},{25,9},{2,18},{10... | collective-permute-start | bytes 221192 | tf_op jit(solution)/shard_map/ppermute | solution.py:446
  28.2 17.3 %collective-permute-start.13 = (bf16[192,512]{1,0:T(8,128)(2,1)}, bf16[192,512]{1,0:T(8,128)(2,1)S(1)}, u32[]{:S(2)}, u32[]{:S(2)}) collective-permute-start(bf16[192,512]{1,0:T(8,128)(2,1)} %get-tuple-element.40), channel_id=1, source_target_pairs={{0,8},{8,16},{16,24},{24,0},{1,9},{9,17},{17,25},{25,1},{2,10},{10... | collective-permute-start | bytes 589832 | tf_op jit(solution)/shard_map/ppermute | solution.py:459
  28.2 17.2 %collective-permute-start.14 = (bf16[192,512]{1,0:T(8,128)(2,1)S(1)}, bf16[192,512]{1,0:T(8,128)(2,1)S(1)}, u32[]{:S(2)}, u32[]{:S(2)}) collective-permute-start(bf16[192,512]{1,0:T(8,128)(2,1)S(1)} %get-tuple-element.41), channel_id=1, source_target_pairs={{0,16},{8,24},{16,0},{24,8},{1,17},{9,25},{17,1},{25,9},{2,18},{10... | collective-permute-start | bytes 589832 | tf_op jit(solution)/shard_map/ppermute | solution.py:459
  30.6 14.8 %collective-permute-start.15 = (bf16[192,512]{1,0:T(8,128)(2,1)S(1)}, bf16[192,512]{1,0:T(8,128)(2,1)S(1)}, u32[]{:S(2)}, u32[]{:S(2)}) collective-permute-start(bf16[192,512]{1,0:T(8,128)(2,1)S(1)} %get-tuple-element.42), channel_id=1, source_target_pairs={{0,24},{8,0},{16,8},{24,16},{1,25},{9,1},{17,9},{25,17},{2,26},{10... | collective-permute-start | bytes 589832 | tf_op jit(solution)/shard_map/ppermute | solution.py:459
  31.6 9.3 %collective-permute-start.4 = (bf16[72,512]{1,0:T(8,128)(2,1)S(1)}, bf16[72,512]{1,0:T(8,128)(2,1)S(1)}, u32[]{:S(2)}, u32[]{:S(2)}) collective-permute-start(bf16[72,512]{1,0:T(8,128)(2,1)S(1)} %pad_maximum_fusion.refs_0_), channel_id=1, source_target_pairs={{0,24},{8,0},{16,8},{24,16},{1,25},{9,1},{17,9},{25,17},{2,26},{10... | collective-permute-start | bytes 221192 | tf_op jit(solution)/shard_map/ppermute | solution.py:446
  41.4 12.1 %collective-permute-start.5 = (bf16[4,72,512]{2,1,0:T(8,128)(2,1)S(1)}, bf16[4,72,512]{2,1,0:T(8,128)(2,1)S(1)}, u32[]{:S(2)}, u32[]{:S(2)}) collective-permute-start(bf16[4,72,512]{2,1,0:T(8,128)(2,1)S(1)} %sort_out.1.refs_0_), channel_id=1, source_target_pairs={{0,32},{32,64},{64,96},{96,0},{1,33},{33,65},{65,97},{97,1},{2,34}... | collective-permute-start | bytes 884744 | tf_op jit(solution)/shard_map/ppermute | solution.py:462
  42.6 10.9 %collective-permute-start.6 = (bf16[4,72,512]{2,1,0:T(8,128)(2,1)S(1)}, bf16[4,72,512]{2,1,0:T(8,128)(2,1)S(1)}, u32[]{:S(2)}, u32[]{:S(2)}) collective-permute-start(bf16[4,72,512]{2,1,0:T(8,128)(2,1)S(1)} %sort_out.1.refs_0_), channel_id=1, source_target_pairs={{0,96},{32,0},{64,32},{96,64},{1,97},{33,1},{65,33},{97,65},{2,98}... | collective-permute-start | bytes 884744 | tf_op jit(solution)/shard_map/ppermute | solution.py:462
  44.8 0.6 copy-start.13
  45.4 0.6 copy-start.11
  45.4 27.3 %copy-start.5 = (f32[2,16,512]{2,1,0:T(8,128)}, f32[2,16,512]{2,1,0:T(8,128)S(1)}, u32[]{:S(2)}) copy-start(f32[2,16,512]{2,1,0:T(8,128)S(1)} %get-tuple-element.27.qk) | copy-start | bytes 196612
  47.1 46.2 %collective-permute-start.16 = (bf16[4,192,512]{2,1,0:T(8,128)(2,1)S(1)}, bf16[4,192,512]{2,1,0:T(8,128)(2,1)S(1)}, u32[]{:S(2)}, u32[]{:S(2)}) collective-permute-start(bf16[4,192,512]{2,1,0:T(8,128)(2,1)S(1)} %sort_ffn.1.refs_0_), channel_id=1, source_target_pairs={{0,32},{32,64},{64,96},{96,0},{1,33},{33,65},{65,97},{97,1},{2,34}... | collective-permute-start | bytes 2359304 | tf_op jit(solution)/shard_map/ppermute | solution.py:462
  47.1 46.2 %collective-permute-start.17 = (bf16[4,192,512]{2,1,0:T(8,128)(2,1)S(1)}, bf16[4,192,512]{2,1,0:T(8,128)(2,1)S(1)}, u32[]{:S(2)}, u32[]{:S(2)}) collective-permute-start(bf16[4,192,512]{2,1,0:T(8,128)(2,1)S(1)} %sort_ffn.1.refs_0_), channel_id=1, source_target_pairs={{0,96},{32,0},{64,32},{96,64},{1,97},{33,1},{65,33},{97,65},{2,98}... | collective-permute-start | bytes 2359304 | tf_op jit(solution)/shard_map/ppermute | solution.py:462
  49.9 25.4 %collective-permute-start.9 = (bf16[4,72,512]{2,1,0:T(8,128)(2,1)S(1)}, bf16[4,72,512]{2,1,0:T(8,128)(2,1)}, u32[]{:S(2)}, u32[]{:S(2)}) collective-permute-start(bf16[4,72,512]{2,1,0:T(8,128)(2,1)S(1)} %sort_out.1.refs_0_), channel_id=1, source_target_pairs={{0,4},{4,0},{1,5},{5,1},{2,6},{6,2},{3,7},{7,3},{8,12},{12,8},{9,1... | collective-permute-start | bytes 884744 | tf_op jit(solution)/shard_map/ppermute | solution.py:472
  54.2 14.8 %collective-permute-start.7 = (bf16[2,72,512]{2,1,0:T(8,128)(2,1)}, bf16[2,72,512]{2,1,0:T(8,128)(2,1)S(1)}, u32[]{:S(2)}, u32[]{:S(2)}) collective-permute-start(bf16[2,72,512]{2,1,0:T(8,128)(2,1)} %get-tuple-element.33), channel_id=1, source_target_pairs={{0,32},{32,64},{64,96},{96,0},{1,33},{33,65},{65,97},{97,1},{2,34}... | collective-permute-start | bytes 442376 | tf_op jit(solution)/shard_map/ppermute | solution.py:467
  54.3 18.4 %collective-permute-start.8 = (bf16[2,72,512]{2,1,0:T(8,128)(2,1)}, bf16[2,72,512]{2,1,0:T(8,128)(2,1)}, u32[]{:S(2)}, u32[]{:S(2)}) collective-permute-start(bf16[2,72,512]{2,1,0:T(8,128)(2,1)} %get-tuple-element.34), channel_id=1, source_target_pairs={{0,96},{32,0},{64,32},{96,64},{1,97},{33,1},{65,33},{97,65},{2,98}... | collective-permute-start | bytes 442376 | tf_op jit(solution)/shard_map/ppermute | solution.py:468
  59.5 1.0 copy-start
  60.5 0.6 copy-start.18
  69.0 0.7 copy-start.7
  69.7 10.2 %collective-permute-start.10 = (bf16[4,72,512]{2,1,0:T(8,128)(2,1)S(1)}, bf16[4,72,512]{2,1,0:T(8,128)(2,1)}, u32[]{:S(2)}, u32[]{:S(2)}) collective-permute-start(bf16[4,72,512]{2,1,0:T(8,128)(2,1)S(1)} %collective-permute-done.5.up.refs_1_), channel_id=1, source_target_pairs={{0,4},{4,0},{1,5},{5,1},{2,6},{6,2},{3,7},{7,3},{8,12},{12,8},{9,1... | collective-permute-start | bytes 884744 | tf_op jit(solution)/shard_map/ppermute | solution.py:472
  72.8 7.1 %collective-permute-start.11 = (bf16[4,72,512]{2,1,0:T(8,128)(2,1)S(1)}, bf16[4,72,512]{2,1,0:T(8,128)(2,1)}, u32[]{:S(2)}, u32[]{:S(2)}) collective-permute-start(bf16[4,72,512]{2,1,0:T(8,128)(2,1)S(1)} %collective-permute-done.6.dn.refs_2_), channel_id=1, source_target_pairs={{0,4},{4,0},{1,5},{5,1},{2,6},{6,2},{3,7},{7,3},{8,12},{12,8},{9,1... | collective-permute-start | bytes 884744 | tf_op jit(solution)/shard_map/ppermute | solution.py:472
  72.8 0.9 copy-start.8
  74.8 0.6 copy-start.9
  75.4 8.9 %collective-permute-start.12 = (bf16[4,72,512]{2,1,0:T(8,128)(2,1)S(1)}, bf16[4,72,512]{2,1,0:T(8,128)(2,1)}, u32[]{:S(2)}, u32[]{:S(2)}) collective-permute-start(bf16[4,72,512]{2,1,0:T(8,128)(2,1)S(1)} %join.2.refs_3_), channel_id=1, source_target_pairs={{0,4},{4,0},{1,5},{5,1},{2,6},{6,2},{3,7},{7,3},{8,12},{12,8},{9,1... | collective-permute-start | bytes 884744 | tf_op jit(solution)/shard_map/ppermute | solution.py:472
  75.9 8.4 %all-to-all-start.1 = ((f32[4,16,128]{2,1,0:T(8,128)}), f32[4,16,128]{2,1,0:T(8,128)}, u32[]{:S(2)}, u32[]{:S(2)}) async-start(f32[4,16,128]{2,1,0:T(8,128)} %copy-done.11), calls=%async_computation.1 | async-start | bytes 65536 | tf_op jit(solution)/shard_map/all_to_all | solution.py:493
  84.3 1.2 copy-start.1
  85.5 0.8 copy-start.6
  86.4 0.8 copy-start.10
  87.1 0.7 copy-start.16
  87.8 0.7 copy-start.17
  88.5 0.7 copy-start.19
  89.2 0.7 copy-start.21
  93.3 4.3 %copy-start.12 = (f32[4,4,2048]{2,1,0:T(4,128)}, f32[4,4,2048]{2,1,0:T(4,128)S(1)}, u32[]{:S(2)}) copy-start(f32[4,4,2048]{2,1,0:T(4,128)S(1)} %get-tuple-element.35) | copy-start | bytes 393220
  94.3 0.6 copy-start.2
  94.9 16.0 %collective-permute-start.18 = (bf16[2,192,512]{2,1,0:T(8,128)(2,1)}, bf16[2,192,512]{2,1,0:T(8,128)(2,1)}, u32[]{:S(2)}, u32[]{:S(2)}) collective-permute-start(bf16[2,192,512]{2,1,0:T(8,128)(2,1)} %get-tuple-element.43), channel_id=1, source_target_pairs={{0,32},{32,64},{64,96},{96,0},{1,33},{33,65},{65,97},{97,1},{2,34}... | collective-permute-start | bytes 1179656 | tf_op jit(solution)/shard_map/ppermute | solution.py:467
  95.0 16.0 %collective-permute-start.19 = (bf16[2,192,512]{2,1,0:T(8,128)(2,1)}, bf16[2,192,512]{2,1,0:T(8,128)(2,1)}, u32[]{:S(2)}, u32[]{:S(2)}) collective-permute-start(bf16[2,192,512]{2,1,0:T(8,128)(2,1)} %get-tuple-element.44), channel_id=1, source_target_pairs={{0,96},{32,0},{64,32},{96,64},{1,97},{33,1},{65,33},{97,65},{2,98}... | collective-permute-start | bytes 1179656 | tf_op jit(solution)/shard_map/ppermute | solution.py:468
  97.6 8.1 %all-to-all-start.2 = ((f32[4,4,2048]{2,1,0:T(4,128)}), f32[4,4,2048]{2,1,0:T(4,128)S(1)}, u32[]{:S(2)}, u32[]{:S(2)}) async-start(f32[4,4,2048]{2,1,0:T(4,128)} %copy-done.12), calls=%async_computation.2 | async-start | bytes 262144 | tf_op jit(solution)/shard_map/all_to_all | solution.py:544
  100.9 25.3 %collective-permute-start.20 = (bf16[4,192,512]{2,1,0:T(8,128)(2,1)S(1)}, bf16[4,192,512]{2,1,0:T(8,128)(2,1)S(1)}, u32[]{:S(2)}, u32[]{:S(2)}) collective-permute-start(bf16[4,192,512]{2,1,0:T(8,128)(2,1)S(1)} %sort_ffn.1.refs_0_), channel_id=1, source_target_pairs={{0,4},{4,0},{1,5},{5,1},{2,6},{6,2},{3,7},{7,3},{8,12},{12,8},{9,1... | collective-permute-start | bytes 2359304 | tf_op jit(solution)/shard_map/ppermute | solution.py:472
  105.7 0.8 copy-start.3
  106.5 0.8 copy-start.14
  107.4 18.8 %collective-permute-start.21 = (bf16[4,192,512]{2,1,0:T(8,128)(2,1)S(1)}, bf16[4,192,512]{2,1,0:T(8,128)(2,1)S(1)}, u32[]{:S(2)}, u32[]{:S(2)}) collective-permute-start(bf16[4,192,512]{2,1,0:T(8,128)(2,1)S(1)} %collective-permute-done.16.up.refs_1_), channel_id=1, source_target_pairs={{0,4},{4,0},{1,5},{5,1},{2,6},{6,2},{3,7},{7,3},{8,12},{12,8},{9,1... | collective-permute-start | bytes 2359304 | tf_op jit(solution)/shard_map/ppermute | solution.py:472
  110.8 15.4 %collective-permute-start.22 = (bf16[4,192,512]{2,1,0:T(8,128)(2,1)S(1)}, bf16[4,192,512]{2,1,0:T(8,128)(2,1)S(1)}, u32[]{:S(2)}, u32[]{:S(2)}) collective-permute-start(bf16[4,192,512]{2,1,0:T(8,128)(2,1)S(1)} %collective-permute-done.17.dn.refs_2_), channel_id=1, source_target_pairs={{0,4},{4,0},{1,5},{5,1},{2,6},{6,2},{3,7},{7,3},{8,12},{12,8},{9,1... | collective-permute-start | bytes 2359304 | tf_op jit(solution)/shard_map/ppermute | solution.py:472
  112.1 14.2 %collective-permute-start.23 = (bf16[4,192,512]{2,1,0:T(8,128)(2,1)S(1)}, bf16[4,192,512]{2,1,0:T(8,128)(2,1)S(1)}, u32[]{:S(2)}, u32[]{:S(2)}) collective-permute-start(bf16[4,192,512]{2,1,0:T(8,128)(2,1)S(1)} %join.3.refs_3_), channel_id=1, source_target_pairs={{0,4},{4,0},{1,5},{5,1},{2,6},{6,2},{3,7},{7,3},{8,12},{12,8},{9,1... | collective-permute-start | bytes 2359304 | tf_op jit(solution)/shard_map/ppermute | solution.py:472
  126.2 14.9 %copy-start.4 = (f32[4,8,512]{2,1,0:T(8,128)S(1)}, f32[4,8,512]{2,1,0:T(8,128)}, u32[]{:S(2)}) copy-start(f32[4,8,512]{2,1,0:T(8,128)} %copy-done.2) | copy-start | bytes 196612

commit v4 on v3

v4 whole, which is shorter than its diff:
```python
import functools

import jax
import jax.numpy as jnp
from jax import lax
from jax.experimental import pallas as pl
from jax.experimental.pallas import tpu as pltpu
from jax.sharding import Mesh, PartitionSpec as P

HEAD_DIM = 128
EPS = 1e-06
THETA = 500000.0
NT = (((1,), (1,)), ((), ()))
BLOCK = 512
F32 = jnp.float32
BF16 = jnp.bfloat16
NZ, NY, NC, NX = 4, 4, 2, 4
X = ("xh", "xl")
VMEM = pl.BlockSpec(memory_space=pltpu.VMEM)
HBM = pl.BlockSpec(memory_space=pltpu.HBM)
ANY = pl.BlockSpec(memory_space=pl.ANY)
SMEM = pl.BlockSpec(memory_space=pltpu.SMEM)


def call(kernel, out_shape, in_specs, out_specs, scratch=(), cost=(1 << 20, 1 << 20), name=None, limit=4):
    return pl.pallas_call(
        kernel,
        out_shape=out_shape,
        in_specs=in_specs,
        out_specs=out_specs,
        scratch_shapes=list(scratch),
        compiler_params=pltpu.CompilerParams(vmem_limit_bytes=limit * 1024 * 1024),
        cost_estimate=pl.CostEstimate(flops=cost[0], bytes_accessed=cost[1], transcendentals=0),
        name=name,
    )


def hbm(array):
    return pltpu.with_memory_space_constraint(array, pltpu.HBM)


def shape(dims, dtype):
    return jax.ShapeDtypeStruct(dims, dtype)


def run(copies, sem):
    copies = [pltpu.make_async_copy(a, b, sem.at[i]) for i, (a, b) in enumerate(copies)]
    for copy in copies:
        copy.start()
    for copy in copies:
        copy.wait()


def sort_kernel(*refs):
    pieces, (out, sem) = refs[:NY], refs[NY:]
    y = lax.axis_index("y")
    run([(pieces[s], out.at[lax.rem(y + NY - s, NY)]) for s in range(NY)], sem)


def join_kernel(*refs):
    out, sem = refs[-2:]
    pieces = refs[:-3]
    run([(piece, out.at[i]) for i, piece in enumerate(pieces)], sem)


def join(pieces, token, name):
    return call(
        join_kernel,
        shape((len(pieces),) + pieces[0].shape, BF16),
        [ANY] * (len(pieces) + 1),
        ANY,
        [pltpu.SemaphoreType.DMA((len(pieces),))],
        (0, 2 << 20),
        name,
        1,
    )(*pieces, token)


def piece_copies(pieces, buf, sem):
    z = lax.axis_index("z")
    core = lax.axis_index("c")
    copies = []
    for m in range(NC):
        c = core if m == 0 else 1 - core
        for i, shift in enumerate((0, NZ - 1, NZ - 2, NZ - 3)):
            target = buf.at[lax.rem(z + shift, NZ), c]
            copies.append(pltpu.make_async_copy(pieces[m].at[i], target, sem.at[m, i]))
    return copies


def project_kernel(h_own, h_mate, w_own, w_mate, gate_up, down, out, hbuf, wbuf, rows_buf, gbuf, dbuf, sem):
    core = lax.axis_index("c")
    copies = [
        pltpu.make_async_copy(h_own, hbuf.at[core], sem.at[0]),
        pltpu.make_async_copy(h_mate, hbuf.at[1 - core], sem.at[1]),
        pltpu.make_async_copy(w_own, wbuf.at[core], sem.at[2]),
        pltpu.make_async_copy(w_mate, wbuf.at[1 - core], sem.at[3]),
        pltpu.make_async_copy(gate_up, gbuf, sem.at[4]),
        pltpu.make_async_copy(down, dbuf, sem.at[5]),
    ]
    for copy in copies:
        copy.start()
    copies[0].wait()
    copies[1].wait()
    rows_buf[...] = jnp.concatenate([hbuf[0].astype(F32).T, hbuf[1].astype(F32).T], axis=1)
    blocks, lines, lanes = out.shape
    feats, width = w_own.shape[1:]
    rows = rows_buf.shape[0] // (blocks * NC)
    chosen = jnp.concatenate(
        [
            rows_buf[pl.ds(pl.multiple_of((2 * b + core) * rows, rows), rows), :]
            for b in range(blocks)
        ],
        axis=0,
    ).astype(BF16)
    copies[2].wait()
    copies[3].wait()
    at = 0
    for g in range(3):
        weights = jnp.concatenate([wbuf[0, g], wbuf[1, g]], axis=0)
        part = jnp.dot(chosen, weights, preferred_element_type=F32).astype(BF16)
        for t in range(width // lanes):
            out[:, at : at + rows] = part[:, t * lanes : (t + 1) * lanes].reshape(blocks, rows, lanes)
            at += rows
    out[:, at : at + rows] = chosen.reshape(blocks, rows, lanes)
    at += rows
    copies[4].wait()
    copies[5].wait()
    for b in range(blocks):
        cols = pl.ds(b * lanes, lanes)
        out[b, at : at + feats] = gbuf[0, :, cols]
        out[b, at + feats : at + 2 * feats] = gbuf[1, :, cols]
        out[b, at + 2 * feats : at + 3 * feats] = dbuf[:, cols]


def quarter(ref, x):
    pair = ref[pl.ds(pl.multiple_of(x // 2 * 8, 8), 8), :]
    return jnp.where(lax.rem(x, 2) == 0, pair[:4], pair[4:])


def collect_kernel(got, after, tables, bounds, gains, qk, value, squares, rest, ffn, rest_buf, sem):
    rows, width = value.shape
    blocks, lines, lanes = got.shape
    tiles = width // lanes
    at = (3 * tiles + 1) * rows
    copy = pltpu.make_async_copy(got.at[:, pl.ds(at, lines - at)], ffn, sem)
    copy.start()
    total = got[0, : 3 * width // lanes * rows].astype(F32)
    for i in range(1, blocks):
        total += got[i, : 3 * width // lanes * rows].astype(F32)

    def part(g):
        return jnp.concatenate(
            [total[(g * tiles + t) * rows : (g * tiles + t + 1) * rows] for t in range(tiles)], axis=1
        )

    q, k = part(0), part(1)
    qk[0] = q
    qk[1] = k
    value[...] = part(2).astype(BF16)
    lane = lax.broadcasted_iota(jnp.int32, squares.shape[1:], 1)
    both = jnp.where(
        lane < 64, jnp.sum(q * q, axis=1, keepdims=True), jnp.sum(k * k, axis=1, keepdims=True)
    )
    for i in range(NX):
        squares[i] = both
    for i in range(blocks):
        rest_buf[:, i * lanes : (i + 1) * lanes] = got[i, at - rows : at].astype(F32)
    rest[...] = quarter(rest_buf, lax.axis_index("xh") * 2 + lax.axis_index("xl"))
    copy.wait()


def turn(values, cosine, sine):
    heads = values.shape[1] // HEAD_DIM
    parts = []
    for h in range(heads):
        v = values[:, h * HEAD_DIM : (h + 1) * HEAD_DIM]
        parts.append(v * cosine + pltpu.roll(v, HEAD_DIM // 2, 1) * sine)
    return jnp.concatenate(parts, axis=1)


def spread(values, heads):
    rows, width = values.shape
    wide = rows * heads
    row_head = lax.broadcasted_iota(jnp.int32, (wide, width), 0) // rows
    col_head = lax.broadcasted_iota(jnp.int32, (wide, width), 1) // HEAD_DIM
    return jnp.where(row_head == col_head, jnp.concatenate([values] * heads, axis=0), 0.0)


def attend_kernel(squares_in, qk, value, gains, tables, bounds, keys, values, key_out,
                  out, score, top, kbuf, vbuf, acc, total, ksem, vsem):
    rows, width = value.shape
    heads = width // HEAD_DIM
    blocks = score.shape[0]
    model = width * NX
    used = jnp.max(bounds[...].astype(F32))

    def fetch(source, buf, sem, i):
        return pltpu.make_async_copy(source.at[pl.ds(i * BLOCK, BLOCK)], buf.at[i], sem.at[i])

    for source, buf, sem in ((keys, kbuf, ksem), (values, vbuf, vsem)):
        for i in range(blocks):
            @pl.when(i * BLOCK < used)
            def _():
                fetch(source, buf, sem, i).start()

    squares = squares_in[0] + squares_in[1] + squares_in[2] + squares_in[3]
    q_factor = lax.rsqrt(squares[:, 0:1] / model + EPS)
    k_factor = lax.rsqrt(squares[:, 64:65] / model + EPS)
    query = turn(qk[0] * q_factor * gains[0:1, :], tables[0], tables[1]).astype(BF16)
    new_key = turn(qk[1] * k_factor * gains[1:2, :], tables[0], tables[1]).astype(BF16)
    key_out[...] = new_key
    scale = HEAD_DIM ** (-0.5)
    q_all = spread(query.astype(F32), heads)
    q_block = q_all.astype(BF16)
    k_all = jnp.concatenate([new_key.astype(F32)] * heads, axis=0)
    v_all = jnp.concatenate([value[...].astype(F32)] * heads, axis=0)
    own = jnp.sum(q_all * k_all, axis=1, keepdims=True) * scale
    starts = bounds[:, 0:1]
    ends = bounds[:, 1:2]
    top[...] = jnp.broadcast_to(own, top.shape)
    for i in range(blocks):
        @pl.when(i * BLOCK < used)
        def _():
            fetch(keys, kbuf, ksem, i).wait()
            s = lax.dot_general(q_block, kbuf[i], NT, preferred_element_type=F32) * scale
            place = lax.broadcasted_iota(jnp.int32, s.shape, 1) + i * BLOCK
            s = jnp.where((place >= starts) & (place < ends), s, -jnp.inf)
            score[i] = s
            top[...] = jnp.maximum(top[...], jnp.max(s, axis=1, keepdims=True))
    highest = top[:, 0:1]
    own_weight = jnp.exp(own - highest).astype(BF16).astype(F32)
    total[...] = jnp.broadcast_to(own_weight, total.shape)
    acc[...] = own_weight * v_all
    for i in range(blocks):
        @pl.when(i * BLOCK < used)
        def _():
            fetch(values, vbuf, vsem, i).wait()
            w = jnp.exp(score[i] - highest).astype(BF16)
            total[...] += jnp.sum(w.astype(F32), axis=1, keepdims=True)
            acc[...] += jnp.dot(w, vbuf[i], preferred_element_type=F32)
    result = acc[...] / total[:, 0:1]
    out[...] = jnp.concatenate(
        [
            result[h * rows : (h + 1) * rows, h * HEAD_DIM : (h + 1) * HEAD_DIM]
            for h in range(heads)
        ],
        axis=1,
    ).astype(BF16)


def out_kernel(attended, *refs):
    pieces = refs[:NC]
    partial, gain_out, wbuf, sem = refs[NC:]
    rows, width = attended.shape
    copies = piece_copies(pieces, wbuf, sem)
    for copy in copies:
        copy.start()
    for copy in copies:
        copy.wait()
    feats = width // (NY * NC)
    mine = rows // NX
    for b in range(NZ):
        weights = jnp.concatenate(
            [wbuf[b, c, y, :feats] for y in range(NY) for c in range(NC)], axis=0
        )
        a = lax.dot_general(attended[...], weights, NT, preferred_element_type=F32)
        for x in range(NX):
            partial[x, :, b * width : (b + 1) * width] = a[x * mine : (x + 1) * mine]
        both = wbuf[b, 0, 0, feats:].astype(F32)
        for y in range(NY):
            for c in range(NC):
                if y or c:
                    both += wbuf[b, c, y, feats:].astype(F32)
        gain_out[b, 0:1] = both[0:1] + both[1:2]
        gain_out[b, 1:2] = both[2:3] + both[3:4]


def fan_kernel(got, rest, gains, own_mid, out):
    total = got[0] + got[1] + got[2] + got[3]
    model = total.shape[1]
    power = jnp.sum(total * total, axis=1, keepdims=True) / model
    gain = jnp.concatenate([gains[z, 0:1] for z in range(NZ)], axis=1)
    mid = (rest[...] + total * lax.rsqrt(power + EPS) * gain).astype(BF16)
    mid32 = mid.astype(F32)
    own_mid[...] = mid32
    message = jnp.concatenate([mid32[:, : model // 2], mid32[:, model // 2 :]], axis=0).astype(BF16)
    for i in range(out.shape[0]):
        out[i] = message


def ffn_kernel(got, own, own_mate, near, near_mate, out, wbuf, sem):
    core = lax.axis_index("c")
    copies = [
        pltpu.make_async_copy(own, wbuf.at[0, core], sem.at[0]),
        pltpu.make_async_copy(own_mate, wbuf.at[0, 1 - core], sem.at[1]),
        pltpu.make_async_copy(near, wbuf.at[1, core], sem.at[2]),
        pltpu.make_async_copy(near_mate, wbuf.at[1, 1 - core], sem.at[3]),
    ]
    for copy in copies:
        copy.start()
    places, lines, span = got.shape
    mine = lines // 2
    whole = [got[d].astype(F32) for d in range(places)]
    mid = [
        jnp.concatenate([w[half * mine : (half + 1) * mine] for w in whole], axis=0).astype(BF16)
        for half in range(2)
    ]
    blocks = wbuf.shape[2]
    feats = wbuf.shape[3] // 3
    for copy in copies:
        copy.wait()

    def weights(part, half):
        rows = range(half * blocks // 2, (half + 1) * blocks // 2)
        return jnp.concatenate(
            [
                jnp.concatenate(
                    [
                        wbuf[p, c, b, part * feats : (part + 1) * feats]
                        for b in rows
                        for c in range(NC)
                    ],
                    axis=0,
                )
                for p in range(2)
            ],
            axis=1,
        )

    gate = jnp.dot(mid[0], weights(0, 0), preferred_element_type=F32)
    gate += jnp.dot(mid[1], weights(0, 1), preferred_element_type=F32)
    lift = jnp.dot(mid[0], weights(1, 0), preferred_element_type=F32)
    lift += jnp.dot(mid[1], weights(1, 1), preferred_element_type=F32)
    act = (gate / (1.0 + jnp.exp(-gate)) * lift).astype(BF16)
    flat = [lax.dot_general(act, weights(2, h), NT, preferred_element_type=F32) for h in range(2)]
    for d in range(places):
        out[d] = jnp.concatenate([f[d * mine : (d + 1) * mine] for f in flat], axis=0).astype(BF16)


def finish_kernel(got, own_mid, gains, out):
    total = got[0].astype(F32)
    for i in range(1, got.shape[0]):
        total += got[i].astype(F32)
    mine = own_mid.shape[0]
    total = jnp.concatenate([total[:mine], total[mine:]], axis=1)
    model = total.shape[1]
    power = jnp.sum(total * total, axis=1, keepdims=True) / model
    gain = jnp.concatenate([gains[z, 1:2] for z in range(NZ)], axis=1)
    hidden = (own_mid[...] + total * lax.rsqrt(power + EPS) * gain).astype(BF16)
    feats = out.shape[2]
    for r in range(model // feats):
        part = hidden[:, r * feats : (r + 1) * feats]
        for x in range(NX):
            out[r * NX + x] = part


def ring(shift, size):
    return [(i, (i + shift) % size) for i in range(size)]


def body(hidden_in, lengths, w_qkv, qk_gain, cache_keys, cache_values, w_out, norm_gain,
         w_gate_up, w_down):
    rows = lengths.shape[0]
    width = w_qkv.shape[2]
    heads = width // HEAD_DIM
    feats = hidden_in.shape[1]
    model = width * NX
    wide = rows * heads
    blocks = cache_keys.shape[0] // BLOCK
    y_here = lax.axis_index("y")
    c_here = lax.axis_index("c")

    flipped = hidden_in.T
    mate_rows = lax.ppermute(flipped, "c", ring(1, NC))
    mate_w = lax.ppermute(w_qkv, "c", ring(1, NC))
    places = NZ * NY
    size = 3 * feats
    lanes = 128
    lines = (3 * width // lanes + 1) * rows + size
    message = call(
        project_kernel,
        shape((places, lines, lanes), BF16),
        [ANY] * 6,
        VMEM,
        [
            pltpu.VMEM((2, feats, flipped.shape[1]), BF16),
            pltpu.VMEM((2,) + w_qkv.shape, BF16),
            pltpu.VMEM((flipped.shape[1], 2 * feats), F32),
            pltpu.VMEM(w_gate_up.shape, BF16),
            pltpu.VMEM(w_down.shape, BF16),
            pltpu.SemaphoreType.DMA((6,)),
        ],
        (1 << 27, 2 << 20),
        "project",
        8,
    )(hbm(flipped), mate_rows, hbm(w_qkv), mate_w, hbm(w_gate_up), hbm(w_down))
    got = lax.all_to_all(message, ("z", "y"), 0, 0, tiled=True)

    high = norm_gain.astype(BF16)
    low = (norm_gain - high.astype(F32)).astype(BF16)
    gain_rows = jnp.stack([high[0], low[0], high[1], low[1]])
    gain_tile = jnp.zeros((8, width), BF16)
    gain_tile = lax.dynamic_update_slice(
        gain_tile, gain_rows, (jnp.int32(0), (y_here * NC + c_here) * feats)
    )
    part = jnp.concatenate([w_out, gain_tile], axis=0)
    part = call(
        sort_kernel,
        shape((NY,) + part.shape, BF16),
        [ANY] * NY,
        ANY,
        [pltpu.SemaphoreType.DMA((NY,))],
        (0, 1 << 20),
        "sort",
        1,
    )(part, *[lax.ppermute(part, "y", ring(s, NY)) for s in range(1, NY)])
    out_pieces = [part] + [lax.ppermute(part, "z", ring(s, NZ)) for s in range(1, NZ)]

    half = HEAD_DIM // 2
    freqs = jnp.power(THETA, -(jnp.arange(half, dtype=F32) * 2.0 / HEAD_DIM))
    angles = lengths.astype(F32)[:, None] * freqs[None, :]
    cosine = jnp.cos(angles)
    sine = jnp.sin(angles)
    tables = jnp.stack(
        [jnp.concatenate([cosine, cosine], axis=1), jnp.concatenate([-sine, sine], axis=1)]
    )
    ends = jnp.cumsum(lengths)
    bounds = jnp.tile(jnp.stack([ends - lengths, ends], axis=1), (heads, 1))
    gain_table = jnp.concatenate([qk_gain, jnp.zeros((6, width), F32)], axis=0)
    qk, value_new, squares, rest, ffn_own = call(
        collect_kernel,
        (
            shape((2, rows, width), F32),
            shape((rows, width), BF16),
            shape((NX, rows, 128), F32),
            shape((rows // NX, model), F32),
            shape((places, size, lanes), BF16),
        ),
        [VMEM] + [ANY] * 4,
        (VMEM,) * 4 + (ANY,),
        [pltpu.VMEM((rows, model), F32), pltpu.SemaphoreType.DMA],
        (1 << 20, 96 << 20),
        "collect",
        8,
    )(got, part, tables, bounds, gain_table)
    squares = lax.all_to_all(squares, X, 0, 0, tiled=True)
    out_own = join(out_pieces, squares, "join_out")
    out_mate = lax.ppermute(out_own, "c", ring(1, NC))
    key_new, attended = call(
        attend_kernel,
        (shape((rows, width), BF16), shape((rows, width), BF16)),
        [VMEM] * 6 + [ANY] * 2,
        (VMEM,) * 2,
        [
            pltpu.VMEM((blocks, wide, BLOCK), F32),
            pltpu.VMEM((wide, 128), F32),
            pltpu.VMEM((blocks, BLOCK, width), BF16),
            pltpu.VMEM((blocks, BLOCK, width), BF16),
            pltpu.VMEM((wide, width), F32),
            pltpu.VMEM((wide, 128), F32),
            pltpu.SemaphoreType.DMA((blocks,)),
            pltpu.SemaphoreType.DMA((blocks,)),
        ],
        (1 << 29, 8 << 20),
        "attend",
        16,
    )(squares, qk, value_new, gain_table, tables, bounds, hbm(cache_keys), hbm(cache_values))
    partial, gains = call(
        out_kernel,
        (shape((NX, rows // NX, model), F32), shape((NZ, 8, width), F32)),
        [VMEM] + [ANY] * NC,
        (VMEM,) * 2,
        [
            pltpu.VMEM((NZ, NC) + part.shape, BF16),
            pltpu.SemaphoreType.DMA((NC, 4)),
        ],
        (1 << 26, 2 << 20),
        "project_out",
        8,
    )(attended, out_own, out_mate)

    near = [(i, i ^ 1) for i in range(2)]
    ffn_near = lax.ppermute(ffn_own, "xl", near)
    got = lax.all_to_all(partial, X, 0, 0, tiled=True)
    mine = rows // NX
    group = ("z", "y", "xh")
    members = NZ * NY * NX // 2
    own_mid, message = call(
        fan_kernel,
        (shape((mine, model), F32), shape((members, 2 * mine, model // 2), BF16)),
        [VMEM] * 3,
        (VMEM, VMEM),
        (),
        (1 << 16, 1 << 19),
        "fan",
    )(got, rest, gains)
    ffn_near = join([ffn_near], own_mid, "hold")[0]
    ffn_pieces = []
    for piece in (ffn_own, ffn_near):
        ffn_pieces += [piece, lax.ppermute(piece, "c", ring(1, NC))]
    got = lax.all_to_all(message, group, 0, 0, tiled=True)
    partial = call(
        ffn_kernel,
        shape((members, 2 * mine, model // 2), BF16),
        [VMEM] + [ANY] * 4,
        VMEM,
        [
            pltpu.VMEM((2, NC) + ffn_own.shape, BF16),
            pltpu.SemaphoreType.DMA((4,)),
        ],
        (1 << 28, 4 << 20),
        "feed_forward",
        16,
    )(got, *ffn_pieces)
    got = lax.all_to_all(partial, group, 0, 0, tiled=True)
    message = call(
        finish_kernel,
        shape((NZ * NY * NC * NX, mine, feats), BF16),
        [VMEM] * 3,
        VMEM,
        (),
        (1 << 18, 1 << 19),
        "finish",
    )(got, own_mid, gains)
    hidden = lax.all_to_all(message, ("z", "y", "c") + X, 0, 0, tiled=True)
    return hidden.reshape(-1, feats), key_new, value_new


def solution(mesh):
    fine = Mesh(mesh.devices.reshape(NZ, NY, NC, 2, 2), ("z", "y", "c") + X)
    req = ("z", "y", "c")
    return jax.shard_map(
        body,
        mesh=fine,
        in_specs=(
            P(None, req),
            P(req),
            P(None, req, X),
            P(None, X),
            P(req, X),
            P(req, X),
            P(req, X),
            P(None, req),
            P(None, req, X),
            P(req, X),
        ),
        out_specs=(P(None, req), P(req, X), P(req, X)),
        check_vma=False,
    )
```

time: 159 us -> 138 us (0.87)
  waiting for transfers between devices: 25.1 us -> 49.6 us
  local copies, waits for them, and re-layouts: 15.1 us -> 1.74 us
  Pallas kernels: 24.1 us -> 13.2 us
  blocking collectives: 41.5 us -> 30.8 us
  starting transfers between devices: 47.9 us -> 40.7 us
  other arithmetic: 2.73 us -> 0.4 us
    all_to_all x2 -> x3, waiting for transfers between devices: 7.11 us -> 20.2 us  [the longest x1 12.5 us: body(): got = lax.all_to_all(message, group, 0, 0, tiled=True)]
    ppermute x22 -> x10, starting transfers between devices: 31.1 us -> 18 us  [the longest x2 5.65 us: body(): ffn_pieces += [piece, lax.ppermute(piece, 'c', ring(1, NC))]]
    unnamed x48 -> x16, local copies, waits for them, and re-layouts: 13.8 us -> 1.06 us
    ppermute x22 -> x10, waiting for transfers between devices: 16.6 us -> 28 us  [the longest x3 21.4 us: body(): lax.ppermute(part, 'y', ring(s, NY))]
    pallas_call x12 -> x8, Pallas kernels: 23.2 us -> 12.1 us  [the longest x1 3.39 us: body(): call(attend_kernel, (shape((rows, width), BF16), shape((rows, width), BF1...]
    all_to_all x3 -> x2, blocking collectives: 41.5 us -> 30.8 us  [the longest x1 16 us: body(): hidden = lax.all_to_all(message, ('z', 'y', 'c') + X, 0, 0, tiled=True)]
    all_to_all x2 -> x3, starting transfers between devices: 7.34 us -> 13.1 us  [the longest x1 5.3 us: body(): got = lax.all_to_all(message, group, 0, 0, tiled=True)]
  transfers between devices with their start and end apart: 27 -> 16, of which waited for: 5 -> 7; matrix products, arithmetic and copies ran while one was open for 3% -> 1% of each run, Pallas kernels for 12% -> 5%
where the time goes in v4:
time: 138 us; the launch traced here: 137 us
  waiting for transfers between devices  49.6 us (36%)
  starting transfers between devices  40.7 us (29%)
  blocking collectives  30.8 us (22%)
  Pallas kernels  13.2 us (10%)
  local copies, waits for them, and re-layouts  1.74 us (1%)
    ppermute x3, waiting for transfers between devices, body(): lax.ppermute(part, 'y', ring(s, NY))  21.4 us
    all_to_all x1, blocking collectives, body(): hidden = lax.all_to_all(message, ('z', 'y', 'c') + X, 0, 0, tiled=True)  16 us
    all_to_all x1, blocking collectives, body(): got = lax.all_to_all(partial, group, 0, 0, tiled=True)  14.8 us
    all_to_all x1, waiting for transfers between devices, body(): got = lax.all_to_all(message, group, 0, 0, tiled=True)  12.5 us
    all_to_all x1, starting transfers between devices, body(): got = lax.all_to_all(message, ('z', 'y'), 0, 0, tiled=True)  8 us
    all_to_all x1, waiting for transfers between devices, body(): got = lax.all_to_all(partial, X, 0, 0, tiled=True)  7.7 us
    ppermute x3, waiting for transfers between devices, body(): lax.ppermute(part, 'z', ring(s, NZ))  6.6 us
    ppermute x2, starting transfers between devices, body(): ffn_pieces += [piece, lax.ppermute(piece, 'c', ring(1, NC))]  5.65 us
  transfers between devices with their start and end apart: 16, of which 7 were waited for; matrix products, arithmetic and copies ran while one was open for 1% of the time, Pallas kernels for 5%

profile of v4, /device:TPU:1, one launch (start us, length us, event | category | flops | bytes accessed | tf_op | source)
XLA Modules:
  0.0 137.3 jit_solution(10836932205647770356)
XLA Ops:
  0.6 1.5 %collective-permute-start.1 = (bf16[3,64,512]{2,1,0:T(8,128)(2,1)}, bf16[3,64,512]{2,1,0:T(8,128)(2,1)S(1)}, u32[]{:S(2)}, u32[]{:S(2)}) collective-permute-start(bf16[3,64,512]{2,1,0:T(8,128)(2,1)} %w_own.1), channel_id=1, source_target_pairs={{0,4},{4,0},{1,5},{5,1},{2,6},{6,2},{3,7},{7,3},{8,12},{12,8},{9,1... | collective-permute-start | bytes 589832 | tf_op jit(solution)/shard_map/ppermute | solution.py:376
  2.1 0.1 collective-permute-start
  2.2 1.4 collective-permute-done.h_mate
  3.6 0.0 collective-permute-done.1.w_mate
  3.6 2.9 %project.1 = bf16[16,400,128]{2,1,0:T(8,128)(2,1)} custom-call(bf16[64,512]{1,0:T(8,128)(2,1)} %bitcast.17, bf16[64,512]{1,0:T(8,128)(2,1)S(1)} %collective-permute-done.h_mate, bf16[3,64,512]{2,1,0:T(8,128)(2,1)} %w_own.1, bf16[3,64,512]{2,1,0:T(8,128)(2,1)S(1)} %collective-permute-done.1.w_mate, bf16[2,64,2048]{2,1,0:T(8,128)(2,1)} %gate_up.1, ...), custom_call_target="tpu_custom_call" | custom-call | flops 134217728 | bytes 2097152 | tf_op jit(solution)/shard_map/project/pallas_call | solution.py:381
  6.5 0.0 copy-start.5
  6.5 0.0 copy-start.2
  6.5 0.0 copy-start.4
  6.5 0.0 copy-start.3
  6.5 8.0 %all-to-all-start = ((bf16[16,400,128]{2,1,0:T(8,128)(2,1)}), bf16[16,400,128]{2,1,0:T(8,128)(2,1)S(1)}, u32[]{:S(2)}, u32[]{:S(2)}) async-start(bf16[16,400,128]{2,1,0:T(8,128)(2,1)} %project.1), calls=%async_computation | async-start | bytes 3276800 | tf_op jit(solution)/shard_map/all_to_all | solution.py:398
  14.5 0.0 copy-done.5
  14.6 0.5 dynamic_update_slice.3
  15.1 0.0 copy-done.2
  15.1 1.4 %collective-permute-start.2 = (bf16[72,512]{1,0:T(8,128)(2,1)S(1)}, bf16[72,512]{1,0:T(8,128)(2,1)S(1)}, u32[]{:S(2)}, u32[]{:S(2)}) collective-permute-start(bf16[72,512]{1,0:T(8,128)(2,1)S(1)} %pad_maximum_fusion.refs_0_), channel_id=1, source_target_pairs={{0,8},{8,16},{16,24},{24,0},{1,9},{9,17},{17,25},{25,1},{2,10},{10... | collective-permute-start | bytes 221192 | tf_op jit(solution)/shard_map/ppermute | solution.py:417
  16.5 2.4 %collective-permute-start.3 = (bf16[72,512]{1,0:T(8,128)(2,1)S(1)}, bf16[72,512]{1,0:T(8,128)(2,1)S(1)}, u32[]{:S(2)}, u32[]{:S(2)}) collective-permute-start(bf16[72,512]{1,0:T(8,128)(2,1)S(1)} %pad_maximum_fusion.refs_0_), channel_id=1, source_target_pairs={{0,16},{8,24},{16,0},{24,8},{1,17},{9,25},{17,1},{25,9},{2,18},{10... | collective-permute-start | bytes 221192 | tf_op jit(solution)/shard_map/ppermute | solution.py:417
  18.9 1.2 collective-permute-start.4
  20.1 0.0 copy-done.4
  20.1 0.1 copy.25
  20.2 0.1 reduce
  20.4 0.1 multiply_cosine_fusion
  20.5 0.1 copy.26
  20.6 16.3 %collective-permute-done.2.refs_1_ = bf16[72,512]{1,0:T(8,128)(2,1)S(1)} collective-permute-done((bf16[72,512]{1,0:T(8,128)(2,1)S(1)}, bf16[72,512]{1,0:T(8,128)(2,1)S(1)}, u32[]{:S(2)}, u32[]{:S(2)}) %collective-permute-start.2) | collective-permute-done | bytes 73760 | tf_op jit(solution)/shard_map/ppermute | solution.py:417
  36.9 5.0 %collective-permute-done.3.refs_2_ = bf16[72,512]{1,0:T(8,128)(2,1)S(1)} collective-permute-done((bf16[72,512]{1,0:T(8,128)(2,1)S(1)}, bf16[72,512]{1,0:T(8,128)(2,1)S(1)}, u32[]{:S(2)}, u32[]{:S(2)}) %collective-permute-start.3) | collective-permute-done | bytes 73760 | tf_op jit(solution)/shard_map/ppermute | solution.py:417
  41.9 0.0 collective-permute-done.4.refs_3_
  41.9 0.4 sort.1.after.refs_0_
  42.4 0.3 collective-permute-start.5
  42.7 2.3 %collective-permute-start.6 = (bf16[4,72,512]{2,1,0:T(8,128)(2,1)S(1)}, bf16[4,72,512]{2,1,0:T(8,128)(2,1)S(1)}, u32[]{:S(2)}, u32[]{:S(2)}) collective-permute-start(bf16[4,72,512]{2,1,0:T(8,128)(2,1)S(1)} %sort.1.after.refs_0_), channel_id=1, source_target_pairs={{0,64},{32,96},{64,0},{96,32},{1,65},{33,97},{65,1},{97,33},{2,66}... | collective-permute-start | bytes 884744 | tf_op jit(solution)/shard_map/ppermute | solution.py:418
  45.0 1.8 %collective-permute-start.7 = (bf16[4,72,512]{2,1,0:T(8,128)(2,1)S(1)}, bf16[4,72,512]{2,1,0:T(8,128)(2,1)}, u32[]{:S(2)}, u32[]{:S(2)}) collective-permute-start(bf16[4,72,512]{2,1,0:T(8,128)(2,1)S(1)} %sort.1.after.refs_0_), channel_id=1, source_target_pairs={{0,96},{32,0},{64,32},{96,64},{1,97},{33,1},{65,33},{97,65},{2,98}... | collective-permute-start | bytes 884744 | tf_op jit(solution)/shard_map/ppermute | solution.py:418
  46.8 0.1 copy.31
  46.8 0.0 copy-done.3
  46.9 0.1 maximum_bitcast_fusion
  46.9 0.0 all-to-all-done.got
  46.9 0.8 collect.1
  47.8 0.0 copy-start.1
  47.8 4.0 %all-to-all-start.1 = ((f32[4,16,128]{2,1,0:T(8,128)}), f32[4,16,128]{2,1,0:T(8,128)S(1)}, u32[]{:S(2)}, u32[]{:S(2)}) async-start(f32[4,16,128]{2,1,0:T(8,128)} %get-tuple-element.14), calls=%async_computation.1 | async-start | bytes 65536 | tf_op jit(solution)/shard_map/all_to_all | solution.py:447
  51.8 0.0 collective-permute-done.5.refs_1_
  51.8 5.0 %collective-permute-done.6.refs_2_ = bf16[4,72,512]{2,1,0:T(8,128)(2,1)S(1)} collective-permute-done((bf16[4,72,512]{2,1,0:T(8,128)(2,1)S(1)}, bf16[4,72,512]{2,1,0:T(8,128)(2,1)S(1)}, u32[]{:S(2)}, u32[]{:S(2)}) %collective-permute-start.6) | collective-permute-done | bytes 294944 | tf_op jit(solution)/shard_map/ppermute | solution.py:418
  56.8 1.6 %collective-permute-done.7.refs_3_ = bf16[4,72,512]{2,1,0:T(8,128)(2,1)} collective-permute-done((bf16[4,72,512]{2,1,0:T(8,128)(2,1)S(1)}, bf16[4,72,512]{2,1,0:T(8,128)(2,1)}, u32[]{:S(2)}, u32[]{:S(2)}) %collective-permute-start.7) | collective-permute-done | bytes 294944 | tf_op jit(solution)/shard_map/ppermute | solution.py:418
  58.4 0.0 all-to-all-done.1.squares_in.refs_4_
  58.4 1.2 join_out.1.refs_0_
  59.6 1.8 %collective-permute-start.8 = (bf16[4,4,72,512]{3,2,1,0:T(8,128)(2,1)S(1)}, bf16[4,4,72,512]{3,2,1,0:T(8,128)(2,1)S(1)}, u32[]{:S(2)}, u32[]{:S(2)}) collective-permute-start(bf16[4,4,72,512]{3,2,1,0:T(8,128)(2,1)S(1)} %join_out.1.refs_0_), channel_id=1, source_target_pairs={{0,4},{4,0},{1,5},{5,1},{2,6},{6,2},{3,7},{7,3},{8,12},{12,8},{9,1... | collective-permute-start | bytes 3538952 | tf_op jit(solution)/shard_map/ppermute | solution.py:449
  61.4 1.2 collective-permute-start.10
  62.6 0.0 copy-done.1
  62.6 3.4 %attend.1 = (bf16[16,512]{1,0:T(8,128)(2,1)}, bf16[16,512]{1,0:T(8,128)(2,1)S(1)}) custom-call(f32[4,16,128]{2,1,0:T(8,128)S(1)} %all-to-all-done.1.squares_in.refs_4_, f32[2,16,512]{2,1,0:T(8,128)S(1)} %get-tuple-element.15.qk, bf16[16,512]{1,0:T(8,128)(2,1)S(1)} %copy-done.1, f32[8,512]{1,0:T(8,128)S(1)} %concatenate.15.gains, ...), custom_call_target="tpu_custom_call" | custom-call | flops 536870912 | bytes 8388608 | tf_op jit(solution)/shard_map/attend/pallas_call | solution.py:450
  66.0 0.0 collective-permute-done.8.refs_1_
  66.0 1.9 %project_out.1 = (f32[4,4,2048]{2,1,0:T(4,128)}, f32[4,8,512]{2,1,0:T(8,128)S(1)}) custom-call(bf16[16,512]{1,0:T(8,128)(2,1)S(1)} %get-tuple-element.17.attended, bf16[4,4,72,512]{3,2,1,0:T(8,128)(2,1)S(1)} %join_out.1.refs_0_, bf16[4,4,72,512]{3,2,1,0:T(8,128)(2,1)S(1)} %collective-permute-done.8.refs_1_), custom_call_target="tpu_custom_call" | custom-call | flops 67108864 | bytes 2097152 | tf_op jit(solution)/shard_map/project_out/pallas_call | solution.py:469
  67.9 3.7 %all-to-all-start.2 = ((f32[4,4,2048]{2,1,0:T(4,128)}), f32[4,4,2048]{2,1,0:T(4,128)S(1)}, u32[]{:S(2)}, u32[]{:S(2)}) async-start(f32[4,4,2048]{2,1,0:T(4,128)} %get-tuple-element.18), calls=%async_computation.2 | async-start | bytes 262144 | tf_op jit(solution)/shard_map/all_to_all | solution.py:485
  71.7 4.4 %collective-permute-start.9 = (bf16[16,192,128]{2,1,0:T(8,128)(2,1)S(1)}, bf16[16,192,128]{2,1,0:T(8,128)(2,1)S(1)}, u32[]{:S(2)}, u32[]{:S(2)}) collective-permute-start(bf16[16,192,128]{2,1,0:T(8,128)(2,1)S(1)} %get-tuple-element.22.own), channel_id=1, source_target_pairs={{0,4},{4,0},{1,5},{5,1},{2,6},{6,2},{3,7},{7,3},{8,12},{12,8},{9,1... | collective-permute-start | bytes 2359304 | tf_op jit(solution)/shard_map/ppermute | solution.py:501
  76.1 7.7 %all-to-all-done.2.got = f32[4,4,2048]{2,1,0:T(4,128)S(1)} async-done(((f32[4,4,2048]{2,1,0:T(4,128)}), f32[4,4,2048]{2,1,0:T(4,128)S(1)}, u32[]{:S(2)}, u32[]{:S(2)}) %all-to-all-start.2) | async-done | bytes 131104 | tf_op jit(solution)/shard_map/all_to_all | solution.py:485
  83.8 0.1 fan.1
  83.9 0.0 collective-permute-done.10.refs_0_
  84.0 0.1 hold.1
  84.0 1.2 collective-permute-start.11
  85.3 5.3 %all-to-all-start.3 = ((bf16[32,8,1024]{2,1,0:T(8,128)(2,1)}), bf16[32,8,1024]{2,1,0:T(8,128)(2,1)S(1)}, u32[]{:S(2)}, u32[]{:S(2)}) async-start(bf16[32,8,1024]{2,1,0:T(8,128)(2,1)} %copy-done), calls=%async_computation.3 | async-start | bytes 1048576 | tf_op jit(solution)/shard_map/all_to_all | solution.py:502
  90.6 0.0 collective-permute-done.9.own_mate
  90.6 12.5 %all-to-all-done.3.got = bf16[32,8,1024]{2,1,0:T(8,128)(2,1)S(1)} async-done(((bf16[32,8,1024]{2,1,0:T(8,128)(2,1)}), bf16[32,8,1024]{2,1,0:T(8,128)(2,1)S(1)}, u32[]{:S(2)}, u32[]{:S(2)}) %all-to-all-start.3) | async-done | bytes 524320 | tf_op jit(solution)/shard_map/all_to_all | solution.py:502
  103.1 0.0 collective-permute-done.11.near_mate
  103.1 2.2 %feed_forward.1 = bf16[32,8,1024]{2,1,0:T(8,128)(2,1)S(1)} custom-call(bf16[32,8,1024]{2,1,0:T(8,128)(2,1)S(1)} %all-to-all-done.3.got, bf16[16,192,128]{2,1,0:T(8,128)(2,1)S(1)} %get-tuple-element.22.own, bf16[16,192,128]{2,1,0:T(8,128)(2,1)S(1)} %collective-permute-done.9.own_mate, bf16[16,192,128]{2,1,0:T(8,128)(2,1)S(1)} %bitcast.12, ...), custom_call_target="tpu_custom_call" | custom-call | flops 268435456 | bytes 4194304 | tf_op jit(solution)/shard_map/feed_forward/pallas_call | solution.py:503
  105.3 14.8 %all_to_all.30.got = bf16[32,8,1024]{2,1,0:T(8,128)(2,1)S(1)} all-to-all(bf16[32,8,1024]{2,1,0:T(8,128)(2,1)S(1)} %feed_forward.1), channel_id=1, replica_groups=mesh['z'=4,'y'=4,'c'=2,'xh'=2,'xl'=2] {'z','y','xh'}, dimensions={0} | all-to-all | bytes 1048576 | tf_op jit(solution)/shard_map/all_to_all | solution.py:516
  120.1 0.3 finish.1
  120.3 0.1 reshape.31
  120.5 16.0 %all_to_all.31 = bf16[128,2,128]{2,1,0:T(2,128)(2,1)S(1)} all-to-all(bf16[128,2,128]{2,1,0:T(2,128)(2,1)S(1)} %reshape.31), channel_id=1, replica_groups=mesh['z'=4,'y'=4,'c'=2,'xh'=2,'xl'=2] {'z','y','c','xh','xl'}, dimensions={0} | all-to-all | bytes 131072 | tf_op jit(solution)/shard_map/all_to_all | solution.py:526
  136.4 0.1 reshape.32
  136.5 0.7 copy.29
  (14 shorter events, 0.1 us)
Async XLA Ops:
  0.6 3.0 %collective-permute-start.1 = (bf16[3,64,512]{2,1,0:T(8,128)(2,1)}, bf16[3,64,512]{2,1,0:T(8,128)(2,1)S(1)}, u32[]{:S(2)}, u32[]{:S(2)}) collective-permute-start(bf16[3,64,512]{2,1,0:T(8,128)(2,1)} %w_own.1), channel_id=1, source_target_pairs={{0,4},{4,0},{1,5},{5,1},{2,6},{6,2},{3,7},{7,3},{8,12},{12,8},{9,1... | collective-permute-start | bytes 589832 | tf_op jit(solution)/shard_map/ppermute | solution.py:376
  2.1 1.5 %collective-permute-start = (bf16[64,512]{1,0:T(8,128)(2,1)}, bf16[64,512]{1,0:T(8,128)(2,1)S(1)}, u32[]{:S(2)}, u32[]{:S(2)}) collective-permute-start(bf16[64,512]{1,0:T(8,128)(2,1)} %bitcast.16), channel_id=1, source_target_pairs={{0,4},{4,0},{1,5},{5,1},{2,6},{6,2},{3,7},{7,3},{8,12},{12,8},{9,1... | collective-permute-start | bytes 196616 | tf_op jit(solution)/shard_map/ppermute | solution.py:375
  6.5 8.1 %copy-start.5 = (f32[2,64]{1,0:T(2,128)S(1)}, f32[2,64]{1,0:T(2,128)}, u32[]{:S(2)}) copy-start(f32[2,64]{1,0:T(2,128)} %param.17) | copy-start | bytes 1540
  6.5 8.6 %copy-start.2 = (bf16[64,512]{1,0:T(8,128)(2,1)S(1)}, bf16[64,512]{1,0:T(8,128)(2,1)}, u32[]{:S(2)}) copy-start(bf16[64,512]{1,0:T(8,128)(2,1)} %param.16) | copy-start | bytes 196612
  6.5 13.6 %copy-start.4 = (s32[16]{0:T(128)S(1)}, s32[16]{0:T(128)}, u32[]{:S(2)}) copy-start(s32[16]{0:T(128)} %param.11) | copy-start | bytes 196
  6.5 40.3 %copy-start.3 = (f32[2,512]{1,0:T(2,128)S(1)}, f32[2,512]{1,0:T(2,128)}, u32[]{:S(2)}) copy-start(f32[2,512]{1,0:T(2,128)} %param.13) | copy-start | bytes 12292
  6.5 40.4 %all-to-all-start = ((bf16[16,400,128]{2,1,0:T(8,128)(2,1)}), bf16[16,400,128]{2,1,0:T(8,128)(2,1)S(1)}, u32[]{:S(2)}, u32[]{:S(2)}) async-start(bf16[16,400,128]{2,1,0:T(8,128)(2,1)} %project.1), calls=%async_computation | async-start | bytes 3276800 | tf_op jit(solution)/shard_map/all_to_all | solution.py:398
  15.1 21.8 %collective-permute-start.2 = (bf16[72,512]{1,0:T(8,128)(2,1)S(1)}, bf16[72,512]{1,0:T(8,128)(2,1)S(1)}, u32[]{:S(2)}, u32[]{:S(2)}) collective-permute-start(bf16[72,512]{1,0:T(8,128)(2,1)S(1)} %pad_maximum_fusion.refs_0_), channel_id=1, source_target_pairs={{0,8},{8,16},{16,24},{24,0},{1,9},{9,17},{17,25},{25,1},{2,10},{10... | collective-permute-start | bytes 221192 | tf_op jit(solution)/shard_map/ppermute | solution.py:417
  16.5 25.4 %collective-permute-start.3 = (bf16[72,512]{1,0:T(8,128)(2,1)S(1)}, bf16[72,512]{1,0:T(8,128)(2,1)S(1)}, u32[]{:S(2)}, u32[]{:S(2)}) collective-permute-start(bf16[72,512]{1,0:T(8,128)(2,1)S(1)} %pad_maximum_fusion.refs_0_), channel_id=1, source_target_pairs={{0,16},{8,24},{16,0},{24,8},{1,17},{9,25},{17,1},{25,9},{2,18},{10... | collective-permute-start | bytes 221192 | tf_op jit(solution)/shard_map/ppermute | solution.py:417
  18.9 23.0 %collective-permute-start.4 = (bf16[72,512]{1,0:T(8,128)(2,1)S(1)}, bf16[72,512]{1,0:T(8,128)(2,1)S(1)}, u32[]{:S(2)}, u32[]{:S(2)}) collective-permute-start(bf16[72,512]{1,0:T(8,128)(2,1)S(1)} %pad_maximum_fusion.refs_0_), channel_id=1, source_target_pairs={{0,24},{8,0},{16,8},{24,16},{1,25},{9,1},{17,9},{25,17},{2,26},{10... | collective-permute-start | bytes 221192 | tf_op jit(solution)/shard_map/ppermute | solution.py:417
  42.4 9.5 %collective-permute-start.5 = (bf16[4,72,512]{2,1,0:T(8,128)(2,1)S(1)}, bf16[4,72,512]{2,1,0:T(8,128)(2,1)S(1)}, u32[]{:S(2)}, u32[]{:S(2)}) collective-permute-start(bf16[4,72,512]{2,1,0:T(8,128)(2,1)S(1)} %sort.1.after.refs_0_), channel_id=1, source_target_pairs={{0,32},{32,64},{64,96},{96,0},{1,33},{33,65},{65,97},{97,1},{2,34}... | collective-permute-start | bytes 884744 | tf_op jit(solution)/shard_map/ppermute | solution.py:418
  42.7 14.2 %collective-permute-start.6 = (bf16[4,72,512]{2,1,0:T(8,128)(2,1)S(1)}, bf16[4,72,512]{2,1,0:T(8,128)(2,1)S(1)}, u32[]{:S(2)}, u32[]{:S(2)}) collective-permute-start(bf16[4,72,512]{2,1,0:T(8,128)(2,1)S(1)} %sort.1.after.refs_0_), channel_id=1, source_target_pairs={{0,64},{32,96},{64,0},{96,32},{1,65},{33,97},{65,1},{97,33},{2,66}... | collective-permute-start | bytes 884744 | tf_op jit(solution)/shard_map/ppermute | solution.py:418
  45.0 13.5 %collective-permute-start.7 = (bf16[4,72,512]{2,1,0:T(8,128)(2,1)S(1)}, bf16[4,72,512]{2,1,0:T(8,128)(2,1)}, u32[]{:S(2)}, u32[]{:S(2)}) collective-permute-start(bf16[4,72,512]{2,1,0:T(8,128)(2,1)S(1)} %sort.1.after.refs_0_), channel_id=1, source_target_pairs={{0,96},{32,0},{64,32},{96,64},{1,97},{33,1},{65,33},{97,65},{2,98}... | collective-permute-start | bytes 884744 | tf_op jit(solution)/shard_map/ppermute | solution.py:418
  47.8 14.8 %copy-start.1 = (bf16[16,512]{1,0:T(8,128)(2,1)S(1)}, bf16[16,512]{1,0:T(8,128)(2,1)}, u32[]{:S(2)}) copy-start(bf16[16,512]{1,0:T(8,128)(2,1)} %get-tuple-element.33.value) | copy-start | bytes 49156
  47.8 10.6 %all-to-all-start.1 = ((f32[4,16,128]{2,1,0:T(8,128)}), f32[4,16,128]{2,1,0:T(8,128)S(1)}, u32[]{:S(2)}, u32[]{:S(2)}) async-start(f32[4,16,128]{2,1,0:T(8,128)} %get-tuple-element.14), calls=%async_computation.1 | async-start | bytes 65536 | tf_op jit(solution)/shard_map/all_to_all | solution.py:447
  59.6 6.4 %collective-permute-start.8 = (bf16[4,4,72,512]{3,2,1,0:T(8,128)(2,1)S(1)}, bf16[4,4,72,512]{3,2,1,0:T(8,128)(2,1)S(1)}, u32[]{:S(2)}, u32[]{:S(2)}) collective-permute-start(bf16[4,4,72,512]{3,2,1,0:T(8,128)(2,1)S(1)} %join_out.1.refs_0_), channel_id=1, source_target_pairs={{0,4},{4,0},{1,5},{5,1},{2,6},{6,2},{3,7},{7,3},{8,12},{12,8},{9,1... | collective-permute-start | bytes 3538952 | tf_op jit(solution)/shard_map/ppermute | solution.py:449
  61.4 22.6 %collective-permute-start.10 = (bf16[16,192,128]{2,1,0:T(8,128)(2,1)S(1)}, bf16[16,192,128]{2,1,0:T(8,128)(2,1)S(1)}, u32[]{:S(2)}, u32[]{:S(2)}) collective-permute-start(bf16[16,192,128]{2,1,0:T(8,128)(2,1)S(1)} %get-tuple-element.22.own), channel_id=1, source_target_pairs={{0,1},{1,0},{2,3},{3,2},{4,5},{5,4},{6,7},{7,6},{8,9},{9,8},{10,11... | collective-permute-start | bytes 2359304 | tf_op jit(solution)/shard_map/ppermute | solution.py:484
  67.9 15.8 %all-to-all-start.2 = ((f32[4,4,2048]{2,1,0:T(4,128)}), f32[4,4,2048]{2,1,0:T(4,128)S(1)}, u32[]{:S(2)}, u32[]{:S(2)}) async-start(f32[4,4,2048]{2,1,0:T(4,128)} %get-tuple-element.18), calls=%async_computation.2 | async-start | bytes 262144 | tf_op jit(solution)/shard_map/all_to_all | solution.py:485
  71.7 18.9 %collective-permute-start.9 = (bf16[16,192,128]{2,1,0:T(8,128)(2,1)S(1)}, bf16[16,192,128]{2,1,0:T(8,128)(2,1)S(1)}, u32[]{:S(2)}, u32[]{:S(2)}) collective-permute-start(bf16[16,192,128]{2,1,0:T(8,128)(2,1)S(1)} %get-tuple-element.22.own), channel_id=1, source_target_pairs={{0,4},{4,0},{1,5},{5,1},{2,6},{6,2},{3,7},{7,3},{8,12},{12,8},{9,1... | collective-permute-start | bytes 2359304 | tf_op jit(solution)/shard_map/ppermute | solution.py:501
  83.9 1.3 copy-start
  84.0 19.1 %collective-permute-start.11 = (bf16[16,192,128]{2,1,0:T(8,128)(2,1)S(1)}, bf16[16,192,128]{2,1,0:T(8,128)(2,1)}, u32[]{:S(2)}, u32[]{:S(2)}) collective-permute-start(bf16[16,192,128]{2,1,0:T(8,128)(2,1)S(1)} %bitcast.11), channel_id=1, source_target_pairs={{0,4},{4,0},{1,5},{5,1},{2,6},{6,2},{3,7},{7,3},{8,12},{12,8},{9,1... | collective-permute-start | bytes 2359304 | tf_op jit(solution)/shard_map/ppermute | solution.py:501
  85.3 17.8 %all-to-all-start.3 = ((bf16[32,8,1024]{2,1,0:T(8,128)(2,1)}), bf16[32,8,1024]{2,1,0:T(8,128)(2,1)S(1)}, u32[]{:S(2)}, u32[]{:S(2)}) async-start(bf16[32,8,1024]{2,1,0:T(8,128)(2,1)} %copy-done), calls=%async_computation.3 | async-start | bytes 1048576 | tf_op jit(solution)/shard_map/all_to_all | solution.py:502

commit v5 on v4

--- a/solution.py
+++ b/solution.py
@@ -15,7 +15,7 @@
 F32 = jnp.float32
 BF16 = jnp.bfloat16
 NZ, NY, NC, NX = 4, 4, 2, 4
-X = ("xh", "xl")
+Z = ("zh", "zl")
 VMEM = pl.BlockSpec(memory_space=pltpu.VMEM)
 HBM = pl.BlockSpec(memory_space=pltpu.HBM)
 ANY = pl.BlockSpec(memory_space=pl.ANY)
@@ -51,12 +51,6 @@
         copy.wait()
 
 
-def sort_kernel(*refs):
-    pieces, (out, sem) = refs[:NY], refs[NY:]
-    y = lax.axis_index("y")
-    run([(pieces[s], out.at[lax.rem(y + NY - s, NY)]) for s in range(NY)], sem)
-
-
 def join_kernel(*refs):
     out, sem = refs[-2:]
     pieces = refs[:-3]
@@ -76,19 +70,8 @@
     )(*pieces, token)
 
 
-def piece_copies(pieces, buf, sem):
-    z = lax.axis_index("z")
-    core = lax.axis_index("c")
-    copies = []
-    for m in range(NC):
-        c = core if m == 0 else 1 - core
-        for i, shift in enumerate((0, NZ - 1, NZ - 2, NZ - 3)):
-            target = buf.at[lax.rem(z + shift, NZ), c]
-            copies.append(pltpu.make_async_copy(pieces[m].at[i], target, sem.at[m, i]))
-    return copies
-
-
-def project_kernel(h_own, h_mate, w_own, w_mate, gate_up, down, out, hbuf, wbuf, rows_buf, gbuf, dbuf, sem):
+def project_kernel(h_own, h_mate, w_own, w_mate, gate_up, down, out_w, gains, out, hbuf, wbuf, rows_buf,
+                   gbuf, dbuf, obuf, nbuf, sem):
     core = lax.axis_index("c")
     copies = [
         pltpu.make_async_copy(h_own, hbuf.at[core], sem.at[0]),
@@ -97,6 +80,8 @@
         pltpu.make_async_copy(w_mate, wbuf.at[1 - core], sem.at[3]),
         pltpu.make_async_copy(gate_up, gbuf, sem.at[4]),
         pltpu.make_async_copy(down, dbuf, sem.at[5]),
+        pltpu.make_async_copy(out_w, obuf, sem.at[6]),
+        pltpu.make_async_copy(gains, nbuf, sem.at[7]),
     ]
     for copy in copies:
         copy.start()
@@ -126,6 +111,20 @@
     at += rows
     copies[4].wait()
     copies[5].wait()
+    copies[6].wait()
+    copies[7].wait()
+    tile = jnp.concatenate([nbuf[...]] * (width // feats), axis=1)
+    place = lax.axis_index("y") * NC + core
+    tile = jnp.where(lax.broadcasted_iota(jnp.int32, tile.shape, 1) // feats == place, tile, 0.0)
+    high = tile.astype(BF16).astype(F32)
+    tile = jnp.concatenate([high, tile - high, jnp.zeros_like(tile), jnp.zeros_like(tile)], axis=0)
+    tile = tile.astype(BF16)
+    for t in range(width // lanes):
+        low = at + 3 * feats + t * (feats + 8)
+        cols = slice(t * lanes, (t + 1) * lanes)
+        for b in range(blocks):
+            out[b, low : low + feats] = obuf[:, cols]
+            out[b, low + feats : low + feats + 8] = tile[:, cols]
     for b in range(blocks):
         cols = pl.ds(b * lanes, lanes)
         out[b, at : at + feats] = gbuf[0, :, cols]
@@ -138,16 +137,21 @@
     return jnp.where(lax.rem(x, 2) == 0, pair[:4], pair[4:])
 
 
-def collect_kernel(got, after, tables, bounds, gains, qk, value, squares, rest, ffn, rest_buf, sem):
+def collect_kernel(got, tables, bounds, gains, qk, value, squares, rest, ffn, out_w, buf, rest_buf, sem):
     rows, width = value.shape
     blocks, lines, lanes = got.shape
     tiles = width // lanes
-    at = (3 * tiles + 1) * rows
-    copy = pltpu.make_async_copy(got.at[:, pl.ds(at, lines - at)], ffn, sem)
-    copy.start()
-    total = got[0, : 3 * width // lanes * rows].astype(F32)
+    at = buf.shape[1]
+    first = pltpu.make_async_copy(got.at[:, pl.ds(0, at)], buf, sem.at[0])
+    second = pltpu.make_async_copy(got.at[:, pl.ds(at, ffn.shape[1])], ffn, sem.at[1])
+    third = pltpu.make_async_copy(got.at[:, pl.ds(at + ffn.shape[1], out_w.shape[1])], out_w, sem.at[2])
+    first.start()
+    third.start()
+    second.start()
+    first.wait()
+    total = buf[0, : at - rows].astype(F32)
     for i in range(1, blocks):
-        total += got[i, : 3 * width // lanes * rows].astype(F32)
+        total += buf[i, : at - rows].astype(F32)
 
     def part(g):
         return jnp.concatenate(
@@ -157,7 +161,9 @@
     q, k = part(0), part(1)
     qk[0] = q
     qk[1] = k
-    value[...] = part(2).astype(BF16)
+    new = part(2).astype(BF16)
+    value[...] = new
+    qk[2] = new.astype(F32)
     lane = lax.broadcasted_iota(jnp.int32, squares.shape[1:], 1)
     both = jnp.where(
         lane < 64, jnp.sum(q * q, axis=1, keepdims=True), jnp.sum(k * k, axis=1, keepdims=True)
@@ -165,9 +171,10 @@
     for i in range(NX):
         squares[i] = both
     for i in range(blocks):
-        rest_buf[:, i * lanes : (i + 1) * lanes] = got[i, at - rows : at].astype(F32)
-    rest[...] = quarter(rest_buf, lax.axis_index("xh") * 2 + lax.axis_index("xl"))
-    copy.wait()
+        rest_buf[:, i * lanes : (i + 1) * lanes] = buf[i, at - rows : at].astype(F32)
+    rest[...] = quarter(rest_buf, lax.axis_index("x"))
+    second.wait()
+    third.wait()
 
 
 def turn(values, cosine, sine):
@@ -187,9 +194,9 @@
     return jnp.where(row_head == col_head, jnp.concatenate([values] * heads, axis=0), 0.0)
 
 
-def attend_kernel(squares_in, qk, value, gains, tables, bounds, keys, values, key_out,
+def attend_kernel(squares_in, qk, gains, tables, bounds, keys, values, key_out,
                   out, score, top, kbuf, vbuf, acc, total, ksem, vsem):
-    rows, width = value.shape
+    rows, width = out.shape
     heads = width // HEAD_DIM
     blocks = score.shape[0]
     model = width * NX
@@ -214,7 +221,7 @@
     q_all = spread(query.astype(F32), heads)
     q_block = q_all.astype(BF16)
     k_all = jnp.concatenate([new_key.astype(F32)] * heads, axis=0)
-    v_all = jnp.concatenate([value[...].astype(F32)] * heads, axis=0)
+    v_all = jnp.concatenate([qk[2]] * heads, axis=0)
     own = jnp.sum(q_all * k_all, axis=1, keepdims=True) * scale
     starts = bounds[:, 0:1]
     ends = bounds[:, 1:2]
@@ -249,31 +256,40 @@
     ).astype(BF16)
 
 
-def out_kernel(attended, *refs):
-    pieces = refs[:NC]
-    partial, gain_out, wbuf, sem = refs[NC:]
+def out_kernel(attended, own, mate, partial, gain_out, wbuf, sem):
     rows, width = attended.shape
-    copies = piece_copies(pieces, wbuf, sem)
+    core = lax.axis_index("c")
+    copies = [
+        pltpu.make_async_copy(own, wbuf.at[core], sem.at[0]),
+        pltpu.make_async_copy(mate, wbuf.at[1 - core], sem.at[1]),
+    ]
     for copy in copies:
         copy.start()
     for copy in copies:
         copy.wait()
     feats = width // (NY * NC)
+    lanes = wbuf.shape[3]
+    tiles = width // lanes
+    step = wbuf.shape[2] // tiles
     mine = rows // NX
     for b in range(NZ):
+        places = [(c, b * NY + y) for y in range(NY) for c in range(NC)]
         weights = jnp.concatenate(
-            [wbuf[b, c, y, :feats] for y in range(NY) for c in range(NC)], axis=0
+            [
+                jnp.concatenate([wbuf[c, p, t * step : t * step + feats] for c, p in places], axis=0)
+                for t in range(tiles)
+            ],
+            axis=1,
         )
         a = lax.dot_general(attended[...], weights, NT, preferred_element_type=F32)
         for x in range(NX):
             partial[x, :, b * width : (b + 1) * width] = a[x * mine : (x + 1) * mine]
-        both = wbuf[b, 0, 0, feats:].astype(F32)
-        for y in range(NY):
-            for c in range(NC):
-                if y or c:
-                    both += wbuf[b, c, y, feats:].astype(F32)
-        gain_out[b, 0:1] = both[0:1] + both[1:2]
-        gain_out[b, 1:2] = both[2:3] + both[3:4]
+        for t in range(tiles):
+            both = None
+            for c, p in places:
+                piece = wbuf[c, p, t * step + feats : (t + 1) * step].astype(F32)
+                both = piece if both is None else both + piece
+            gain_out[b, 0:2, t * lanes : (t + 1) * lanes] = both[0:2] + both[2:4]
 
 
 def fan_kernel(got, rest, gains, own_mid, out):
@@ -368,8 +384,6 @@
     model = width * NX
     wide = rows * heads
     blocks = cache_keys.shape[0] // BLOCK
-    y_here = lax.axis_index("y")
-    c_here = lax.axis_index("c")
 
     flipped = hidden_in.T
     mate_rows = lax.ppermute(flipped, "c", ring(1, NC))
@@ -377,11 +391,13 @@
     places = NZ * NY
     size = 3 * feats
     lanes = 128
-    lines = (3 * width // lanes + 1) * rows + size
+    tiles = width // lanes
+    head_lines = (3 * tiles + 1) * rows
+    out_lines = tiles * (feats + 8)
     message = call(
         project_kernel,
-        shape((places, lines, lanes), BF16),
-        [ANY] * 6,
+        shape((places, head_lines + size + out_lines, lanes), BF16),
+        [ANY] * 8,
         VMEM,
         [
             pltpu.VMEM((2, feats, flipped.shape[1]), BF16),
@@ -389,33 +405,15 @@
             pltpu.VMEM((flipped.shape[1], 2 * feats), F32),
             pltpu.VMEM(w_gate_up.shape, BF16),
             pltpu.VMEM(w_down.shape, BF16),
-            pltpu.SemaphoreType.DMA((6,)),
+            pltpu.VMEM(w_out.shape, BF16),
+            pltpu.VMEM(norm_gain.shape, F32),
+            pltpu.SemaphoreType.DMA((8,)),
         ],
         (1 << 27, 2 << 20),
         "project",
         8,
-    )(hbm(flipped), mate_rows, hbm(w_qkv), mate_w, hbm(w_gate_up), hbm(w_down))
-    got = lax.all_to_all(message, ("z", "y"), 0, 0, tiled=True)
-
-    high = norm_gain.astype(BF16)
-    low = (norm_gain - high.astype(F32)).astype(BF16)
-    gain_rows = jnp.stack([high[0], low[0], high[1], low[1]])
-    gain_tile = jnp.zeros((8, width), BF16)
-    gain_tile = lax.dynamic_update_slice(
-        gain_tile, gain_rows, (jnp.int32(0), (y_here * NC + c_here) * feats)
-    )
-    part = jnp.concatenate([w_out, gain_tile], axis=0)
-    part = call(
-        sort_kernel,
-        shape((NY,) + part.shape, BF16),
-        [ANY] * NY,
-        ANY,
-        [pltpu.SemaphoreType.DMA((NY,))],
-        (0, 1 << 20),
-        "sort",
-        1,
-    )(part, *[lax.ppermute(part, "y", ring(s, NY)) for s in range(1, NY)])
-    out_pieces = [part] + [lax.ppermute(part, "z", ring(s, NZ)) for s in range(1, NZ)]
+    )(hbm(flipped), mate_rows, hbm(w_qkv), mate_w, hbm(w_gate_up), hbm(w_down), hbm(w_out), hbm(norm_gain))
+    got = lax.all_to_all(hbm(message), Z + ("y",), 0, 0, tiled=True)
 
     half = HEAD_DIM // 2
     freqs = jnp.power(THETA, -(jnp.arange(half, dtype=F32) * 2.0 / HEAD_DIM))
@@ -428,29 +426,35 @@
     ends = jnp.cumsum(lengths)
     bounds = jnp.tile(jnp.stack([ends - lengths, ends], axis=1), (heads, 1))
     gain_table = jnp.concatenate([qk_gain, jnp.zeros((6, width), F32)], axis=0)
-    qk, value_new, squares, rest, ffn_own = call(
+    qk, value_new, squares, rest, ffn_own, out_own = call(
         collect_kernel,
         (
-            shape((2, rows, width), F32),
+            shape((3, rows, width), F32),
             shape((rows, width), BF16),
             shape((NX, rows, 128), F32),
             shape((rows // NX, model), F32),
             shape((places, size, lanes), BF16),
+            shape((places, out_lines, lanes), BF16),
         ),
-        [VMEM] + [ANY] * 4,
-        (VMEM,) * 4 + (ANY,),
-        [pltpu.VMEM((rows, model), F32), pltpu.SemaphoreType.DMA],
-        (1 << 20, 96 << 20),
+        [ANY] * 4,
+        (VMEM,) * 4 + (ANY,) * 2,
+        [
+            pltpu.VMEM((places, head_lines, lanes), BF16),
+            pltpu.VMEM((rows, model), F32),
+            pltpu.SemaphoreType.DMA((3,)),
+        ],
+        (1 << 20, 4 << 20),
         "collect",
         8,
-    )(got, part, tables, bounds, gain_table)
-    squares = lax.all_to_all(squares, X, 0, 0, tiled=True)
-    out_own = join(out_pieces, squares, "join_out")
+    )(got, tables, bounds, gain_table)
     out_mate = lax.ppermute(out_own, "c", ring(1, NC))
+    ffn_own = hbm(ffn_own)
+    ffn_near = hbm(lax.ppermute(ffn_own, "zl", ring(1, 2)))
+    squares = lax.all_to_all(squares, "x", 0, 0, tiled=True)
     key_new, attended = call(
         attend_kernel,
         (shape((rows, width), BF16), shape((rows, width), BF16)),
-        [VMEM] * 6 + [ANY] * 2,
+        [VMEM] * 5 + [ANY] * 2,
         (VMEM,) * 2,
         [
             pltpu.VMEM((blocks, wide, BLOCK), F32),
@@ -465,26 +469,24 @@
         (1 << 29, 8 << 20),
         "attend",
         16,
-    )(squares, qk, value_new, gain_table, tables, bounds, hbm(cache_keys), hbm(cache_values))
+    )(squares, qk, gain_table, tables, bounds, hbm(cache_keys), hbm(cache_values))
     partial, gains = call(
         out_kernel,
         (shape((NX, rows // NX, model), F32), shape((NZ, 8, width), F32)),
         [VMEM] + [ANY] * NC,
         (VMEM,) * 2,
         [
-            pltpu.VMEM((NZ, NC) + part.shape, BF16),
-            pltpu.SemaphoreType.DMA((NC, 4)),
+            pltpu.VMEM((NC,) + out_own.shape, BF16),
+            pltpu.SemaphoreType.DMA((2,)),
         ],
         (1 << 26, 2 << 20),
         "project_out",
         8,
     )(attended, out_own, out_mate)
 
-    near = [(i, i ^ 1) for i in range(2)]
-    ffn_near = lax.ppermute(ffn_own, "xl", near)
-    got = lax.all_to_all(partial, X, 0, 0, tiled=True)
+    got = lax.all_to_all(partial, "x", 0, 0, tiled=True)
     mine = rows // NX
-    group = ("z", "y", "xh")
+    group = ("zh", "y", "x")
     members = NZ * NY * NX // 2
     own_mid, message = call(
         fan_kernel,
@@ -495,10 +497,10 @@
         (1 << 16, 1 << 19),
         "fan",
     )(got, rest, gains)
-    ffn_near = join([ffn_near], own_mid, "hold")[0]
+    ffn_near = hbm(join([ffn_near], own_mid, "hold")[0])
     ffn_pieces = []
     for piece in (ffn_own, ffn_near):
-        ffn_pieces += [piece, lax.ppermute(piece, "c", ring(1, NC))]
+        ffn_pieces += [piece, hbm(lax.ppermute(piece, "c", ring(1, NC)))]
     got = lax.all_to_all(message, group, 0, 0, tiled=True)
     partial = call(
         ffn_kernel,
@@ -523,28 +525,28 @@
         (1 << 18, 1 << 19),
         "finish",
     )(got, own_mid, gains)
-    hidden = lax.all_to_all(message, ("z", "y", "c") + X, 0, 0, tiled=True)
+    hidden = lax.all_to_all(message, Z + ("y", "c", "x"), 0, 0, tiled=True)
     return hidden.reshape(-1, feats), key_new, value_new
 
 
 def solution(mesh):
-    fine = Mesh(mesh.devices.reshape(NZ, NY, NC, 2, 2), ("z", "y", "c") + X)
-    req = ("z", "y", "c")
+    fine = Mesh(mesh.devices.reshape(2, 2, NY, NC, NX), Z + ("y", "c", "x"))
+    req = Z + ("y", "c")
     return jax.shard_map(
         body,
         mesh=fine,
         in_specs=(
             P(None, req),
             P(req),
-            P(None, req, X),
-            P(None, X),
-            P(req, X),
-            P(req, X),
-            P(req, X),
+            P(None, req, "x"),
+            P(None, "x"),
+            P(req, "x"),
+            P(req, "x"),
+            P(req, "x"),
             P(None, req),
-            P(None, req, X),
-            P(req, X),
+            P(None, req, "x"),
+            P(req, "x"),
         ),
-        out_specs=(P(None, req), P(req, X), P(req, X)),
+        out_specs=(P(None, req), P(req, "x"), P(req, "x")),
         check_vma=False,
     )

time: 138 us -> 145 us (1.051)
  starting transfers between devices: 40.7 us -> 18.6 us
  waiting for transfers between devices: 49.6 us -> 60.2 us
  blocking collectives: 30.8 us -> 39.8 us
  Pallas kernels: 13.2 us -> 19.8 us
  local copies, waits for them, and re-layouts: 1.74 us -> 3.7 us
    all_to_all x3 -> x2, waiting for transfers between devices: 7.71 us -> 46.9 us  [the longest x1 42.2 us: body(): got = lax.all_to_all(hbm(message), Z + ('y',), 0, 0, tiled=True)]
    ppermute x9 -> x3, waiting for transfers between devices: 28 us -> 0.01 us  [the longest x2 0.01 us: body(): ffn_pieces += [piece, hbm(lax.ppermute(piece, 'c', ring(1, NC)))]]
    ppermute x9 -> x3, starting transfers between devices: 16.3 us -> 0.38 us  [the longest x1 0.21 us: body(): ffn_near = hbm(lax.ppermute(ffn_own, 'zl', ring(1, 2)))]
    all_to_all x1 -> x2, blocking collectives: 16 us -> 25.1 us  [the longest x1 17 us: body(): hidden = lax.all_to_all(message, Z + ('y', 'c', 'x'), 0, 0, tiled=True)]
    all_to_all x3 -> x2, starting transfers between devices: 15.8 us -> 11.2 us  [the longest x1 7.86 us: body(): got = lax.all_to_all(hbm(message), Z + ('y',), 0, 0, tiled=True)]
    pallas_call x1, Pallas kernels: 3.39 us -> 7.16 us  [body(): call(attend_kernel, (shape((rows, width), BF16), shape((rows, width), BF1...]
    unnamed x16 -> x18, local copies, waits for them, and re-layouts: 1.06 us -> 3.53 us
    pallas_call x3 -> x2, Pallas kernels: 4.1 us -> 5.75 us  [the longest x1 3.38 us: body(): call(project_kernel, shape((places, head_lines + size + out_lines, lanes)...]
  transfers between devices with their start and end apart: 16 -> 9, of which waited for: 7 -> 4; matrix products, arithmetic and copies ran while one was open for 1% -> 0% of each run, Pallas kernels for 5% -> 8%
where the time goes in v5:
time: 145 us; the launch traced here: 143 us
  waiting for transfers between devices  60.2 us (42%)
  blocking collectives  39.8 us (27%)
  Pallas kernels  19.8 us (14%)
  starting transfers between devices  18.6 us (13%)
  local copies, waits for them, and re-layouts  3.7 us (3%)
    all_to_all x1, waiting for transfers between devices, body(): got = lax.all_to_all(hbm(message), Z + ('y',), 0, 0, tiled=True)  42.2 us
    all_to_all x1, blocking collectives, body(): hidden = lax.all_to_all(message, Z + ('y', 'c', 'x'), 0, 0, tiled=True)  17 us
    all_to_all x1, blocking collectives, body(): got = lax.all_to_all(partial, group, 0, 0, tiled=True)  14.7 us
    all_to_all x1, waiting for transfers between devices, body(): got = lax.all_to_all(message, group, 0, 0, tiled=True)  12 us
    all_to_all x1, blocking collectives, body(): squares = lax.all_to_all(squares, 'x', 0, 0, tiled=True)  8.1 us
    all_to_all x1, starting transfers between devices, body(): got = lax.all_to_all(hbm(message), Z + ('y',), 0, 0, tiled=True)  7.86 us
    pallas_call x1, Pallas kernels, body(): call(attend_kernel, (shape((rows, width), BF16), shape((rows, width), BF1...  7.16 us
    all_to_all x1, waiting for transfers between devices, body(): got = lax.all_to_all(partial, 'x', 0, 0, tiled=True)  4.69 us
  transfers between devices with their start and end apart: 9, of which 4 were waited for; matrix products, arithmetic and copies ran while one was open for 0% of the time, Pallas kernels for 8%

profile of v5, /device:TPU:1, one launch (start us, length us, event | category | flops | bytes accessed | tf_op | source)
XLA Modules:
  0.0 143.4 jit_solution(12788488000658543274)
XLA Ops:
  0.6 1.5 %collective-permute-start.1 = (bf16[3,64,512]{2,1,0:T(8,128)(2,1)}, bf16[3,64,512]{2,1,0:T(8,128)(2,1)S(1)}, u32[]{:S(2)}, u32[]{:S(2)}) collective-permute-start(bf16[3,64,512]{2,1,0:T(8,128)(2,1)} %w_own.1), channel_id=1, source_target_pairs={{0,4},{4,0},{1,5},{5,1},{2,6},{6,2},{3,7},{7,3},{8,12},{12,8},{9,1... | collective-permute-start | bytes 589832 | tf_op jit(solution)/shard_map/ppermute | solution.py:390
  2.1 0.1 collective-permute-start
  2.2 1.4 collective-permute-done.h_mate
  3.6 0.0 collective-permute-done.1.w_mate
  3.6 3.4 %project.1 = bf16[16,688,128]{2,1,0:T(8,128)(2,1)} custom-call(bf16[64,512]{1,0:T(8,128)(2,1)} %bitcast.17, bf16[64,512]{1,0:T(8,128)(2,1)S(1)} %collective-permute-done.h_mate, bf16[3,64,512]{2,1,0:T(8,128)(2,1)} %w_own.1, bf16[3,64,512]{2,1,0:T(8,128)(2,1)S(1)} %collective-permute-done.1.w_mate, bf16[2,64,2048]{2,1,0:T(8,128)(2,1)} %gate_up.1, ...), custom_call_target="tpu_custom_call" | custom-call | flops 134217728 | bytes 2097152 | tf_op jit(solution)/shard_map/project/pallas_call | solution.py:397
  7.0 0.0 copy-start.6
  7.0 0.0 copy-start.5
  7.0 7.9 %all-to-all-start = ((bf16[16,688,128]{2,1,0:T(8,128)(2,1)}), bf16[16,688,128]{2,1,0:T(8,128)(2,1)S(1)}, u32[]{:S(2)}, u32[]{:S(2)}) async-start(bf16[16,688,128]{2,1,0:T(8,128)(2,1)} %project.1), calls=%async_computation | async-start | bytes 5636096 | tf_op jit(solution)/shard_map/all_to_all | solution.py:416
  14.9 0.0 copy-done.6
  14.9 0.1 copy.25
  15.0 0.1 reduce
  15.1 0.1 copy.26
  15.2 0.1 copy.31
  15.3 0.0 copy-done.5
  15.3 0.1 multiply_cosine_fusion
  15.5 0.1 maximum_bitcast_fusion
  15.5 42.2 %all-to-all-done.got = bf16[16,688,128]{2,1,0:T(8,128)(2,1)S(1)} async-done(((bf16[16,688,128]{2,1,0:T(8,128)(2,1)}), bf16[16,688,128]{2,1,0:T(8,128)(2,1)S(1)}, u32[]{:S(2)}, u32[]{:S(2)}) %all-to-all-start) | async-done | bytes 2818080 | tf_op jit(solution)/shard_map/all_to_all | solution.py:416
  57.7 0.0 copy-start.2
  57.7 1.6 %copy-done.2 = bf16[16,688,128]{2,1,0:T(8,128)(2,1)} copy-done((bf16[16,688,128]{2,1,0:T(8,128)(2,1)}, bf16[16,688,128]{2,1,0:T(8,128)(2,1)S(1)}, u32[]{:S(2)}) %copy-start.2) | copy-done | bytes 2818072
  59.3 2.4 %collect.1 = (f32[3,16,512]{2,1,0:T(8,128)S(1)}, bf16[16,512]{1,0:T(8,128)(2,1)}, f32[4,16,128]{2,1,0:T(8,128)S(1)}, f32[4,2048]{1,0:T(4,128)S(1)}, bf16[16,192,...) custom-call(bf16[16,688,128]{2,1,0:T(8,128)(2,1)} %copy-done.2, f32[2,16,128]{2,1,0:T(8,128)S(1)} %pad_maximum_fusion.tables, ...), custom_call_target="tpu_custom_call" | custom-call | flops 1048576 | bytes 4194304 | tf_op jit(solution)/shard_map/collect/pallas_call | solution.py:429
  61.7 0.0 copy-start.1
  61.7 1.5 %collective-permute-start.2 = (bf16[16,288,128]{2,1,0:T(8,128)(2,1)S(1)}, bf16[16,288,128]{2,1,0:T(8,128)(2,1)S(1)}, u32[]{:S(2)}, u32[]{:S(2)}) collective-permute-start(bf16[16,288,128]{2,1,0:T(8,128)(2,1)S(1)} %get-tuple-element.18.own), channel_id=1, source_target_pairs={{0,4},{4,0},{1,5},{5,1},{2,6},{6,2},{3,7},{7,3},{8,12},{12,8},{9,1... | collective-permute-start | bytes 3538952 | tf_op jit(solution)/shard_map/ppermute | solution.py:450
  63.1 0.2 collective-permute-start.4
  63.4 8.1 %all_to_all.30.squares_in = f32[4,16,128]{2,1,0:T(8,128)S(1)} all-to-all(f32[4,16,128]{2,1,0:T(8,128)S(1)} %get-tuple-element.15), channel_id=1, replica_groups=mesh['zh'=2,'zl'=2,'y'=4,'c'=2,'x'=4] {'x'}, dimensions={0} | all-to-all | bytes 65536 | tf_op jit(solution)/shard_map/all_to_all | solution.py:453
  71.5 7.2 %attend.1 = (bf16[16,512]{1,0:T(8,128)(2,1)}, bf16[16,512]{1,0:T(8,128)(2,1)S(1)}) custom-call(f32[4,16,128]{2,1,0:T(8,128)S(1)} %all_to_all.30.squares_in, f32[3,16,512]{2,1,0:T(8,128)S(1)} %get-tuple-element.16.qk, f32[8,512]{1,0:T(8,128)S(1)} %concatenate.11.gains, f32[2,16,128]{2,1,0:T(8,128)S(1)} %pad_maximum_fusion.tables, s32[64,2]{1,0:T(8,128)S(1)} %bitcast.14, ...), custom_call_target="tpu_custom_call" | custom-call | flops 536870912 | bytes 8388608 | tf_op jit(solution)/shard_map/attend/pallas_call | solution.py:454
  78.6 0.0 collective-permute-done.2.mate
  78.6 1.8 %project_out.1 = (f32[4,4,2048]{2,1,0:T(4,128)}, f32[4,8,512]{2,1,0:T(8,128)S(1)}) custom-call(bf16[16,512]{1,0:T(8,128)(2,1)S(1)} %get-tuple-element.17.attended, bf16[16,288,128]{2,1,0:T(8,128)(2,1)S(1)} %get-tuple-element.18.own, bf16[16,288,128]{2,1,0:T(8,128)(2,1)S(1)} %collective-permute-done.2.mate), custom_call_target="tpu_custom_call" | custom-call | flops 67108864 | bytes 2097152 | tf_op jit(solution)/shard_map/project_out/pallas_call | solution.py:473
  80.5 3.3 %all-to-all-start.2 = ((f32[4,4,2048]{2,1,0:T(4,128)}), f32[4,4,2048]{2,1,0:T(4,128)S(1)}, u32[]{:S(2)}, u32[]{:S(2)}) async-start(f32[4,4,2048]{2,1,0:T(4,128)} %get-tuple-element.19), calls=%async_computation.2 | async-start | bytes 262144 | tf_op jit(solution)/shard_map/all_to_all | solution.py:487
  83.8 0.0 copy-done.1
  83.8 0.1 collective-permute-start.3
  83.9 4.7 %all-to-all-done.2.got = f32[4,4,2048]{2,1,0:T(4,128)S(1)} async-done(((f32[4,4,2048]{2,1,0:T(4,128)}), f32[4,4,2048]{2,1,0:T(4,128)S(1)}, u32[]{:S(2)}, u32[]{:S(2)}) %all-to-all-start.2) | async-done | bytes 131104 | tf_op jit(solution)/shard_map/all_to_all | solution.py:487
  88.6 0.9 fan.1
  89.6 0.0 collective-permute-done.4.refs_0_
  89.6 0.0 copy-start.4
  89.6 0.9 copy-done.4
  90.5 1.1 hold.1
  91.6 0.0 copy-start
  91.6 0.1 collective-permute-start.5
  91.7 4.0 %all-to-all-start.3 = ((bf16[32,8,1024]{2,1,0:T(8,128)(2,1)}), bf16[32,8,1024]{2,1,0:T(8,128)(2,1)S(1)}, u32[]{:S(2)}, u32[]{:S(2)}) async-start(bf16[32,8,1024]{2,1,0:T(8,128)(2,1)} %get-tuple-element.22), calls=%async_computation.3 | async-start | bytes 1048576 | tf_op jit(solution)/shard_map/all_to_all | solution.py:504
  95.8 0.0 collective-permute-done.3.own_mate
  95.8 0.0 copy-start.3
  95.8 12.0 %all-to-all-done.3.got = bf16[32,8,1024]{2,1,0:T(8,128)(2,1)S(1)} async-done(((bf16[32,8,1024]{2,1,0:T(8,128)(2,1)}), bf16[32,8,1024]{2,1,0:T(8,128)(2,1)S(1)}, u32[]{:S(2)}, u32[]{:S(2)}) %all-to-all-start.3) | async-done | bytes 524320 | tf_op jit(solution)/shard_map/all_to_all | solution.py:504
  107.7 0.0 collective-permute-done.5.near_mate
  107.7 0.0 copy-done
  107.7 0.0 copy-done.3
  107.7 2.7 %feed_forward.1 = bf16[32,8,1024]{2,1,0:T(8,128)(2,1)S(1)} custom-call(bf16[32,8,1024]{2,1,0:T(8,128)(2,1)S(1)} %all-to-all-done.3.got, bf16[16,192,128]{2,1,0:T(8,128)(2,1)} %copy-done.1, bf16[16,192,128]{2,1,0:T(8,128)(2,1)} %copy-done.3, bf16[16,192,128]{2,1,0:T(8,128)(2,1)} %bitcast.12, bf16[16,192,128]{2,1,0:T(8,128)(2,1)} %collective-permute-done.5.near_mate), custom_call_target="tpu_custom_call" | custom-call | flops 268435456 | bytes 4194304 | tf_op jit(solution)/shard_map/feed_forward/pallas_call | solution.py:505
  110.5 14.7 %all_to_all.31.got = bf16[32,8,1024]{2,1,0:T(8,128)(2,1)S(1)} all-to-all(bf16[32,8,1024]{2,1,0:T(8,128)(2,1)S(1)} %feed_forward.1), channel_id=1, replica_groups=mesh['zh'=2,'zl'=2,'y'=4,'c'=2,'x'=4] {'zh','y','x'}, dimensions={0} | all-to-all | bytes 1048576 | tf_op jit(solution)/shard_map/all_to_all | solution.py:518
  125.2 0.3 finish.1
  125.4 0.1 reshape.31
  125.6 17.0 %all_to_all.32 = bf16[128,2,128]{2,1,0:T(2,128)(2,1)S(1)} all-to-all(bf16[128,2,128]{2,1,0:T(2,128)(2,1)S(1)} %reshape.31), channel_id=1, replica_groups=mesh['zh'=2,'zl'=2,'y'=4,'c'=2,'x'=4] {'zh','zl','y','c','x'}, dimensions={0} | all-to-all | bytes 131072 | tf_op jit(solution)/shard_map/all_to_all | solution.py:528
  142.6 0.1 reshape.32
  142.7 0.7 copy.29
  (7 shorter events, 0.1 us)
Async XLA Ops:
  0.6 3.0 %collective-permute-start.1 = (bf16[3,64,512]{2,1,0:T(8,128)(2,1)}, bf16[3,64,512]{2,1,0:T(8,128)(2,1)S(1)}, u32[]{:S(2)}, u32[]{:S(2)}) collective-permute-start(bf16[3,64,512]{2,1,0:T(8,128)(2,1)} %w_own.1), channel_id=1, source_target_pairs={{0,4},{4,0},{1,5},{5,1},{2,6},{6,2},{3,7},{7,3},{8,12},{12,8},{9,1... | collective-permute-start | bytes 589832 | tf_op jit(solution)/shard_map/ppermute | solution.py:390
  2.1 1.5 %collective-permute-start = (bf16[64,512]{1,0:T(8,128)(2,1)}, bf16[64,512]{1,0:T(8,128)(2,1)S(1)}, u32[]{:S(2)}, u32[]{:S(2)}) collective-permute-start(bf16[64,512]{1,0:T(8,128)(2,1)} %bitcast.16), channel_id=1, source_target_pairs={{0,4},{4,0},{1,5},{5,1},{2,6},{6,2},{3,7},{7,3},{8,12},{12,8},{9,1... | collective-permute-start | bytes 196616 | tf_op jit(solution)/shard_map/ppermute | solution.py:389
  7.0 7.9 %copy-start.6 = (s32[16]{0:T(128)S(1)}, s32[16]{0:T(128)}, u32[]{:S(2)}) copy-start(s32[16]{0:T(128)} %param.11) | copy-start | bytes 196
  7.0 8.3 %copy-start.5 = (f32[2,512]{1,0:T(2,128)S(1)}, f32[2,512]{1,0:T(2,128)}, u32[]{:S(2)}) copy-start(f32[2,512]{1,0:T(2,128)} %param.13) | copy-start | bytes 12292
  7.0 50.7 %all-to-all-start = ((bf16[16,688,128]{2,1,0:T(8,128)(2,1)}), bf16[16,688,128]{2,1,0:T(8,128)(2,1)S(1)}, u32[]{:S(2)}, u32[]{:S(2)}) async-start(bf16[16,688,128]{2,1,0:T(8,128)(2,1)} %project.1), calls=%async_computation | async-start | bytes 5636096 | tf_op jit(solution)/shard_map/all_to_all | solution.py:416
  57.7 1.6 %copy-start.2 = (bf16[16,688,128]{2,1,0:T(8,128)(2,1)}, bf16[16,688,128]{2,1,0:T(8,128)(2,1)S(1)}, u32[]{:S(2)}) copy-start(bf16[16,688,128]{2,1,0:T(8,128)(2,1)S(1)} %all-to-all-done.got) | copy-start | bytes 8454148
  61.7 22.1 %copy-start.1 = (bf16[16,192,128]{2,1,0:T(8,128)(2,1)}, bf16[16,192,128]{2,1,0:T(8,128)(2,1)S(1)}, u32[]{:S(2)}) copy-start(bf16[16,192,128]{2,1,0:T(8,128)(2,1)S(1)} %get-tuple-element.23.own) | copy-start | bytes 2359300
  61.7 16.9 %collective-permute-start.2 = (bf16[16,288,128]{2,1,0:T(8,128)(2,1)S(1)}, bf16[16,288,128]{2,1,0:T(8,128)(2,1)S(1)}, u32[]{:S(2)}, u32[]{:S(2)}) collective-permute-start(bf16[16,288,128]{2,1,0:T(8,128)(2,1)S(1)} %get-tuple-element.18.own), channel_id=1, source_target_pairs={{0,4},{4,0},{1,5},{5,1},{2,6},{6,2},{3,7},{7,3},{8,12},{12,8},{9,1... | collective-permute-start | bytes 3538952 | tf_op jit(solution)/shard_map/ppermute | solution.py:450
  63.1 26.4 %collective-permute-start.4 = (bf16[16,192,128]{2,1,0:T(8,128)(2,1)S(1)}, bf16[16,192,128]{2,1,0:T(8,128)(2,1)S(1)}, u32[]{:S(2)}, u32[]{:S(2)}) collective-permute-start(bf16[16,192,128]{2,1,0:T(8,128)(2,1)S(1)} %get-tuple-element.23.own), channel_id=1, source_target_pairs={{0,32},{32,0},{1,33},{33,1},{2,34},{34,2},{3,35},{35,3},{4,36},{36... | collective-permute-start | bytes 2359304 | tf_op jit(solution)/shard_map/ppermute | solution.py:452
  80.5 8.1 %all-to-all-start.2 = ((f32[4,4,2048]{2,1,0:T(4,128)}), f32[4,4,2048]{2,1,0:T(4,128)S(1)}, u32[]{:S(2)}, u32[]{:S(2)}) async-start(f32[4,4,2048]{2,1,0:T(4,128)} %get-tuple-element.19), calls=%async_computation.2 | async-start | bytes 262144 | tf_op jit(solution)/shard_map/all_to_all | solution.py:487
  83.8 11.9 %collective-permute-start.3 = (bf16[16,192,128]{2,1,0:T(8,128)(2,1)S(1)}, bf16[16,192,128]{2,1,0:T(8,128)(2,1)S(1)}, u32[]{:S(2)}, u32[]{:S(2)}) collective-permute-start(bf16[16,192,128]{2,1,0:T(8,128)(2,1)S(1)} %get-tuple-element.23.own), channel_id=1, source_target_pairs={{0,4},{4,0},{1,5},{5,1},{2,6},{6,2},{3,7},{7,3},{8,12},{12,8},{9,1... | collective-permute-start | bytes 2359304 | tf_op jit(solution)/shard_map/ppermute | solution.py:503
  89.6 0.9 copy-start.4
  91.6 16.1 %copy-start = (bf16[1,16,192,128]{3,2,1,0:T(8,128)(2,1)}, bf16[1,16,192,128]{3,2,1,0:T(8,128)(2,1)S(1)}, u32[]{:S(2)}) copy-start(bf16[1,16,192,128]{3,2,1,0:T(8,128)(2,1)S(1)} %hold.1) | copy-start | bytes 2359300
  91.6 16.1 %collective-permute-start.5 = (bf16[16,192,128]{2,1,0:T(8,128)(2,1)S(1)}, bf16[16,192,128]{2,1,0:T(8,128)(2,1)}, u32[]{:S(2)}, u32[]{:S(2)}) collective-permute-start(bf16[16,192,128]{2,1,0:T(8,128)(2,1)S(1)} %bitcast.11), channel_id=1, source_target_pairs={{0,4},{4,0},{1,5},{5,1},{2,6},{6,2},{3,7},{7,3},{8,12},{12,8},{9,1... | collective-permute-start | bytes 2359304 | tf_op jit(solution)/shard_map/ppermute | solution.py:503
  91.7 16.0 %all-to-all-start.3 = ((bf16[32,8,1024]{2,1,0:T(8,128)(2,1)}), bf16[32,8,1024]{2,1,0:T(8,128)(2,1)S(1)}, u32[]{:S(2)}, u32[]{:S(2)}) async-start(bf16[32,8,1024]{2,1,0:T(8,128)(2,1)} %get-tuple-element.22), calls=%async_computation.3 | async-start | bytes 1048576 | tf_op jit(solution)/shard_map/all_to_all | solution.py:504
  95.8 12.0 %copy-start.3 = (bf16[16,192,128]{2,1,0:T(8,128)(2,1)}, bf16[16,192,128]{2,1,0:T(8,128)(2,1)S(1)}, u32[]{:S(2)}) copy-start(bf16[16,192,128]{2,1,0:T(8,128)(2,1)S(1)} %collective-permute-done.3.own_mate) | copy-start | bytes 2359300

commit v6 on v5

--- a/solution.py
+++ b/solution.py
@@ -1,5 +1,3 @@
-import functools
-
 import jax
 import jax.numpy as jnp
 from jax import lax
@@ -43,35 +41,14 @@
     return jax.ShapeDtypeStruct(dims, dtype)
 
 
-def run(copies, sem):
-    copies = [pltpu.make_async_copy(a, b, sem.at[i]) for i, (a, b) in enumerate(copies)]
-    for copy in copies:
-        copy.start()
-    for copy in copies:
-        copy.wait()
-
-
-def join_kernel(*refs):
-    out, sem = refs[-2:]
-    pieces = refs[:-3]
-    run([(piece, out.at[i]) for i, piece in enumerate(pieces)], sem)
-
-
-def join(pieces, token, name):
-    return call(
-        join_kernel,
-        shape((len(pieces),) + pieces[0].shape, BF16),
-        [ANY] * (len(pieces) + 1),
-        ANY,
-        [pltpu.SemaphoreType.DMA((len(pieces),))],
-        (0, 2 << 20),
-        name,
-        1,
-    )(*pieces, token)
-
-
-def project_kernel(h_own, h_mate, w_own, w_mate, gate_up, down, out_w, gains, out, hbuf, wbuf, rows_buf,
-                   gbuf, dbuf, obuf, nbuf, sem):
+def hold_kernel(piece, token, out, sem):
+    copy = pltpu.make_async_copy(piece, out, sem)
+    copy.start()
+    copy.wait()
+
+
+def project_kernel(h_own, h_mate, w_own, w_mate, gate_up, down, out_w, gains, tables, bounds, scales,
+                   out, hbuf, wbuf, rows_buf, gbuf, dbuf, obuf, nbuf, sem):
     core = lax.axis_index("c")
     copies = [
         pltpu.make_async_copy(h_own, hbuf.at[core], sem.at[0]),
@@ -137,16 +114,14 @@
     return jnp.where(lax.rem(x, 2) == 0, pair[:4], pair[4:])
 
 
-def collect_kernel(got, tables, bounds, gains, qk, value, squares, rest, ffn, out_w, buf, rest_buf, sem):
+def collect_kernel(got, qk, value, squares, rest, ffn, buf, rest_buf, sem):
     rows, width = value.shape
     blocks, lines, lanes = got.shape
     tiles = width // lanes
     at = buf.shape[1]
     first = pltpu.make_async_copy(got.at[:, pl.ds(0, at)], buf, sem.at[0])
     second = pltpu.make_async_copy(got.at[:, pl.ds(at, ffn.shape[1])], ffn, sem.at[1])
-    third = pltpu.make_async_copy(got.at[:, pl.ds(at + ffn.shape[1], out_w.shape[1])], out_w, sem.at[2])
     first.start()
-    third.start()
     second.start()
     first.wait()
     total = buf[0, : at - rows].astype(F32)
@@ -174,7 +149,6 @@
         rest_buf[:, i * lanes : (i + 1) * lanes] = buf[i, at - rows : at].astype(F32)
     rest[...] = quarter(rest_buf, lax.axis_index("x"))
     second.wait()
-    third.wait()
 
 
 def turn(values, cosine, sine):
@@ -256,12 +230,13 @@
     ).astype(BF16)
 
 
-def out_kernel(attended, own, mate, partial, gain_out, wbuf, sem):
+def out_kernel(attended, own, mate, after, partial, gain_out, wbuf, sem):
     rows, width = attended.shape
     core = lax.axis_index("c")
+    last = pl.ds(own.shape[1] - wbuf.shape[2], wbuf.shape[2])
     copies = [
-        pltpu.make_async_copy(own, wbuf.at[core], sem.at[0]),
-        pltpu.make_async_copy(mate, wbuf.at[1 - core], sem.at[1]),
+        pltpu.make_async_copy(got.at[:, last], wbuf.at[place], sem.at[i])
+        for i, (got, place) in enumerate(((own, core), (mate, 1 - core)))
     ]
     for copy in copies:
         copy.start()
@@ -388,33 +363,6 @@
     flipped = hidden_in.T
     mate_rows = lax.ppermute(flipped, "c", ring(1, NC))
     mate_w = lax.ppermute(w_qkv, "c", ring(1, NC))
-    places = NZ * NY
-    size = 3 * feats
-    lanes = 128
-    tiles = width // lanes
-    head_lines = (3 * tiles + 1) * rows
-    out_lines = tiles * (feats + 8)
-    message = call(
-        project_kernel,
-        shape((places, head_lines + size + out_lines, lanes), BF16),
-        [ANY] * 8,
-        VMEM,
-        [
-            pltpu.VMEM((2, feats, flipped.shape[1]), BF16),
-            pltpu.VMEM((2,) + w_qkv.shape, BF16),
-            pltpu.VMEM((flipped.shape[1], 2 * feats), F32),
-            pltpu.VMEM(w_gate_up.shape, BF16),
-            pltpu.VMEM(w_down.shape, BF16),
-            pltpu.VMEM(w_out.shape, BF16),
-            pltpu.VMEM(norm_gain.shape, F32),
-            pltpu.SemaphoreType.DMA((8,)),
-        ],
-        (1 << 27, 2 << 20),
-        "project",
-        8,
-    )(hbm(flipped), mate_rows, hbm(w_qkv), mate_w, hbm(w_gate_up), hbm(w_down), hbm(w_out), hbm(norm_gain))
-    got = lax.all_to_all(hbm(message), Z + ("y",), 0, 0, tiled=True)
-
     half = HEAD_DIM // 2
     freqs = jnp.power(THETA, -(jnp.arange(half, dtype=F32) * 2.0 / HEAD_DIM))
     angles = lengths.astype(F32)[:, None] * freqs[None, :]
@@ -426,7 +374,36 @@
     ends = jnp.cumsum(lengths)
     bounds = jnp.tile(jnp.stack([ends - lengths, ends], axis=1), (heads, 1))
     gain_table = jnp.concatenate([qk_gain, jnp.zeros((6, width), F32)], axis=0)
-    qk, value_new, squares, rest, ffn_own, out_own = call(
+    places = NZ * NY
+    size = 3 * feats
+    lanes = 128
+    tiles = width // lanes
+    head_lines = (3 * tiles + 1) * rows
+    out_lines = tiles * (feats + 8)
+    message = call(
+        project_kernel,
+        shape((places, head_lines + size + out_lines, lanes), BF16),
+        [ANY] * 11,
+        VMEM,
+        [
+            pltpu.VMEM((2, feats, flipped.shape[1]), BF16),
+            pltpu.VMEM((2,) + w_qkv.shape, BF16),
+            pltpu.VMEM((flipped.shape[1], 2 * feats), F32),
+            pltpu.VMEM(w_gate_up.shape, BF16),
+            pltpu.VMEM(w_down.shape, BF16),
+            pltpu.VMEM(w_out.shape, BF16),
+            pltpu.VMEM(norm_gain.shape, F32),
+            pltpu.SemaphoreType.DMA((8,)),
+        ],
+        (1 << 27, 2 << 20),
+        "project",
+        8,
+    )(hbm(flipped), mate_rows, hbm(w_qkv), mate_w, hbm(w_gate_up), hbm(w_down), hbm(w_out), hbm(norm_gain),
+      tables, bounds, gain_table)
+    got = lax.all_to_all(message, Z + ("y",), 0, 0, tiled=True)
+
+    mate = lax.ppermute(got, "c", ring(1, NC))
+    qk, value_new, squares, rest, ffn_own = call(
         collect_kernel,
         (
             shape((3, rows, width), F32),
@@ -434,22 +411,20 @@
             shape((NX, rows, 128), F32),
             shape((rows // NX, model), F32),
             shape((places, size, lanes), BF16),
-            shape((places, out_lines, lanes), BF16),
         ),
-        [ANY] * 4,
-        (VMEM,) * 4 + (ANY,) * 2,
+        [ANY],
+        (VMEM,) * 4 + (ANY,),
         [
             pltpu.VMEM((places, head_lines, lanes), BF16),
             pltpu.VMEM((rows, model), F32),
-            pltpu.SemaphoreType.DMA((3,)),
+            pltpu.SemaphoreType.DMA((2,)),
         ],
         (1 << 20, 4 << 20),
         "collect",
         8,
-    )(got, tables, bounds, gain_table)
-    out_mate = lax.ppermute(out_own, "c", ring(1, NC))
-    ffn_own = hbm(ffn_own)
-    ffn_near = hbm(lax.ppermute(ffn_own, "zl", ring(1, 2)))
+    )(got)
+    ffn_mate = lax.ppermute(ffn_own, "c", ring(1, NC))
+    near = lax.ppermute(ffn_own, "zl", ring(1, 2))
     squares = lax.all_to_all(squares, "x", 0, 0, tiled=True)
     key_new, attended = call(
         attend_kernel,
@@ -473,18 +448,18 @@
     partial, gains = call(
         out_kernel,
         (shape((NX, rows // NX, model), F32), shape((NZ, 8, width), F32)),
-        [VMEM] + [ANY] * NC,
+        [VMEM] + [ANY] * 3,
         (VMEM,) * 2,
         [
-            pltpu.VMEM((NC,) + out_own.shape, BF16),
+            pltpu.VMEM((NC, places, out_lines, lanes), BF16),
             pltpu.SemaphoreType.DMA((2,)),
         ],
         (1 << 26, 2 << 20),
         "project_out",
         8,
-    )(attended, out_own, out_mate)
-
-    got = lax.all_to_all(partial, "x", 0, 0, tiled=True)
+    )(attended, got, mate, ffn_mate)
+
+    summed = lax.all_to_all(partial, "x", 0, 0, tiled=True)
     mine = rows // NX
     group = ("zh", "y", "x")
     members = NZ * NY * NX // 2
@@ -496,11 +471,18 @@
         (),
         (1 << 16, 1 << 19),
         "fan",
-    )(got, rest, gains)
-    ffn_near = hbm(join([ffn_near], own_mid, "hold")[0])
-    ffn_pieces = []
-    for piece in (ffn_own, ffn_near):
-        ffn_pieces += [piece, hbm(lax.ppermute(piece, "c", ring(1, NC)))]
+    )(summed, rest, gains)
+    near = call(
+        hold_kernel,
+        shape(near.shape, BF16),
+        [ANY] * 2,
+        ANY,
+        [pltpu.SemaphoreType.DMA],
+        (0, 1 << 20),
+        "hold",
+        1,
+    )(near, own_mid)
+    near_mate = lax.ppermute(near, "c", ring(1, NC))
     got = lax.all_to_all(message, group, 0, 0, tiled=True)
     partial = call(
         ffn_kernel,
@@ -514,7 +496,7 @@
         (1 << 28, 4 << 20),
         "feed_forward",
         16,
-    )(got, *ffn_pieces)
+    )(got, ffn_own, ffn_mate, near, near_mate)
     got = lax.all_to_all(partial, group, 0, 0, tiled=True)
     message = call(
         finish_kernel,

time: 145 us -> 130 us (0.90)
  blocking collectives: 39.8 us -> 109 us
  waiting for transfers between devices: 60.2 us -> 0.02 us
  starting transfers between devices: 18.6 us -> 3.38 us
  Pallas kernels: 19.8 us -> 12.6 us
    all_to_all x0 -> x3, blocking collectives: none -> 70.3 us  [the longest x1 43.2 us: body(): got = lax.all_to_all(message, Z + ('y',), 0, 0, tiled=True)]
    all_to_all x3 -> x0, waiting for transfers between devices: 58.8 us -> none  [the longest x1 42.2 us: body(): got = lax.all_to_all(hbm(message), Z + ('y',), 0, 0, tiled=True)]
    all_to_all x3 -> x0, starting transfers between devices: 15.2 us -> none  [the longest x1 7.86 us: body(): got = lax.all_to_all(hbm(message), Z + ('y',), 0, 0, tiled=True)]
    unnamed x18 -> x4, local copies, waits for them, and re-layouts: 3.53 us -> 1.03 us
    pallas_call x1, Pallas kernels: 3.38 us -> 1.84 us  [body(): call(project_kernel, shape((places, head_lines + size + out_lines, lanes)...]
    pallas_call x1, Pallas kernels: 2.37 us -> 0.88 us  [body(): call(collect_kernel, (shape((3, rows, width), F32), shape((rows, width),...]
  transfers between devices with their start and end apart: 9 -> 6, of which waited for: 4 -> 0; matrix products, arithmetic and copies ran while one was open for 0% -> 2% of each run, Pallas kernels for 8% -> 7%
where the time goes in v6:
time: 130 us
  blocking collectives  109 us (84%)
  Pallas kernels  12.6 us (10%)
  starting transfers between devices  3.38 us (3%)
  local copies, waits for them, and re-layouts  2.54 us (2%)
    all_to_all x1, blocking collectives, body(): got = lax.all_to_all(message, Z + ('y',), 0, 0, tiled=True)  43.2 us
    all_to_all x1, blocking collectives, body(): got = lax.all_to_all(message, group, 0, 0, tiled=True)  19.9 us
    all_to_all x1, blocking collectives, body(): hidden = lax.all_to_all(message, Z + ('y', 'c', 'x'), 0, 0, tiled=True)  16.4 us
    all_to_all x1, blocking collectives, body(): got = lax.all_to_all(partial, group, 0, 0, tiled=True)  14.6 us
    all_to_all x1, blocking collectives, body(): squares = lax.all_to_all(squares, 'x', 0, 0, tiled=True)  8.11 us
    all_to_all x1, blocking collectives, body(): summed = lax.all_to_all(partial, 'x', 0, 0, tiled=True)  7.21 us
    pallas_call x1, Pallas kernels, body(): call(attend_kernel, (shape((rows, width), BF16), shape((rows, width), BF1...  7.17 us
  transfers between devices with their start and end apart: 6, of which 0 were waited for; matrix products, arithmetic and copies ran while one was open for 2% of the time, Pallas kernels for 7%

profile of v6, /device:TPU:1, one launch (start us, length us, event | category | flops | bytes accessed | tf_op | source)
XLA Modules:
  0.0 129.9 jit_solution(12599063804919965584)
XLA Ops:
  0.6 1.5 %collective-permute-start = (bf16[64,512]{1,0:T(8,128)(2,1)}, bf16[64,512]{1,0:T(8,128)(2,1)S(1)}, u32[]{:S(2)}, u32[]{:S(2)}) collective-permute-start(bf16[64,512]{1,0:T(8,128)(2,1)} %bitcast.13), channel_id=1, source_target_pairs={{0,4},{4,0},{1,5},{5,1},{2,6},{6,2},{3,7},{7,3},{8,12},{12,8},{9,1... | collective-permute-start | bytes 196616 | tf_op jit(solution)/shard_map/ppermute | solution.py:364
  2.1 0.1 collective-permute-start.1
  2.2 0.7 copy.25
  3.0 0.1 reduce
  3.1 0.1 copy.26
  3.2 0.7 subtract_bitcast_fusion
  4.0 0.1 copy.31
  4.0 0.1 multiply_cosine_fusion
  4.2 0.7 concatenate.11.scales.gains
  4.9 0.1 maximum_bitcast_fusion
  4.9 0.0 collective-permute-done.h_mate
  4.9 0.0 collective-permute-done.1.w_mate
  5.0 1.8 %project.1 = bf16[16,688,128]{2,1,0:T(8,128)(2,1)S(1)} custom-call(bf16[64,512]{1,0:T(8,128)(2,1)} %bitcast.14, bf16[64,512]{1,0:T(8,128)(2,1)S(1)} %collective-permute-done.h_mate, bf16[3,64,512]{2,1,0:T(8,128)(2,1)} %w_own.1, bf16[3,64,512]{2,1,0:T(8,128)(2,1)S(1)} %collective-permute-done.1.w_mate, bf16[2,64,2048]{2,1,0:T(8,128)(2,1)} %gate_up.1, ...), custom_call_target="tpu_custom_call" | custom-call | flops 134217728 | bytes 2097152 | tf_op jit(solution)/shard_map/project/pallas_call | solution.py:383
  6.8 43.2 %all_to_all.30.got.own = bf16[16,688,128]{2,1,0:T(8,128)(2,1)S(1)} all-to-all(bf16[16,688,128]{2,1,0:T(8,128)(2,1)S(1)} %project.1), channel_id=1, replica_groups=mesh['zh'=2,'zl'=2,'y'=4,'c'=2,'x'=4] {'zh','zl','y'}, dimensions={0} | all-to-all | bytes 5636096 | tf_op jit(solution)/shard_map/all_to_all | solution.py:403
  50.0 1.5 %collective-permute-start.2 = (bf16[16,688,128]{2,1,0:T(8,128)(2,1)S(1)}, bf16[16,688,128]{2,1,0:T(8,128)(2,1)S(1)}, u32[]{:S(2)}, u32[]{:S(2)}) collective-permute-start(bf16[16,688,128]{2,1,0:T(8,128)(2,1)S(1)} %all_to_all.30.got.own), channel_id=1, source_target_pairs={{0,4},{4,0},{1,5},{5,1},{2,6},{6,2},{3,7},{7,3},{8,12},{12,8},{9,1... | collective-permute-start | bytes 8454152 | tf_op jit(solution)/shard_map/ppermute | solution.py:405
  51.5 0.9 collect.1
  52.4 0.1 collective-permute-start.3
  52.5 0.1 collective-permute-start.4
  52.6 8.1 %all_to_all.31.squares_in = f32[4,16,128]{2,1,0:T(8,128)S(1)} all-to-all(f32[4,16,128]{2,1,0:T(8,128)S(1)} %get-tuple-element.14), channel_id=1, replica_groups=mesh['zh'=2,'zl'=2,'y'=4,'c'=2,'x'=4] {'x'}, dimensions={0} | all-to-all | bytes 65536 | tf_op jit(solution)/shard_map/all_to_all | solution.py:428
  60.7 7.2 %attend.1 = (bf16[16,512]{1,0:T(8,128)(2,1)}, bf16[16,512]{1,0:T(8,128)(2,1)S(1)}) custom-call(f32[4,16,128]{2,1,0:T(8,128)S(1)} %all_to_all.31.squares_in, f32[3,16,512]{2,1,0:T(8,128)S(1)} %get-tuple-element.15.qk, f32[8,512]{1,0:T(8,128)S(1)} %concatenate.11.scales.gains, f32[2,16,128]{2,1,0:T(8,128)S(1)} %pad_maximum_fusion.tables, ...), custom_call_target="tpu_custom_call" | custom-call | flops 536870912 | bytes 8388608 | tf_op jit(solution)/shard_map/attend/pallas_call | solution.py:429
  67.9 0.0 collective-permute-done.3.after.own_mate
  67.9 0.0 collective-permute-done.2.mate
  67.9 0.9 project_out.1
  68.8 7.2 %all_to_all.32.got = f32[4,4,2048]{2,1,0:T(4,128)S(1)} all-to-all(f32[4,4,2048]{2,1,0:T(4,128)S(1)} %get-tuple-element.18), channel_id=1, replica_groups=mesh['zh'=2,'zl'=2,'y'=4,'c'=2,'x'=4] {'x'}, dimensions={0} | all-to-all | bytes 262144 | tf_op jit(solution)/shard_map/all_to_all | solution.py:462
  76.0 0.1 fan.1
  76.2 0.0 collective-permute-done.4.piece
  76.2 0.1 hold.1.near
  76.3 0.1 collective-permute-start.5
  76.3 19.9 %all_to_all.33.got = bf16[32,8,1024]{2,1,0:T(8,128)(2,1)S(1)} all-to-all(bf16[32,8,1024]{2,1,0:T(8,128)(2,1)S(1)} %get-tuple-element.21), channel_id=1, replica_groups=mesh['zh'=2,'zl'=2,'y'=4,'c'=2,'x'=4] {'zh','y','x'}, dimensions={0} | all-to-all | bytes 1048576 | tf_op jit(solution)/shard_map/all_to_all | solution.py:486
  96.2 0.0 collective-permute-done.5.near_mate
  96.3 1.4 %feed_forward.1 = bf16[32,8,1024]{2,1,0:T(8,128)(2,1)S(1)} custom-call(bf16[32,8,1024]{2,1,0:T(8,128)(2,1)S(1)} %all_to_all.33.got, bf16[16,192,128]{2,1,0:T(8,128)(2,1)S(1)} %get-tuple-element.17.own, bf16[16,192,128]{2,1,0:T(8,128)(2,1)S(1)} %collective-permute-done.3.after.own_mate, bf16[16,192,128]{2,1,0:T(8,128)(2,1)S(1)} %hold.1.near, ...), custom_call_target="tpu_custom_call" | custom-call | flops 268435456 | bytes 4194304 | tf_op jit(solution)/shard_map/feed_forward/pallas_call | solution.py:487
  97.6 14.6 %all_to_all.34.got = bf16[32,8,1024]{2,1,0:T(8,128)(2,1)S(1)} all-to-all(bf16[32,8,1024]{2,1,0:T(8,128)(2,1)S(1)} %feed_forward.1), channel_id=1, replica_groups=mesh['zh'=2,'zl'=2,'y'=4,'c'=2,'x'=4] {'zh','y','x'}, dimensions={0} | all-to-all | bytes 1048576 | tf_op jit(solution)/shard_map/all_to_all | solution.py:500
  112.3 0.3 finish.1
  112.5 0.1 reshape.31
  112.7 16.4 %all_to_all.35 = bf16[128,2,128]{2,1,0:T(2,128)(2,1)S(1)} all-to-all(bf16[128,2,128]{2,1,0:T(2,128)(2,1)S(1)} %reshape.31), channel_id=1, replica_groups=mesh['zh'=2,'zl'=2,'y'=4,'c'=2,'x'=4] {'zh','zl','y','c','x'}, dimensions={0} | all-to-all | bytes 131072 | tf_op jit(solution)/shard_map/all_to_all | solution.py:510
  129.0 0.1 reshape.32
  129.1 0.7 copy.29
  (5 shorter events, 0.1 us)
Async XLA Ops:
  0.6 4.3 %collective-permute-start = (bf16[64,512]{1,0:T(8,128)(2,1)}, bf16[64,512]{1,0:T(8,128)(2,1)S(1)}, u32[]{:S(2)}, u32[]{:S(2)}) collective-permute-start(bf16[64,512]{1,0:T(8,128)(2,1)} %bitcast.13), channel_id=1, source_target_pairs={{0,4},{4,0},{1,5},{5,1},{2,6},{6,2},{3,7},{7,3},{8,12},{12,8},{9,1... | collective-permute-start | bytes 196616 | tf_op jit(solution)/shard_map/ppermute | solution.py:364
  2.1 2.8 %collective-permute-start.1 = (bf16[3,64,512]{2,1,0:T(8,128)(2,1)}, bf16[3,64,512]{2,1,0:T(8,128)(2,1)S(1)}, u32[]{:S(2)}, u32[]{:S(2)}) collective-permute-start(bf16[3,64,512]{2,1,0:T(8,128)(2,1)} %w_own.1), channel_id=1, source_target_pairs={{0,4},{4,0},{1,5},{5,1},{2,6},{6,2},{3,7},{7,3},{8,12},{12,8},{9,1... | collective-permute-start | bytes 589832 | tf_op jit(solution)/shard_map/ppermute | solution.py:365
  50.0 17.9 %collective-permute-start.2 = (bf16[16,688,128]{2,1,0:T(8,128)(2,1)S(1)}, bf16[16,688,128]{2,1,0:T(8,128)(2,1)S(1)}, u32[]{:S(2)}, u32[]{:S(2)}) collective-permute-start(bf16[16,688,128]{2,1,0:T(8,128)(2,1)S(1)} %all_to_all.30.got.own), channel_id=1, source_target_pairs={{0,4},{4,0},{1,5},{5,1},{2,6},{6,2},{3,7},{7,3},{8,12},{12,8},{9,1... | collective-permute-start | bytes 8454152 | tf_op jit(solution)/shard_map/ppermute | solution.py:405
  52.4 15.5 %collective-permute-start.3 = (bf16[16,192,128]{2,1,0:T(8,128)(2,1)S(1)}, bf16[16,192,128]{2,1,0:T(8,128)(2,1)S(1)}, u32[]{:S(2)}, u32[]{:S(2)}) collective-permute-start(bf16[16,192,128]{2,1,0:T(8,128)(2,1)S(1)} %get-tuple-element.17.own), channel_id=1, source_target_pairs={{0,4},{4,0},{1,5},{5,1},{2,6},{6,2},{3,7},{7,3},{8,12},{12,8},{9,1... | collective-permute-start | bytes 2359304 | tf_op jit(solution)/shard_map/ppermute | solution.py:426
  52.5 23.7 %collective-permute-start.4 = (bf16[16,192,128]{2,1,0:T(8,128)(2,1)S(1)}, bf16[16,192,128]{2,1,0:T(8,128)(2,1)S(1)}, u32[]{:S(2)}, u32[]{:S(2)}) collective-permute-start(bf16[16,192,128]{2,1,0:T(8,128)(2,1)S(1)} %get-tuple-element.17.own), channel_id=1, source_target_pairs={{0,32},{32,0},{1,33},{33,1},{2,34},{34,2},{3,35},{35,3},{4,36},{36... | collective-permute-start | bytes 2359304 | tf_op jit(solution)/shard_map/ppermute | solution.py:427
  76.3 20.0 %collective-permute-start.5 = (bf16[16,192,128]{2,1,0:T(8,128)(2,1)S(1)}, bf16[16,192,128]{2,1,0:T(8,128)(2,1)S(1)}, u32[]{:S(2)}, u32[]{:S(2)}) collective-permute-start(bf16[16,192,128]{2,1,0:T(8,128)(2,1)S(1)} %hold.1.near), channel_id=1, source_target_pairs={{0,4},{4,0},{1,5},{5,1},{2,6},{6,2},{3,7},{7,3},{8,12},{12,8},{9,1... | collective-permute-start | bytes 2359304 | tf_op jit(solution)/shard_map/ppermute | solution.py:485

commit v7 on v6

--- a/solution.py
+++ b/solution.py
@@ -47,27 +47,28 @@
     copy.wait()
 
 
-def project_kernel(h_own, h_mate, w_own, w_mate, gate_up, down, out_w, gains, tables, bounds, scales,
-                   out, hbuf, wbuf, rows_buf, gbuf, dbuf, obuf, nbuf, sem):
+def project_kernel(h_own, h_mate, w_own, w_mate, gate_up, down, out_w, gains, trig, places, out, hbuf,
+                   wbuf, rows_buf, gbuf, dbuf, obuf, nbuf, sem):
     core = lax.axis_index("c")
-    copies = [
-        pltpu.make_async_copy(h_own, hbuf.at[core], sem.at[0]),
-        pltpu.make_async_copy(h_mate, hbuf.at[1 - core], sem.at[1]),
-        pltpu.make_async_copy(w_own, wbuf.at[core], sem.at[2]),
-        pltpu.make_async_copy(w_mate, wbuf.at[1 - core], sem.at[3]),
-        pltpu.make_async_copy(gate_up, gbuf, sem.at[4]),
-        pltpu.make_async_copy(down, dbuf, sem.at[5]),
-        pltpu.make_async_copy(out_w, obuf, sem.at[6]),
-        pltpu.make_async_copy(gains, nbuf, sem.at[7]),
-    ]
+    pairs = (
+        (h_own, hbuf.at[core]),
+        (h_mate, hbuf.at[1 - core]),
+        (w_own, wbuf.at[core]),
+        (w_mate, wbuf.at[1 - core]),
+        (gate_up, gbuf),
+        (down, dbuf),
+        (out_w, obuf),
+        (gains, nbuf),
+    )
+    copies = [pltpu.make_async_copy(a, b, sem.at[i]) for i, (a, b) in enumerate(pairs)]
     for copy in copies:
         copy.start()
     copies[0].wait()
     copies[1].wait()
     rows_buf[...] = jnp.concatenate([hbuf[0].astype(F32).T, hbuf[1].astype(F32).T], axis=1)
-    blocks, lines, lanes = out.shape
+    blocks, rows, _ = out.shape
     feats, width = w_own.shape[1:]
-    rows = rows_buf.shape[0] // (blocks * NC)
+    lanes = 2 * feats
     chosen = jnp.concatenate(
         [
             rows_buf[pl.ds(pl.multiple_of((2 * b + core) * rows, rows), rows), :]
@@ -77,36 +78,30 @@
     ).astype(BF16)
     copies[2].wait()
     copies[3].wait()
-    at = 0
     for g in range(3):
         weights = jnp.concatenate([wbuf[0, g], wbuf[1, g]], axis=0)
         part = jnp.dot(chosen, weights, preferred_element_type=F32).astype(BF16)
-        for t in range(width // lanes):
-            out[:, at : at + rows] = part[:, t * lanes : (t + 1) * lanes].reshape(blocks, rows, lanes)
-            at += rows
-    out[:, at : at + rows] = chosen.reshape(blocks, rows, lanes)
-    at += rows
-    copies[4].wait()
-    copies[5].wait()
-    copies[6].wait()
-    copies[7].wait()
-    tile = jnp.concatenate([nbuf[...]] * (width // feats), axis=1)
-    place = lax.axis_index("y") * NC + core
-    tile = jnp.where(lax.broadcasted_iota(jnp.int32, tile.shape, 1) // feats == place, tile, 0.0)
-    high = tile.astype(BF16).astype(F32)
-    tile = jnp.concatenate([high, tile - high, jnp.zeros_like(tile), jnp.zeros_like(tile)], axis=0)
-    tile = tile.astype(BF16)
-    for t in range(width // lanes):
-        low = at + 3 * feats + t * (feats + 8)
-        cols = slice(t * lanes, (t + 1) * lanes)
-        for b in range(blocks):
-            out[b, low : low + feats] = obuf[:, cols]
-            out[b, low + feats : low + feats + 8] = tile[:, cols]
+        out[:, :, g * width : (g + 1) * width] = part.reshape(blocks, rows, width)
+    at = 3 * width
+    out[:, :, at : at + lanes] = chosen.reshape(blocks, rows, lanes)
+    at += lanes
+    for copy in copies[4:]:
+        copy.wait()
+    steps = feats // rows
+    for part in range(3):
+        for i in range(steps):
+            low = slice(i * rows, (i + 1) * rows)
+            for b in range(blocks):
+                cols = slice(b * lanes, (b + 1) * lanes)
+                out[b, :, at : at + lanes] = dbuf[low, cols] if part == 2 else gbuf[part, low, cols]
+            at += lanes
+    both = jnp.concatenate([nbuf[0:1, :], nbuf[1:2, :]], axis=1)
+    high = both.astype(BF16).astype(F32)
+    tile = jnp.concatenate([high, both - high, jnp.zeros((rows - 2, lanes), F32)], axis=0).astype(BF16)
     for b in range(blocks):
-        cols = pl.ds(b * lanes, lanes)
-        out[b, at : at + feats] = gbuf[0, :, cols]
-        out[b, at + feats : at + 2 * feats] = gbuf[1, :, cols]
-        out[b, at + 2 * feats : at + 3 * feats] = dbuf[:, cols]
+        for i in range(steps):
+            out[b, :, at + i * width : at + (i + 1) * width] = obuf[i * rows : (i + 1) * rows]
+        out[b, :, at + steps * width :] = tile
 
 
 def quarter(ref, x):
@@ -116,27 +111,19 @@
 
 def collect_kernel(got, qk, value, squares, rest, ffn, buf, rest_buf, sem):
     rows, width = value.shape
-    blocks, lines, lanes = got.shape
-    tiles = width // lanes
-    at = buf.shape[1]
-    first = pltpu.make_async_copy(got.at[:, pl.ds(0, at)], buf, sem.at[0])
-    second = pltpu.make_async_copy(got.at[:, pl.ds(at, ffn.shape[1])], ffn, sem.at[1])
+    at = buf.shape[2]
+    first = pltpu.make_async_copy(got.at[:, :, pl.ds(0, at)], buf, sem.at[0])
+    second = pltpu.make_async_copy(got.at[:, :, pl.ds(at, ffn.shape[2])], ffn, sem.at[1])
     first.start()
     second.start()
     first.wait()
-    total = buf[0, : at - rows].astype(F32)
-    for i in range(1, blocks):
-        total += buf[i, : at - rows].astype(F32)
-
-    def part(g):
-        return jnp.concatenate(
-            [total[(g * tiles + t) * rows : (g * tiles + t + 1) * rows] for t in range(tiles)], axis=1
-        )
-
-    q, k = part(0), part(1)
+    total = buf[0, :, : 3 * width].astype(F32)
+    for i in range(1, buf.shape[0]):
+        total += buf[i, :, : 3 * width].astype(F32)
+    q, k = total[:, :width], total[:, width : 2 * width]
     qk[0] = q
     qk[1] = k
-    new = part(2).astype(BF16)
+    new = total[:, 2 * width :].astype(BF16)
     value[...] = new
     qk[2] = new.astype(F32)
     lane = lax.broadcasted_iota(jnp.int32, squares.shape[1:], 1)
@@ -145,8 +132,9 @@
     )
     for i in range(NX):
         squares[i] = both
-    for i in range(blocks):
-        rest_buf[:, i * lanes : (i + 1) * lanes] = buf[i, at - rows : at].astype(F32)
+    lanes = at - 3 * width
+    for i in range(buf.shape[0]):
+        rest_buf[:, i * lanes : (i + 1) * lanes] = buf[i, :, 3 * width :].astype(F32)
     rest[...] = quarter(rest_buf, lax.axis_index("x"))
     second.wait()
 
@@ -168,13 +156,15 @@
     return jnp.where(row_head == col_head, jnp.concatenate([values] * heads, axis=0), 0.0)
 
 
-def attend_kernel(squares_in, qk, gains, tables, bounds, keys, values, key_out,
-                  out, score, top, kbuf, vbuf, acc, total, ksem, vsem):
+def attend_kernel(squares_in, qk, trig, places, gains_in, keys, values, key_out,
+                  out, score, top, kbuf, vbuf, acc, total, gains, ksem, vsem, gsem):
     rows, width = out.shape
     heads = width // HEAD_DIM
     blocks = score.shape[0]
     model = width * NX
-    used = jnp.max(bounds[...].astype(F32))
+    used = jnp.sum(places[0:1, :])
+    gain_copy = pltpu.make_async_copy(gains_in, gains, gsem)
+    gain_copy.start()
 
     def fetch(source, buf, sem, i):
         return pltpu.make_async_copy(source.at[pl.ds(i * BLOCK, BLOCK)], buf.at[i], sem.at[i])
@@ -185,11 +175,24 @@
             def _():
                 fetch(source, buf, sem, i).start()
 
+    wide = heads * rows
+    request = lax.rem(lax.broadcasted_iota(jnp.int32, (wide, 128), 0), rows)
+    lane = lax.broadcasted_iota(jnp.int32, (wide, 128), 1)
+    lengths = jnp.broadcast_to(places[0:1, :], (wide, 128))
+    starts = jnp.sum(jnp.where(lane < request, lengths, 0.0), axis=1, keepdims=True)
+    ends = jnp.sum(jnp.where(lane <= request, lengths, 0.0), axis=1, keepdims=True)
+    starts = starts.astype(jnp.int32)
+    ends = ends.astype(jnp.int32)
+    angles = trig[...].T
+    half = HEAD_DIM // 2
+    cosine = jnp.concatenate([angles[:rows, :half], angles[:rows, :half]], axis=1)
+    sine = jnp.concatenate([-angles[:rows, half:], angles[:rows, half:]], axis=1)
     squares = squares_in[0] + squares_in[1] + squares_in[2] + squares_in[3]
+    gain_copy.wait()
     q_factor = lax.rsqrt(squares[:, 0:1] / model + EPS)
     k_factor = lax.rsqrt(squares[:, 64:65] / model + EPS)
-    query = turn(qk[0] * q_factor * gains[0:1, :], tables[0], tables[1]).astype(BF16)
-    new_key = turn(qk[1] * k_factor * gains[1:2, :], tables[0], tables[1]).astype(BF16)
+    query = turn(qk[0] * q_factor * gains[0:1, :], cosine, sine).astype(BF16)
+    new_key = turn(qk[1] * k_factor * gains[1:2, :], cosine, sine).astype(BF16)
     key_out[...] = new_key
     scale = HEAD_DIM ** (-0.5)
     q_all = spread(query.astype(F32), heads)
@@ -197,8 +200,6 @@
     k_all = jnp.concatenate([new_key.astype(F32)] * heads, axis=0)
     v_all = jnp.concatenate([qk[2]] * heads, axis=0)
     own = jnp.sum(q_all * k_all, axis=1, keepdims=True) * scale
-    starts = bounds[:, 0:1]
-    ends = bounds[:, 1:2]
     top[...] = jnp.broadcast_to(own, top.shape)
     for i in range(blocks):
         @pl.when(i * BLOCK < used)
@@ -233,38 +234,37 @@
 def out_kernel(attended, own, mate, after, partial, gain_out, wbuf, sem):
     rows, width = attended.shape
     core = lax.axis_index("c")
-    last = pl.ds(own.shape[1] - wbuf.shape[2], wbuf.shape[2])
+    last = pl.ds(own.shape[2] - wbuf.shape[3], wbuf.shape[3])
     copies = [
-        pltpu.make_async_copy(got.at[:, last], wbuf.at[place], sem.at[i])
+        pltpu.make_async_copy(got.at[:, :, last], wbuf.at[place], sem.at[i])
         for i, (got, place) in enumerate(((own, core), (mate, 1 - core)))
     ]
     for copy in copies:
         copy.start()
     for copy in copies:
         copy.wait()
-    feats = width // (NY * NC)
-    lanes = wbuf.shape[3]
-    tiles = width // lanes
-    step = wbuf.shape[2] // tiles
+    steps = (wbuf.shape[3] - 128) // width
     mine = rows // NX
     for b in range(NZ):
-        places = [(c, b * NY + y) for y in range(NY) for c in range(NC)]
         weights = jnp.concatenate(
             [
-                jnp.concatenate([wbuf[c, p, t * step : t * step + feats] for c, p in places], axis=0)
-                for t in range(tiles)
+                wbuf[c, b * NY + y, :, i * width : (i + 1) * width]
+                for y in range(NY)
+                for c in range(NC)
+                for i in range(steps)
             ],
-            axis=1,
+            axis=0,
         )
         a = lax.dot_general(attended[...], weights, NT, preferred_element_type=F32)
         for x in range(NX):
             partial[x, :, b * width : (b + 1) * width] = a[x * mine : (x + 1) * mine]
-        for t in range(tiles):
-            both = None
-            for c, p in places:
-                piece = wbuf[c, p, t * step + feats : (t + 1) * step].astype(F32)
-                both = piece if both is None else both + piece
-            gain_out[b, 0:2, t * lanes : (t + 1) * lanes] = both[0:2] + both[2:4]
+        for y in range(NY):
+            two = [wbuf[c, b * NY + y, 0:8, steps * width :].astype(F32) for c in range(NC)]
+            two = [t[0:1] + t[1:2] for t in two]
+            for g in range(2):
+                gain_out[b, g : g + 1, y * 128 : (y + 1) * 128] = jnp.concatenate(
+                    [t[:, g * 64 : (g + 1) * 64] for t in two], axis=1
+                )
 
 
 def fan_kernel(got, rest, gains, own_mid, out):
@@ -298,7 +298,8 @@
         for half in range(2)
     ]
     blocks = wbuf.shape[2]
-    feats = wbuf.shape[3] // 3
+    lanes = 128
+    steps = wbuf.shape[4] // (3 * lanes)
     for copy in copies:
         copy.wait()
 
@@ -308,9 +309,10 @@
             [
                 jnp.concatenate(
                     [
-                        wbuf[p, c, b, part * feats : (part + 1) * feats]
+                        wbuf[p, c, b, :, (part * steps + i) * lanes : (part * steps + i + 1) * lanes]
                         for b in rows
                         for c in range(NC)
+                        for i in range(steps)
                     ],
                     axis=0,
                 )
@@ -375,15 +377,20 @@
     bounds = jnp.tile(jnp.stack([ends - lengths, ends], axis=1), (heads, 1))
     gain_table = jnp.concatenate([qk_gain, jnp.zeros((6, width), F32)], axis=0)
     places = NZ * NY
-    size = 3 * feats
+    half = HEAD_DIM // 2
+    freqs = jnp.power(THETA, -(jnp.arange(half, dtype=F32) * 2.0 / HEAD_DIM))
+    spots = jnp.pad(lengths.astype(F32), (0, 128 - rows))[None, :]
+    angles = freqs[:, None] * spots
+    trig = jnp.concatenate([jnp.cos(angles), jnp.sin(angles)], axis=0)
+    spots = jnp.broadcast_to(spots, (8, 128))
     lanes = 128
-    tiles = width // lanes
-    head_lines = (3 * tiles + 1) * rows
-    out_lines = tiles * (feats + 8)
+    head_lanes = 3 * width + lanes
+    tile_lanes = 3 * feats // rows * lanes
+    out_lanes = feats // rows * width + lanes
     message = call(
         project_kernel,
-        shape((places, head_lines + size + out_lines, lanes), BF16),
-        [ANY] * 11,
+        shape((places, rows, head_lanes + tile_lanes + out_lanes), BF16),
+        [ANY] * 10,
         VMEM,
         [
             pltpu.VMEM((2, feats, flipped.shape[1]), BF16),
@@ -398,8 +405,7 @@
         (1 << 27, 2 << 20),
         "project",
         8,
-    )(hbm(flipped), mate_rows, hbm(w_qkv), mate_w, hbm(w_gate_up), hbm(w_down), hbm(w_out), hbm(norm_gain),
-      tables, bounds, gain_table)
+    )(hbm(flipped), mate_rows, hbm(w_qkv), mate_w, hbm(w_gate_up), hbm(w_down), hbm(w_out), hbm(norm_gain), trig, spots)
     got = lax.all_to_all(message, Z + ("y",), 0, 0, tiled=True)
 
     mate = lax.ppermute(got, "c", ring(1, NC))
@@ -410,12 +416,12 @@
             shape((rows, width), BF16),
             shape((NX, rows, 128), F32),
             shape((rows // NX, model), F32),
-            shape((places, size, lanes), BF16),
+            shape((places, rows, tile_lanes), BF16),
         ),
         [ANY],
         (VMEM,) * 4 + (ANY,),
         [
-            pltpu.VMEM((places, head_lines, lanes), BF16),
+            pltpu.VMEM((places, rows, head_lanes), BF16),
             pltpu.VMEM((rows, model), F32),
             pltpu.SemaphoreType.DMA((2,)),
         ],
@@ -429,7 +435,7 @@
     key_new, attended = call(
         attend_kernel,
         (shape((rows, width), BF16), shape((rows, width), BF16)),
-        [VMEM] * 5 + [ANY] * 2,
+        [VMEM] * 4 + [ANY] * 3,
         (VMEM,) * 2,
         [
             pltpu.VMEM((blocks, wide, BLOCK), F32),
@@ -438,20 +444,22 @@
             pltpu.VMEM((blocks, BLOCK, width), BF16),
             pltpu.VMEM((wide, width), F32),
             pltpu.VMEM((wide, 128), F32),
+            pltpu.VMEM((2, width), F32),
             pltpu.SemaphoreType.DMA((blocks,)),
             pltpu.SemaphoreType.DMA((blocks,)),
+            pltpu.SemaphoreType.DMA,
         ],
         (1 << 29, 8 << 20),
         "attend",
         16,
-    )(squares, qk, gain_table, tables, bounds, hbm(cache_keys), hbm(cache_values))
+    )(squares, qk, trig, spots, hbm(qk_gain), hbm(cache_keys), hbm(cache_values))
     partial, gains = call(
         out_kernel,
         (shape((NX, rows // NX, model), F32), shape((NZ, 8, width), F32)),
         [VMEM] + [ANY] * 3,
         (VMEM,) * 2,
         [
-            pltpu.VMEM((NC, places, out_lines, lanes), BF16),
+            pltpu.VMEM((NC, places, rows, out_lanes), BF16),
             pltpu.SemaphoreType.DMA((2,)),
         ],
         (1 << 26, 2 << 20),

time: 130 us -> 128 us (0.985)
  Pallas kernels: 12.6 us -> 8.62 us
  starting transfers between devices: 3.38 us -> 6.33 us
  local copies, waits for them, and re-layouts: 2.54 us -> 0.95 us
    pallas_call x1, Pallas kernels: 7.17 us -> 3.28 us  [body(): call(attend_kernel, (shape((rows, width), BF16), shape((rows, width), BF1...]
    ppermute x1, starting transfers between devices: 0.09 us -> 3.29 us  [body(): near_mate = lax.ppermute(near, 'c', ring(1, NC))]
  transfers between devices with their start and end apart: 6 -> 6, of which waited for: 0 -> 2; matrix products, arithmetic and copies ran while one was open for 2% -> 1% of each run, Pallas kernels for 7% -> 4%
where the time goes in v7:
time: 128 us
  blocking collectives  110 us (86%)
  Pallas kernels  8.62 us (7%)
  starting transfers between devices  6.33 us (5%)
    all_to_all x1, blocking collectives, body(): got = lax.all_to_all(message, Z + ('y',), 0, 0, tiled=True)  42.9 us
    all_to_all x1, blocking collectives, body(): got = lax.all_to_all(message, group, 0, 0, tiled=True)  20.4 us
    all_to_all x1, blocking collectives, body(): hidden = lax.all_to_all(message, Z + ('y', 'c', 'x'), 0, 0, tiled=True)  16.4 us
    all_to_all x1, blocking collectives, body(): got = lax.all_to_all(partial, group, 0, 0, tiled=True)  14.6 us
    all_to_all x1, blocking collectives, body(): squares = lax.all_to_all(squares, 'x', 0, 0, tiled=True)  8.11 us
    all_to_all x1, blocking collectives, body(): summed = lax.all_to_all(partial, 'x', 0, 0, tiled=True)  7.21 us
    ppermute x1, starting transfers between devices, body(): near_mate = lax.ppermute(near, 'c', ring(1, NC))  3.29 us
    pallas_call x1, Pallas kernels, body(): call(attend_kernel, (shape((rows, width), BF16), shape((rows, width), BF1...  3.28 us
  transfers between devices with their start and end apart: 6, of which 2 were waited for; matrix products, arithmetic and copies ran while one was open for 1% of the time, Pallas kernels for 4%

profile of v7, /device:TPU:1, one launch (start us, length us, event | category | flops | bytes accessed | tf_op | source)
XLA Modules:
  0.0 127.8 jit_solution(7025276158025552568)
XLA Ops:
  0.6 1.5 %collective-permute-start = (bf16[64,512]{1,0:T(8,128)(2,1)}, bf16[64,512]{1,0:T(8,128)(2,1)S(1)}, u32[]{:S(2)}, u32[]{:S(2)}) collective-permute-start(bf16[64,512]{1,0:T(8,128)(2,1)} %bitcast.3), channel_id=1, source_target_pairs={{0,4},{4,0},{1,5},{5,1},{2,6},{6,2},{3,7},{7,3},{8,12},{12,8},{9,1... | collective-permute-start | bytes 196616 | tf_op jit(solution)/shard_map/ppermute | solution.py:366
  2.1 0.1 collective-permute-start.1
  2.2 0.7 convert_element_type.5
  2.9 0.2 multiply_cosine_fusion
  3.1 0.1 collective-permute-done.h_mate
  3.2 0.5 collective-permute-done.1.w_mate
  3.8 1.7 %project.1 = bf16[16,16,5376]{2,1,0:T(8,128)(2,1)S(1)} custom-call(bf16[64,512]{1,0:T(8,128)(2,1)} %bitcast.4, bf16[64,512]{1,0:T(8,128)(2,1)S(1)} %collective-permute-done.h_mate, bf16[3,64,512]{2,1,0:T(8,128)(2,1)} %w_own.1, bf16[3,64,512]{2,1,0:T(8,128)(2,1)S(1)} %collective-permute-done.1.w_mate, bf16[2,64,2048]{2,1,0:T(8,128)(2,1)} %gate_up.1, ...), custom_call_target="tpu_custom_call" | custom-call | flops 134217728 | bytes 2097152 | tf_op jit(solution)/shard_map/project/pallas_call | solution.py:390
  5.5 42.9 %all_to_all.30.got.own = bf16[16,16,5376]{2,1,0:T(8,128)(2,1)S(1)} all-to-all(bf16[16,16,5376]{2,1,0:T(8,128)(2,1)S(1)} %project.1), channel_id=1, replica_groups=mesh['zh'=2,'zl'=2,'y'=4,'c'=2,'x'=4] {'zh','zl','y'}, dimensions={0} | all-to-all | bytes 5505024 | tf_op jit(solution)/shard_map/all_to_all | solution.py:409
  48.5 1.3 collective-permute-start.2
  49.7 0.9 collect.1
  50.6 0.1 collective-permute-start.3
  50.7 0.1 collective-permute-start.4
  50.8 8.1 %all_to_all.31.squares_in = f32[4,16,128]{2,1,0:T(8,128)S(1)} all-to-all(f32[4,16,128]{2,1,0:T(8,128)S(1)} %get-tuple-element.14), channel_id=1, replica_groups=mesh['zh'=2,'zl'=2,'y'=4,'c'=2,'x'=4] {'x'}, dimensions={0} | all-to-all | bytes 65536 | tf_op jit(solution)/shard_map/all_to_all | solution.py:434
  58.9 3.3 %attend.1 = (bf16[16,512]{1,0:T(8,128)(2,1)}, bf16[16,512]{1,0:T(8,128)(2,1)S(1)}) custom-call(f32[4,16,128]{2,1,0:T(8,128)S(1)} %all_to_all.31.squares_in, f32[3,16,512]{2,1,0:T(8,128)S(1)} %get-tuple-element.15.qk, f32[128,128]{1,0:T(8,128)S(1)} %pad_maximum_fusion.trig, f32[8,128]{1,0:T(8,128)S(1)} %broadcast_in_dim.2.places, f32[2,512]{1,0:T(2,128)} %gains_in.1, ...), custom_call_target="tpu_custom_call" | custom-call | flops 536870912 | bytes 8388608 | tf_op jit(solution)/shard_map/attend/pallas_call | solution.py:435
  62.2 0.0 collective-permute-done.3.after.own_mate
  62.2 0.0 collective-permute-done.2.mate
  62.2 0.9 project_out.1
  63.1 7.2 %all_to_all.32.got = f32[4,4,2048]{2,1,0:T(4,128)S(1)} all-to-all(f32[4,4,2048]{2,1,0:T(4,128)S(1)} %get-tuple-element.18), channel_id=1, replica_groups=mesh['zh'=2,'zl'=2,'y'=4,'c'=2,'x'=4] {'x'}, dimensions={0} | all-to-all | bytes 262144 | tf_op jit(solution)/shard_map/all_to_all | solution.py:470
  70.3 0.1 fan.1
  70.5 0.0 collective-permute-done.4.piece
  70.5 0.1 hold.1.near
  70.6 3.3 %collective-permute-start.5 = (bf16[16,16,1536]{2,1,0:T(8,128)(2,1)S(1)}, bf16[16,16,1536]{2,1,0:T(8,128)(2,1)S(1)}, u32[]{:S(2)}, u32[]{:S(2)}) collective-permute-start(bf16[16,16,1536]{2,1,0:T(8,128)(2,1)S(1)} %hold.1.near), channel_id=1, source_target_pairs={{0,4},{4,0},{1,5},{5,1},{2,6},{6,2},{3,7},{7,3},{8,12},{12,8},{9,1... | collective-permute-start | bytes 2359304 | tf_op jit(solution)/shard_map/ppermute | solution.py:493
  73.9 20.4 %all_to_all.33.got = bf16[32,8,1024]{2,1,0:T(8,128)(2,1)S(1)} all-to-all(bf16[32,8,1024]{2,1,0:T(8,128)(2,1)S(1)} %get-tuple-element.21), channel_id=1, replica_groups=mesh['zh'=2,'zl'=2,'y'=4,'c'=2,'x'=4] {'zh','y','x'}, dimensions={0} | all-to-all | bytes 1048576 | tf_op jit(solution)/shard_map/all_to_all | solution.py:494
  94.2 0.0 collective-permute-done.5.near_mate
  94.2 1.4 %feed_forward.1 = bf16[32,8,1024]{2,1,0:T(8,128)(2,1)S(1)} custom-call(bf16[32,8,1024]{2,1,0:T(8,128)(2,1)S(1)} %all_to_all.33.got, bf16[16,16,1536]{2,1,0:T(8,128)(2,1)S(1)} %get-tuple-element.17.own, bf16[16,16,1536]{2,1,0:T(8,128)(2,1)S(1)} %collective-permute-done.3.after.own_mate, bf16[16,16,1536]{2,1,0:T(8,128)(2,1)S(1)} %hold.1.near, ...), custom_call_target="tpu_custom_call" | custom-call | flops 268435456 | bytes 4194304 | tf_op jit(solution)/shard_map/feed_forward/pallas_call | solution.py:495
  95.6 14.6 %all_to_all.34.got = bf16[32,8,1024]{2,1,0:T(8,128)(2,1)S(1)} all-to-all(bf16[32,8,1024]{2,1,0:T(8,128)(2,1)S(1)} %feed_forward.1), channel_id=1, replica_groups=mesh['zh'=2,'zl'=2,'y'=4,'c'=2,'x'=4] {'zh','y','x'}, dimensions={0} | all-to-all | bytes 1048576 | tf_op jit(solution)/shard_map/all_to_all | solution.py:508
  110.2 0.3 finish.1
  110.5 0.1 reshape.17
  110.6 16.4 %all_to_all.35 = bf16[128,2,128]{2,1,0:T(2,128)(2,1)S(1)} all-to-all(bf16[128,2,128]{2,1,0:T(2,128)(2,1)S(1)} %reshape.17), channel_id=1, replica_groups=mesh['zh'=2,'zl'=2,'y'=4,'c'=2,'x'=4] {'zh','zl','y','c','x'}, dimensions={0} | all-to-all | bytes 131072 | tf_op jit(solution)/shard_map/all_to_all | solution.py:518
  127.0 0.1 reshape.18
  127.1 0.7 copy.13
  (4 shorter events, 0.0 us)
Async XLA Ops:
  0.6 2.6 %collective-permute-start = (bf16[64,512]{1,0:T(8,128)(2,1)}, bf16[64,512]{1,0:T(8,128)(2,1)S(1)}, u32[]{:S(2)}, u32[]{:S(2)}) collective-permute-start(bf16[64,512]{1,0:T(8,128)(2,1)} %bitcast.3), channel_id=1, source_target_pairs={{0,4},{4,0},{1,5},{5,1},{2,6},{6,2},{3,7},{7,3},{8,12},{12,8},{9,1... | collective-permute-start | bytes 196616 | tf_op jit(solution)/shard_map/ppermute | solution.py:366
  2.1 1.7 %collective-permute-start.1 = (bf16[3,64,512]{2,1,0:T(8,128)(2,1)}, bf16[3,64,512]{2,1,0:T(8,128)(2,1)S(1)}, u32[]{:S(2)}, u32[]{:S(2)}) collective-permute-start(bf16[3,64,512]{2,1,0:T(8,128)(2,1)} %w_own.1), channel_id=1, source_target_pairs={{0,4},{4,0},{1,5},{5,1},{2,6},{6,2},{3,7},{7,3},{8,12},{12,8},{9,1... | collective-permute-start | bytes 589832 | tf_op jit(solution)/shard_map/ppermute | solution.py:367
  48.5 13.8 %collective-permute-start.2 = (bf16[16,16,5376]{2,1,0:T(8,128)(2,1)S(1)}, bf16[16,16,5376]{2,1,0:T(8,128)(2,1)S(1)}, u32[]{:S(2)}, u32[]{:S(2)}) collective-permute-start(bf16[16,16,5376]{2,1,0:T(8,128)(2,1)S(1)} %all_to_all.30.got.own), channel_id=1, source_target_pairs={{0,4},{4,0},{1,5},{5,1},{2,6},{6,2},{3,7},{7,3},{8,12},{12,8},{9,1... | collective-permute-start | bytes 8257544 | tf_op jit(solution)/shard_map/ppermute | solution.py:411
  50.6 11.6 %collective-permute-start.3 = (bf16[16,16,1536]{2,1,0:T(8,128)(2,1)S(1)}, bf16[16,16,1536]{2,1,0:T(8,128)(2,1)S(1)}, u32[]{:S(2)}, u32[]{:S(2)}) collective-permute-start(bf16[16,16,1536]{2,1,0:T(8,128)(2,1)S(1)} %get-tuple-element.17.own), channel_id=1, source_target_pairs={{0,4},{4,0},{1,5},{5,1},{2,6},{6,2},{3,7},{7,3},{8,12},{12,8},{9,1... | collective-permute-start | bytes 2359304 | tf_op jit(solution)/shard_map/ppermute | solution.py:432
  50.7 19.8 %collective-permute-start.4 = (bf16[16,16,1536]{2,1,0:T(8,128)(2,1)S(1)}, bf16[16,16,1536]{2,1,0:T(8,128)(2,1)S(1)}, u32[]{:S(2)}, u32[]{:S(2)}) collective-permute-start(bf16[16,16,1536]{2,1,0:T(8,128)(2,1)S(1)} %get-tuple-element.17.own), channel_id=1, source_target_pairs={{0,32},{32,0},{1,33},{33,1},{2,34},{34,2},{3,35},{35,3},{4,36},{36... | collective-permute-start | bytes 2359304 | tf_op jit(solution)/shard_map/ppermute | solution.py:433
  70.6 23.6 %collective-permute-start.5 = (bf16[16,16,1536]{2,1,0:T(8,128)(2,1)S(1)}, bf16[16,16,1536]{2,1,0:T(8,128)(2,1)S(1)}, u32[]{:S(2)}, u32[]{:S(2)}) collective-permute-start(bf16[16,16,1536]{2,1,0:T(8,128)(2,1)S(1)} %hold.1.near), channel_id=1, source_target_pairs={{0,4},{4,0},{1,5},{5,1},{2,6},{6,2},{3,7},{7,3},{8,12},{12,8},{9,1... | collective-permute-start | bytes 2359304 | tf_op jit(solution)/shard_map/ppermute | solution.py:493

commit v8 on v7

--- a/solution.py
+++ b/solution.py
@@ -109,12 +109,14 @@
     return jnp.where(lax.rem(x, 2) == 0, pair[:4], pair[4:])
 
 
-def collect_kernel(got, qk, value, squares, rest, ffn, buf, rest_buf, sem):
+def collect_kernel(got, gains, qk, value, squares, rest, gains_out, ffn, buf, rest_buf, sem):
     rows, width = value.shape
     at = buf.shape[2]
     first = pltpu.make_async_copy(got.at[:, :, pl.ds(0, at)], buf, sem.at[0])
     second = pltpu.make_async_copy(got.at[:, :, pl.ds(at, ffn.shape[2])], ffn, sem.at[1])
+    third = pltpu.make_async_copy(gains, gains_out, sem.at[2])
     first.start()
+    third.start()
     second.start()
     first.wait()
     total = buf[0, :, : 3 * width].astype(F32)
@@ -137,6 +139,7 @@
         rest_buf[:, i * lanes : (i + 1) * lanes] = buf[i, :, 3 * width :].astype(F32)
     rest[...] = quarter(rest_buf, lax.axis_index("x"))
     second.wait()
+    third.wait()
 
 
 def turn(values, cosine, sine):
@@ -156,25 +159,13 @@
     return jnp.where(row_head == col_head, jnp.concatenate([values] * heads, axis=0), 0.0)
 
 
-def attend_kernel(squares_in, qk, trig, places, gains_in, keys, values, key_out,
-                  out, score, top, kbuf, vbuf, acc, total, gains, ksem, vsem, gsem):
+def attend_kernel(squares_in, qk, trig, places, gains, keys, values, key_out,
+                  out, score):
     rows, width = out.shape
     heads = width // HEAD_DIM
     blocks = score.shape[0]
     model = width * NX
     used = jnp.sum(places[0:1, :])
-    gain_copy = pltpu.make_async_copy(gains_in, gains, gsem)
-    gain_copy.start()
-
-    def fetch(source, buf, sem, i):
-        return pltpu.make_async_copy(source.at[pl.ds(i * BLOCK, BLOCK)], buf.at[i], sem.at[i])
-
-    for source, buf, sem in ((keys, kbuf, ksem), (values, vbuf, vsem)):
-        for i in range(blocks):
-            @pl.when(i * BLOCK < used)
-            def _():
-                fetch(source, buf, sem, i).start()
-
     wide = heads * rows
     request = lax.rem(lax.broadcasted_iota(jnp.int32, (wide, 128), 0), rows)
     lane = lax.broadcasted_iota(jnp.int32, (wide, 128), 1)
@@ -188,7 +179,6 @@
     cosine = jnp.concatenate([angles[:rows, :half], angles[:rows, :half]], axis=1)
     sine = jnp.concatenate([-angles[:rows, half:], angles[:rows, half:]], axis=1)
     squares = squares_in[0] + squares_in[1] + squares_in[2] + squares_in[3]
-    gain_copy.wait()
     q_factor = lax.rsqrt(squares[:, 0:1] / model + EPS)
     k_factor = lax.rsqrt(squares[:, 64:65] / model + EPS)
     query = turn(qk[0] * q_factor * gains[0:1, :], cosine, sine).astype(BF16)
@@ -200,35 +190,43 @@
     k_all = jnp.concatenate([new_key.astype(F32)] * heads, axis=0)
     v_all = jnp.concatenate([qk[2]] * heads, axis=0)
     own = jnp.sum(q_all * k_all, axis=1, keepdims=True) * scale
-    top[...] = jnp.broadcast_to(own, top.shape)
-    for i in range(blocks):
-        @pl.when(i * BLOCK < used)
-        def _():
-            fetch(keys, kbuf, ksem, i).wait()
-            s = lax.dot_general(q_block, kbuf[i], NT, preferred_element_type=F32) * scale
-            place = lax.broadcasted_iota(jnp.int32, s.shape, 1) + i * BLOCK
-            s = jnp.where((place >= starts) & (place < ends), s, -jnp.inf)
+    def raw(i):
+        rows_here = keys[pl.ds(i * BLOCK, BLOCK), :]
+        s = lax.dot_general(q_block, rows_here, NT, preferred_element_type=F32) * scale
+        place = lax.broadcasted_iota(jnp.int32, s.shape, 1) + i * BLOCK
+        return jnp.where((place >= starts) & (place < ends), s, -jnp.inf)
+
+    def finish(size):
+        highest = own
+        for i in range(size):
+            s = raw(i)
             score[i] = s
-            top[...] = jnp.maximum(top[...], jnp.max(s, axis=1, keepdims=True))
-    highest = top[:, 0:1]
-    own_weight = jnp.exp(own - highest).astype(BF16).astype(F32)
-    total[...] = jnp.broadcast_to(own_weight, total.shape)
-    acc[...] = own_weight * v_all
-    for i in range(blocks):
-        @pl.when(i * BLOCK < used)
-        def _():
-            fetch(values, vbuf, vsem, i).wait()
+            highest = jnp.maximum(highest, jnp.max(s, axis=1, keepdims=True))
+        own_weight = jnp.exp(own - highest).astype(BF16).astype(F32)
+        total = own_weight
+        acc = own_weight * v_all
+        for i in range(size):
             w = jnp.exp(score[i] - highest).astype(BF16)
-            total[...] += jnp.sum(w.astype(F32), axis=1, keepdims=True)
-            acc[...] += jnp.dot(w, vbuf[i], preferred_element_type=F32)
-    result = acc[...] / total[:, 0:1]
-    out[...] = jnp.concatenate(
-        [
-            result[h * rows : (h + 1) * rows, h * HEAD_DIM : (h + 1) * HEAD_DIM]
-            for h in range(heads)
-        ],
-        axis=1,
-    ).astype(BF16)
+            total += jnp.sum(w.astype(F32), axis=1, keepdims=True)
+            acc += jnp.dot(w, values[pl.ds(i * BLOCK, BLOCK), :], preferred_element_type=F32)
+        result = acc / total
+        out[...] = jnp.concatenate(
+            [
+                result[h * rows : (h + 1) * rows, h * HEAD_DIM : (h + 1) * HEAD_DIM]
+                for h in range(heads)
+            ],
+            axis=1,
+        ).astype(BF16)
+
+    short = 2
+
+    @pl.when(used <= short * BLOCK)
+    def _():
+        finish(short)
+
+    @pl.when(used > short * BLOCK)
+    def _():
+        finish(blocks)
 
 
 def out_kernel(attended, own, mate, after, partial, gain_out, wbuf, sem):
@@ -409,50 +407,40 @@
     got = lax.all_to_all(message, Z + ("y",), 0, 0, tiled=True)
 
     mate = lax.ppermute(got, "c", ring(1, NC))
-    qk, value_new, squares, rest, ffn_own = call(
+    qk, value_new, squares, rest, gains_here, ffn_own = call(
         collect_kernel,
         (
             shape((3, rows, width), F32),
             shape((rows, width), BF16),
             shape((NX, rows, 128), F32),
             shape((rows // NX, model), F32),
+            shape(qk_gain.shape, F32),
             shape((places, rows, tile_lanes), BF16),
         ),
-        [ANY],
-        (VMEM,) * 4 + (ANY,),
+        [ANY] * 2,
+        (VMEM,) * 5 + (ANY,),
         [
             pltpu.VMEM((places, rows, head_lanes), BF16),
             pltpu.VMEM((rows, model), F32),
-            pltpu.SemaphoreType.DMA((2,)),
+            pltpu.SemaphoreType.DMA((3,)),
         ],
         (1 << 20, 4 << 20),
         "collect",
         8,
-    )(got)
+    )(got, hbm(qk_gain))
     ffn_mate = lax.ppermute(ffn_own, "c", ring(1, NC))
     near = lax.ppermute(ffn_own, "zl", ring(1, 2))
     squares = lax.all_to_all(squares, "x", 0, 0, tiled=True)
     key_new, attended = call(
         attend_kernel,
         (shape((rows, width), BF16), shape((rows, width), BF16)),
-        [VMEM] * 4 + [ANY] * 3,
+        [VMEM] * 7,
         (VMEM,) * 2,
-        [
-            pltpu.VMEM((blocks, wide, BLOCK), F32),
-            pltpu.VMEM((wide, 128), F32),
-            pltpu.VMEM((blocks, BLOCK, width), BF16),
-            pltpu.VMEM((blocks, BLOCK, width), BF16),
-            pltpu.VMEM((wide, width), F32),
-            pltpu.VMEM((wide, 128), F32),
-            pltpu.VMEM((2, width), F32),
-            pltpu.SemaphoreType.DMA((blocks,)),
-            pltpu.SemaphoreType.DMA((blocks,)),
-            pltpu.SemaphoreType.DMA,
-        ],
+        [pltpu.VMEM((blocks, wide, BLOCK), F32)],
         (1 << 29, 8 << 20),
         "attend",
         16,
-    )(squares, qk, trig, spots, hbm(qk_gain), hbm(cache_keys), hbm(cache_values))
+    )(squares, qk, trig, spots, gains_here, cache_keys, cache_values)
     partial, gains = call(
         out_kernel,
         (shape((NX, rows // NX, model), F32), shape((NZ, 8, width), F32)),

time: 128 us -> 124 us (0.969)
  blocking collectives: 110 us -> 107 us
    all_to_all x1, blocking collectives: 20.4 us -> 16.8 us  [body(): got = lax.all_to_all(message, group, 0, 0, tiled=True)]
    pallas_call x1, Pallas kernels: 3.28 us -> 1.69 us  [body(): call(attend_kernel, (shape((rows, width), BF16), shape((rows, width), BF1...]
  transfers between devices with their start and end apart: 6 -> 6, of which waited for: 2 -> 3; matrix products, arithmetic and copies ran while one was open for 1% -> 1% of each run, Pallas kernels for 4% -> 3%
where the time goes in v8:
time: 124 us; the launch traced here: 125 us
  blocking collectives  107 us (86%)
  Pallas kernels  7.64 us (6%)
  starting transfers between devices  5.69 us (5%)
  waiting for transfers between devices  1.32 us (1%)
    all_to_all x1, blocking collectives, body(): got = lax.all_to_all(message, Z + ('y',), 0, 0, tiled=True)  43.2 us
    all_to_all x1, blocking collectives, body(): hidden = lax.all_to_all(message, Z + ('y', 'c', 'x'), 0, 0, tiled=True)  17.4 us
    all_to_all x1, blocking collectives, body(): got = lax.all_to_all(message, group, 0, 0, tiled=True)  16.8 us
    all_to_all x1, blocking collectives, body(): got = lax.all_to_all(partial, group, 0, 0, tiled=True)  14.7 us
    all_to_all x1, blocking collectives, body(): squares = lax.all_to_all(squares, 'x', 0, 0, tiled=True)  8.12 us
    all_to_all x1, blocking collectives, body(): summed = lax.all_to_all(partial, 'x', 0, 0, tiled=True)  7.21 us
    ppermute x1, starting transfers between devices, body(): near_mate = lax.ppermute(near, 'c', ring(1, NC))  2.66 us
  transfers between devices with their start and end apart: 6, of which 3 were waited for; matrix products, arithmetic and copies ran while one was open for 1% of the time, Pallas kernels for 3%

profile of v8, /device:TPU:1, one launch (start us, length us, event | category | flops | bytes accessed | tf_op | source)
XLA Modules:
  0.0 124.7 jit_solution(18237482283601598018)
XLA Ops:
  0.6 1.5 %collective-permute-start = (bf16[64,512]{1,0:T(8,128)(2,1)}, bf16[64,512]{1,0:T(8,128)(2,1)S(1)}, u32[]{:S(2)}, u32[]{:S(2)}) collective-permute-start(bf16[64,512]{1,0:T(8,128)(2,1)} %bitcast.3), channel_id=1, source_target_pairs={{0,4},{4,0},{1,5},{5,1},{2,6},{6,2},{3,7},{7,3},{8,12},{12,8},{9,1... | collective-permute-start | bytes 196616 | tf_op jit(solution)/shard_map/ppermute | solution.py:364
  2.1 0.1 collective-permute-start.1
  2.2 0.7 convert_element_type.5
  2.9 0.2 multiply_cosine_fusion
  3.1 0.1 collective-permute-done.h_mate
  3.2 0.5 collective-permute-done.1.w_mate
  3.8 0.0 copy-start.1
  3.8 1.9 %project.1 = bf16[16,16,5376]{2,1,0:T(8,128)(2,1)S(1)} custom-call(bf16[64,512]{1,0:T(8,128)(2,1)} %bitcast.4, bf16[64,512]{1,0:T(8,128)(2,1)S(1)} %collective-permute-done.h_mate, bf16[3,64,512]{2,1,0:T(8,128)(2,1)} %w_own.1, bf16[3,64,512]{2,1,0:T(8,128)(2,1)S(1)} %collective-permute-done.1.w_mate, bf16[2,64,2048]{2,1,0:T(8,128)(2,1)} %gate_up.1, ...), custom_call_target="tpu_custom_call" | custom-call | flops 134217728 | bytes 2097152 | tf_op jit(solution)/shard_map/project/pallas_call | solution.py:388
  5.7 0.0 copy-start
  5.7 43.2 %all_to_all.30.got.own = bf16[16,16,5376]{2,1,0:T(8,128)(2,1)S(1)} all-to-all(bf16[16,16,5376]{2,1,0:T(8,128)(2,1)S(1)} %project.1), channel_id=1, replica_groups=mesh['zh'=2,'zl'=2,'y'=4,'c'=2,'x'=4] {'zh','zl','y'}, dimensions={0} | all-to-all | bytes 5505024 | tf_op jit(solution)/shard_map/all_to_all | solution.py:407
  48.9 1.3 %collective-permute-start.2 = (bf16[16,16,5376]{2,1,0:T(8,128)(2,1)S(1)}, bf16[16,16,5376]{2,1,0:T(8,128)(2,1)S(1)}, u32[]{:S(2)}, u32[]{:S(2)}) collective-permute-start(bf16[16,16,5376]{2,1,0:T(8,128)(2,1)S(1)} %all_to_all.30.got.own), channel_id=1, source_target_pairs={{0,4},{4,0},{1,5},{5,1},{2,6},{6,2},{3,7},{7,3},{8,12},{12,8},{9,1... | collective-permute-start | bytes 8257544 | tf_op jit(solution)/shard_map/ppermute | solution.py:409
  50.2 1.4 %collect.1 = (f32[3,16,512]{2,1,0:T(8,128)S(1)}, bf16[16,512]{1,0:T(8,128)(2,1)}, f32[4,16,128]{2,1,0:T(8,128)S(1)}, f32[4,2048]{1,0:T(4,128)S(1)}, f32[2,512]{1...) custom-call(bf16[16,16,5376]{2,1,0:T(8,128)(2,1)S(1)} %all_to_all.30.got.own, f32[2,512]{1,0:T(2,128)} %gains.3), custom_call_target="tpu_custom_call" | custom-call | flops 1048576 | bytes 4194304 | tf_op jit(solution)/shard_map/collect/pallas_call | solution.py:410
  51.5 0.1 collective-permute-start.3
  51.6 0.1 collective-permute-start.4
  51.7 8.1 %all_to_all.31.squares_in = f32[4,16,128]{2,1,0:T(8,128)S(1)} all-to-all(f32[4,16,128]{2,1,0:T(8,128)S(1)} %get-tuple-element.15), channel_id=1, replica_groups=mesh['zh'=2,'zl'=2,'y'=4,'c'=2,'x'=4] {'x'}, dimensions={0} | all-to-all | bytes 65536 | tf_op jit(solution)/shard_map/all_to_all | solution.py:433
  59.9 0.0 copy-done.1
  59.9 0.0 copy-done
  59.9 1.7 %attend.1 = (bf16[16,512]{1,0:T(8,128)(2,1)}, bf16[16,512]{1,0:T(8,128)(2,1)S(1)}) custom-call(f32[4,16,128]{2,1,0:T(8,128)S(1)} %all_to_all.31.squares_in, f32[3,16,512]{2,1,0:T(8,128)S(1)} %get-tuple-element.16.qk, f32[128,128]{1,0:T(8,128)S(1)} %pad_maximum_fusion.trig, f32[8,128]{1,0:T(8,128)S(1)} %broadcast_in_dim.2.places, ...), custom_call_target="tpu_custom_call" | custom-call | flops 536870912 | bytes 8388608 | tf_op jit(solution)/shard_map/attend/pallas_call | solution.py:434
  61.5 0.0 collective-permute-done.3.after.own_mate
  61.6 0.0 collective-permute-done.2.mate
  61.6 0.8 project_out.1
  62.4 7.2 %all_to_all.32.got = f32[4,4,2048]{2,1,0:T(4,128)S(1)} all-to-all(f32[4,4,2048]{2,1,0:T(4,128)S(1)} %get-tuple-element.20), channel_id=1, replica_groups=mesh['zh'=2,'zl'=2,'y'=4,'c'=2,'x'=4] {'x'}, dimensions={0} | all-to-all | bytes 262144 | tf_op jit(solution)/shard_map/all_to_all | solution.py:458
  69.6 0.1 fan.1
  69.8 0.6 collective-permute-done.4.piece
  70.4 0.1 hold.1.near
  70.5 2.7 %collective-permute-start.5 = (bf16[16,16,1536]{2,1,0:T(8,128)(2,1)S(1)}, bf16[16,16,1536]{2,1,0:T(8,128)(2,1)S(1)}, u32[]{:S(2)}, u32[]{:S(2)}) collective-permute-start(bf16[16,16,1536]{2,1,0:T(8,128)(2,1)S(1)} %hold.1.near), channel_id=1, source_target_pairs={{0,4},{4,0},{1,5},{5,1},{2,6},{6,2},{3,7},{7,3},{8,12},{12,8},{9,1... | collective-permute-start | bytes 2359304 | tf_op jit(solution)/shard_map/ppermute | solution.py:481
  73.2 16.8 %all_to_all.33.got = bf16[32,8,1024]{2,1,0:T(8,128)(2,1)S(1)} all-to-all(bf16[32,8,1024]{2,1,0:T(8,128)(2,1)S(1)} %get-tuple-element.23), channel_id=1, replica_groups=mesh['zh'=2,'zl'=2,'y'=4,'c'=2,'x'=4] {'zh','y','x'}, dimensions={0} | all-to-all | bytes 1048576 | tf_op jit(solution)/shard_map/all_to_all | solution.py:482
  90.0 0.0 collective-permute-done.5.near_mate
  90.0 1.4 %feed_forward.1 = bf16[32,8,1024]{2,1,0:T(8,128)(2,1)S(1)} custom-call(bf16[32,8,1024]{2,1,0:T(8,128)(2,1)S(1)} %all_to_all.33.got, bf16[16,16,1536]{2,1,0:T(8,128)(2,1)S(1)} %get-tuple-element.19.own, bf16[16,16,1536]{2,1,0:T(8,128)(2,1)S(1)} %collective-permute-done.3.after.own_mate, bf16[16,16,1536]{2,1,0:T(8,128)(2,1)S(1)} %hold.1.near, ...), custom_call_target="tpu_custom_call" | custom-call | flops 268435456 | bytes 4194304 | tf_op jit(solution)/shard_map/feed_forward/pallas_call | solution.py:483
  91.4 14.7 %all_to_all.34.got = bf16[32,8,1024]{2,1,0:T(8,128)(2,1)S(1)} all-to-all(bf16[32,8,1024]{2,1,0:T(8,128)(2,1)S(1)} %feed_forward.1), channel_id=1, replica_groups=mesh['zh'=2,'zl'=2,'y'=4,'c'=2,'x'=4] {'zh','y','x'}, dimensions={0} | all-to-all | bytes 1048576 | tf_op jit(solution)/shard_map/all_to_all | solution.py:496
  106.0 0.3 finish.1
  106.3 0.1 reshape.17
  106.4 17.4 %all_to_all.35 = bf16[128,2,128]{2,1,0:T(2,128)(2,1)S(1)} all-to-all(bf16[128,2,128]{2,1,0:T(2,128)(2,1)S(1)} %reshape.17), channel_id=1, replica_groups=mesh['zh'=2,'zl'=2,'y'=4,'c'=2,'x'=4] {'zh','zl','y','c','x'}, dimensions={0} | all-to-all | bytes 131072 | tf_op jit(solution)/shard_map/all_to_all | solution.py:506
  123.8 0.1 reshape.18
  123.9 0.7 copy.13
  (4 shorter events, 0.0 us)
Async XLA Ops:
  0.6 2.6 %collective-permute-start = (bf16[64,512]{1,0:T(8,128)(2,1)}, bf16[64,512]{1,0:T(8,128)(2,1)S(1)}, u32[]{:S(2)}, u32[]{:S(2)}) collective-permute-start(bf16[64,512]{1,0:T(8,128)(2,1)} %bitcast.3), channel_id=1, source_target_pairs={{0,4},{4,0},{1,5},{5,1},{2,6},{6,2},{3,7},{7,3},{8,12},{12,8},{9,1... | collective-permute-start | bytes 196616 | tf_op jit(solution)/shard_map/ppermute | solution.py:364
  2.1 1.7 %collective-permute-start.1 = (bf16[3,64,512]{2,1,0:T(8,128)(2,1)}, bf16[3,64,512]{2,1,0:T(8,128)(2,1)S(1)}, u32[]{:S(2)}, u32[]{:S(2)}) collective-permute-start(bf16[3,64,512]{2,1,0:T(8,128)(2,1)} %w_own.1), channel_id=1, source_target_pairs={{0,4},{4,0},{1,5},{5,1},{2,6},{6,2},{3,7},{7,3},{8,12},{12,8},{9,1... | collective-permute-start | bytes 589832 | tf_op jit(solution)/shard_map/ppermute | solution.py:365
  3.8 56.1 %copy-start.1 = (bf16[4096,512]{1,0:T(8,128)(2,1)S(1)}, bf16[4096,512]{1,0:T(8,128)(2,1)}, u32[]{:S(2)}) copy-start(bf16[4096,512]{1,0:T(8,128)(2,1)} %values.1) | copy-start | bytes 12582916
  5.7 54.2 %copy-start = (bf16[4096,512]{1,0:T(8,128)(2,1)S(1)}, bf16[4096,512]{1,0:T(8,128)(2,1)}, u32[]{:S(2)}) copy-start(bf16[4096,512]{1,0:T(8,128)(2,1)} %keys.1) | copy-start | bytes 12582916
  48.9 12.7 %collective-permute-start.2 = (bf16[16,16,5376]{2,1,0:T(8,128)(2,1)S(1)}, bf16[16,16,5376]{2,1,0:T(8,128)(2,1)S(1)}, u32[]{:S(2)}, u32[]{:S(2)}) collective-permute-start(bf16[16,16,5376]{2,1,0:T(8,128)(2,1)S(1)} %all_to_all.30.got.own), channel_id=1, source_target_pairs={{0,4},{4,0},{1,5},{5,1},{2,6},{6,2},{3,7},{7,3},{8,12},{12,8},{9,1... | collective-permute-start | bytes 8257544 | tf_op jit(solution)/shard_map/ppermute | solution.py:409
  51.5 10.0 %collective-permute-start.3 = (bf16[16,16,1536]{2,1,0:T(8,128)(2,1)S(1)}, bf16[16,16,1536]{2,1,0:T(8,128)(2,1)S(1)}, u32[]{:S(2)}, u32[]{:S(2)}) collective-permute-start(bf16[16,16,1536]{2,1,0:T(8,128)(2,1)S(1)} %get-tuple-element.19.own), channel_id=1, source_target_pairs={{0,4},{4,0},{1,5},{5,1},{2,6},{6,2},{3,7},{7,3},{8,12},{12,8},{9,1... | collective-permute-start | bytes 2359304 | tf_op jit(solution)/shard_map/ppermute | solution.py:431
  51.6 18.8 %collective-permute-start.4 = (bf16[16,16,1536]{2,1,0:T(8,128)(2,1)S(1)}, bf16[16,16,1536]{2,1,0:T(8,128)(2,1)S(1)}, u32[]{:S(2)}, u32[]{:S(2)}) collective-permute-start(bf16[16,16,1536]{2,1,0:T(8,128)(2,1)S(1)} %get-tuple-element.19.own), channel_id=1, source_target_pairs={{0,32},{32,0},{1,33},{33,1},{2,34},{34,2},{3,35},{35,3},{4,36},{36... | collective-permute-start | bytes 2359304 | tf_op jit(solution)/shard_map/ppermute | solution.py:432
  70.5 19.5 %collective-permute-start.5 = (bf16[16,16,1536]{2,1,0:T(8,128)(2,1)S(1)}, bf16[16,16,1536]{2,1,0:T(8,128)(2,1)S(1)}, u32[]{:S(2)}, u32[]{:S(2)}) collective-permute-start(bf16[16,16,1536]{2,1,0:T(8,128)(2,1)S(1)} %hold.1.near), channel_id=1, source_target_pairs={{0,4},{4,0},{1,5},{5,1},{2,6},{6,2},{3,7},{7,3},{8,12},{12,8},{9,1... | collective-permute-start | bytes 2359304 | tf_op jit(solution)/shard_map/ppermute | solution.py:481

commit v9 on v8

--- a/solution.py
+++ b/solution.py
@@ -109,14 +109,12 @@
     return jnp.where(lax.rem(x, 2) == 0, pair[:4], pair[4:])
 
 
-def collect_kernel(got, gains, qk, value, squares, rest, gains_out, ffn, buf, rest_buf, sem):
+def collect_kernel(got, qk, value, squares, rest, ffn, buf, rest_buf, sem):
     rows, width = value.shape
     at = buf.shape[2]
     first = pltpu.make_async_copy(got.at[:, :, pl.ds(0, at)], buf, sem.at[0])
     second = pltpu.make_async_copy(got.at[:, :, pl.ds(at, ffn.shape[2])], ffn, sem.at[1])
-    third = pltpu.make_async_copy(gains, gains_out, sem.at[2])
     first.start()
-    third.start()
     second.start()
     first.wait()
     total = buf[0, :, : 3 * width].astype(F32)
@@ -139,7 +137,6 @@
         rest_buf[:, i * lanes : (i + 1) * lanes] = buf[i, :, 3 * width :].astype(F32)
     rest[...] = quarter(rest_buf, lax.axis_index("x"))
     second.wait()
-    third.wait()
 
 
 def turn(values, cosine, sine):
@@ -344,6 +341,11 @@
         part = hidden[:, r * feats : (r + 1) * feats]
         for x in range(NX):
             out[r * NX + x] = part
+
+
+def turn_kernel(got, out):
+    rows = jnp.concatenate([got[i].astype(F32) for i in range(got.shape[0])], axis=0)
+    out[...] = rows.T.astype(BF16)
 
 
 def ring(shift, size):
@@ -407,27 +409,26 @@
     got = lax.all_to_all(message, Z + ("y",), 0, 0, tiled=True)
 
     mate = lax.ppermute(got, "c", ring(1, NC))
-    qk, value_new, squares, rest, gains_here, ffn_own = call(
+    qk, value_new, squares, rest, ffn_own = call(
         collect_kernel,
         (
             shape((3, rows, width), F32),
             shape((rows, width), BF16),
             shape((NX, rows, 128), F32),
             shape((rows // NX, model), F32),
-            shape(qk_gain.shape, F32),
             shape((places, rows, tile_lanes), BF16),
         ),
-        [ANY] * 2,
-        (VMEM,) * 5 + (ANY,),
+        [ANY],
+        (VMEM,) * 4 + (ANY,),
         [
             pltpu.VMEM((places, rows, head_lanes), BF16),
             pltpu.VMEM((rows, model), F32),
-            pltpu.SemaphoreType.DMA((3,)),
+            pltpu.SemaphoreType.DMA((2,)),
         ],
         (1 << 20, 4 << 20),
         "collect",
         8,
-    )(got, hbm(qk_gain))
+    )(got)
     ffn_mate = lax.ppermute(ffn_own, "c", ring(1, NC))
     near = lax.ppermute(ffn_own, "zl", ring(1, 2))
     squares = lax.all_to_all(squares, "x", 0, 0, tiled=True)
@@ -440,7 +441,7 @@
         (1 << 29, 8 << 20),
         "attend",
         16,
-    )(squares, qk, trig, spots, gains_here, cache_keys, cache_values)
+    )(squares, qk, trig, spots, qk_gain, cache_keys, cache_values)
     partial, gains = call(
         out_kernel,
         (shape((NX, rows // NX, model), F32), shape((NZ, 8, width), F32)),
@@ -504,7 +505,16 @@
         "finish",
     )(got, own_mid, gains)
     hidden = lax.all_to_all(message, Z + ("y", "c", "x"), 0, 0, tiled=True)
-    return hidden.reshape(-1, feats), key_new, value_new
+    hidden = call(
+        turn_kernel,
+        shape((feats, hidden.shape[0] * mine), BF16),
+        [VMEM],
+        VMEM,
+        (),
+        (1 << 16, 1 << 18),
+        "turn",
+    )(hidden)
+    return hidden.T, key_new, value_new
 
 
 def solution(mesh):

time: 124 us -> 124 us (level)
  Pallas kernels: 7.64 us -> 9.44 us
    pallas_call x1, Pallas kernels: 1.69 us -> 3.25 us  [body(): call(attend_kernel, (shape((rows, width), BF16), shape((rows, width), BF1...]
  transfers between devices with their start and end apart: 6 -> 6, of which waited for: 3 -> 2; matrix products, arithmetic and copies ran while one was open for 1% -> 1% of each run, Pallas kernels for 3% -> 4%
where the time goes in v9:
time: 124 us
  blocking collectives  107 us (86%)
  Pallas kernels  9.44 us (8%)
  starting transfers between devices  4.77 us (4%)
    all_to_all x1, blocking collectives, body(): got = lax.all_to_all(message, Z + ('y',), 0, 0, tiled=True)  43.2 us
    all_to_all x1, blocking collectives, body(): hidden = lax.all_to_all(message, Z + ('y', 'c', 'x'), 0, 0, tiled=True)  17.1 us
    all_to_all x1, blocking collectives, body(): got = lax.all_to_all(message, group, 0, 0, tiled=True)  16.8 us
    all_to_all x1, blocking collectives, body(): got = lax.all_to_all(partial, group, 0, 0, tiled=True)  14.7 us
    all_to_all x1, blocking collectives, body(): squares = lax.all_to_all(squares, 'x', 0, 0, tiled=True)  8.12 us
    all_to_all x1, blocking collectives, body(): summed = lax.all_to_all(partial, 'x', 0, 0, tiled=True)  7.21 us
    pallas_call x1, Pallas kernels, body(): call(attend_kernel, (shape((rows, width), BF16), shape((rows, width), BF1...  3.25 us
  transfers between devices with their start and end apart: 6, of which 2 were waited for; matrix products, arithmetic and copies ran while one was open for 1% of the time, Pallas kernels for 4%

profile of v9, /device:TPU:1, one launch (start us, length us, event | category | flops | bytes accessed | tf_op | source)
XLA Modules:
  0.0 123.8 jit_solution(14720477020135853459)
XLA Ops:
  0.6 1.5 %collective-permute-start = (bf16[64,512]{1,0:T(8,128)(2,1)}, bf16[64,512]{1,0:T(8,128)(2,1)S(1)}, u32[]{:S(2)}, u32[]{:S(2)}) collective-permute-start(bf16[64,512]{1,0:T(8,128)(2,1)} %bitcast.2), channel_id=1, source_target_pairs={{0,4},{4,0},{1,5},{5,1},{2,6},{6,2},{3,7},{7,3},{8,12},{12,8},{9,1... | collective-permute-start | bytes 196616 | tf_op jit(solution)/shard_map/ppermute | solution.py:366
  2.1 0.1 collective-permute-start.1
  2.2 0.7 convert_element_type.5
  2.9 0.2 multiply_cosine_fusion
  3.1 0.1 collective-permute-done.h_mate
  3.2 0.5 collective-permute-done.1.w_mate
  3.8 0.0 copy-start.1
  3.8 1.9 %project.1 = bf16[16,16,5376]{2,1,0:T(8,128)(2,1)S(1)} custom-call(bf16[64,512]{1,0:T(8,128)(2,1)} %bitcast.3, bf16[64,512]{1,0:T(8,128)(2,1)S(1)} %collective-permute-done.h_mate, bf16[3,64,512]{2,1,0:T(8,128)(2,1)} %w_own.1, bf16[3,64,512]{2,1,0:T(8,128)(2,1)S(1)} %collective-permute-done.1.w_mate, bf16[2,64,2048]{2,1,0:T(8,128)(2,1)} %gate_up.1, ...), custom_call_target="tpu_custom_call" | custom-call | flops 134217728 | bytes 2097152 | tf_op jit(solution)/shard_map/project/pallas_call | solution.py:390
  5.7 0.0 copy-start
  5.7 43.2 %all_to_all.30.got.own = bf16[16,16,5376]{2,1,0:T(8,128)(2,1)S(1)} all-to-all(bf16[16,16,5376]{2,1,0:T(8,128)(2,1)S(1)} %project.1), channel_id=1, replica_groups=mesh['zh'=2,'zl'=2,'y'=4,'c'=2,'x'=4] {'zh','zl','y'}, dimensions={0} | all-to-all | bytes 5505024 | tf_op jit(solution)/shard_map/all_to_all | solution.py:409
  48.9 0.0 copy-start.2
  48.9 1.3 %collective-permute-start.2 = (bf16[16,16,5376]{2,1,0:T(8,128)(2,1)S(1)}, bf16[16,16,5376]{2,1,0:T(8,128)(2,1)S(1)}, u32[]{:S(2)}, u32[]{:S(2)}) collective-permute-start(bf16[16,16,5376]{2,1,0:T(8,128)(2,1)S(1)} %all_to_all.30.got.own), channel_id=1, source_target_pairs={{0,4},{4,0},{1,5},{5,1},{2,6},{6,2},{3,7},{7,3},{8,12},{12,8},{9,1... | collective-permute-start | bytes 8257544 | tf_op jit(solution)/shard_map/ppermute | solution.py:411
  50.2 0.9 collect.1
  51.1 0.1 collective-permute-start.3
  51.2 0.1 collective-permute-start.4
  51.2 8.1 %all_to_all.31.squares_in = f32[4,16,128]{2,1,0:T(8,128)S(1)} all-to-all(f32[4,16,128]{2,1,0:T(8,128)S(1)} %get-tuple-element.14), channel_id=1, replica_groups=mesh['zh'=2,'zl'=2,'y'=4,'c'=2,'x'=4] {'x'}, dimensions={0} | all-to-all | bytes 65536 | tf_op jit(solution)/shard_map/all_to_all | solution.py:434
  59.4 0.0 copy-done.1
  59.4 0.0 copy-done
  59.4 0.0 copy-done.2
  59.4 3.3 %attend.1 = (bf16[16,512]{1,0:T(8,128)(2,1)}, bf16[16,512]{1,0:T(8,128)(2,1)S(1)}) custom-call(f32[4,16,128]{2,1,0:T(8,128)S(1)} %all_to_all.31.squares_in, f32[3,16,512]{2,1,0:T(8,128)S(1)} %get-tuple-element.15.qk, f32[128,128]{1,0:T(8,128)S(1)} %pad_maximum_fusion.trig, f32[8,128]{1,0:T(8,128)S(1)} %broadcast_in_dim.2.places, f32[2,512]{1,0:T(2,128)S(1)} %copy-done.2, ...), custom_call_target="tpu_custom_call" | custom-call | flops 536870912 | bytes 8388608 | tf_op jit(solution)/shard_map/attend/pallas_call | solution.py:435
  62.6 0.0 collective-permute-done.3.after.own_mate
  62.6 0.0 collective-permute-done.2.mate
  62.6 0.8 project_out.1
  63.5 7.2 %all_to_all.32.got = f32[4,4,2048]{2,1,0:T(4,128)S(1)} all-to-all(f32[4,4,2048]{2,1,0:T(4,128)S(1)} %get-tuple-element.18), channel_id=1, replica_groups=mesh['zh'=2,'zl'=2,'y'=4,'c'=2,'x'=4] {'x'}, dimensions={0} | all-to-all | bytes 262144 | tf_op jit(solution)/shard_map/all_to_all | solution.py:459
  70.7 0.1 fan.1
  70.9 0.0 collective-permute-done.4.piece
  70.9 0.1 hold.1.near
  70.9 1.7 %collective-permute-start.5 = (bf16[16,16,1536]{2,1,0:T(8,128)(2,1)S(1)}, bf16[16,16,1536]{2,1,0:T(8,128)(2,1)S(1)}, u32[]{:S(2)}, u32[]{:S(2)}) collective-permute-start(bf16[16,16,1536]{2,1,0:T(8,128)(2,1)S(1)} %hold.1.near), channel_id=1, source_target_pairs={{0,4},{4,0},{1,5},{5,1},{2,6},{6,2},{3,7},{7,3},{8,12},{12,8},{9,1... | collective-permute-start | bytes 2359304 | tf_op jit(solution)/shard_map/ppermute | solution.py:482
  72.7 16.8 %all_to_all.33.got = bf16[32,8,1024]{2,1,0:T(8,128)(2,1)S(1)} all-to-all(bf16[32,8,1024]{2,1,0:T(8,128)(2,1)S(1)} %get-tuple-element.21), channel_id=1, replica_groups=mesh['zh'=2,'zl'=2,'y'=4,'c'=2,'x'=4] {'zh','y','x'}, dimensions={0} | all-to-all | bytes 1048576 | tf_op jit(solution)/shard_map/all_to_all | solution.py:483
  89.5 0.0 collective-permute-done.5.near_mate
  89.5 1.4 %feed_forward.1 = bf16[32,8,1024]{2,1,0:T(8,128)(2,1)S(1)} custom-call(bf16[32,8,1024]{2,1,0:T(8,128)(2,1)S(1)} %all_to_all.33.got, bf16[16,16,1536]{2,1,0:T(8,128)(2,1)S(1)} %get-tuple-element.17.own, bf16[16,16,1536]{2,1,0:T(8,128)(2,1)S(1)} %collective-permute-done.3.after.own_mate, bf16[16,16,1536]{2,1,0:T(8,128)(2,1)S(1)} %hold.1.near, ...), custom_call_target="tpu_custom_call" | custom-call | flops 268435456 | bytes 4194304 | tf_op jit(solution)/shard_map/feed_forward/pallas_call | solution.py:484
  90.9 14.7 %all_to_all.34.got = bf16[32,8,1024]{2,1,0:T(8,128)(2,1)S(1)} all-to-all(bf16[32,8,1024]{2,1,0:T(8,128)(2,1)S(1)} %feed_forward.1), channel_id=1, replica_groups=mesh['zh'=2,'zl'=2,'y'=4,'c'=2,'x'=4] {'zh','y','x'}, dimensions={0} | all-to-all | bytes 1048576 | tf_op jit(solution)/shard_map/all_to_all | solution.py:497
  105.5 0.3 finish.1
  105.8 0.1 reshape.13
  105.9 17.1 %all_to_all.35 = bf16[128,2,128]{2,1,0:T(2,128)(2,1)S(1)} all-to-all(bf16[128,2,128]{2,1,0:T(2,128)(2,1)S(1)} %reshape.13), channel_id=1, replica_groups=mesh['zh'=2,'zl'=2,'y'=4,'c'=2,'x'=4] {'zh','zl','y','c','x'}, dimensions={0} | all-to-all | bytes 131072 | tf_op jit(solution)/shard_map/all_to_all | solution.py:507
  123.0 0.1 reshape.14.got
  123.1 0.7 turn.1
  (4 shorter events, 0.0 us)
Async XLA Ops:
  0.6 2.6 %collective-permute-start = (bf16[64,512]{1,0:T(8,128)(2,1)}, bf16[64,512]{1,0:T(8,128)(2,1)S(1)}, u32[]{:S(2)}, u32[]{:S(2)}) collective-permute-start(bf16[64,512]{1,0:T(8,128)(2,1)} %bitcast.2), channel_id=1, source_target_pairs={{0,4},{4,0},{1,5},{5,1},{2,6},{6,2},{3,7},{7,3},{8,12},{12,8},{9,1... | collective-permute-start | bytes 196616 | tf_op jit(solution)/shard_map/ppermute | solution.py:366
  2.1 1.7 %collective-permute-start.1 = (bf16[3,64,512]{2,1,0:T(8,128)(2,1)}, bf16[3,64,512]{2,1,0:T(8,128)(2,1)S(1)}, u32[]{:S(2)}, u32[]{:S(2)}) collective-permute-start(bf16[3,64,512]{2,1,0:T(8,128)(2,1)} %w_own.1), channel_id=1, source_target_pairs={{0,4},{4,0},{1,5},{5,1},{2,6},{6,2},{3,7},{7,3},{8,12},{12,8},{9,1... | collective-permute-start | bytes 589832 | tf_op jit(solution)/shard_map/ppermute | solution.py:367
  3.8 55.6 %copy-start.1 = (bf16[4096,512]{1,0:T(8,128)(2,1)S(1)}, bf16[4096,512]{1,0:T(8,128)(2,1)}, u32[]{:S(2)}) copy-start(bf16[4096,512]{1,0:T(8,128)(2,1)} %values.1) | copy-start | bytes 12582916
  5.7 53.7 %copy-start = (bf16[4096,512]{1,0:T(8,128)(2,1)S(1)}, bf16[4096,512]{1,0:T(8,128)(2,1)}, u32[]{:S(2)}) copy-start(bf16[4096,512]{1,0:T(8,128)(2,1)} %keys.1) | copy-start | bytes 12582916
  48.9 10.5 %copy-start.2 = (f32[2,512]{1,0:T(2,128)S(1)}, f32[2,512]{1,0:T(2,128)}, u32[]{:S(2)}) copy-start(f32[2,512]{1,0:T(2,128)} %gains.3) | copy-start | bytes 12292
  48.9 13.7 %collective-permute-start.2 = (bf16[16,16,5376]{2,1,0:T(8,128)(2,1)S(1)}, bf16[16,16,5376]{2,1,0:T(8,128)(2,1)S(1)}, u32[]{:S(2)}, u32[]{:S(2)}) collective-permute-start(bf16[16,16,5376]{2,1,0:T(8,128)(2,1)S(1)} %all_to_all.30.got.own), channel_id=1, source_target_pairs={{0,4},{4,0},{1,5},{5,1},{2,6},{6,2},{3,7},{7,3},{8,12},{12,8},{9,1... | collective-permute-start | bytes 8257544 | tf_op jit(solution)/shard_map/ppermute | solution.py:411
  51.1 11.6 %collective-permute-start.3 = (bf16[16,16,1536]{2,1,0:T(8,128)(2,1)S(1)}, bf16[16,16,1536]{2,1,0:T(8,128)(2,1)S(1)}, u32[]{:S(2)}, u32[]{:S(2)}) collective-permute-start(bf16[16,16,1536]{2,1,0:T(8,128)(2,1)S(1)} %get-tuple-element.17.own), channel_id=1, source_target_pairs={{0,4},{4,0},{1,5},{5,1},{2,6},{6,2},{3,7},{7,3},{8,12},{12,8},{9,1... | collective-permute-start | bytes 2359304 | tf_op jit(solution)/shard_map/ppermute | solution.py:432
  51.2 19.7 %collective-permute-start.4 = (bf16[16,16,1536]{2,1,0:T(8,128)(2,1)S(1)}, bf16[16,16,1536]{2,1,0:T(8,128)(2,1)S(1)}, u32[]{:S(2)}, u32[]{:S(2)}) collective-permute-start(bf16[16,16,1536]{2,1,0:T(8,128)(2,1)S(1)} %get-tuple-element.17.own), channel_id=1, source_target_pairs={{0,32},{32,0},{1,33},{33,1},{2,34},{34,2},{3,35},{35,3},{4,36},{36... | collective-permute-start | bytes 2359304 | tf_op jit(solution)/shard_map/ppermute | solution.py:433
  70.9 18.6 %collective-permute-start.5 = (bf16[16,16,1536]{2,1,0:T(8,128)(2,1)S(1)}, bf16[16,16,1536]{2,1,0:T(8,128)(2,1)S(1)}, u32[]{:S(2)}, u32[]{:S(2)}) collective-permute-start(bf16[16,16,1536]{2,1,0:T(8,128)(2,1)S(1)} %hold.1.near), channel_id=1, source_target_pairs={{0,4},{4,0},{1,5},{5,1},{2,6},{6,2},{3,7},{7,3},{8,12},{12,8},{9,1... | collective-permute-start | bytes 2359304 | tf_op jit(solution)/shard_map/ppermute | solution.py:482

commit v10 on v9

--- a/solution.py
+++ b/solution.py
@@ -82,11 +82,19 @@
         weights = jnp.concatenate([wbuf[0, g], wbuf[1, g]], axis=0)
         part = jnp.dot(chosen, weights, preferred_element_type=F32).astype(BF16)
         out[:, :, g * width : (g + 1) * width] = part.reshape(blocks, rows, width)
-    at = 3 * width
-    out[:, :, at : at + lanes] = chosen.reshape(blocks, rows, lanes)
-    at += lanes
     for copy in copies[4:]:
         copy.wait()
+    at = 3 * width
+    x = lax.axis_index("x")
+    both = jnp.concatenate([nbuf[0:1, :], nbuf[1:2, :]], axis=1)
+    high = both.astype(BF16).astype(F32)
+    rest = jnp.zeros((rows - 6, lanes), F32)
+    for b in range(blocks):
+        low = pl.multiple_of((2 * b + core) * rows + x // 2 * 8, 8)
+        pair = rows_buf[pl.ds(low, 8), :]
+        own = jnp.where(lax.rem(x, 2) == 0, pair[:4], pair[4:])
+        out[b, :, at : at + lanes] = jnp.concatenate([own, high, both - high, rest], axis=0).astype(BF16)
+    at += lanes
     steps = feats // rows
     for part in range(3):
         for i in range(steps):
@@ -95,21 +103,12 @@
                 cols = slice(b * lanes, (b + 1) * lanes)
                 out[b, :, at : at + lanes] = dbuf[low, cols] if part == 2 else gbuf[part, low, cols]
             at += lanes
-    both = jnp.concatenate([nbuf[0:1, :], nbuf[1:2, :]], axis=1)
-    high = both.astype(BF16).astype(F32)
-    tile = jnp.concatenate([high, both - high, jnp.zeros((rows - 2, lanes), F32)], axis=0).astype(BF16)
     for b in range(blocks):
         for i in range(steps):
             out[b, :, at + i * width : at + (i + 1) * width] = obuf[i * rows : (i + 1) * rows]
-        out[b, :, at + steps * width :] = tile
-
-
-def quarter(ref, x):
-    pair = ref[pl.ds(pl.multiple_of(x // 2 * 8, 8), 8), :]
-    return jnp.where(lax.rem(x, 2) == 0, pair[:4], pair[4:])
-
-
-def collect_kernel(got, qk, value, squares, rest, ffn, buf, rest_buf, sem):
+
+
+def collect_kernel(got, qk, value, squares, rest, ffn, buf, sem):
     rows, width = value.shape
     at = buf.shape[2]
     first = pltpu.make_async_copy(got.at[:, :, pl.ds(0, at)], buf, sem.at[0])
@@ -134,8 +133,7 @@
         squares[i] = both
     lanes = at - 3 * width
     for i in range(buf.shape[0]):
-        rest_buf[:, i * lanes : (i + 1) * lanes] = buf[i, :, 3 * width :].astype(F32)
-    rest[...] = quarter(rest_buf, lax.axis_index("x"))
+        rest[:, i * lanes : (i + 1) * lanes] = buf[i, :, 3 * width :].astype(F32)[:4]
     second.wait()
 
 
@@ -226,19 +224,20 @@
         finish(blocks)
 
 
-def out_kernel(attended, own, mate, after, partial, gain_out, wbuf, sem):
+def out_kernel(attended, own, mate, after, partial, gain_out, wbuf, gbuf, sem):
     rows, width = attended.shape
     core = lax.axis_index("c")
     last = pl.ds(own.shape[2] - wbuf.shape[3], wbuf.shape[3])
-    copies = [
-        pltpu.make_async_copy(got.at[:, :, last], wbuf.at[place], sem.at[i])
-        for i, (got, place) in enumerate(((own, core), (mate, 1 - core)))
-    ]
+    head = pl.ds(3 * width, gbuf.shape[3])
+    copies = []
+    for i, (got, place) in enumerate(((own, core), (mate, 1 - core))):
+        copies.append(pltpu.make_async_copy(got.at[:, :, last], wbuf.at[place], sem.at[i, 0]))
+        copies.append(pltpu.make_async_copy(got.at[:, :, head], gbuf.at[place], sem.at[i, 1]))
     for copy in copies:
         copy.start()
     for copy in copies:
         copy.wait()
-    steps = (wbuf.shape[3] - 128) // width
+    steps = wbuf.shape[3] // width
     mine = rows // NX
     for b in range(NZ):
         weights = jnp.concatenate(
@@ -254,8 +253,8 @@
         for x in range(NX):
             partial[x, :, b * width : (b + 1) * width] = a[x * mine : (x + 1) * mine]
         for y in range(NY):
-            two = [wbuf[c, b * NY + y, 0:8, steps * width :].astype(F32) for c in range(NC)]
-            two = [t[0:1] + t[1:2] for t in two]
+            two = [gbuf[c, b * NY + y].astype(F32) for c in range(NC)]
+            two = [t[4:5] + t[5:6] for t in two]
             for g in range(2):
                 gain_out[b, g : g + 1, y * 128 : (y + 1) * 128] = jnp.concatenate(
                     [t[:, g * 64 : (g + 1) * 64] for t in two], axis=1
@@ -386,7 +385,7 @@
     lanes = 128
     head_lanes = 3 * width + lanes
     tile_lanes = 3 * feats // rows * lanes
-    out_lanes = feats // rows * width + lanes
+    out_lanes = feats // rows * width
     message = call(
         project_kernel,
         shape((places, rows, head_lanes + tile_lanes + out_lanes), BF16),
@@ -422,7 +421,6 @@
         (VMEM,) * 4 + (ANY,),
         [
             pltpu.VMEM((places, rows, head_lanes), BF16),
-            pltpu.VMEM((rows, model), F32),
             pltpu.SemaphoreType.DMA((2,)),
         ],
         (1 << 20, 4 << 20),
@@ -449,7 +447,8 @@
         (VMEM,) * 2,
         [
             pltpu.VMEM((NC, places, rows, out_lanes), BF16),
-            pltpu.SemaphoreType.DMA((2,)),
+            pltpu.VMEM((NC, places, rows, lanes), BF16),
+            pltpu.SemaphoreType.DMA((2, 2)),
         ],
         (1 << 26, 2 << 20),
         "project_out",

time: 124 us -> 123 us (level)
  blocking collectives: 107 us -> 105 us
  Pallas kernels: 9.44 us -> 7.92 us
  starting transfers between devices: 4.77 us -> 6.27 us
    pallas_call x1, Pallas kernels: 3.25 us -> 1.69 us  [body(): call(attend_kernel, (shape((rows, width), BF16), shape((rows, width), BF1...]
  transfers between devices with their start and end apart: 6 -> 6, of which waited for: 2 -> 3; matrix products, arithmetic and copies ran while one was open for 1% -> 1% of each run, Pallas kernels for 4% -> 3%
where the time goes in v10:
time: 123 us
  blocking collectives  105 us (85%)
  Pallas kernels  7.92 us (6%)
  starting transfers between devices  6.27 us (5%)
    all_to_all x1, blocking collectives, body(): got = lax.all_to_all(message, Z + ('y',), 0, 0, tiled=True)  42.5 us
    all_to_all x1, blocking collectives, body(): got = lax.all_to_all(message, group, 0, 0, tiled=True)  16.7 us
    all_to_all x1, blocking collectives, body(): hidden = lax.all_to_all(message, Z + ('y', 'c', 'x'), 0, 0, tiled=True)  16.4 us
    all_to_all x1, blocking collectives, body(): got = lax.all_to_all(partial, group, 0, 0, tiled=True)  14.7 us
    all_to_all x1, blocking collectives, body(): squares = lax.all_to_all(squares, 'x', 0, 0, tiled=True)  8.1 us
    all_to_all x1, blocking collectives, body(): summed = lax.all_to_all(partial, 'x', 0, 0, tiled=True)  7.21 us
    ppermute x1, starting transfers between devices, body(): near_mate = lax.ppermute(near, 'c', ring(1, NC))  2.96 us
  transfers between devices with their start and end apart: 6, of which 3 were waited for; matrix products, arithmetic and copies ran while one was open for 1% of the time, Pallas kernels for 3%

profile of v10, /device:TPU:1, one launch (start us, length us, event | category | flops | bytes accessed | tf_op | source)
XLA Modules:
  0.0 122.6 jit_solution(9964668840233695375)
XLA Ops:
  0.6 1.5 %collective-permute-start = (bf16[64,512]{1,0:T(8,128)(2,1)}, bf16[64,512]{1,0:T(8,128)(2,1)S(1)}, u32[]{:S(2)}, u32[]{:S(2)}) collective-permute-start(bf16[64,512]{1,0:T(8,128)(2,1)} %bitcast.2), channel_id=1, source_target_pairs={{0,4},{4,0},{1,5},{5,1},{2,6},{6,2},{3,7},{7,3},{8,12},{12,8},{9,1... | collective-permute-start | bytes 196616 | tf_op jit(solution)/shard_map/ppermute | solution.py:365
  2.1 0.1 collective-permute-start.1
  2.2 0.7 convert_element_type.5
  2.9 0.2 multiply_cosine_fusion
  3.1 0.1 collective-permute-done.h_mate
  3.2 0.5 collective-permute-done.1.w_mate
  3.8 0.0 copy-start.1
  3.8 1.9 %project.1 = bf16[16,16,5248]{2,1,0:T(8,128)(2,1)S(1)} custom-call(bf16[64,512]{1,0:T(8,128)(2,1)} %bitcast.3, bf16[64,512]{1,0:T(8,128)(2,1)S(1)} %collective-permute-done.h_mate, bf16[3,64,512]{2,1,0:T(8,128)(2,1)} %w_own.1, bf16[3,64,512]{2,1,0:T(8,128)(2,1)S(1)} %collective-permute-done.1.w_mate, bf16[2,64,2048]{2,1,0:T(8,128)(2,1)} %gate_up.1, ...), custom_call_target="tpu_custom_call" | custom-call | flops 134217728 | bytes 2097152 | tf_op jit(solution)/shard_map/project/pallas_call | solution.py:389
  5.7 0.0 copy-start
  5.7 42.5 %all_to_all.30.got.own = bf16[16,16,5248]{2,1,0:T(8,128)(2,1)S(1)} all-to-all(bf16[16,16,5248]{2,1,0:T(8,128)(2,1)S(1)} %project.1), channel_id=1, replica_groups=mesh['zh'=2,'zl'=2,'y'=4,'c'=2,'x'=4] {'zh','zl','y'}, dimensions={0} | all-to-all | bytes 5373952 | tf_op jit(solution)/shard_map/all_to_all | solution.py:408
  48.2 0.0 copy-start.2
  48.2 1.3 %collective-permute-start.2 = (bf16[16,16,5248]{2,1,0:T(8,128)(2,1)S(1)}, bf16[16,16,5248]{2,1,0:T(8,128)(2,1)S(1)}, u32[]{:S(2)}, u32[]{:S(2)}) collective-permute-start(bf16[16,16,5248]{2,1,0:T(8,128)(2,1)S(1)} %all_to_all.30.got.own), channel_id=1, source_target_pairs={{0,4},{4,0},{1,5},{5,1},{2,6},{6,2},{3,7},{7,3},{8,12},{12,8},{9,1... | collective-permute-start | bytes 8060936 | tf_op jit(solution)/shard_map/ppermute | solution.py:410
  49.5 0.9 collect.1
  50.4 0.1 collective-permute-start.3
  50.5 0.3 collective-permute-start.4
  50.8 8.1 %all_to_all.31.squares_in = f32[4,16,128]{2,1,0:T(8,128)S(1)} all-to-all(f32[4,16,128]{2,1,0:T(8,128)S(1)} %get-tuple-element.14), channel_id=1, replica_groups=mesh['zh'=2,'zl'=2,'y'=4,'c'=2,'x'=4] {'x'}, dimensions={0} | all-to-all | bytes 65536 | tf_op jit(solution)/shard_map/all_to_all | solution.py:432
  58.9 0.0 copy-done.1
  58.9 0.0 copy-done
  58.9 0.0 copy-done.2
  58.9 1.7 %attend.1 = (bf16[16,512]{1,0:T(8,128)(2,1)}, bf16[16,512]{1,0:T(8,128)(2,1)S(1)}) custom-call(f32[4,16,128]{2,1,0:T(8,128)S(1)} %all_to_all.31.squares_in, f32[3,16,512]{2,1,0:T(8,128)S(1)} %get-tuple-element.15.qk, f32[128,128]{1,0:T(8,128)S(1)} %pad_maximum_fusion.trig, f32[8,128]{1,0:T(8,128)S(1)} %broadcast_in_dim.2.places, f32[2,512]{1,0:T(2,128)S(1)} %copy-done.2, ...), custom_call_target="tpu_custom_call" | custom-call | flops 536870912 | bytes 8388608 | tf_op jit(solution)/shard_map/attend/pallas_call | solution.py:433
  60.6 0.0 collective-permute-done.3.after.own_mate
  60.6 0.0 collective-permute-done.2.mate
  60.6 0.9 project_out.1
  61.5 7.2 %all_to_all.32.got = f32[4,4,2048]{2,1,0:T(4,128)S(1)} all-to-all(f32[4,4,2048]{2,1,0:T(4,128)S(1)} %get-tuple-element.18), channel_id=1, replica_groups=mesh['zh'=2,'zl'=2,'y'=4,'c'=2,'x'=4] {'x'}, dimensions={0} | all-to-all | bytes 262144 | tf_op jit(solution)/shard_map/all_to_all | solution.py:458
  68.7 0.1 fan.1
  68.9 0.4 collective-permute-done.4.piece
  69.3 0.1 hold.1.near
  69.3 3.0 %collective-permute-start.5 = (bf16[16,16,1536]{2,1,0:T(8,128)(2,1)S(1)}, bf16[16,16,1536]{2,1,0:T(8,128)(2,1)S(1)}, u32[]{:S(2)}, u32[]{:S(2)}) collective-permute-start(bf16[16,16,1536]{2,1,0:T(8,128)(2,1)S(1)} %hold.1.near), channel_id=1, source_target_pairs={{0,4},{4,0},{1,5},{5,1},{2,6},{6,2},{3,7},{7,3},{8,12},{12,8},{9,1... | collective-permute-start | bytes 2359304 | tf_op jit(solution)/shard_map/ppermute | solution.py:481
  72.3 16.7 %all_to_all.33.got = bf16[32,8,1024]{2,1,0:T(8,128)(2,1)S(1)} all-to-all(bf16[32,8,1024]{2,1,0:T(8,128)(2,1)S(1)} %get-tuple-element.21), channel_id=1, replica_groups=mesh['zh'=2,'zl'=2,'y'=4,'c'=2,'x'=4] {'zh','y','x'}, dimensions={0} | all-to-all | bytes 1048576 | tf_op jit(solution)/shard_map/all_to_all | solution.py:482
  89.0 0.0 collective-permute-done.5.near_mate
  89.0 1.4 %feed_forward.1 = bf16[32,8,1024]{2,1,0:T(8,128)(2,1)S(1)} custom-call(bf16[32,8,1024]{2,1,0:T(8,128)(2,1)S(1)} %all_to_all.33.got, bf16[16,16,1536]{2,1,0:T(8,128)(2,1)S(1)} %get-tuple-element.17.own, bf16[16,16,1536]{2,1,0:T(8,128)(2,1)S(1)} %collective-permute-done.3.after.own_mate, bf16[16,16,1536]{2,1,0:T(8,128)(2,1)S(1)} %hold.1.near, ...), custom_call_target="tpu_custom_call" | custom-call | flops 268435456 | bytes 4194304 | tf_op jit(solution)/shard_map/feed_forward/pallas_call | solution.py:483
  90.3 14.7 %all_to_all.34.got = bf16[32,8,1024]{2,1,0:T(8,128)(2,1)S(1)} all-to-all(bf16[32,8,1024]{2,1,0:T(8,128)(2,1)S(1)} %feed_forward.1), channel_id=1, replica_groups=mesh['zh'=2,'zl'=2,'y'=4,'c'=2,'x'=4] {'zh','y','x'}, dimensions={0} | all-to-all | bytes 1048576 | tf_op jit(solution)/shard_map/all_to_all | solution.py:496
  105.0 0.3 finish.1
  105.3 0.1 reshape.13
  105.4 16.4 %all_to_all.35 = bf16[128,2,128]{2,1,0:T(2,128)(2,1)S(1)} all-to-all(bf16[128,2,128]{2,1,0:T(2,128)(2,1)S(1)} %reshape.13), channel_id=1, replica_groups=mesh['zh'=2,'zl'=2,'y'=4,'c'=2,'x'=4] {'zh','zl','y','c','x'}, dimensions={0} | all-to-all | bytes 131072 | tf_op jit(solution)/shard_map/all_to_all | solution.py:506
  121.7 0.1 reshape.14.got
  121.8 0.7 turn.1
  (4 shorter events, 0.0 us)
Async XLA Ops:
  0.6 2.6 %collective-permute-start = (bf16[64,512]{1,0:T(8,128)(2,1)}, bf16[64,512]{1,0:T(8,128)(2,1)S(1)}, u32[]{:S(2)}, u32[]{:S(2)}) collective-permute-start(bf16[64,512]{1,0:T(8,128)(2,1)} %bitcast.2), channel_id=1, source_target_pairs={{0,4},{4,0},{1,5},{5,1},{2,6},{6,2},{3,7},{7,3},{8,12},{12,8},{9,1... | collective-permute-start | bytes 196616 | tf_op jit(solution)/shard_map/ppermute | solution.py:365
  2.1 1.7 %collective-permute-start.1 = (bf16[3,64,512]{2,1,0:T(8,128)(2,1)}, bf16[3,64,512]{2,1,0:T(8,128)(2,1)S(1)}, u32[]{:S(2)}, u32[]{:S(2)}) collective-permute-start(bf16[3,64,512]{2,1,0:T(8,128)(2,1)} %w_own.1), channel_id=1, source_target_pairs={{0,4},{4,0},{1,5},{5,1},{2,6},{6,2},{3,7},{7,3},{8,12},{12,8},{9,1... | collective-permute-start | bytes 589832 | tf_op jit(solution)/shard_map/ppermute | solution.py:366
  3.8 55.1 %copy-start.1 = (bf16[4096,512]{1,0:T(8,128)(2,1)S(1)}, bf16[4096,512]{1,0:T(8,128)(2,1)}, u32[]{:S(2)}) copy-start(bf16[4096,512]{1,0:T(8,128)(2,1)} %values.1) | copy-start | bytes 12582916
  5.7 53.2 %copy-start = (bf16[4096,512]{1,0:T(8,128)(2,1)S(1)}, bf16[4096,512]{1,0:T(8,128)(2,1)}, u32[]{:S(2)}) copy-start(bf16[4096,512]{1,0:T(8,128)(2,1)} %keys.1) | copy-start | bytes 12582916
  48.2 10.7 %copy-start.2 = (f32[2,512]{1,0:T(2,128)S(1)}, f32[2,512]{1,0:T(2,128)}, u32[]{:S(2)}) copy-start(f32[2,512]{1,0:T(2,128)} %gains.3) | copy-start | bytes 12292
  48.2 12.4 %collective-permute-start.2 = (bf16[16,16,5248]{2,1,0:T(8,128)(2,1)S(1)}, bf16[16,16,5248]{2,1,0:T(8,128)(2,1)S(1)}, u32[]{:S(2)}, u32[]{:S(2)}) collective-permute-start(bf16[16,16,5248]{2,1,0:T(8,128)(2,1)S(1)} %all_to_all.30.got.own), channel_id=1, source_target_pairs={{0,4},{4,0},{1,5},{5,1},{2,6},{6,2},{3,7},{7,3},{8,12},{12,8},{9,1... | collective-permute-start | bytes 8060936 | tf_op jit(solution)/shard_map/ppermute | solution.py:410
  50.4 10.2 %collective-permute-start.3 = (bf16[16,16,1536]{2,1,0:T(8,128)(2,1)S(1)}, bf16[16,16,1536]{2,1,0:T(8,128)(2,1)S(1)}, u32[]{:S(2)}, u32[]{:S(2)}) collective-permute-start(bf16[16,16,1536]{2,1,0:T(8,128)(2,1)S(1)} %get-tuple-element.17.own), channel_id=1, source_target_pairs={{0,4},{4,0},{1,5},{5,1},{2,6},{6,2},{3,7},{7,3},{8,12},{12,8},{9,1... | collective-permute-start | bytes 2359304 | tf_op jit(solution)/shard_map/ppermute | solution.py:430
  50.5 18.8 %collective-permute-start.4 = (bf16[16,16,1536]{2,1,0:T(8,128)(2,1)S(1)}, bf16[16,16,1536]{2,1,0:T(8,128)(2,1)S(1)}, u32[]{:S(2)}, u32[]{:S(2)}) collective-permute-start(bf16[16,16,1536]{2,1,0:T(8,128)(2,1)S(1)} %get-tuple-element.17.own), channel_id=1, source_target_pairs={{0,32},{32,0},{1,33},{33,1},{2,34},{34,2},{3,35},{35,3},{4,36},{36... | collective-permute-start | bytes 2359304 | tf_op jit(solution)/shard_map/ppermute | solution.py:431
  69.3 19.6 %collective-permute-start.5 = (bf16[16,16,1536]{2,1,0:T(8,128)(2,1)S(1)}, bf16[16,16,1536]{2,1,0:T(8,128)(2,1)S(1)}, u32[]{:S(2)}, u32[]{:S(2)}) collective-permute-start(bf16[16,16,1536]{2,1,0:T(8,128)(2,1)S(1)} %hold.1.near), channel_id=1, source_target_pairs={{0,4},{4,0},{1,5},{5,1},{2,6},{6,2},{3,7},{7,3},{8,12},{12,8},{9,1... | collective-permute-start | bytes 2359304 | tf_op jit(solution)/shard_map/ppermute | solution.py:481

commit v11 on v10

--- a/solution.py
+++ b/solution.py
@@ -108,17 +108,16 @@
             out[b, :, at + i * width : at + (i + 1) * width] = obuf[i * rows : (i + 1) * rows]
 
 
-def collect_kernel(got, qk, value, squares, rest, ffn, buf, sem):
+def collect_kernel(got, qk, value, squares, rest, ffn, sem):
     rows, width = value.shape
-    at = buf.shape[2]
-    first = pltpu.make_async_copy(got.at[:, :, pl.ds(0, at)], buf, sem.at[0])
-    second = pltpu.make_async_copy(got.at[:, :, pl.ds(at, ffn.shape[2])], ffn, sem.at[1])
-    first.start()
-    second.start()
-    first.wait()
-    total = buf[0, :, : 3 * width].astype(F32)
-    for i in range(1, buf.shape[0]):
-        total += buf[i, :, : 3 * width].astype(F32)
+    lanes = 128
+    at = 3 * width + lanes
+    copy = pltpu.make_async_copy(got.at[:, :, pl.ds(at, ffn.shape[2])], ffn, sem)
+    copy.start()
+    blocks = got.shape[0]
+    total = got[0, :, : 3 * width].astype(F32)
+    for i in range(1, blocks):
+        total += got[i, :, : 3 * width].astype(F32)
     q, k = total[:, :width], total[:, width : 2 * width]
     qk[0] = q
     qk[1] = k
@@ -131,10 +130,9 @@
     )
     for i in range(NX):
         squares[i] = both
-    lanes = at - 3 * width
-    for i in range(buf.shape[0]):
-        rest[:, i * lanes : (i + 1) * lanes] = buf[i, :, 3 * width :].astype(F32)[:4]
-    second.wait()
+    for i in range(blocks):
+        rest[:, i * lanes : (i + 1) * lanes] = got[i, :, 3 * width : at].astype(F32)[:4]
+    copy.wait()
 
 
 def turn(values, cosine, sine):
@@ -224,41 +222,49 @@
         finish(blocks)
 
 
-def out_kernel(attended, own, mate, after, partial, gain_out, wbuf, gbuf, sem):
+def by_core(work, own, mate):
+    core = lax.axis_index("c")
+
+    @pl.when(core == 0)
+    def _():
+        work(own, mate)
+
+    @pl.when(core == 1)
+    def _():
+        work(mate, own)
+
+
+def out_kernel(attended, own, mate, after, partial, gain_out):
     rows, width = attended.shape
-    core = lax.axis_index("c")
-    last = pl.ds(own.shape[2] - wbuf.shape[3], wbuf.shape[3])
-    head = pl.ds(3 * width, gbuf.shape[3])
-    copies = []
-    for i, (got, place) in enumerate(((own, core), (mate, 1 - core))):
-        copies.append(pltpu.make_async_copy(got.at[:, :, last], wbuf.at[place], sem.at[i, 0]))
-        copies.append(pltpu.make_async_copy(got.at[:, :, head], gbuf.at[place], sem.at[i, 1]))
-    for copy in copies:
-        copy.start()
-    for copy in copies:
-        copy.wait()
-    steps = wbuf.shape[3] // width
+    head = 3 * width
+    lanes = 128
+    steps = 4
+    last = own.shape[2] - steps * width
     mine = rows // NX
-    for b in range(NZ):
-        weights = jnp.concatenate(
-            [
-                wbuf[c, b * NY + y, :, i * width : (i + 1) * width]
-                for y in range(NY)
-                for c in range(NC)
-                for i in range(steps)
-            ],
-            axis=0,
-        )
-        a = lax.dot_general(attended[...], weights, NT, preferred_element_type=F32)
-        for x in range(NX):
-            partial[x, :, b * width : (b + 1) * width] = a[x * mine : (x + 1) * mine]
-        for y in range(NY):
-            two = [gbuf[c, b * NY + y].astype(F32) for c in range(NC)]
-            two = [t[4:5] + t[5:6] for t in two]
-            for g in range(2):
-                gain_out[b, g : g + 1, y * 128 : (y + 1) * 128] = jnp.concatenate(
-                    [t[:, g * 64 : (g + 1) * 64] for t in two], axis=1
-                )
+
+    def work(*cores):
+        for b in range(NZ):
+            weights = jnp.concatenate(
+                [
+                    cores[c][b * NY + y, :, last + i * width : last + (i + 1) * width]
+                    for y in range(NY)
+                    for c in range(NC)
+                    for i in range(steps)
+                ],
+                axis=0,
+            )
+            a = lax.dot_general(attended[...], weights, NT, preferred_element_type=F32)
+            for x in range(NX):
+                partial[x, :, b * width : (b + 1) * width] = a[x * mine : (x + 1) * mine]
+            for y in range(NY):
+                two = [cores[c][b * NY + y, :, head : head + lanes].astype(F32) for c in range(NC)]
+                two = [t[4:5] + t[5:6] for t in two]
+                for g in range(2):
+                    gain_out[b, g : g + 1, y * lanes : (y + 1) * lanes] = jnp.concatenate(
+                        [t[:, g * 64 : (g + 1) * 64] for t in two], axis=1
+                    )
+
+    by_core(work, own, mate)
 
 
 def fan_kernel(got, rest, gains, own_mid, out):
@@ -274,16 +280,7 @@
         out[i] = message
 
 
-def ffn_kernel(got, own, own_mate, near, near_mate, out, wbuf, sem):
-    core = lax.axis_index("c")
-    copies = [
-        pltpu.make_async_copy(own, wbuf.at[0, core], sem.at[0]),
-        pltpu.make_async_copy(own_mate, wbuf.at[0, 1 - core], sem.at[1]),
-        pltpu.make_async_copy(near, wbuf.at[1, core], sem.at[2]),
-        pltpu.make_async_copy(near_mate, wbuf.at[1, 1 - core], sem.at[3]),
-    ]
-    for copy in copies:
-        copy.start()
+def ffn_kernel(got, own, own_mate, near, near_mate, out):
     places, lines, span = got.shape
     mine = lines // 2
     whole = [got[d].astype(F32) for d in range(places)]
@@ -291,38 +288,39 @@
         jnp.concatenate([w[half * mine : (half + 1) * mine] for w in whole], axis=0).astype(BF16)
         for half in range(2)
     ]
-    blocks = wbuf.shape[2]
+    blocks = own.shape[0]
     lanes = 128
-    steps = wbuf.shape[4] // (3 * lanes)
-    for copy in copies:
-        copy.wait()
-
-    def weights(part, half):
-        rows = range(half * blocks // 2, (half + 1) * blocks // 2)
-        return jnp.concatenate(
-            [
-                jnp.concatenate(
-                    [
-                        wbuf[p, c, b, :, (part * steps + i) * lanes : (part * steps + i + 1) * lanes]
-                        for b in rows
-                        for c in range(NC)
-                        for i in range(steps)
-                    ],
-                    axis=0,
-                )
-                for p in range(2)
-            ],
-            axis=1,
-        )
-
-    gate = jnp.dot(mid[0], weights(0, 0), preferred_element_type=F32)
-    gate += jnp.dot(mid[1], weights(0, 1), preferred_element_type=F32)
-    lift = jnp.dot(mid[0], weights(1, 0), preferred_element_type=F32)
-    lift += jnp.dot(mid[1], weights(1, 1), preferred_element_type=F32)
-    act = (gate / (1.0 + jnp.exp(-gate)) * lift).astype(BF16)
-    flat = [lax.dot_general(act, weights(2, h), NT, preferred_element_type=F32) for h in range(2)]
-    for d in range(places):
-        out[d] = jnp.concatenate([f[d * mine : (d + 1) * mine] for f in flat], axis=0).astype(BF16)
+    steps = own.shape[2] // (3 * lanes)
+
+    def work(*cores):
+        def weights(part, half):
+            rows = range(half * blocks // 2, (half + 1) * blocks // 2)
+            return jnp.concatenate(
+                [
+                    jnp.concatenate(
+                        [
+                            cores[c][p][b, :, (part * steps + i) * lanes : (part * steps + i + 1) * lanes]
+                            for b in rows
+                            for c in range(NC)
+                            for i in range(steps)
+                        ],
+                        axis=0,
+                    )
+                    for p in range(2)
+                ],
+                axis=1,
+            )
+
+        gate = jnp.dot(mid[0], weights(0, 0), preferred_element_type=F32)
+        gate += jnp.dot(mid[1], weights(0, 1), preferred_element_type=F32)
+        lift = jnp.dot(mid[0], weights(1, 0), preferred_element_type=F32)
+        lift += jnp.dot(mid[1], weights(1, 1), preferred_element_type=F32)
+        act = (gate / (1.0 + jnp.exp(-gate)) * lift).astype(BF16)
+        flat = [lax.dot_general(act, weights(2, h), NT, preferred_element_type=F32) for h in range(2)]
+        for d in range(places):
+            out[d] = jnp.concatenate([f[d * mine : (d + 1) * mine] for f in flat], axis=0).astype(BF16)
+
+    by_core(work, (own, near), (own_mate, near_mate))
 
 
 def finish_kernel(got, own_mid, gains, out):
@@ -417,12 +415,9 @@
             shape((rows // NX, model), F32),
             shape((places, rows, tile_lanes), BF16),
         ),
-        [ANY],
+        [VMEM],
         (VMEM,) * 4 + (ANY,),
-        [
-            pltpu.VMEM((places, rows, head_lanes), BF16),
-            pltpu.SemaphoreType.DMA((2,)),
-        ],
+        [pltpu.SemaphoreType.DMA],
         (1 << 20, 4 << 20),
         "collect",
         8,
@@ -443,13 +438,9 @@
     partial, gains = call(
         out_kernel,
         (shape((NX, rows // NX, model), F32), shape((NZ, 8, width), F32)),
-        [VMEM] + [ANY] * 3,
+        [VMEM] * 3 + [ANY],
         (VMEM,) * 2,
-        [
-            pltpu.VMEM((NC, places, rows, out_lanes), BF16),
-            pltpu.VMEM((NC, places, rows, lanes), BF16),
-            pltpu.SemaphoreType.DMA((2, 2)),
-        ],
+        (),
         (1 << 26, 2 << 20),
         "project_out",
         8,
@@ -483,12 +474,9 @@
     partial = call(
         ffn_kernel,
         shape((members, 2 * mine, model // 2), BF16),
-        [VMEM] + [ANY] * 4,
+        [VMEM] * 5,
         VMEM,
-        [
-            pltpu.VMEM((2, NC) + ffn_own.shape, BF16),
-            pltpu.SemaphoreType.DMA((4,)),
-        ],
+        (),
         (1 << 28, 4 << 20),
         "feed_forward",
         16,

time: 123 us -> 123 us (level)
  no operation moved by 1% of the time
where the time goes in v11:
time: 123 us
  blocking collectives  106 us (86%)
  Pallas kernels  7.35 us (6%)
  starting transfers between devices  6.03 us (5%)
  waiting for transfers between devices  1.32 us (1%)
    all_to_all x1, blocking collectives, body(): got = lax.all_to_all(message, Z + ('y',), 0, 0, tiled=True)  42.5 us
    all_to_all x1, blocking collectives, body(): hidden = lax.all_to_all(message, Z + ('y', 'c', 'x'), 0, 0, tiled=True)  17.1 us
    all_to_all x1, blocking collectives, body(): got = lax.all_to_all(message, group, 0, 0, tiled=True)  16.7 us
    all_to_all x1, blocking collectives, body(): got = lax.all_to_all(partial, group, 0, 0, tiled=True)  14.6 us
    all_to_all x1, blocking collectives, body(): squares = lax.all_to_all(squares, 'x', 0, 0, tiled=True)  8.1 us
    all_to_all x1, blocking collectives, body(): summed = lax.all_to_all(partial, 'x', 0, 0, tiled=True)  7.21 us
    ppermute x1, starting transfers between devices, body(): near_mate = lax.ppermute(near, 'c', ring(1, NC))  2.73 us
  transfers between devices with their start and end apart: 6, of which 3 were waited for; matrix products, arithmetic and copies ran while one was open for 1% of the time, Pallas kernels for 3%

profile of v11, /device:TPU:1, one launch (start us, length us, event | category | flops | bytes accessed | tf_op | source)
XLA Modules:
  0.0 122.8 jit_solution(9270297551197009035)
XLA Ops:
  0.6 1.5 %collective-permute-start = (bf16[64,512]{1,0:T(8,128)(2,1)}, bf16[64,512]{1,0:T(8,128)(2,1)S(1)}, u32[]{:S(2)}, u32[]{:S(2)}) collective-permute-start(bf16[64,512]{1,0:T(8,128)(2,1)} %bitcast.2), channel_id=1, source_target_pairs={{0,4},{4,0},{1,5},{5,1},{2,6},{6,2},{3,7},{7,3},{8,12},{12,8},{9,1... | collective-permute-start | bytes 196616 | tf_op jit(solution)/shard_map/ppermute | solution.py:363
  2.1 0.1 collective-permute-start.1
  2.2 0.7 convert_element_type.5
  2.9 0.2 multiply_cosine_fusion
  3.1 0.1 collective-permute-done.h_mate
  3.2 0.5 collective-permute-done.1.w_mate
  3.8 0.0 copy-start.1
  3.8 1.9 %project.1 = bf16[16,16,5248]{2,1,0:T(8,128)(2,1)S(1)} custom-call(bf16[64,512]{1,0:T(8,128)(2,1)} %bitcast.3, bf16[64,512]{1,0:T(8,128)(2,1)S(1)} %collective-permute-done.h_mate, bf16[3,64,512]{2,1,0:T(8,128)(2,1)} %w_own.1, bf16[3,64,512]{2,1,0:T(8,128)(2,1)S(1)} %collective-permute-done.1.w_mate, bf16[2,64,2048]{2,1,0:T(8,128)(2,1)} %gate_up.1, ...), custom_call_target="tpu_custom_call" | custom-call | flops 134217728 | bytes 2097152 | tf_op jit(solution)/shard_map/project/pallas_call | solution.py:387
  5.7 0.0 copy-start
  5.7 42.5 %all_to_all.30.got.own = bf16[16,16,5248]{2,1,0:T(8,128)(2,1)S(1)} all-to-all(bf16[16,16,5248]{2,1,0:T(8,128)(2,1)S(1)} %project.1), channel_id=1, replica_groups=mesh['zh'=2,'zl'=2,'y'=4,'c'=2,'x'=4] {'zh','zl','y'}, dimensions={0} | all-to-all | bytes 5373952 | tf_op jit(solution)/shard_map/all_to_all | solution.py:406
  48.2 0.0 copy-start.2
  48.2 1.3 %collective-permute-start.2 = (bf16[16,16,5248]{2,1,0:T(8,128)(2,1)S(1)}, bf16[16,16,5248]{2,1,0:T(8,128)(2,1)S(1)}, u32[]{:S(2)}, u32[]{:S(2)}) collective-permute-start(bf16[16,16,5248]{2,1,0:T(8,128)(2,1)S(1)} %all_to_all.30.got.own), channel_id=1, source_target_pairs={{0,4},{4,0},{1,5},{5,1},{2,6},{6,2},{3,7},{7,3},{8,12},{12,8},{9,1... | collective-permute-start | bytes 8060936 | tf_op jit(solution)/shard_map/ppermute | solution.py:408
  49.5 0.8 collect.1
  50.3 0.1 collective-permute-start.3
  50.4 0.3 collective-permute-start.4
  50.7 8.1 %all_to_all.31.squares_in = f32[4,16,128]{2,1,0:T(8,128)S(1)} all-to-all(f32[4,16,128]{2,1,0:T(8,128)S(1)} %get-tuple-element.14), channel_id=1, replica_groups=mesh['zh'=2,'zl'=2,'y'=4,'c'=2,'x'=4] {'x'}, dimensions={0} | all-to-all | bytes 65536 | tf_op jit(solution)/shard_map/all_to_all | solution.py:427
  58.8 0.0 copy-done.1
  58.8 0.0 copy-done
  58.8 0.0 copy-done.2
  58.8 1.7 %attend.1 = (bf16[16,512]{1,0:T(8,128)(2,1)}, bf16[16,512]{1,0:T(8,128)(2,1)S(1)}) custom-call(f32[4,16,128]{2,1,0:T(8,128)S(1)} %all_to_all.31.squares_in, f32[3,16,512]{2,1,0:T(8,128)S(1)} %get-tuple-element.15.qk, f32[128,128]{1,0:T(8,128)S(1)} %pad_maximum_fusion.trig, f32[8,128]{1,0:T(8,128)S(1)} %broadcast_in_dim.2.places, f32[2,512]{1,0:T(2,128)S(1)} %copy-done.2, ...), custom_call_target="tpu_custom_call" | custom-call | flops 536870912 | bytes 8388608 | tf_op jit(solution)/shard_map/attend/pallas_call | solution.py:428
  60.5 0.0 collective-permute-done.3.after.own_mate
  60.5 0.0 collective-permute-done.2.mate
  60.5 0.7 project_out.1
  61.2 7.2 %all_to_all.32.got = f32[4,4,2048]{2,1,0:T(4,128)S(1)} all-to-all(f32[4,4,2048]{2,1,0:T(4,128)S(1)} %get-tuple-element.18), channel_id=1, replica_groups=mesh['zh'=2,'zl'=2,'y'=4,'c'=2,'x'=4] {'x'}, dimensions={0} | all-to-all | bytes 262144 | tf_op jit(solution)/shard_map/all_to_all | solution.py:449
  68.4 0.1 fan.1
  68.5 0.6 collective-permute-done.4.piece
  69.2 0.1 hold.1.near
  69.3 2.7 %collective-permute-start.5 = (bf16[16,16,1536]{2,1,0:T(8,128)(2,1)S(1)}, bf16[16,16,1536]{2,1,0:T(8,128)(2,1)S(1)}, u32[]{:S(2)}, u32[]{:S(2)}) collective-permute-start(bf16[16,16,1536]{2,1,0:T(8,128)(2,1)S(1)} %hold.1.near), channel_id=1, source_target_pairs={{0,4},{4,0},{1,5},{5,1},{2,6},{6,2},{3,7},{7,3},{8,12},{12,8},{9,1... | collective-permute-start | bytes 2359304 | tf_op jit(solution)/shard_map/ppermute | solution.py:472
  72.0 16.7 %all_to_all.33.got = bf16[32,8,1024]{2,1,0:T(8,128)(2,1)S(1)} all-to-all(bf16[32,8,1024]{2,1,0:T(8,128)(2,1)S(1)} %get-tuple-element.21), channel_id=1, replica_groups=mesh['zh'=2,'zl'=2,'y'=4,'c'=2,'x'=4] {'zh','y','x'}, dimensions={0} | all-to-all | bytes 1048576 | tf_op jit(solution)/shard_map/all_to_all | solution.py:473
  88.7 0.0 collective-permute-done.5.near_mate
  88.7 1.1 feed_forward.1
  89.8 14.6 %all_to_all.34.got = bf16[32,8,1024]{2,1,0:T(8,128)(2,1)S(1)} all-to-all(bf16[32,8,1024]{2,1,0:T(8,128)(2,1)S(1)} %feed_forward.1), channel_id=1, replica_groups=mesh['zh'=2,'zl'=2,'y'=4,'c'=2,'x'=4] {'zh','y','x'}, dimensions={0} | all-to-all | bytes 1048576 | tf_op jit(solution)/shard_map/all_to_all | solution.py:484
  104.5 0.3 finish.1
  104.8 0.1 reshape.13
  104.9 17.1 %all_to_all.35 = bf16[128,2,128]{2,1,0:T(2,128)(2,1)S(1)} all-to-all(bf16[128,2,128]{2,1,0:T(2,128)(2,1)S(1)} %reshape.13), channel_id=1, replica_groups=mesh['zh'=2,'zl'=2,'y'=4,'c'=2,'x'=4] {'zh','zl','y','c','x'}, dimensions={0} | all-to-all | bytes 131072 | tf_op jit(solution)/shard_map/all_to_all | solution.py:494
  122.0 0.1 reshape.14.got
  122.1 0.7 turn.1
  (4 shorter events, 0.0 us)
Async XLA Ops:
  0.6 2.6 %collective-permute-start = (bf16[64,512]{1,0:T(8,128)(2,1)}, bf16[64,512]{1,0:T(8,128)(2,1)S(1)}, u32[]{:S(2)}, u32[]{:S(2)}) collective-permute-start(bf16[64,512]{1,0:T(8,128)(2,1)} %bitcast.2), channel_id=1, source_target_pairs={{0,4},{4,0},{1,5},{5,1},{2,6},{6,2},{3,7},{7,3},{8,12},{12,8},{9,1... | collective-permute-start | bytes 196616 | tf_op jit(solution)/shard_map/ppermute | solution.py:363
  2.1 1.7 %collective-permute-start.1 = (bf16[3,64,512]{2,1,0:T(8,128)(2,1)}, bf16[3,64,512]{2,1,0:T(8,128)(2,1)S(1)}, u32[]{:S(2)}, u32[]{:S(2)}) collective-permute-start(bf16[3,64,512]{2,1,0:T(8,128)(2,1)} %w_own.1), channel_id=1, source_target_pairs={{0,4},{4,0},{1,5},{5,1},{2,6},{6,2},{3,7},{7,3},{8,12},{12,8},{9,1... | collective-permute-start | bytes 589832 | tf_op jit(solution)/shard_map/ppermute | solution.py:364
  3.8 55.0 %copy-start.1 = (bf16[4096,512]{1,0:T(8,128)(2,1)S(1)}, bf16[4096,512]{1,0:T(8,128)(2,1)}, u32[]{:S(2)}) copy-start(bf16[4096,512]{1,0:T(8,128)(2,1)} %values.1) | copy-start | bytes 12582916
  5.7 53.1 %copy-start = (bf16[4096,512]{1,0:T(8,128)(2,1)S(1)}, bf16[4096,512]{1,0:T(8,128)(2,1)}, u32[]{:S(2)}) copy-start(bf16[4096,512]{1,0:T(8,128)(2,1)} %keys.1) | copy-start | bytes 12582916
  48.2 10.6 %copy-start.2 = (f32[2,512]{1,0:T(2,128)S(1)}, f32[2,512]{1,0:T(2,128)}, u32[]{:S(2)}) copy-start(f32[2,512]{1,0:T(2,128)} %gains.3) | copy-start | bytes 12292
  48.2 12.3 %collective-permute-start.2 = (bf16[16,16,5248]{2,1,0:T(8,128)(2,1)S(1)}, bf16[16,16,5248]{2,1,0:T(8,128)(2,1)S(1)}, u32[]{:S(2)}, u32[]{:S(2)}) collective-permute-start(bf16[16,16,5248]{2,1,0:T(8,128)(2,1)S(1)} %all_to_all.30.got.own), channel_id=1, source_target_pairs={{0,4},{4,0},{1,5},{5,1},{2,6},{6,2},{3,7},{7,3},{8,12},{12,8},{9,1... | collective-permute-start | bytes 8060936 | tf_op jit(solution)/shard_map/ppermute | solution.py:408
  50.3 10.2 %collective-permute-start.3 = (bf16[16,16,1536]{2,1,0:T(8,128)(2,1)S(1)}, bf16[16,16,1536]{2,1,0:T(8,128)(2,1)S(1)}, u32[]{:S(2)}, u32[]{:S(2)}) collective-permute-start(bf16[16,16,1536]{2,1,0:T(8,128)(2,1)S(1)} %get-tuple-element.17.own), channel_id=1, source_target_pairs={{0,4},{4,0},{1,5},{5,1},{2,6},{6,2},{3,7},{7,3},{8,12},{12,8},{9,1... | collective-permute-start | bytes 2359304 | tf_op jit(solution)/shard_map/ppermute | solution.py:425
  50.4 18.8 %collective-permute-start.4 = (bf16[16,16,1536]{2,1,0:T(8,128)(2,1)S(1)}, bf16[16,16,1536]{2,1,0:T(8,128)(2,1)S(1)}, u32[]{:S(2)}, u32[]{:S(2)}) collective-permute-start(bf16[16,16,1536]{2,1,0:T(8,128)(2,1)S(1)} %get-tuple-element.17.own), channel_id=1, source_target_pairs={{0,32},{32,0},{1,33},{33,1},{2,34},{34,2},{3,35},{35,3},{4,36},{36... | collective-permute-start | bytes 2359304 | tf_op jit(solution)/shard_map/ppermute | solution.py:426
  69.3 19.5 %collective-permute-start.5 = (bf16[16,16,1536]{2,1,0:T(8,128)(2,1)S(1)}, bf16[16,16,1536]{2,1,0:T(8,128)(2,1)S(1)}, u32[]{:S(2)}, u32[]{:S(2)}) collective-permute-start(bf16[16,16,1536]{2,1,0:T(8,128)(2,1)S(1)} %hold.1.near), channel_id=1, source_target_pairs={{0,4},{4,0},{1,5},{5,1},{2,6},{6,2},{3,7},{7,3},{8,12},{12,8},{9,1... | collective-permute-start | bytes 2359304 | tf_op jit(solution)/shard_map/ppermute | solution.py:472

commit v12 on v11

--- a/solution.py
+++ b/solution.py
@@ -448,7 +448,7 @@
 
     summed = lax.all_to_all(partial, "x", 0, 0, tiled=True)
     mine = rows // NX
-    group = ("zh", "y", "x")
+    group = ("x", "zh", "y")
     members = NZ * NY * NX // 2
     own_mid, message = call(
         fan_kernel,

time: 123 us -> 123 us (level)
  starting transfers between devices: 6.03 us -> 7.59 us
    ppermute x1, starting transfers between devices: 2.73 us -> 4.29 us  [body(): near_mate = lax.ppermute(near, 'c', ring(1, NC))]
where the time goes in v12:
time: 123 us
  blocking collectives  105 us (85%)
  starting transfers between devices  7.59 us (6%)
  Pallas kernels  7.35 us (6%)
  waiting for transfers between devices  1.32 us (1%)
    all_to_all x1, blocking collectives, body(): got = lax.all_to_all(message, Z + ('y',), 0, 0, tiled=True)  42.5 us
    all_to_all x1, blocking collectives, body(): hidden = lax.all_to_all(message, Z + ('y', 'c', 'x'), 0, 0, tiled=True)  16 us
    all_to_all x1, blocking collectives, body(): got = lax.all_to_all(partial, group, 0, 0, tiled=True)  15.7 us
    all_to_all x1, blocking collectives, body(): got = lax.all_to_all(message, group, 0, 0, tiled=True)  15.6 us
    all_to_all x1, blocking collectives, body(): squares = lax.all_to_all(squares, 'x', 0, 0, tiled=True)  8.1 us
    all_to_all x1, blocking collectives, body(): summed = lax.all_to_all(partial, 'x', 0, 0, tiled=True)  7.21 us
    ppermute x1, starting transfers between devices, body(): near_mate = lax.ppermute(near, 'c', ring(1, NC))  4.29 us
  transfers between devices with their start and end apart: 6, of which 3 were waited for; matrix products, arithmetic and copies ran while one was open for 1% of the time, Pallas kernels for 3%

profile of v12, /device:TPU:1, one launch (start us, length us, event | category | flops | bytes accessed | tf_op | source)
XLA Modules:
  0.0 123.1 jit_solution(5215019916251583309)
XLA Ops:
  0.6 1.5 %collective-permute-start = (bf16[64,512]{1,0:T(8,128)(2,1)}, bf16[64,512]{1,0:T(8,128)(2,1)S(1)}, u32[]{:S(2)}, u32[]{:S(2)}) collective-permute-start(bf16[64,512]{1,0:T(8,128)(2,1)} %bitcast.2), channel_id=1, source_target_pairs={{0,4},{4,0},{1,5},{5,1},{2,6},{6,2},{3,7},{7,3},{8,12},{12,8},{9,1... | collective-permute-start | bytes 196616 | tf_op jit(solution)/shard_map/ppermute | solution.py:363
  2.1 0.1 collective-permute-start.1
  2.2 0.7 convert_element_type.5
  2.9 0.2 multiply_cosine_fusion
  3.1 0.1 collective-permute-done.h_mate
  3.2 0.5 collective-permute-done.1.w_mate
  3.8 0.0 copy-start.1
  3.8 1.9 %project.1 = bf16[16,16,5248]{2,1,0:T(8,128)(2,1)S(1)} custom-call(bf16[64,512]{1,0:T(8,128)(2,1)} %bitcast.3, bf16[64,512]{1,0:T(8,128)(2,1)S(1)} %collective-permute-done.h_mate, bf16[3,64,512]{2,1,0:T(8,128)(2,1)} %w_own.1, bf16[3,64,512]{2,1,0:T(8,128)(2,1)S(1)} %collective-permute-done.1.w_mate, bf16[2,64,2048]{2,1,0:T(8,128)(2,1)} %gate_up.1, ...), custom_call_target="tpu_custom_call" | custom-call | flops 134217728 | bytes 2097152 | tf_op jit(solution)/shard_map/project/pallas_call | solution.py:387
  5.7 0.0 copy-start
  5.7 42.5 %all_to_all.30.got.own = bf16[16,16,5248]{2,1,0:T(8,128)(2,1)S(1)} all-to-all(bf16[16,16,5248]{2,1,0:T(8,128)(2,1)S(1)} %project.1), channel_id=1, replica_groups=mesh['zh'=2,'zl'=2,'y'=4,'c'=2,'x'=4] {'zh','zl','y'}, dimensions={0} | all-to-all | bytes 5373952 | tf_op jit(solution)/shard_map/all_to_all | solution.py:406
  48.2 0.0 copy-start.2
  48.2 1.3 %collective-permute-start.2 = (bf16[16,16,5248]{2,1,0:T(8,128)(2,1)S(1)}, bf16[16,16,5248]{2,1,0:T(8,128)(2,1)S(1)}, u32[]{:S(2)}, u32[]{:S(2)}) collective-permute-start(bf16[16,16,5248]{2,1,0:T(8,128)(2,1)S(1)} %all_to_all.30.got.own), channel_id=1, source_target_pairs={{0,4},{4,0},{1,5},{5,1},{2,6},{6,2},{3,7},{7,3},{8,12},{12,8},{9,1... | collective-permute-start | bytes 8060936 | tf_op jit(solution)/shard_map/ppermute | solution.py:408
  49.5 0.8 collect.1
  50.3 0.1 collective-permute-start.3
  50.4 0.3 collective-permute-start.4
  50.7 8.1 %all_to_all.31.squares_in = f32[4,16,128]{2,1,0:T(8,128)S(1)} all-to-all(f32[4,16,128]{2,1,0:T(8,128)S(1)} %get-tuple-element.14), channel_id=1, replica_groups=mesh['zh'=2,'zl'=2,'y'=4,'c'=2,'x'=4] {'x'}, dimensions={0} | all-to-all | bytes 65536 | tf_op jit(solution)/shard_map/all_to_all | solution.py:427
  58.8 0.0 copy-done.1
  58.8 0.0 copy-done
  58.8 0.0 copy-done.2
  58.8 1.7 %attend.1 = (bf16[16,512]{1,0:T(8,128)(2,1)}, bf16[16,512]{1,0:T(8,128)(2,1)S(1)}) custom-call(f32[4,16,128]{2,1,0:T(8,128)S(1)} %all_to_all.31.squares_in, f32[3,16,512]{2,1,0:T(8,128)S(1)} %get-tuple-element.15.qk, f32[128,128]{1,0:T(8,128)S(1)} %pad_maximum_fusion.trig, f32[8,128]{1,0:T(8,128)S(1)} %broadcast_in_dim.2.places, f32[2,512]{1,0:T(2,128)S(1)} %copy-done.2, ...), custom_call_target="tpu_custom_call" | custom-call | flops 536870912 | bytes 8388608 | tf_op jit(solution)/shard_map/attend/pallas_call | solution.py:428
  60.5 0.0 collective-permute-done.3.after.own_mate
  60.5 0.0 collective-permute-done.2.mate
  60.5 0.7 project_out.1
  61.2 7.2 %all_to_all.32.got = f32[4,4,2048]{2,1,0:T(4,128)S(1)} all-to-all(f32[4,4,2048]{2,1,0:T(4,128)S(1)} %get-tuple-element.18), channel_id=1, replica_groups=mesh['zh'=2,'zl'=2,'y'=4,'c'=2,'x'=4] {'x'}, dimensions={0} | all-to-all | bytes 262144 | tf_op jit(solution)/shard_map/all_to_all | solution.py:449
  68.4 0.1 fan.1
  68.5 0.6 collective-permute-done.4.piece
  69.2 0.1 hold.1.near
  69.3 4.3 %collective-permute-start.5 = (bf16[16,16,1536]{2,1,0:T(8,128)(2,1)S(1)}, bf16[16,16,1536]{2,1,0:T(8,128)(2,1)S(1)}, u32[]{:S(2)}, u32[]{:S(2)}) collective-permute-start(bf16[16,16,1536]{2,1,0:T(8,128)(2,1)S(1)} %hold.1.near), channel_id=1, source_target_pairs={{0,4},{4,0},{1,5},{5,1},{2,6},{6,2},{3,7},{7,3},{8,12},{12,8},{9,1... | collective-permute-start | bytes 2359304 | tf_op jit(solution)/shard_map/ppermute | solution.py:472
  73.6 15.6 %all_to_all.33.got = bf16[32,8,1024]{2,1,0:T(8,128)(2,1)S(1)} all-to-all(bf16[32,8,1024]{2,1,0:T(8,128)(2,1)S(1)} %get-tuple-element.21), channel_id=1, replica_groups=mesh['zh'=2,'zl'=2,'y'=4,'c'=2,'x'=4] {'x','zh','y'}, dimensions={0} | all-to-all | bytes 1048576 | tf_op jit(solution)/shard_map/all_to_all | solution.py:473
  89.2 0.0 collective-permute-done.5.near_mate
  89.2 1.1 feed_forward.1
  90.3 15.7 %all_to_all.34.got = bf16[32,8,1024]{2,1,0:T(8,128)(2,1)S(1)} all-to-all(bf16[32,8,1024]{2,1,0:T(8,128)(2,1)S(1)} %feed_forward.1), channel_id=1, replica_groups=mesh['zh'=2,'zl'=2,'y'=4,'c'=2,'x'=4] {'x','zh','y'}, dimensions={0} | all-to-all | bytes 1048576 | tf_op jit(solution)/shard_map/all_to_all | solution.py:484
  105.9 0.3 finish.1
  106.2 0.1 reshape.13
  106.3 16.0 %all_to_all.35 = bf16[128,2,128]{2,1,0:T(2,128)(2,1)S(1)} all-to-all(bf16[128,2,128]{2,1,0:T(2,128)(2,1)S(1)} %reshape.13), channel_id=1, replica_groups=mesh['zh'=2,'zl'=2,'y'=4,'c'=2,'x'=4] {'zh','zl','y','c','x'}, dimensions={0} | all-to-all | bytes 131072 | tf_op jit(solution)/shard_map/all_to_all | solution.py:494
  122.3 0.1 reshape.14.got
  122.4 0.7 turn.1
  (4 shorter events, 0.0 us)
Async XLA Ops:
  0.6 2.6 %collective-permute-start = (bf16[64,512]{1,0:T(8,128)(2,1)}, bf16[64,512]{1,0:T(8,128)(2,1)S(1)}, u32[]{:S(2)}, u32[]{:S(2)}) collective-permute-start(bf16[64,512]{1,0:T(8,128)(2,1)} %bitcast.2), channel_id=1, source_target_pairs={{0,4},{4,0},{1,5},{5,1},{2,6},{6,2},{3,7},{7,3},{8,12},{12,8},{9,1... | collective-permute-start | bytes 196616 | tf_op jit(solution)/shard_map/ppermute | solution.py:363
  2.1 1.7 %collective-permute-start.1 = (bf16[3,64,512]{2,1,0:T(8,128)(2,1)}, bf16[3,64,512]{2,1,0:T(8,128)(2,1)S(1)}, u32[]{:S(2)}, u32[]{:S(2)}) collective-permute-start(bf16[3,64,512]{2,1,0:T(8,128)(2,1)} %w_own.1), channel_id=1, source_target_pairs={{0,4},{4,0},{1,5},{5,1},{2,6},{6,2},{3,7},{7,3},{8,12},{12,8},{9,1... | collective-permute-start | bytes 589832 | tf_op jit(solution)/shard_map/ppermute | solution.py:364
  3.8 55.0 %copy-start.1 = (bf16[4096,512]{1,0:T(8,128)(2,1)S(1)}, bf16[4096,512]{1,0:T(8,128)(2,1)}, u32[]{:S(2)}) copy-start(bf16[4096,512]{1,0:T(8,128)(2,1)} %values.1) | copy-start | bytes 12582916
  5.7 53.1 %copy-start = (bf16[4096,512]{1,0:T(8,128)(2,1)S(1)}, bf16[4096,512]{1,0:T(8,128)(2,1)}, u32[]{:S(2)}) copy-start(bf16[4096,512]{1,0:T(8,128)(2,1)} %keys.1) | copy-start | bytes 12582916
  48.2 10.6 %copy-start.2 = (f32[2,512]{1,0:T(2,128)S(1)}, f32[2,512]{1,0:T(2,128)}, u32[]{:S(2)}) copy-start(f32[2,512]{1,0:T(2,128)} %gains.3) | copy-start | bytes 12292
  48.2 12.3 %collective-permute-start.2 = (bf16[16,16,5248]{2,1,0:T(8,128)(2,1)S(1)}, bf16[16,16,5248]{2,1,0:T(8,128)(2,1)S(1)}, u32[]{:S(2)}, u32[]{:S(2)}) collective-permute-start(bf16[16,16,5248]{2,1,0:T(8,128)(2,1)S(1)} %all_to_all.30.got.own), channel_id=1, source_target_pairs={{0,4},{4,0},{1,5},{5,1},{2,6},{6,2},{3,7},{7,3},{8,12},{12,8},{9,1... | collective-permute-start | bytes 8060936 | tf_op jit(solution)/shard_map/ppermute | solution.py:408
  50.3 10.2 %collective-permute-start.3 = (bf16[16,16,1536]{2,1,0:T(8,128)(2,1)S(1)}, bf16[16,16,1536]{2,1,0:T(8,128)(2,1)S(1)}, u32[]{:S(2)}, u32[]{:S(2)}) collective-permute-start(bf16[16,16,1536]{2,1,0:T(8,128)(2,1)S(1)} %get-tuple-element.17.own), channel_id=1, source_target_pairs={{0,4},{4,0},{1,5},{5,1},{2,6},{6,2},{3,7},{7,3},{8,12},{12,8},{9,1... | collective-permute-start | bytes 2359304 | tf_op jit(solution)/shard_map/ppermute | solution.py:425
  50.4 18.8 %collective-permute-start.4 = (bf16[16,16,1536]{2,1,0:T(8,128)(2,1)S(1)}, bf16[16,16,1536]{2,1,0:T(8,128)(2,1)S(1)}, u32[]{:S(2)}, u32[]{:S(2)}) collective-permute-start(bf16[16,16,1536]{2,1,0:T(8,128)(2,1)S(1)} %get-tuple-element.17.own), channel_id=1, source_target_pairs={{0,32},{32,0},{1,33},{33,1},{2,34},{34,2},{3,35},{35,3},{4,36},{36... | collective-permute-start | bytes 2359304 | tf_op jit(solution)/shard_map/ppermute | solution.py:426
  69.3 19.9 %collective-permute-start.5 = (bf16[16,16,1536]{2,1,0:T(8,128)(2,1)S(1)}, bf16[16,16,1536]{2,1,0:T(8,128)(2,1)S(1)}, u32[]{:S(2)}, u32[]{:S(2)}) collective-permute-start(bf16[16,16,1536]{2,1,0:T(8,128)(2,1)S(1)} %hold.1.near), channel_id=1, source_target_pairs={{0,4},{4,0},{1,5},{5,1},{2,6},{6,2},{3,7},{7,3},{8,12},{12,8},{9,1... | collective-permute-start | bytes 2359304 | tf_op jit(solution)/shard_map/ppermute | solution.py:472
